TPU v7x, 128 devices: a whole 4x4x4 slice. The times are simulated.
128 devices in a mesh: section: 4 (over z), dp: 32 (over y, x, core).
Axes of the slice: x: 4, y: 4, z: 4, core: 2. Of those that a mesh axis runs over, the one named last changes fastest.
Arguments:
- saved: bfloat16 [4, 128, 4, 8, 384], P('section', 'dp'), may hold values from -6 to 6
- kernels: bfloat16 [4, 384, 3, 3, 384], P('section'), may hold values from -0.109375 to 0.109375
- head: bfloat16 [384, 512], replicated, may hold values from -0.3125 to 0.3125
- counts: int32 [32], P('dp'), may hold values from 1 to 4, as said below
- pairs: int32 [128], P('dp'), may hold values from 0 to 127, as said below
- valid: int32 [128], P('dp'), may hold values 0 or 1
Outputs:
- input_grads: bfloat16 [4, 128, 4, 8, 384], P('section', 'dp')
- weight_grads: float32 [4, 384, 3, 3, 384], P('section', 'dp')
- head_grad: float32 [384, 512], P('dp', 'section')
Inputs may be any that keep to these rules, and one draw needn't show every extreme that they name: Slot d * 4 + r holds a record exactly when r < counts[d]; at least one index of dp holds 4 records. pairs[pairs[i]] = i and pairs[i] != i.
All inputs are finite; a program needn't handle non-finite values. No bound on the sum of `valid` on one device may be relied on, other than what follows from the above.
Results may differ from a plain program's by a relative error of at most 0.012.
Values may be sent and summed in bfloat16 or wider, within the bound.
No kernel may reach another device: no remote copies, remote signals or barrier semaphores. Data moves between devices by JAX's collectives and lax.ppermute only.
A program may use at most 64 MiB of HBM per device.

v0:
```python
import jax
import jax.numpy as jnp
from jax import lax
from jax.sharding import PartitionSpec as P

tau_value = 0.2
loss_scale = 32.0
norm_eps = 1e-06


def from_root(value, axis, source):
    kept = jnp.where(lax.axis_index(axis) == source, value, 0).astype(value.dtype)
    return lax.psum(kept, axis)


def passed_along(value, axis, steps):
    count = lax.axis_size(axis)
    initial, last = (max(0, -steps), min(count, count - steps))
    return lax.ppermute(value, axis, [(source, source + steps) for source in range(initial, last)])


def conv_apply(inputs, kernel):
    return lax.conv_general_dilated(
        inputs,
        kernel,
        (1, 1),
        "SAME",
        dimension_numbers=("NHWC", "IHWO", "NHWC"),
        preferred_element_type=jnp.float32,
    )


def conv_back(grads, kernel):
    return lax.conv_general_dilated(
        grads,
        jnp.flip(kernel, (1, 2)),
        (1, 1),
        "SAME",
        dimension_numbers=("NHWC", "OHWI", "NHWC"),
        preferred_element_type=jnp.float32,
    )


def kernel_grad(inputs, grads):
    return lax.conv_general_dilated(
        inputs,
        grads,
        (1, 1),
        ((1, 1), (1, 1)),
        dimension_numbers=("CHWN", "IHWO", "NHWC"),
        preferred_element_type=jnp.float32,
    )


def per_device(saved, kernels, head, counts, pairs, valid):
    inputs = saved[0]
    kernel = kernels[0]
    cap = inputs.shape[0]
    npos = inputs.shape[1] * inputs.shape[2]
    sections = lax.axis_size("section")
    section = lax.axis_index("section")
    rank = lax.axis_index("dp")
    slots = jnp.arange(cap, dtype=jnp.int32)
    mine = rank * cap + slots
    live = jnp.where((slots < counts[0]) & (valid == 1), 1.0, 0.0).astype(jnp.float32)
    live_b = live.astype(jnp.bfloat16)
    pre = conv_apply(inputs, kernel)
    sigma = jax.nn.sigmoid(pre)
    slope = sigma * (1.0 + pre * (1.0 - sigma))
    pooled = jnp.mean(inputs.astype(jnp.float32) + pre * sigma, axis=(1, 2)).astype(jnp.bfloat16)
    pooled = from_root(pooled, "section", sections - 1)
    proj = jnp.dot(pooled, head, preferred_element_type=jnp.float32)
    inv = lax.rsqrt(jnp.sum(proj * proj, axis=1, keepdims=True) + norm_eps)
    unit = proj * inv
    unit_b = unit.astype(jnp.bfloat16)

    def exp_scores(others):
        ids = jnp.arange(others.shape[0], dtype=jnp.int32)
        scores = (
            lax.dot_general(
                unit_b, others, (((1,), (1,)), ((), ())), preferred_element_type=jnp.float32
            )
            / tau_value
        )
        return (jnp.where(mine[:, None] != ids[None, :], jnp.exp(scores), 0.0), ids)

    start_sums = (jnp.zeros((cap,), jnp.float32), jnp.zeros((cap,), jnp.float32))
    others = lax.all_gather(unit_b, "dp", axis=0, tiled=True)
    flags = lax.all_gather(live_b, "dp", axis=0, tiled=True)
    expo, ids = exp_scores(others)
    flag_f = flags.astype(jnp.float32)
    total = start_sums[0] + jnp.sum(expo * flag_f[None, :], axis=1)
    mate = jnp.sum(jnp.where(pairs[:, None] == ids[None, :], flag_f[None, :], 0.0), axis=1)
    total, mate = (total, mate)
    share = live * mate
    coef = lax.optimization_barrier((share / total).astype(jnp.bfloat16))
    coef_own = coef.astype(jnp.float32)
    start_grad = jnp.zeros(unit.shape, jnp.float32)
    others = lax.all_gather(unit_b, "dp", axis=0, tiled=True)
    flags = lax.all_gather(live_b, "dp", axis=0, tiled=True)
    coefs = lax.all_gather(coef, "dp", axis=0, tiled=True)
    expo, ids = exp_scores(others)
    flag_f = flags.astype(jnp.float32)
    coef_f = coefs.astype(jnp.float32)
    mixing = expo * (
        coef_own[:, None] * flag_f[None, :] + coef_f[None, :] * live[:, None]
    ) - 2.0 * jnp.where(pairs[:, None] == ids[None, :], share[:, None], 0.0)
    dunit = start_grad + jnp.dot(
        mixing.astype(jnp.bfloat16), others, preferred_element_type=jnp.float32
    )
    dunit = dunit * (loss_scale / tau_value)
    along = jnp.sum(unit * dunit, axis=1, keepdims=True)
    dproj = ((dunit - unit * along) * inv).astype(jnp.bfloat16)
    col_width = head.shape[1] // sections
    dproj_cols = lax.dynamic_slice_in_dim(dproj, section * col_width, col_width, 1)
    head_term = lax.dot_general(
        pooled, dproj_cols, (((0,), (0,)), ((), ())), preferred_element_type=jnp.float32
    )
    head_grad = lax.psum_scatter(head_term, "dp", scatter_dimension=0, tiled=True)
    dpooled = lax.dot_general(
        dproj, head, (((1,), (1,)), ((), ())), preferred_element_type=jnp.float32
    ).astype(jnp.bfloat16)
    top = (dpooled.astype(jnp.float32) / npos).astype(jnp.bfloat16)
    cotan = jnp.broadcast_to(top[:, None, None, :], inputs.shape)

    def backward(cot_part, slope_part):
        dpre = (cot_part.astype(jnp.float32) * slope_part).astype(jnp.bfloat16)
        below = (cot_part.astype(jnp.float32) + conv_back(dpre, kernel)).astype(jnp.bfloat16)
        return (below, dpre)

    empty = jnp.zeros(inputs.shape, jnp.bfloat16)
    dx_out = empty
    du_out = empty
    for step in range(sections):
        active = section == sections - 1 - step
        dx_new, du_new = lax.cond(
            active, backward, lambda first, second: (empty, empty), cotan, slope
        )
        dx_out = jnp.where(active, dx_new, dx_out)
        du_out = jnp.where(active, du_new, du_out)
        if step + 1 < sections:
            arrived = passed_along(dx_new, "section", -1)
            cotan = jnp.where(section == sections - 2 - step, arrived, cotan)
    wgrad = lax.psum_scatter(kernel_grad(inputs, du_out), "dp", scatter_dimension=0, tiled=True)
    return (dx_out[None], wgrad[None], head_grad)


def solution(mesh):
    return jax.shard_map(
        per_device,
        mesh=mesh,
        in_specs=(
            P("section", "dp", None, None, None),
            P("section", None, None, None, None),
            P(),
            P("dp"),
            P("dp"),
            P("dp"),
        ),
        out_specs=(
            P("section", "dp", None, None, None),
            P("section", "dp", None, None, None),
            P("dp", "section"),
        ),
        check_vma=False,
    )
```

profile of v0, /device:TPU:1, one launch (start us, length us, event | category | flops | bytes accessed | tf_op | source)
XLA Modules:
  0.0 329.1 jit_solution(7515257159436532148)
XLA Ops:
  7.2 0.0 copy-start
  7.2 0.0 copy-start.2
  7.2 0.0 all-reduce.7.cloned.1.call-start
  8.0 1.4 fusion.38
  10.0 0.7 fusion.37
  10.7 0.2 dynamic-update-slice
  10.9 63.8 %all-reduce = bf16[128]{0:T(256)(128)(2,1)S(1)} all-reduce(bf16[128]{0:T(256)(128)(2,1)S(1)} %dynamic-update-slice), channel_id=1, replica_groups=mesh['section'=4,'dp'=32] {'dp'}, use_global_device_ids=true, to_apply=%add | all-reduce | flops 128 | bytes 512
  74.7 2.8 add_multiply_fusion
  77.5 9.8 %psum.7 = bf16[4,384]{1,0:T(4,128)(2,1)S(1)} all-reduce(bf16[4,384]{1,0:T(4,128)(2,1)S(1)} %fusion.21), channel_id=1, replica_groups=mesh['section'=4,'dp'=32] {'section'}, use_global_device_ids=true, to_apply=%region_1.2 | all-reduce | flops 1536 | bytes 6144 | tf_op jit(solution)/shard_map/psum | solution.py:13
  87.2 0.0 copy-done
  87.2 0.3 multiply_reduce_fusion.1
  87.5 0.1 fusion.36
  87.6 27.8 %all-gather = bf16[32,4,512]{2,1,0:T(4,128)(2,1)S(1)} all-gather(bf16[1,4,512]{2,1,0:T(4,128)(2,1)S(1)} %fusion.36), channel_id=1, replica_groups=mesh['section'=4,'dp'=32] {'dp'}, dimensions={0}, use_global_device_ids=true | all-gather | bytes 135168 | tf_op jit(solution)/shard_map/all_gather | solution.py:99
  115.4 0.0 copy-done.2
  115.4 0.3 multiply_reduce_fusion.2
  115.8 0.2 dynamic-update-slice.1
  116.0 62.4 %all-reduce.1 = bf16[128]{0:T(256)(128)(2,1)S(1)} all-reduce(bf16[128]{0:T(256)(128)(2,1)S(1)} %dynamic-update-slice.1), channel_id=1, replica_groups=mesh['section'=4,'dp'=32] {'dp'}, use_global_device_ids=true, to_apply=%add.1 | all-reduce | flops 128 | bytes 512
  178.4 0.3 multiply_reduce_fusion
  178.7 0.1 multiply_convert_fusion
  178.8 0.2 fusion.11
  179.1 0.1 conditional.4
  179.2 1.3 collective-permute-start
  180.5 4.1 %collective-permute-done = bf16[4,4,8,384]{3,2,1,0:T(8,128)(2,1)S(1)} collective-permute-done((bf16[4,4,8,384]{3,2,1,0:T(8,128)(2,1)S(1)}, bf16[4,4,8,384]{3,2,1,0:T(8,128)(2,1)S(1)}, u32[]{:S(2)}, u32[]{:S(2)}) %collective-permute-start) | collective-permute-done | bytes 98336 | tf_op jit(solution)/shard_map/ppermute | solution.py:19
  184.5 0.1 conditional.5
  184.6 1.3 collective-permute-start.1
  185.9 4.1 %collective-permute-done.1 = bf16[4,4,8,384]{3,2,1,0:T(8,128)(2,1)S(1)} collective-permute-done((bf16[4,4,8,384]{3,2,1,0:T(8,128)(2,1)S(1)}, bf16[4,4,8,384]{3,2,1,0:T(8,128)(2,1)S(1)}, u32[]{:S(2)}, u32[]{:S(2)}) %collective-permute-start.1) | collective-permute-done | bytes 98336 | tf_op jit(solution)/shard_map/ppermute | solution.py:19
  190.0 0.7 conditional.6
  190.0 0.7 broadcast_in_dim.41
  190.7 0.0 copy-start.1
  190.7 1.4 collective-permute-start.2
  192.1 9.4 %collective-permute-done.2 = bf16[4,4,8,384]{3,0,2,1:T(4,128)(2,1)S(1)} collective-permute-done((bf16[4,4,8,384]{3,0,2,1:T(4,128)(2,1)}, bf16[4,4,8,384]{3,0,2,1:T(4,128)(2,1)S(1)}, u32[]{:S(2)}, u32[]{:S(2)}) %collective-permute-start.2) | collective-permute-done | bytes 98336 | tf_op jit(solution)/shard_map/ppermute | solution.py:19
  201.5 3.0 conditional.7
  201.5 0.1 fusion.8
  201.6 2.9 fusion.7
  204.6 0.0 copy-done.1
  204.6 3.4 %fusion.14 = f32[384,3,3,384]{3,0,2,1:T(8,128)} fusion(bf16[4,4,8,384]{3,2,1,0:T(8,128)(2,1)S(1)} %select_select_fusion, bf16[1,4,4,8,384]{4,3,2,1,0:T(8,128)(2,1)S(1)} %copy-done.1), kind=kOutput, calls=%fused_computation.29 | convolution fusion | flops 259522560 | bytes 5505024 | tf_op jit(solution)/shard_map/conv_general_dilated | solution.py:45
  207.9 0.0 all-reduce.7.cloned.1.call-update
  207.9 0.2 fusion.22
  208.2 69.7 %fusion = f32[16,128]{1,0:T(8,128)S(1)} fusion(f32[384,128]{1,0:T(8,128)S(1)} %fusion.22), kind=kCustom, calls=%all-reduce-scatter | all-reduce-scatter fusion | flops 65537 | bytes 205312
  277.9 1.3 collective-permute-start.9
  279.2 1.3 collective-permute-start.8
  280.5 1.3 collective-permute-start.10
  281.8 1.3 collective-permute-start.7
  283.1 8.9 %collective-permute-start.6 = (f32[16,128]{1,0:T(8,128)S(1)}, f32[16,128]{1,0:T(8,128)S(1)}, u32[]{:S(2)}, u32[]{:S(2)}) collective-permute-start(f32[16,128]{1,0:T(8,128)S(1)} %fusion), channel_id=1, source_target_pairs={{0,4},{1,5},{2,6},{3,7},{4,8},{5,9},{6,10},{7,11},{8,12},{9,13},{1... | collective-permute-start | bytes 24584
  292.0 0.0 collective-permute-done.10
  292.0 1.3 collective-permute-start.5
  293.3 0.0 collective-permute-done.9
  293.4 4.0 %collective-permute-start.4 = (f32[16,128]{1,0:T(8,128)S(1)}, f32[16,128]{1,0:T(8,128)S(1)}, u32[]{:S(2)}, u32[]{:S(2)}) collective-permute-start(f32[16,128]{1,0:T(8,128)S(1)} %fusion), channel_id=1, source_target_pairs={{0,2},{1,3},{2,4},{3,5},{4,6},{5,7},{6,8},{7,9},{8,10},{9,11},{10,... | collective-permute-start | bytes 24584
  297.4 0.0 collective-permute-done.8
  297.4 2.2 collective-permute-start.3
  300.7 0.0 collective-permute-done.7
  300.7 0.0 collective-permute-done.6
  300.8 0.0 collective-permute-done.5
  300.8 0.0 collective-permute-done.4
  300.8 0.0 collective-permute-done.3
  300.8 0.9 concatenate
  301.7 0.6 constant_dynamic-slice_fusion
  302.3 0.7 select_bitcast_fusion
  303.0 17.4 %all-reduce.7.cloned.1.call-done = f32[384,3,3,384]{3,0,2,1:T(8,128)} async-done(((f32[384,3,3,384]{3,0,2,1:T(8,128)}), f32[384,3,3,384]{3,0,2,1:T(8,128)}) %all-reduce.7.cloned.1.call-update) | async-done | bytes 5308432
  320.4 1.0 dynamic-slice_bitcast_fusion
  321.4 0.8 copy.42
  (23 shorter events, 0.3 us)
Async XLA Ops:
  7.2 80.1 %copy-start = (bf16[384,512]{1,0:T(8,128)(2,1)S(1)}, bf16[384,512]{1,0:T(8,128)(2,1)}, u32[]{:S(2)}) copy-start(bf16[384,512]{1,0:T(8,128)(2,1)} %param.16) | copy-start | bytes 1179652
  7.2 108.2 %copy-start.2 = (s32[4]{0:T(128)S(1)}, s32[4]{0:T(128)}, u32[]{:S(2)}) copy-start(s32[4]{0:T(128)} %param.18) | copy-start | bytes 52
  7.2 313.3 %all-reduce.7.cloned.1.call-start = ((), (), s32[]{:S(2)}) async-start(), calls=%async_computation | async-start | bytes 10616832
  179.2 5.4 %collective-permute-start = (bf16[4,4,8,384]{3,2,1,0:T(8,128)(2,1)S(1)}, bf16[4,4,8,384]{3,2,1,0:T(8,128)(2,1)S(1)}, u32[]{:S(2)}, u32[]{:S(2)}) collective-permute-start(bf16[4,4,8,384]{3,2,1,0:T(8,128)(2,1)S(1)} %get-tuple-element.97), channel_id=1, source_target_pairs={{32,0},{64,32},{96,64},{33,1},{65,33},{97,65},{34,2},{66,34},{98,6... | collective-permute-start | bytes 294920 | tf_op jit(solution)/shard_map/ppermute | solution.py:19
  184.6 5.4 %collective-permute-start.1 = (bf16[4,4,8,384]{3,2,1,0:T(8,128)(2,1)S(1)}, bf16[4,4,8,384]{3,2,1,0:T(8,128)(2,1)S(1)}, u32[]{:S(2)}, u32[]{:S(2)}) collective-permute-start(bf16[4,4,8,384]{3,2,1,0:T(8,128)(2,1)S(1)} %get-tuple-element.99), channel_id=1, source_target_pairs={{32,0},{64,32},{96,64},{33,1},{65,33},{97,65},{34,2},{66,34},{98,6... | collective-permute-start | bytes 294920 | tf_op jit(solution)/shard_map/ppermute | solution.py:19
  190.7 13.8 %copy-start.1 = (bf16[1,4,4,8,384]{4,3,2,1,0:T(8,128)(2,1)S(1)}, bf16[1,4,4,8,384]{4,3,2,1,0:T(8,128)(2,1)}, u32[]{:S(2)}) copy-start(bf16[1,4,4,8,384]{4,3,2,1,0:T(8,128)(2,1)} %param.14) | copy-start | bytes 294916
  190.7 10.8 %collective-permute-start.2 = (bf16[4,4,8,384]{3,0,2,1:T(4,128)(2,1)}, bf16[4,4,8,384]{3,0,2,1:T(4,128)(2,1)S(1)}, u32[]{:S(2)}, u32[]{:S(2)}) collective-permute-start(bf16[4,4,8,384]{3,0,2,1:T(4,128)(2,1)} %get-tuple-element.57), channel_id=1, source_target_pairs={{32,0},{64,32},{96,64},{33,1},{65,33},{97,65},{34,2},{66,34},{98,6... | collective-permute-start | bytes 294920 | tf_op jit(solution)/shard_map/ppermute | solution.py:19
  277.9 15.5 %collective-permute-start.9 = (f32[16,128]{1,0:T(8,128)S(1)}, f32[16,128]{1,0:T(8,128)S(1)}, u32[]{:S(2)}, u32[]{:S(2)}) collective-permute-start(f32[16,128]{1,0:T(8,128)S(1)} %fusion), channel_id=1, source_target_pairs={{0,7},{1,8},{2,9},{3,10},{4,11},{5,12},{6,13},{7,14},{8,15},{9,16}... | collective-permute-start | bytes 24584
  279.2 18.2 %collective-permute-start.8 = (f32[16,128]{1,0:T(8,128)S(1)}, f32[16,128]{1,0:T(8,128)S(1)}, u32[]{:S(2)}, u32[]{:S(2)}) collective-permute-start(f32[16,128]{1,0:T(8,128)S(1)} %fusion), channel_id=1, source_target_pairs={{0,6},{1,7},{2,8},{3,9},{4,10},{5,11},{6,12},{7,13},{8,14},{9,15},... | collective-permute-start | bytes 24584
  280.5 11.5 %collective-permute-start.10 = (f32[12,128]{1,0:T(8,128)S(1)}, f32[12,128]{1,0:T(8,128)S(1)}, u32[]{:S(2)}, u32[]{:S(2)}) collective-permute-start(f32[12,128]{1,0:T(8,128)S(1)} %slice), channel_id=1, source_target_pairs={{0,8},{1,9},{2,10},{3,11},{4,12},{5,13},{6,14},{7,15},{8,16},{9,17... | collective-permute-start | bytes 18440
  281.8 19.0 %collective-permute-start.7 = (f32[16,128]{1,0:T(8,128)S(1)}, f32[16,128]{1,0:T(8,128)S(1)}, u32[]{:S(2)}, u32[]{:S(2)}) collective-permute-start(f32[16,128]{1,0:T(8,128)S(1)} %fusion), channel_id=1, source_target_pairs={{0,5},{1,6},{2,7},{3,8},{4,9},{5,10},{6,11},{7,12},{8,13},{9,14},{... | collective-permute-start | bytes 24584
  283.1 17.7 %collective-permute-start.6 = (f32[16,128]{1,0:T(8,128)S(1)}, f32[16,128]{1,0:T(8,128)S(1)}, u32[]{:S(2)}, u32[]{:S(2)}) collective-permute-start(f32[16,128]{1,0:T(8,128)S(1)} %fusion), channel_id=1, source_target_pairs={{0,4},{1,5},{2,6},{3,7},{4,8},{5,9},{6,10},{7,11},{8,12},{9,13},{1... | collective-permute-start | bytes 24584
  292.0 8.7 %collective-permute-start.5 = (f32[16,128]{1,0:T(8,128)S(1)}, f32[16,128]{1,0:T(8,128)S(1)}, u32[]{:S(2)}, u32[]{:S(2)}) collective-permute-start(f32[16,128]{1,0:T(8,128)S(1)} %fusion), channel_id=1, source_target_pairs={{0,3},{1,4},{2,5},{3,6},{4,7},{5,8},{6,9},{7,10},{8,11},{9,12},{10... | collective-permute-start | bytes 24584
  293.4 7.4 %collective-permute-start.4 = (f32[16,128]{1,0:T(8,128)S(1)}, f32[16,128]{1,0:T(8,128)S(1)}, u32[]{:S(2)}, u32[]{:S(2)}) collective-permute-start(f32[16,128]{1,0:T(8,128)S(1)} %fusion), channel_id=1, source_target_pairs={{0,2},{1,3},{2,4},{3,5},{4,6},{5,7},{6,8},{7,9},{8,10},{9,11},{10,... | collective-permute-start | bytes 24584
  297.4 3.4 %collective-permute-start.3 = (f32[16,128]{1,0:T(8,128)S(1)}, f32[16,128]{1,0:T(8,128)S(1)}, u32[]{:S(2)}, u32[]{:S(2)}) collective-permute-start(f32[16,128]{1,0:T(8,128)S(1)} %fusion), channel_id=1, source_target_pairs={{0,1},{1,2},{2,3},{3,4},{4,5},{5,6},{6,7},{7,8},{8,9},{9,10},{10,1... | collective-permute-start | bytes 24584
Sparse Core Ops, SparseCore 0:
  208.1 112.3 all-reduce.6
where the time goes:
time: 330 us; the launch traced here: 329 us
  blocking collectives  233 us (71%)
  waiting for transfers between devices  34.9 us (11%)
  starting transfers between devices  25.6 us (8%)
  between operations  16.9 us (5%)
  matrix products  10.3 us (3%)
  local copies, waits for them, and re-layouts  6.07 us (2%)
    unnamed x3, blocking collectives  196 us
    all_gather x1, blocking collectives, per_device(): others = lax.all_gather(unit_b, 'dp', axis=0, tiled=True)  27.8 us
    unnamed x9, starting transfers between devices  21.6 us
    unnamed x10, waiting for transfers between devices  17.5 us
    ppermute x3, waiting for transfers between devices, passed_along(): lax.ppermute(value, axis, [(source, source + steps) for source in range(i...  17.5 us
    psum x1, blocking collectives, from_root(): return lax.psum(kept, axis)  9.76 us
  transfers between devices with their start and end apart: 12, of which 4 were waited for; matrix products, arithmetic and copies ran while one was open for 22% of the time, Pallas kernels for 0%

commit v1 on v0

v1 whole, which is shorter than its diff:
```python
import functools

import jax
import jax.numpy as jnp
from jax import lax
from jax.experimental import pallas as pl
from jax.experimental.pallas import tpu as pltpu
from jax.sharding import PartitionSpec as P

tau_value = 0.2
loss_scale = 32.0
norm_eps = 1e-06
VMEM = pltpu.VMEM
SMEM = pltpu.SMEM
ANY = pl.ANY
f32 = jnp.float32
bf16 = jnp.bfloat16
NN = (((1,), (0,)), ((), ()))
NT = (((1,), (1,)), ((), ()))

ROWS, CELLS, CH, EMB = 128, 32, 384, 512
MSG = 144


def mm(a, b, dims=NN):
    return lax.dot_general(a, b, dims, preferred_element_type=f32)


def row_iota(shape):
    return lax.broadcasted_iota(jnp.int32, shape, 0)


def col_iota(shape):
    return lax.broadcasted_iota(jnp.int32, shape, 1)


def position():
    rank = lax.axis_index("dp")
    return lax.axis_index("section"), rank, (rank >> 3), ((rank >> 1) & 3), (rank & 1)


def column_shifts(v):
    pw = row_iota((ROWS, 1)) & 7
    left = jnp.where(pw > 0, pltpu.roll(v, 1, 0), 0.0)
    right = jnp.where(pw < 7, pltpu.roll(v, ROWS - 1, 0), 0.0)
    return left, v, right


def row_shift(v, dh):
    if dh == 0:
        return v
    v = v.reshape(4, CELLS, CH)
    zero = jnp.zeros((4, 8, CH), v.dtype)
    if dh > 0:
        v = jnp.concatenate([v[:, 8:], zero], axis=1)
    else:
        v = jnp.concatenate([zero, v[:, :24]], axis=1)
    return v.reshape(ROWS, CH)


def weight_copies(w_hbm, w, sem):
    return [pltpu.make_async_copy(w_hbm.at[kh], w.at[kh], sem.at[kh]) for kh in range(3)]


def conv_back(dpre, w, copies):
    cols = column_shifts(dpre)
    total = None
    for kh in range(3):
        lhs = jnp.concatenate(
            [row_shift(cols[2 - kw], 1 - kh).astype(bf16) for kw in range(3)], axis=1
        )
        copies[kh].wait()
        rhs = jnp.concatenate([w[kh, kw] for kw in range(3)], axis=1)
        part = mm(lhs, rhs, NT)
        total = part if total is None else total + part
    return total


def forward_kernel(saved, w_hbm, counts, pairs, valid, slope, message, w, sem):
    copies = weight_copies(w_hbm, w, sem)
    for copy in copies:
        copy.start()
    v = saved[...].astype(f32)
    cols = column_shifts(v)
    pre = None
    for kh in range(3):
        lhs = jnp.concatenate(
            [row_shift(cols[kw], kh - 1).astype(bf16) for kw in range(3)], axis=1
        )
        copies[kh].wait()
        part = mm(lhs, w[kh].reshape(3 * CH, CH))
        pre = part if pre is None else pre + part
    sigma = jax.nn.sigmoid(pre)
    slope[...] = sigma * (1.0 + pre * (1.0 - sigma))
    feature = (v + pre * sigma).reshape(4, CELLS, CH)
    pooled = jnp.sum(feature, axis=1) / CELLS
    at = (row_iota((4, 128)), col_iota((4, 128)))
    extra = jnp.zeros((4, 128), f32)
    for slot in range(4):
        alive = jnp.logical_and(slot < counts[0], valid[slot] == 1)
        here = at[0] == slot
        extra = jnp.where(
            jnp.logical_and(here, at[1] == 0), jnp.where(alive, 1.0, 0.0).astype(f32), extra
        )
        extra = jnp.where(
            jnp.logical_and(here, at[1] == 1), pairs[slot].astype(f32), extra
        )
    packed = jnp.concatenate(
        [pooled[:, :256], jnp.concatenate([pooled[:, 256:], extra], axis=1)], axis=0
    )
    pair = jnp.concatenate([packed, packed], axis=0).astype(bf16)
    for at_row in range(0, 256, 16):
        message[at_row : at_row + 16, :] = pair


def contrast(gathered, head, rank):
    slot = row_iota((128, 256))
    lane = col_iota((128, 256))
    home = ((slot >> 2) << 3) + (slot & 3)
    first = mm(jnp.where(lane == home, 1.0, 0.0).astype(bf16), gathered)
    second = mm(jnp.where(lane == home + 4, 1.0, 0.0).astype(bf16), gathered)
    pooled = jnp.concatenate([first, second[:, :128]], axis=1).astype(bf16)
    live = second[:, 128:129]
    pairs = second[:, 129:130]
    proj = mm(pooled, head)
    inv = lax.rsqrt(jnp.sum(proj * proj, axis=1, keepdims=True) + norm_eps)
    unit = proj * inv
    unit_b = unit.astype(bf16)
    i = row_iota((128, 128))
    j = col_iota((128, 128))
    same = i == j

    def across(column):
        return jnp.sum(jnp.where(same, column, 0.0), axis=0, keepdims=True)

    expo = jnp.where(same, 0.0, jnp.exp(mm(unit_b, unit_b, NT) / tau_value))
    mate = pairs == j.astype(f32)
    live_row = across(live)
    total = jnp.sum(expo * live_row, axis=1, keepdims=True)
    share = live * jnp.sum(jnp.where(mate, live_row, 0.0), axis=1, keepdims=True)
    coef = (share / total).astype(bf16).astype(f32)
    coef_row = across(coef)
    mixing = expo * (coef * live_row + coef_row * live) - 2.0 * jnp.where(mate, share, 0.0)
    dunit = mm(mixing.astype(bf16), unit_b) * (loss_scale / tau_value)
    along = jnp.sum(unit * dunit, axis=1, keepdims=True)
    dproj = ((dunit - unit * along) * inv).astype(bf16)
    own = jnp.where(
        col_iota((16, 128)) == row_iota((16, 128)) + 4 * rank, 1.0, 0.0
    ).astype(bf16)
    dproj_own = mm(own, dproj).astype(bf16)
    dpooled = mm(dproj_own, head, NT).astype(bf16)
    mine = jnp.where(
        col_iota((16, CH)) == row_iota((16, CH)) + 12 * rank, 1.0, 0.0
    ).astype(bf16)
    pooled_mine = mm(mine, pooled, NT).astype(bf16)
    return dpooled[:4].astype(f32), mm(pooled_mine, dproj)


def top_kernel(gathered, head, slope, w_hbm, message, dpre_out, head_out, w, sem):
    section, rank, _, _, _ = position()

    @pl.when(section == 3)
    def _():
        copies = weight_copies(w_hbm, w, sem)
        for copy in copies:
            copy.start()
        dpooled, head_grad = contrast(gathered[...], head[...], rank)
        top = (dpooled / CELLS).astype(bf16).astype(f32)
        cot = jnp.broadcast_to(top[:, None, :], (4, CELLS, CH)).reshape(ROWS, CH)
        dpre = (cot * slope[...]).astype(bf16)
        dpre_out[...] = dpre
        head_out[...] = head_grad[:, 384:]
        message[128:, :] = head_grad[:, :384].astype(bf16)
        below = cot + conv_back(dpre.astype(f32), w, copies)
        message[:128, :] = below.astype(bf16)


def relay_kernel(active, arrived, slope, w_hbm, message, dpre_out, w, sem):
    @pl.when(lax.axis_index("section") == active)
    def _():
        copies = weight_copies(w_hbm, w, sem)
        for copy in copies:
            copy.start()
        cot = arrived[:128, :].astype(f32)
        dpre = (cot * slope[...]).astype(bf16)
        dpre_out[...] = dpre
        message[128:, :] = arrived[128:, :]
        below = cot + conv_back(dpre.astype(f32), w, copies)
        message[:128, :] = below.astype(bf16)


def bottom_kernel(arrived, slope, dpre3, dpre2, dpre1, dpre_out):
    section = lax.axis_index("section")
    for at, held in ((3, dpre3), (2, dpre2), (1, dpre1)):

        @pl.when(section == at)
        def _():
            pltpu.sync_copy(held, dpre_out)

    @pl.when(section == 0)
    def _():
        dpre_out[...] = (arrived[:128, :].astype(f32) * slope[...]).astype(bf16)


def last_kernel(arrived, dpre, w_hbm, head3, msg3, msg2, msg1, grads, head_out, w, held, sem):
    section = lax.axis_index("section")

    @pl.when(section == 3)
    def _():
        pltpu.sync_copy(msg3.at[pl.ds(0, 128)], grads)
        head_out[...] = head3[:12, :]

    for at, sent in ((2, msg2), (1, msg1)):

        @pl.when(section == at)
        def _():
            pltpu.sync_copy(sent.at[pl.ds(0, 128)], grads)
            pltpu.sync_copy(sent.at[pl.ds(128, 16)], held)
            head_out[...] = held[:, at * 128 : at * 128 + 128].astype(f32)[:12]

    @pl.when(section == 0)
    def _():
        copies = weight_copies(w_hbm, w, sem)
        for copy in copies:
            copy.start()
        below = arrived[:128, :].astype(f32) + conv_back(dpre[...].astype(f32), w, copies)
        grads[...] = below.astype(bf16)
        head_out[...] = arrived[128:, :128].astype(f32)[:12]


def split_kernel(saved, order, out0, out1, out2, out3):
    _, _, y, x, c = position()
    m = row_iota((CH, 1))
    q = (m * 43691) >> 19
    i = m - 12 * q
    channel = (y ^ (q & 3)) * 96 + (x ^ (q >> 3)) * 24 + (c ^ ((q >> 2) & 1)) * 12 + i
    pick = jnp.where(col_iota((CH, CH)) == channel, 1.0, 0.0).astype(bf16)
    turned = mm(pick, saved[...], NT).astype(bf16)
    for k, out in enumerate((out0, out1, out2, out3)):
        out[...] = turned[96 * k : 96 * k + 96]


def stack_kernel(*refs):
    near, far, out, scratch = refs[:4], refs[4:8], refs[8], refs[9]
    r = col_iota((48, 128))
    ph, pw = (r >> 3) & 3, r & 7
    for g in range(8):
        held = near[g][0:48, :] if g < 4 else far[g - 4][48:96, :]
        v = held.astype(f32)
        for tap in range(9):
            dh, dw = tap // 3 - 1, tap % 3 - 1
            shift = (-(8 * dh + dw)) % 128
            moved = pltpu.roll(v, shift, 1) if shift else v
            inside = (ph + dh >= 0) & (ph + dh < 4) & (pw + dw >= 0) & (pw + dw < 8)
            moved = jnp.where(inside, moved, 0.0)
            scratch[48 * tap : 48 * tap + 48, 128 * g : 128 * g + 128] = moved.astype(bf16)
    m = row_iota((448, 1))
    j = (m * 37450) >> 22
    rest = m - 112 * j
    i = (rest * 7282) >> 16
    source = jnp.where(rest < 108, (rest - 9 * i) * 48 + j * 12 + i, -1)
    pick = jnp.where(col_iota((448, 432)) == source, 1.0, 0.0).astype(bf16)
    out[...] = mm(pick, scratch[...]).astype(bf16)


def wgrad_kernel(stack, *refs):
    grads, outs = refs[:8], refs[8:]
    rows = jnp.concatenate([g[...] for g in grads], axis=0)
    total = mm(stack[...], rows)
    outs[0][...] = total[:112]
    for k in range(1, 4):
        outs[k][...] = total[112 * k : 112 * k + 112].astype(bf16)


def sum_kernel(own, part1, part2, part3, out):
    total = own[...] + part1[...].astype(f32)
    total = total + part2[...].astype(f32)
    total = total + part3[...].astype(f32)
    out[...] = total[:108].reshape(108, 1, CH)


def call(kernel, name, ins, outs, scratch=()):
    return pl.pallas_call(
        kernel,
        out_shape=outs,
        in_specs=[pl.BlockSpec(memory_space=space) for space in ins],
        out_specs=jax.tree.map(lambda _: pl.BlockSpec(memory_space=VMEM), outs),
        scratch_shapes=list(scratch),
        name=name,
    )


def sds(shape, dtype):
    return jax.ShapeDtypeStruct(shape, dtype)


def per_device(saved, kernels, head, counts, pairs, valid):
    ranks = lax.axis_size("dp")
    rows = saved.reshape(ROWS, CH)
    w_hbm = jnp.transpose(kernels[0], (1, 2, 0, 3))
    weights = [VMEM((3, 3, CH, CH), bf16), pltpu.SemaphoreType.DMA((3,))]
    act = sds((ROWS, CH), bf16)
    msg = sds((MSG, CH), bf16)

    def swap(value, bits):
        return lax.ppermute(value, "dp", [(d, d ^ bits) for d in range(ranks)])

    def relay(value, pairs_of):
        both = [(a, b) for a, b in pairs_of] + [(b, a) for a, b in pairs_of]
        return lax.ppermute(value, "section", both)

    slope, announce = call(
        forward_kernel,
        "forward",
        [VMEM, ANY, SMEM, SMEM, SMEM],
        (sds((ROWS, CH), f32), sds((256, 256), bf16)),
        weights,
    )(rows, w_hbm, counts, pairs, valid)
    gathered = lax.all_to_all(announce.reshape(32, 8, 256), "dp", 0, 0, tiled=True)
    msg3, dpre3, head3 = call(
        top_kernel,
        "top",
        [VMEM, VMEM, VMEM, ANY],
        (msg, act, sds((16, 128), f32)),
        weights,
    )(gathered.reshape(256, 256), head, slope, w_hbm)

    def relay_step(active, arrived):
        return call(
            functools.partial(relay_kernel, active),
            f"relay{active}",
            [VMEM, VMEM, ANY],
            (msg, act),
            weights,
        )(arrived, slope, w_hbm)

    arrived = relay(msg3, [(3, 2), (1, 0)])
    split = call(split_kernel, "split", [VMEM, ANY], (sds((96, 128), bf16),) * 4)(rows, msg3)
    near = [split[0]] + [swap(split[k], 2 * k) for k in range(1, 4)]
    far = [swap(value, 1) for value in near]
    stack = call(
        stack_kernel,
        "stack",
        [VMEM] * 8,
        sds((448, 1024), bf16),
        [VMEM((432, 1024), bf16)],
    )(*near, *far)

    msg2, dpre2 = relay_step(2, arrived)
    arrived = relay(msg2, [(2, 1), (3, 0)])
    msg1, dpre1 = relay_step(1, arrived)
    arrived = relay(msg1, [(1, 0), (3, 2)])
    dpre = call(bottom_kernel, "bottom", [VMEM, VMEM, ANY, ANY, ANY], act)(
        arrived, slope, dpre3, dpre2, dpre1
    )
    near_grads = [dpre] + [swap(dpre, 2 * k) for k in range(1, 4)]
    far_grads = [swap(value, 1) for value in near_grads]
    grads, head_grad = call(
        last_kernel,
        "last",
        [VMEM, VMEM, ANY, VMEM, ANY, ANY, ANY],
        (act, sds((12, 128), f32)),
        [weights[0], VMEM((16, CH), bf16), weights[1]],
    )(arrived, dpre, w_hbm, head3, msg3, msg2, msg1)
    part = sds((112, CH), bf16)
    own, *parts = call(
        wgrad_kernel, "wgrad", [VMEM] * 9, (sds((112, CH), f32), part, part, part)
    )(stack, *near_grads, *far_grads)
    parts = [swap(parts[k - 1], 8 * k) for k in range(1, 4)]
    wgrad = call(sum_kernel, "sum", [VMEM] * 4, sds((108, 1, CH), f32))(own, *parts)
    return (
        grads.reshape(saved.shape),
        wgrad.reshape(1, 12, 3, 3, CH),
        head_grad,
    )


def solution(mesh):
    return jax.shard_map(
        per_device,
        mesh=mesh,
        in_specs=(
            P("section", "dp", None, None, None),
            P("section", None, None, None, None),
            P(),
            P("dp"),
            P("dp"),
            P("dp"),
        ),
        out_specs=(
            P("section", "dp", None, None, None),
            P("section", "dp", None, None, None),
            P("dp", "section"),
        ),
        check_vma=False,
    )
```

time: 330 us -> 92.7 us (0.28)
  blocking collectives: 233 us -> 16.3 us
  Pallas kernels: 0 us -> 24.1 us
  waiting for transfers between devices: 34.9 us -> 12.8 us
  between operations: 16.9 us -> 1.48 us
  matrix products: 10.3 us -> 0 us
  starting transfers between devices: 25.6 us -> 32.7 us
    unnamed x3 -> x0, blocking collectives: 196 us -> none
    ppermute x3 -> x20, starting transfers between devices: 4 us -> 32.7 us  [the longest x17 19.5 us: swap(): return lax.ppermute(value, 'dp', [(d, d ^ bits) for d in range(ranks)])]
    all_gather x1 -> x0, blocking collectives: 27.8 us -> none  [per_device(): others = lax.all_gather(unit_b, 'dp', axis=0, tiled=True)]
    pallas_call x0 -> x10, Pallas kernels: none -> 24.1 us  [the longest x1 4.22 us: per_device(): call(last_kernel, 'last', [VMEM, VMEM, ANY, VMEM, ANY, ANY, ANY], (act, s...]
    unnamed x9 -> x0, starting transfers between devices: 21.6 us -> none
    unnamed x10 -> x0, waiting for transfers between devices: 17.5 us -> none
    all_to_all x0 -> x1, blocking collectives: none -> 16.3 us  [per_device(): lax.all_to_all(announce.reshape(32, 8, 256), 'dp', 0, 0, tiled=True)]
    psum x1 -> x0, blocking collectives: 9.76 us -> none  [from_root(): return lax.psum(kept, axis)]
  transfers between devices with their start and end apart: 12 -> 20, of which waited for: 4 -> 9; matrix products, arithmetic and copies ran while one was open for 22% -> 0% of each run, Pallas kernels for 0% -> 9%
where the time goes in v1:
time: 92.7 us; the launch traced here: 91.9 us
  starting transfers between devices  32.7 us (35%)
  Pallas kernels  24.1 us (26%)
  blocking collectives  16.3 us (18%)
  waiting for transfers between devices  12.8 us (14%)
  local copies, waits for them, and re-layouts  4.5 us (5%)
  between operations  1.48 us (2%)
    ppermute x17, starting transfers between devices, swap(): return lax.ppermute(value, 'dp', [(d, d ^ bits) for d in range(ranks)])  19.5 us
    all_to_all x1, blocking collectives, per_device(): lax.all_to_all(announce.reshape(32, 8, 256), 'dp', 0, 0, tiled=True)  16.3 us
    ppermute x3, starting transfers between devices, relay(): return lax.ppermute(value, 'section', both)  13.2 us
    ppermute x3, waiting for transfers between devices, relay(): return lax.ppermute(value, 'section', both)  7.83 us
    ppermute x17, waiting for transfers between devices, swap(): return lax.ppermute(value, 'dp', [(d, d ^ bits) for d in range(ranks)])  5 us
    unnamed x40, local copies, waits for them, and re-layouts  4.5 us
    pallas_call x1, Pallas kernels, per_device(): call(last_kernel, 'last', [VMEM, VMEM, ANY, VMEM, ANY, ANY, ANY], (act, s...  4.22 us
    pallas_call x1, Pallas kernels, per_device(): call(forward_kernel, 'forward', [VMEM, ANY, SMEM, SMEM, SMEM], (sds((ROWS...  3.93 us
  transfers between devices with their start and end apart: 20, of which 9 were waited for; matrix products, arithmetic and copies ran while one was open for 0% of the time, Pallas kernels for 9%

profile of v1, /device:TPU:1, one launch (start us, length us, event | category | flops | bytes accessed | tf_op | source)
XLA Modules:
  0.0 91.9 jit_solution(11905595086561545137)
XLA Ops:
  1.3 3.9 %forward.1 = (f32[128,384]{1,0:T(8,128)}, bf16[256,256]{1,0:T(8,128)(2,1)}) custom-call(bf16[128,384]{1,0:T(8,128)(2,1)} %bitcast.14, bf16[3,3,384,384]{3,2,1,0:T(8,128)(2,1)} %bitcast.8, s32[1]{0:T(128)S(6)} %copy.9.counts, s32[4]{0:T(128)} %pairs.1, s32[4]{0:T(128)} %valid.1), custom_call_target="tpu_custom_call" | custom-call | tf_op jit(solution)/shard_map/forward/pallas_call | solution.py:312
  5.2 16.3 %all_to_all.5 = bf16[32,8,256]{2,1,0:T(8,128)(2,1)} all-to-all(bf16[32,8,256]{2,1,0:T(8,128)(2,1)} %bitcast.17), channel_id=1, replica_groups=mesh['section'=4,'dp'=32] {'dp'}, dimensions={0} | all-to-all | bytes 262144 | tf_op jit(solution)/shard_map/all_to_all | solution.py:319
  21.5 1.8 %top.1 = (bf16[144,384]{1,0:T(8,128)(2,1)}, bf16[128,384]{1,0:T(8,128)(2,1)}, f32[16,128]{1,0:T(8,128)}) custom-call(bf16[256,256]{1,0:T(8,128)(2,1)} %bitcast.13, bf16[384,512]{1,0:T(8,128)(2,1)} %head.1, f32[128,384]{1,0:T(8,128)} %get-tuple-element.23.slope, bf16[3,3,384,384]{3,2,1,0:T(8,128)(2,1)} %bitcast.9), custom_call_target="tpu_custom_call" | custom-call | tf_op jit(solution)/shard_map/top/pallas_call | solution.py:320
  23.3 1.7 %collective-permute-start = (bf16[144,384]{1,0:T(8,128)(2,1)}, bf16[144,384]{1,0:T(8,128)(2,1)S(1)}, u32[]{:S(2)}, u32[]{:S(2)}) collective-permute-start(bf16[144,384]{1,0:T(8,128)(2,1)} %get-tuple-element.24.msg3.order), channel_id=1, source_target_pairs={{96,64},{32,0},{64,96},{0,32},{97,65},{33,1},{65,97},{1,33},{98,66... | collective-permute-start | bytes 331784 | tf_op jit(solution)/shard_map/ppermute | solution.py:310
  25.0 3.1 %collective-permute-done.arrived = bf16[144,384]{1,0:T(8,128)(2,1)S(1)} collective-permute-done((bf16[144,384]{1,0:T(8,128)(2,1)}, bf16[144,384]{1,0:T(8,128)(2,1)S(1)}, u32[]{:S(2)}, u32[]{:S(2)}) %collective-permute-start) | collective-permute-done | bytes 110624 | tf_op jit(solution)/shard_map/ppermute | solution.py:310
  28.2 0.6 copy-done.1
  28.8 1.7 %relay2.1 = (bf16[144,384]{1,0:T(8,128)(2,1)}, bf16[128,384]{1,0:T(8,128)(2,1)}) custom-call(bf16[144,384]{1,0:T(8,128)(2,1)} %copy-done.1, f32[128,384]{1,0:T(8,128)} %get-tuple-element.23.slope, bf16[3,3,384,384]{3,2,1,0:T(8,128)(2,1)} %bitcast.10), custom_call_target="tpu_custom_call" | custom-call | tf_op jit(solution)/shard_map/relay2/pallas_call | solution.py:329
  30.5 6.2 %collective-permute-start.1 = (bf16[144,384]{1,0:T(8,128)(2,1)}, bf16[144,384]{1,0:T(8,128)(2,1)S(1)}, u32[]{:S(2)}, u32[]{:S(2)}) collective-permute-start(bf16[144,384]{1,0:T(8,128)(2,1)} %get-tuple-element.25.msg2), channel_id=1, source_target_pairs={{64,32},{96,0},{32,64},{0,96},{65,33},{97,1},{33,65},{1,97},{66,34... | collective-permute-start | bytes 331784 | tf_op jit(solution)/shard_map/ppermute | solution.py:310
  36.8 2.3 %collective-permute-done.1.arrived = bf16[144,384]{1,0:T(8,128)(2,1)S(1)} collective-permute-done((bf16[144,384]{1,0:T(8,128)(2,1)}, bf16[144,384]{1,0:T(8,128)(2,1)S(1)}, u32[]{:S(2)}, u32[]{:S(2)}) %collective-permute-start.1) | collective-permute-done | bytes 110624 | tf_op jit(solution)/shard_map/ppermute | solution.py:310
  39.1 0.6 copy-done.2
  39.8 1.7 %relay1.1 = (bf16[144,384]{1,0:T(8,128)(2,1)}, bf16[128,384]{1,0:T(8,128)(2,1)}) custom-call(bf16[144,384]{1,0:T(8,128)(2,1)} %copy-done.2, f32[128,384]{1,0:T(8,128)} %get-tuple-element.23.slope, bf16[3,3,384,384]{3,2,1,0:T(8,128)(2,1)} %bitcast.11), custom_call_target="tpu_custom_call" | custom-call | tf_op jit(solution)/shard_map/relay1/pallas_call | solution.py:329
  41.5 5.3 %collective-permute-start.2 = (bf16[144,384]{1,0:T(8,128)(2,1)}, bf16[144,384]{1,0:T(8,128)(2,1)S(1)}, u32[]{:S(2)}, u32[]{:S(2)}) collective-permute-start(bf16[144,384]{1,0:T(8,128)(2,1)} %get-tuple-element.26.msg1), channel_id=1, source_target_pairs={{32,0},{96,64},{0,32},{64,96},{33,1},{97,65},{1,33},{65,97},{34,2}... | collective-permute-start | bytes 331784 | tf_op jit(solution)/shard_map/ppermute | solution.py:310
  46.7 2.3 %collective-permute-done.2.arrived = bf16[144,384]{1,0:T(8,128)(2,1)S(1)} collective-permute-done((bf16[144,384]{1,0:T(8,128)(2,1)}, bf16[144,384]{1,0:T(8,128)(2,1)S(1)}, u32[]{:S(2)}, u32[]{:S(2)}) %collective-permute-start.2) | collective-permute-done | bytes 110624 | tf_op jit(solution)/shard_map/ppermute | solution.py:310
  49.1 0.6 copy-done
  49.7 1.6 %bottom.1.dpre.refs_0_ = bf16[128,384]{1,0:T(8,128)(2,1)} custom-call(bf16[144,384]{1,0:T(8,128)(2,1)} %copy-done, f32[128,384]{1,0:T(8,128)} %get-tuple-element.23.slope, bf16[128,384]{1,0:T(8,128)(2,1)} %get-tuple-element.27.dpre3, bf16[128,384]{1,0:T(8,128)(2,1)} %get-tuple-element.28.dpre2, bf16[128,384]{1,0:T(8,128)(2,1)} %get-tuple-element.29.dpre1), custom_call_target="tpu_custom_call" | custom-call | tf_op jit(solution)/shard_map/bottom/pallas_call | solution.py:353
  51.4 1.0 %collective-permute-start.12 = (bf16[128,384]{1,0:T(8,128)(2,1)}, bf16[128,384]{1,0:T(8,128)(2,1)S(1)}, u32[]{:S(2)}, u32[]{:S(2)}) collective-permute-start(bf16[128,384]{1,0:T(8,128)(2,1)} %bottom.1.dpre.refs_0_), channel_id=1, source_target_pairs={{0,6},{1,7},{2,4},{3,5},{4,2},{5,3},{6,0},{7,1},{8,14},{9,15},{10,... | collective-permute-start | bytes 294920 | tf_op jit(solution)/shard_map/ppermute | solution.py:306
  52.4 1.2 %collective-permute-start.11 = (bf16[128,384]{1,0:T(8,128)(2,1)}, bf16[128,384]{1,0:T(8,128)(2,1)S(1)}, u32[]{:S(2)}, u32[]{:S(2)}) collective-permute-start(bf16[128,384]{1,0:T(8,128)(2,1)} %bottom.1.dpre.refs_0_), channel_id=1, source_target_pairs={{0,4},{1,5},{2,6},{3,7},{4,0},{5,1},{6,2},{7,3},{8,12},{9,13},{10,... | collective-permute-start | bytes 294920 | tf_op jit(solution)/shard_map/ppermute | solution.py:306
  53.6 1.0 %collective-permute-start.10 = (bf16[128,384]{1,0:T(8,128)(2,1)}, bf16[128,384]{1,0:T(8,128)(2,1)S(1)}, u32[]{:S(2)}, u32[]{:S(2)}) collective-permute-start(bf16[128,384]{1,0:T(8,128)(2,1)} %bottom.1.dpre.refs_0_), channel_id=1, source_target_pairs={{0,2},{1,3},{2,0},{3,1},{4,6},{5,7},{6,4},{7,5},{8,10},{9,11},{10,... | collective-permute-start | bytes 294920 | tf_op jit(solution)/shard_map/ppermute | solution.py:306
  54.6 1.8 %split.1 = (bf16[96,128]{1,0:T(8,128)(2,1)}, bf16[96,128]{1,0:T(8,128)(2,1)}, bf16[96,128]{1,0:T(8,128)(2,1)}, bf16[96,128]{1,0:T(8,128)(2,1)}) custom-call(bf16[128,384]{1,0:T(8,128)(2,1)} %bitcast.15, bf16[144,384]{1,0:T(8,128)(2,1)} %get-tuple-element.24.msg3.order), custom_call_target="tpu_custom_call" | custom-call | tf_op jit(solution)/shard_map/split/pallas_call | solution.py:338
  56.4 0.5 collective-permute-start.3
  56.9 1.7 %collective-permute-start.4 = (bf16[96,128]{1,0:T(8,128)(2,1)}, bf16[96,128]{1,0:T(8,128)(2,1)S(1)}, u32[]{:S(2)}, u32[]{:S(2)}) collective-permute-start(bf16[96,128]{1,0:T(8,128)(2,1)} %get-tuple-element.34), channel_id=1, source_target_pairs={{0,4},{1,5},{2,6},{3,7},{4,0},{5,1},{6,2},{7,3},{8,12},{9,13},{10,... | collective-permute-start | bytes 73736 | tf_op jit(solution)/shard_map/ppermute | solution.py:306
  58.6 0.9 %collective-permute-done.3.refs_1_ = bf16[96,128]{1,0:T(8,128)(2,1)S(1)} collective-permute-done((bf16[96,128]{1,0:T(8,128)(2,1)}, bf16[96,128]{1,0:T(8,128)(2,1)S(1)}, u32[]{:S(2)}, u32[]{:S(2)}) %collective-permute-start.3) | collective-permute-done | bytes 24608 | tf_op jit(solution)/shard_map/ppermute | solution.py:306
  59.6 1.0 %collective-permute-start.5 = (bf16[96,128]{1,0:T(8,128)(2,1)}, bf16[96,128]{1,0:T(8,128)(2,1)S(1)}, u32[]{:S(2)}, u32[]{:S(2)}) collective-permute-start(bf16[96,128]{1,0:T(8,128)(2,1)} %get-tuple-element.35), channel_id=1, source_target_pairs={{0,6},{1,7},{2,4},{3,5},{4,2},{5,3},{6,0},{7,1},{8,14},{9,15},{10,... | collective-permute-start | bytes 73736 | tf_op jit(solution)/shard_map/ppermute | solution.py:306
  60.6 0.9 %collective-permute-done.4.refs_2_ = bf16[96,128]{1,0:T(8,128)(2,1)S(1)} collective-permute-done((bf16[96,128]{1,0:T(8,128)(2,1)}, bf16[96,128]{1,0:T(8,128)(2,1)S(1)}, u32[]{:S(2)}, u32[]{:S(2)}) %collective-permute-start.4) | collective-permute-done | bytes 24608 | tf_op jit(solution)/shard_map/ppermute | solution.py:306
  61.5 4.4 %collective-permute-start.6 = (bf16[96,128]{1,0:T(8,128)(2,1)}, bf16[96,128]{1,0:T(8,128)(2,1)S(1)}, u32[]{:S(2)}, u32[]{:S(2)}) collective-permute-start(bf16[96,128]{1,0:T(8,128)(2,1)} %get-tuple-element.32.refs_0_), channel_id=1, source_target_pairs={{0,1},{1,0},{2,3},{3,2},{4,5},{5,4},{6,7},{7,6},{8,9},{9,8},{10,11... | collective-permute-start | bytes 73736 | tf_op jit(solution)/shard_map/ppermute | solution.py:306
  65.9 0.0 collective-permute-done.5.refs_3_
  65.9 3.0 %collective-permute-start.13 = (bf16[128,384]{1,0:T(8,128)(2,1)}, bf16[128,384]{1,0:T(8,128)(2,1)S(1)}, u32[]{:S(2)}, u32[]{:S(2)}) collective-permute-start(bf16[128,384]{1,0:T(8,128)(2,1)} %bottom.1.dpre.refs_0_), channel_id=1, source_target_pairs={{0,1},{1,0},{2,3},{3,2},{4,5},{5,4},{6,7},{7,6},{8,9},{9,8},{10,11... | collective-permute-start | bytes 294920 | tf_op jit(solution)/shard_map/ppermute | solution.py:306
  69.0 0.0 collective-permute-done.12.refs_3_
  69.0 0.1 collective-permute-start.16
  69.1 0.0 collective-permute-done.11.refs_2_
  69.1 0.4 collective-permute-start.15
  69.5 0.0 collective-permute-done.10.refs_1_
  69.5 0.1 collective-permute-start.14
  69.6 0.0 collective-permute-done.6.refs_4_
  69.6 0.4 collective-permute-start.7
  70.0 0.8 collective-permute-done.7.refs_5_
  70.9 0.3 collective-permute-start.8
  71.2 0.8 collective-permute-done.8.refs_6_
  72.1 0.3 collective-permute-start.9
  72.4 0.8 collective-permute-done.9.refs_7_
  73.3 0.0 copy-done.13
  73.3 0.6 copy-done.19
  73.9 2.7 %stack.1 = bf16[448,1024]{1,0:T(8,128)(2,1)} custom-call(bf16[96,128]{1,0:T(8,128)(2,1)} %get-tuple-element.32.refs_0_, bf16[96,128]{1,0:T(8,128)(2,1)} %copy-done.13, bf16[96,128]{1,0:T(8,128)(2,1)} %copy-done.14, bf16[96,128]{1,0:T(8,128)(2,1)} %copy-done.15, bf16[96,128]{1,0:T(8,128)(2,1)} %copy-done.16, bf16[96,128]{1,0:T(8,128)(2,1)} %copy-done.17, ...), custom_call_target="tpu_custom_call" | custom-call | tf_op jit(solution)/shard_map/stack/pallas_call | solution.py:341
  76.6 0.0 collective-permute-done.13.refs_4_
  76.6 0.0 collective-permute-done.16.refs_7_
  76.6 0.0 copy-start.7
  76.6 0.0 collective-permute-done.15.refs_6_
  76.7 0.0 collective-permute-done.14.refs_5_
  76.7 0.6 copy-done.6
  77.3 0.0 copy-done.7
  77.3 0.0 copy-done.8
  77.3 0.6 copy-done.9
  78.0 2.8 %wgrad.1 = (f32[112,384]{1,0:T(8,128)}, bf16[112,384]{1,0:T(8,128)(2,1)}, bf16[112,384]{1,0:T(8,128)(2,1)}, bf16[112,384]{1,0:T(8,128)(2,1)}) custom-call(bf16[448,1024]{1,0:T(8,128)(2,1)} %stack.1, bf16[128,384]{1,0:T(8,128)(2,1)} %bottom.1.dpre.refs_0_, bf16[128,384]{1,0:T(8,128)(2,1)} %copy-done.5, bf16[128,384]{1,0:T(8,128)(2,1)} %copy-done.4, ...), custom_call_target="tpu_custom_call" | custom-call | tf_op jit(solution)/shard_map/wgrad/pallas_call | solution.py:366
  80.8 0.4 collective-permute-start.17
  81.1 1.7 %collective-permute-start.18 = (bf16[112,384]{1,0:T(8,128)(2,1)}, bf16[112,384]{1,0:T(8,128)(2,1)S(1)}, u32[]{:S(2)}, u32[]{:S(2)}) collective-permute-start(bf16[112,384]{1,0:T(8,128)(2,1)} %get-tuple-element.38), channel_id=1, source_target_pairs={{0,16},{1,17},{2,18},{3,19},{4,20},{5,21},{6,22},{7,23},{8,24},{9,... | collective-permute-start | bytes 258056 | tf_op jit(solution)/shard_map/ppermute | solution.py:306
  82.8 1.8 %collective-permute-start.19 = (bf16[112,384]{1,0:T(8,128)(2,1)}, bf16[112,384]{1,0:T(8,128)(2,1)S(1)}, u32[]{:S(2)}, u32[]{:S(2)}) collective-permute-start(bf16[112,384]{1,0:T(8,128)(2,1)} %get-tuple-element.39), channel_id=1, source_target_pairs={{0,24},{1,25},{2,26},{3,27},{4,28},{5,29},{6,30},{7,31},{8,16},{9,... | collective-permute-start | bytes 258056 | tf_op jit(solution)/shard_map/ppermute | solution.py:306
  84.6 4.2 %last.1 = (bf16[128,384]{1,0:T(8,128)(2,1)}, f32[12,128]{1,0:T(8,128)}) custom-call(bf16[144,384]{1,0:T(8,128)(2,1)} %copy-done, bf16[128,384]{1,0:T(8,128)(2,1)} %bottom.1.dpre.refs_0_, bf16[3,3,384,384]{3,2,1,0:T(8,128)(2,1)} %bitcast.12, f32[16,128]{1,0:T(8,128)} %get-tuple-element.30.head3, bf16[144,384]{1,0:T(8,128)(2,1)} %get-tuple-element.24.msg3.order, ...), custom_call_target="tpu_custom_call" | custom-call | tf_op jit(solution)/shard_map/last/pallas_call | solution.py:358
  88.9 0.0 collective-permute-done.17.part1
  88.9 0.0 collective-permute-done.18.part2
  88.9 0.6 collective-permute-done.19.part3
  89.5 0.0 copy-done.10
  89.5 0.0 copy-done.11
  89.5 0.6 copy-done.12
  90.1 1.8 %sum.1 = f32[108,1,384]{2,1,0:T(1,128)} custom-call(f32[112,384]{1,0:T(8,128)} %get-tuple-element.36.own, bf16[112,384]{1,0:T(8,128)(2,1)} %copy-done.10, bf16[112,384]{1,0:T(8,128)(2,1)} %copy-done.11, bf16[112,384]{1,0:T(8,128)(2,1)} %copy-done.12), custom_call_target="tpu_custom_call" | custom-call | tf_op jit(solution)/shard_map/sum/pallas_call | solution.py:370
  (27 shorter events, 0.0 us)
Async XLA Ops:
  23.3 4.9 %collective-permute-start = (bf16[144,384]{1,0:T(8,128)(2,1)}, bf16[144,384]{1,0:T(8,128)(2,1)S(1)}, u32[]{:S(2)}, u32[]{:S(2)}) collective-permute-start(bf16[144,384]{1,0:T(8,128)(2,1)} %get-tuple-element.24.msg3.order), channel_id=1, source_target_pairs={{96,64},{32,0},{64,96},{0,32},{97,65},{33,1},{65,97},{1,33},{98,66... | collective-permute-start | bytes 331784 | tf_op jit(solution)/shard_map/ppermute | solution.py:310
  28.2 0.7 copy-start.1
  30.5 8.6 %collective-permute-start.1 = (bf16[144,384]{1,0:T(8,128)(2,1)}, bf16[144,384]{1,0:T(8,128)(2,1)S(1)}, u32[]{:S(2)}, u32[]{:S(2)}) collective-permute-start(bf16[144,384]{1,0:T(8,128)(2,1)} %get-tuple-element.25.msg2), channel_id=1, source_target_pairs={{64,32},{96,0},{32,64},{0,96},{65,33},{97,1},{33,65},{1,97},{66,34... | collective-permute-start | bytes 331784 | tf_op jit(solution)/shard_map/ppermute | solution.py:310
  39.1 0.7 copy-start.2
  41.5 7.6 %collective-permute-start.2 = (bf16[144,384]{1,0:T(8,128)(2,1)}, bf16[144,384]{1,0:T(8,128)(2,1)S(1)}, u32[]{:S(2)}, u32[]{:S(2)}) collective-permute-start(bf16[144,384]{1,0:T(8,128)(2,1)} %get-tuple-element.26.msg1), channel_id=1, source_target_pairs={{32,0},{96,64},{0,32},{64,96},{33,1},{97,65},{1,33},{65,97},{34,2}... | collective-permute-start | bytes 331784 | tf_op jit(solution)/shard_map/ppermute | solution.py:310
  49.1 0.6 copy-start
  51.4 17.6 %collective-permute-start.12 = (bf16[128,384]{1,0:T(8,128)(2,1)}, bf16[128,384]{1,0:T(8,128)(2,1)S(1)}, u32[]{:S(2)}, u32[]{:S(2)}) collective-permute-start(bf16[128,384]{1,0:T(8,128)(2,1)} %bottom.1.dpre.refs_0_), channel_id=1, source_target_pairs={{0,6},{1,7},{2,4},{3,5},{4,2},{5,3},{6,0},{7,1},{8,14},{9,15},{10,... | collective-permute-start | bytes 294920 | tf_op jit(solution)/shard_map/ppermute | solution.py:306
  52.4 16.7 %collective-permute-start.11 = (bf16[128,384]{1,0:T(8,128)(2,1)}, bf16[128,384]{1,0:T(8,128)(2,1)S(1)}, u32[]{:S(2)}, u32[]{:S(2)}) collective-permute-start(bf16[128,384]{1,0:T(8,128)(2,1)} %bottom.1.dpre.refs_0_), channel_id=1, source_target_pairs={{0,4},{1,5},{2,6},{3,7},{4,0},{5,1},{6,2},{7,3},{8,12},{9,13},{10,... | collective-permute-start | bytes 294920 | tf_op jit(solution)/shard_map/ppermute | solution.py:306
  53.6 15.9 %collective-permute-start.10 = (bf16[128,384]{1,0:T(8,128)(2,1)}, bf16[128,384]{1,0:T(8,128)(2,1)S(1)}, u32[]{:S(2)}, u32[]{:S(2)}) collective-permute-start(bf16[128,384]{1,0:T(8,128)(2,1)} %bottom.1.dpre.refs_0_), channel_id=1, source_target_pairs={{0,2},{1,3},{2,0},{3,1},{4,6},{5,7},{6,4},{7,5},{8,10},{9,11},{10,... | collective-permute-start | bytes 294920 | tf_op jit(solution)/shard_map/ppermute | solution.py:306
  56.4 3.1 %collective-permute-start.3 = (bf16[96,128]{1,0:T(8,128)(2,1)}, bf16[96,128]{1,0:T(8,128)(2,1)S(1)}, u32[]{:S(2)}, u32[]{:S(2)}) collective-permute-start(bf16[96,128]{1,0:T(8,128)(2,1)} %get-tuple-element.33), channel_id=1, source_target_pairs={{0,2},{1,3},{2,0},{3,1},{4,6},{5,7},{6,4},{7,5},{8,10},{9,11},{10,... | collective-permute-start | bytes 73736 | tf_op jit(solution)/shard_map/ppermute | solution.py:306
  56.9 4.7 %collective-permute-start.4 = (bf16[96,128]{1,0:T(8,128)(2,1)}, bf16[96,128]{1,0:T(8,128)(2,1)S(1)}, u32[]{:S(2)}, u32[]{:S(2)}) collective-permute-start(bf16[96,128]{1,0:T(8,128)(2,1)} %get-tuple-element.34), channel_id=1, source_target_pairs={{0,4},{1,5},{2,6},{3,7},{4,0},{5,1},{6,2},{7,3},{8,12},{9,13},{10,... | collective-permute-start | bytes 73736 | tf_op jit(solution)/shard_map/ppermute | solution.py:306
  59.6 13.7 %copy-start.13 = (bf16[96,128]{1,0:T(8,128)(2,1)}, bf16[96,128]{1,0:T(8,128)(2,1)S(1)}, u32[]{:S(2)}) copy-start(bf16[96,128]{1,0:T(8,128)(2,1)S(1)} %collective-permute-done.3.refs_1_) | copy-start | bytes 73732
  59.6 6.4 %collective-permute-start.5 = (bf16[96,128]{1,0:T(8,128)(2,1)}, bf16[96,128]{1,0:T(8,128)(2,1)S(1)}, u32[]{:S(2)}, u32[]{:S(2)}) collective-permute-start(bf16[96,128]{1,0:T(8,128)(2,1)} %get-tuple-element.35), channel_id=1, source_target_pairs={{0,6},{1,7},{2,4},{3,5},{4,2},{5,3},{6,0},{7,1},{8,14},{9,15},{10,... | collective-permute-start | bytes 73736 | tf_op jit(solution)/shard_map/ppermute | solution.py:306
  61.5 11.7 %copy-start.14 = (bf16[96,128]{1,0:T(8,128)(2,1)}, bf16[96,128]{1,0:T(8,128)(2,1)S(1)}, u32[]{:S(2)}) copy-start(bf16[96,128]{1,0:T(8,128)(2,1)S(1)} %collective-permute-done.4.refs_2_) | copy-start | bytes 73732
  61.5 8.1 %collective-permute-start.6 = (bf16[96,128]{1,0:T(8,128)(2,1)}, bf16[96,128]{1,0:T(8,128)(2,1)S(1)}, u32[]{:S(2)}, u32[]{:S(2)}) collective-permute-start(bf16[96,128]{1,0:T(8,128)(2,1)} %get-tuple-element.32.refs_0_), channel_id=1, source_target_pairs={{0,1},{1,0},{2,3},{3,2},{4,5},{5,4},{6,7},{7,6},{8,9},{9,8},{10,11... | collective-permute-start | bytes 73736 | tf_op jit(solution)/shard_map/ppermute | solution.py:306
  65.9 7.3 %copy-start.15 = (bf16[96,128]{1,0:T(8,128)(2,1)}, bf16[96,128]{1,0:T(8,128)(2,1)S(1)}, u32[]{:S(2)}) copy-start(bf16[96,128]{1,0:T(8,128)(2,1)S(1)} %collective-permute-done.5.refs_3_) | copy-start | bytes 73732
  65.9 10.7 %collective-permute-start.13 = (bf16[128,384]{1,0:T(8,128)(2,1)}, bf16[128,384]{1,0:T(8,128)(2,1)S(1)}, u32[]{:S(2)}, u32[]{:S(2)}) collective-permute-start(bf16[128,384]{1,0:T(8,128)(2,1)} %bottom.1.dpre.refs_0_), channel_id=1, source_target_pairs={{0,1},{1,0},{2,3},{3,2},{4,5},{5,4},{6,7},{7,6},{8,9},{9,8},{10,11... | collective-permute-start | bytes 294920 | tf_op jit(solution)/shard_map/ppermute | solution.py:306
  69.0 7.7 %copy-start.3 = (bf16[128,384]{1,0:T(8,128)(2,1)}, bf16[128,384]{1,0:T(8,128)(2,1)S(1)}, u32[]{:S(2)}) copy-start(bf16[128,384]{1,0:T(8,128)(2,1)S(1)} %collective-permute-done.12.refs_3_) | copy-start | bytes 294916
  69.0 7.7 %collective-permute-start.16 = (bf16[128,384]{1,0:T(8,128)(2,1)S(1)}, bf16[128,384]{1,0:T(8,128)(2,1)S(1)}, u32[]{:S(2)}, u32[]{:S(2)}) collective-permute-start(bf16[128,384]{1,0:T(8,128)(2,1)S(1)} %collective-permute-done.12.refs_3_), channel_id=1, source_target_pairs={{0,1},{1,0},{2,3},{3,2},{4,5},{5,4},{6,7},{7,6},{8,9},{9,8},{10,11... | collective-permute-start | bytes 294920 | tf_op jit(solution)/shard_map/ppermute | solution.py:306
  69.1 7.6 %copy-start.4 = (bf16[128,384]{1,0:T(8,128)(2,1)}, bf16[128,384]{1,0:T(8,128)(2,1)S(1)}, u32[]{:S(2)}) copy-start(bf16[128,384]{1,0:T(8,128)(2,1)S(1)} %collective-permute-done.11.refs_2_) | copy-start | bytes 294916
  69.1 7.6 %collective-permute-start.15 = (bf16[128,384]{1,0:T(8,128)(2,1)S(1)}, bf16[128,384]{1,0:T(8,128)(2,1)S(1)}, u32[]{:S(2)}, u32[]{:S(2)}) collective-permute-start(bf16[128,384]{1,0:T(8,128)(2,1)S(1)} %collective-permute-done.11.refs_2_), channel_id=1, source_target_pairs={{0,1},{1,0},{2,3},{3,2},{4,5},{5,4},{6,7},{7,6},{8,9},{9,8},{10,11... | collective-permute-start | bytes 294920 | tf_op jit(solution)/shard_map/ppermute | solution.py:306
  69.5 7.2 %copy-start.5 = (bf16[128,384]{1,0:T(8,128)(2,1)}, bf16[128,384]{1,0:T(8,128)(2,1)S(1)}, u32[]{:S(2)}) copy-start(bf16[128,384]{1,0:T(8,128)(2,1)S(1)} %collective-permute-done.10.refs_1_) | copy-start | bytes 294916
  69.5 7.2 %collective-permute-start.14 = (bf16[128,384]{1,0:T(8,128)(2,1)S(1)}, bf16[128,384]{1,0:T(8,128)(2,1)S(1)}, u32[]{:S(2)}, u32[]{:S(2)}) collective-permute-start(bf16[128,384]{1,0:T(8,128)(2,1)S(1)} %collective-permute-done.10.refs_1_), channel_id=1, source_target_pairs={{0,1},{1,0},{2,3},{3,2},{4,5},{5,4},{6,7},{7,6},{8,9},{9,8},{10,11... | collective-permute-start | bytes 294920 | tf_op jit(solution)/shard_map/ppermute | solution.py:306
  69.6 3.7 %copy-start.16 = (bf16[96,128]{1,0:T(8,128)(2,1)}, bf16[96,128]{1,0:T(8,128)(2,1)S(1)}, u32[]{:S(2)}) copy-start(bf16[96,128]{1,0:T(8,128)(2,1)S(1)} %collective-permute-done.6.refs_4_) | copy-start | bytes 73732
  69.6 1.3 %collective-permute-start.7 = (bf16[96,128]{1,0:T(8,128)(2,1)S(1)}, bf16[96,128]{1,0:T(8,128)(2,1)S(1)}, u32[]{:S(2)}, u32[]{:S(2)}) collective-permute-start(bf16[96,128]{1,0:T(8,128)(2,1)S(1)} %collective-permute-done.3.refs_1_), channel_id=1, source_target_pairs={{0,1},{1,0},{2,3},{3,2},{4,5},{5,4},{6,7},{7,6},{8,9},{9,8},{10,11... | collective-permute-start | bytes 73736 | tf_op jit(solution)/shard_map/ppermute | solution.py:306
  70.9 2.4 %copy-start.17 = (bf16[96,128]{1,0:T(8,128)(2,1)}, bf16[96,128]{1,0:T(8,128)(2,1)S(1)}, u32[]{:S(2)}) copy-start(bf16[96,128]{1,0:T(8,128)(2,1)S(1)} %collective-permute-done.7.refs_5_) | copy-start | bytes 73732
  70.9 1.2 %collective-permute-start.8 = (bf16[96,128]{1,0:T(8,128)(2,1)S(1)}, bf16[96,128]{1,0:T(8,128)(2,1)S(1)}, u32[]{:S(2)}, u32[]{:S(2)}) collective-permute-start(bf16[96,128]{1,0:T(8,128)(2,1)S(1)} %collective-permute-done.4.refs_2_), channel_id=1, source_target_pairs={{0,1},{1,0},{2,3},{3,2},{4,5},{5,4},{6,7},{7,6},{8,9},{9,8},{10,11... | collective-permute-start | bytes 73736 | tf_op jit(solution)/shard_map/ppermute | solution.py:306
  72.1 1.2 %copy-start.18 = (bf16[96,128]{1,0:T(8,128)(2,1)}, bf16[96,128]{1,0:T(8,128)(2,1)S(1)}, u32[]{:S(2)}) copy-start(bf16[96,128]{1,0:T(8,128)(2,1)S(1)} %collective-permute-done.8.refs_6_) | copy-start | bytes 73732
  72.1 1.2 %collective-permute-start.9 = (bf16[96,128]{1,0:T(8,128)(2,1)S(1)}, bf16[96,128]{1,0:T(8,128)(2,1)S(1)}, u32[]{:S(2)}, u32[]{:S(2)}) collective-permute-start(bf16[96,128]{1,0:T(8,128)(2,1)S(1)} %collective-permute-done.5.refs_3_), channel_id=1, source_target_pairs={{0,1},{1,0},{2,3},{3,2},{4,5},{5,4},{6,7},{7,6},{8,9},{9,8},{10,11... | collective-permute-start | bytes 73736 | tf_op jit(solution)/shard_map/ppermute | solution.py:306
  73.3 0.6 copy-start.19
  76.6 0.6 copy-start.6
  76.6 0.7 copy-start.7
  76.6 0.7 copy-start.8
  77.3 0.6 copy-start.9
  80.8 8.1 %collective-permute-start.17 = (bf16[112,384]{1,0:T(8,128)(2,1)}, bf16[112,384]{1,0:T(8,128)(2,1)S(1)}, u32[]{:S(2)}, u32[]{:S(2)}) collective-permute-start(bf16[112,384]{1,0:T(8,128)(2,1)} %get-tuple-element.37), channel_id=1, source_target_pairs={{0,8},{1,9},{2,10},{3,11},{4,12},{5,13},{6,14},{7,15},{8,0},{9,1},... | collective-permute-start | bytes 258056 | tf_op jit(solution)/shard_map/ppermute | solution.py:306
  81.1 7.7 %collective-permute-start.18 = (bf16[112,384]{1,0:T(8,128)(2,1)}, bf16[112,384]{1,0:T(8,128)(2,1)S(1)}, u32[]{:S(2)}, u32[]{:S(2)}) collective-permute-start(bf16[112,384]{1,0:T(8,128)(2,1)} %get-tuple-element.38), channel_id=1, source_target_pairs={{0,16},{1,17},{2,18},{3,19},{4,20},{5,21},{6,22},{7,23},{8,24},{9,... | collective-permute-start | bytes 258056 | tf_op jit(solution)/shard_map/ppermute | solution.py:306
  82.8 6.6 %collective-permute-start.19 = (bf16[112,384]{1,0:T(8,128)(2,1)}, bf16[112,384]{1,0:T(8,128)(2,1)S(1)}, u32[]{:S(2)}, u32[]{:S(2)}) collective-permute-start(bf16[112,384]{1,0:T(8,128)(2,1)} %get-tuple-element.39), channel_id=1, source_target_pairs={{0,24},{1,25},{2,26},{3,27},{4,28},{5,29},{6,30},{7,31},{8,16},{9,... | collective-permute-start | bytes 258056 | tf_op jit(solution)/shard_map/ppermute | solution.py:306
  88.9 0.6 copy-start.10
  88.9 0.6 copy-start.11
  89.5 0.7 copy-start.12

commit v2 on v1

--- a/solution.py
+++ b/solution.py
@@ -1,5 +1,3 @@
-import functools
-
 import jax
 import jax.numpy as jnp
 from jax import lax
@@ -7,12 +5,13 @@
 from jax.experimental.pallas import tpu as pltpu
 from jax.sharding import PartitionSpec as P
 
+
 tau_value = 0.2
 loss_scale = 32.0
 norm_eps = 1e-06
 VMEM = pltpu.VMEM
 SMEM = pltpu.SMEM
-ANY = pl.ANY
+HBM = pltpu.HBM
 f32 = jnp.float32
 bf16 = jnp.bfloat16
 NN = (((1,), (0,)), ((), ()))
@@ -58,28 +57,31 @@
     return v.reshape(ROWS, CH)
 
 
-def weight_copies(w_hbm, w, sem):
-    return [pltpu.make_async_copy(w_hbm.at[kh], w.at[kh], sem.at[kh]) for kh in range(3)]
-
-
-def conv_back(dpre, w, copies):
+def conv_back(dpre, w):
     cols = column_shifts(dpre)
     total = None
     for kh in range(3):
         lhs = jnp.concatenate(
             [row_shift(cols[2 - kw], 1 - kh).astype(bf16) for kw in range(3)], axis=1
         )
-        copies[kh].wait()
         rhs = jnp.concatenate([w[kh, kw] for kw in range(3)], axis=1)
         part = mm(lhs, rhs, NT)
         total = part if total is None else total + part
     return total
 
 
-def forward_kernel(saved, w_hbm, counts, pairs, valid, slope, message, w, sem):
-    copies = weight_copies(w_hbm, w, sem)
+def forward_kernel(
+    saved_hbm, w_hbm, head_hbm, counts, pairs, valid, slope, message, saved, w, head, sem
+):
+    sources = [saved_hbm, w_hbm.at[0], w_hbm.at[1], w_hbm.at[2], head_hbm]
+    targets = [saved, w.at[0], w.at[1], w.at[2], head]
+    copies = [
+        pltpu.make_async_copy(source, target, sem.at[n])
+        for n, (source, target) in enumerate(zip(sources, targets, strict=True))
+    ]
     for copy in copies:
         copy.start()
+    copies[0].wait()
     v = saved[...].astype(f32)
     cols = column_shifts(v)
     pre = None
@@ -87,13 +89,14 @@
         lhs = jnp.concatenate(
             [row_shift(cols[kw], kh - 1).astype(bf16) for kw in range(3)], axis=1
         )
-        copies[kh].wait()
+        copies[1 + kh].wait()
         part = mm(lhs, w[kh].reshape(3 * CH, CH))
         pre = part if pre is None else pre + part
     sigma = jax.nn.sigmoid(pre)
     slope[...] = sigma * (1.0 + pre * (1.0 - sigma))
     feature = (v + pre * sigma).reshape(4, CELLS, CH)
     pooled = jnp.sum(feature, axis=1) / CELLS
+    copies[4].wait()
     at = (row_iota((4, 128)), col_iota((4, 128)))
     extra = jnp.zeros((4, 128), f32)
     for slot in range(4):
@@ -156,14 +159,23 @@
     return dpooled[:4].astype(f32), mm(pooled_mine, dproj)
 
 
-def top_kernel(gathered, head, slope, w_hbm, message, dpre_out, head_out, w, sem):
+def split_saved(saved, outs):
+    _, _, y, x, c = position()
+    m = row_iota((CH, 1))
+    q = (m * 43691) >> 19
+    i = m - 12 * q
+    channel = (y ^ (q & 3)) * 96 + (x ^ (q >> 3)) * 24 + (c ^ ((q >> 2) & 1)) * 12 + i
+    pick = jnp.where(col_iota((CH, CH)) == channel, 1.0, 0.0).astype(bf16)
+    turned = mm(pick, saved[...], NT).astype(bf16)
+    for k, out in enumerate(outs):
+        out[...] = turned[96 * k : 96 * k + 96]
+
+
+def top_kernel(gathered, head, slope, w, saved, message, dpre_out, head_out, *split):
     section, rank, _, _, _ = position()
 
     @pl.when(section == 3)
     def _():
-        copies = weight_copies(w_hbm, w, sem)
-        for copy in copies:
-            copy.start()
         dpooled, head_grad = contrast(gathered[...], head[...], rank)
         top = (dpooled / CELLS).astype(bf16).astype(f32)
         cot = jnp.broadcast_to(top[:, None, :], (4, CELLS, CH)).reshape(ROWS, CH)
@@ -171,77 +183,75 @@
         dpre_out[...] = dpre
         head_out[...] = head_grad[:, 384:]
         message[128:, :] = head_grad[:, :384].astype(bf16)
-        below = cot + conv_back(dpre.astype(f32), w, copies)
+        below = cot + conv_back(dpre.astype(f32), w)
         message[:128, :] = below.astype(bf16)
 
-
-def relay_kernel(active, arrived, slope, w_hbm, message, dpre_out, w, sem):
+    @pl.when(section != 3)
+    def _():
+        split_saved(saved, split)
+
+
+def relay(active, arrived, slope, w, message, dpre_out):
     @pl.when(lax.axis_index("section") == active)
     def _():
-        copies = weight_copies(w_hbm, w, sem)
-        for copy in copies:
-            copy.start()
         cot = arrived[:128, :].astype(f32)
         dpre = (cot * slope[...]).astype(bf16)
         dpre_out[...] = dpre
         message[128:, :] = arrived[128:, :]
-        below = cot + conv_back(dpre.astype(f32), w, copies)
+        below = cot + conv_back(dpre.astype(f32), w)
         message[:128, :] = below.astype(bf16)
 
 
-def bottom_kernel(arrived, slope, dpre3, dpre2, dpre1, dpre_out):
+def relay2_kernel(arrived, slope, w, saved, *refs):
+    relay(2, arrived, slope, w, refs[4], refs[5])
+
+    @pl.when(lax.axis_index("section") == 3)
+    def _():
+        split_saved(saved, refs[6:])
+
+
+def relay1_kernel(arrived, slope, w, message, dpre_out):
+    relay(1, arrived, slope, w, message, dpre_out)
+
+
+def bottom_kernel(arrived, slope, dpre3, dpre2, dpre1, *refs):
     section = lax.axis_index("section")
+    dpre_out = refs[-1]
     for at, held in ((3, dpre3), (2, dpre2), (1, dpre1)):
 
         @pl.when(section == at)
         def _():
-            pltpu.sync_copy(held, dpre_out)
+            dpre_out[...] = held[...]
 
     @pl.when(section == 0)
     def _():
         dpre_out[...] = (arrived[:128, :].astype(f32) * slope[...]).astype(bf16)
 
 
-def last_kernel(arrived, dpre, w_hbm, head3, msg3, msg2, msg1, grads, head_out, w, held, sem):
+def last_kernel(arrived, dpre, w, head3, msg3, msg2, msg1, own, grads, head_out):
     section = lax.axis_index("section")
 
     @pl.when(section == 3)
     def _():
-        pltpu.sync_copy(msg3.at[pl.ds(0, 128)], grads)
+        grads[...] = msg3[:128, :]
         head_out[...] = head3[:12, :]
 
     for at, sent in ((2, msg2), (1, msg1)):
 
         @pl.when(section == at)
         def _():
-            pltpu.sync_copy(sent.at[pl.ds(0, 128)], grads)
-            pltpu.sync_copy(sent.at[pl.ds(128, 16)], held)
-            head_out[...] = held[:, at * 128 : at * 128 + 128].astype(f32)[:12]
+            grads[...] = sent[:128, :]
+            head_out[...] = sent[128:, at * 128 : at * 128 + 128].astype(f32)[:12]
 
     @pl.when(section == 0)
     def _():
-        copies = weight_copies(w_hbm, w, sem)
-        for copy in copies:
-            copy.start()
-        below = arrived[:128, :].astype(f32) + conv_back(dpre[...].astype(f32), w, copies)
+        below = arrived[:128, :].astype(f32) + conv_back(dpre[...].astype(f32), w)
         grads[...] = below.astype(bf16)
         head_out[...] = arrived[128:, :128].astype(f32)[:12]
 
 
-def split_kernel(saved, order, out0, out1, out2, out3):
-    _, _, y, x, c = position()
-    m = row_iota((CH, 1))
-    q = (m * 43691) >> 19
-    i = m - 12 * q
-    channel = (y ^ (q & 3)) * 96 + (x ^ (q >> 3)) * 24 + (c ^ ((q >> 2) & 1)) * 12 + i
-    pick = jnp.where(col_iota((CH, CH)) == channel, 1.0, 0.0).astype(bf16)
-    turned = mm(pick, saved[...], NT).astype(bf16)
-    for k, out in enumerate((out0, out1, out2, out3)):
-        out[...] = turned[96 * k : 96 * k + 96]
-
-
 def stack_kernel(*refs):
-    near, far, out, scratch = refs[:4], refs[4:8], refs[8], refs[9]
+    near, far, out, scratch = refs[:4], refs[4:8], refs[9], refs[10]
     r = col_iota((48, 128))
     ph, pw = (r >> 3) & 3, r & 7
     for g in range(8):
@@ -279,15 +289,30 @@
     out[...] = total[:108].reshape(108, 1, CH)
 
 
-def call(kernel, name, ins, outs, scratch=()):
-    return pl.pallas_call(
+def call(kernel, ins, outs, scratch=(), aliases=None):
+    run = pl.pallas_call(
         kernel,
         out_shape=outs,
         in_specs=[pl.BlockSpec(memory_space=space) for space in ins],
-        out_specs=jax.tree.map(lambda _: pl.BlockSpec(memory_space=VMEM), outs),
+        out_specs=jax.tree.map(
+            lambda _: pl.BlockSpec(memory_space=VMEM), outs, is_leaf=lambda o: not isinstance(o, tuple)
+        ),
         scratch_shapes=list(scratch),
-        name=name,
-    )
+        input_output_aliases=aliases or {},
+        compiler_params=pltpu.CompilerParams(vmem_limit_bytes=24 << 20),
+    )
+
+    def with_operands(*operands):
+        return run(
+            *[
+                value
+                if space is SMEM
+                else pltpu.with_memory_space_constraint(value, space)
+                for value, space in zip(operands, ins, strict=True)
+            ]
+        )
+
+    return with_operands
 
 
 def sds(shape, dtype):
@@ -296,78 +321,69 @@
 
 def per_device(saved, kernels, head, counts, pairs, valid):
     ranks = lax.axis_size("dp")
-    rows = saved.reshape(ROWS, CH)
-    w_hbm = jnp.transpose(kernels[0], (1, 2, 0, 3))
-    weights = [VMEM((3, 3, CH, CH), bf16), pltpu.SemaphoreType.DMA((3,))]
-    act = sds((ROWS, CH), bf16)
-    msg = sds((MSG, CH), bf16)
+    act = VMEM((ROWS, CH), bf16)
+    msg = VMEM((MSG, CH), bf16)
+    piece = VMEM((96, 128), bf16)
 
     def swap(value, bits):
         return lax.ppermute(value, "dp", [(d, d ^ bits) for d in range(ranks)])
 
-    def relay(value, pairs_of):
+    def relayed(value, pairs_of):
         both = [(a, b) for a, b in pairs_of] + [(b, a) for a, b in pairs_of]
         return lax.ppermute(value, "section", both)
 
-    slope, announce = call(
+    slope, announce, rows, w, head = call(
         forward_kernel,
-        "forward",
-        [VMEM, ANY, SMEM, SMEM, SMEM],
-        (sds((ROWS, CH), f32), sds((256, 256), bf16)),
-        weights,
-    )(rows, w_hbm, counts, pairs, valid)
+        [HBM] * 3 + [SMEM] * 3,
+        (
+            VMEM((ROWS, CH), f32),
+            VMEM((256, 256), bf16),
+            act,
+            VMEM((3, 3, CH, CH), bf16),
+            VMEM((CH, EMB), bf16),
+        ),
+        [pltpu.SemaphoreType.DMA((5,))],
+    )(
+        saved.reshape(ROWS, CH),
+        jnp.transpose(kernels[0], (1, 2, 0, 3)),
+        head,
+        counts,
+        pairs,
+        valid,
+    )
     gathered = lax.all_to_all(announce.reshape(32, 8, 256), "dp", 0, 0, tiled=True)
-    msg3, dpre3, head3 = call(
-        top_kernel,
-        "top",
-        [VMEM, VMEM, VMEM, ANY],
-        (msg, act, sds((16, 128), f32)),
-        weights,
-    )(gathered.reshape(256, 256), head, slope, w_hbm)
-
-    def relay_step(active, arrived):
-        return call(
-            functools.partial(relay_kernel, active),
-            f"relay{active}",
-            [VMEM, VMEM, ANY],
-            (msg, act),
-            weights,
-        )(arrived, slope, w_hbm)
-
-    arrived = relay(msg3, [(3, 2), (1, 0)])
-    split = call(split_kernel, "split", [VMEM, ANY], (sds((96, 128), bf16),) * 4)(rows, msg3)
+    msg3, dpre3, head3, *split = call(
+        top_kernel, [VMEM] * 5, (msg, act, VMEM((16, 128), f32)) + (piece,) * 4
+    )(gathered.reshape(256, 256), head, slope, w, rows)
+    arrived = relayed(msg3, [(3, 2), (1, 0)])
+    msg2, dpre2, *split = call(
+        relay2_kernel,
+        [VMEM] * 8,
+        (msg, act) + (piece,) * 4,
+        aliases={4 + k: 2 + k for k in range(4)},
+    )(arrived, slope, w, rows, *split)
+    arrived = relayed(msg2, [(2, 1), (3, 0)])
     near = [split[0]] + [swap(split[k], 2 * k) for k in range(1, 4)]
+    msg1, dpre1 = call(relay1_kernel, [VMEM] * 3, (msg, act))(arrived, slope, w)
+    arrived = relayed(msg1, [(1, 0), (3, 2)])
     far = [swap(value, 1) for value in near]
+    dpre = call(bottom_kernel, [VMEM] * 9, act)(
+        arrived, slope, dpre3, dpre2, dpre1, *far
+    )
+    near_grads = [dpre] + [swap(dpre, 2 * k) for k in range(1, 4)]
     stack = call(
-        stack_kernel,
-        "stack",
-        [VMEM] * 8,
-        sds((448, 1024), bf16),
-        [VMEM((432, 1024), bf16)],
-    )(*near, *far)
-
-    msg2, dpre2 = relay_step(2, arrived)
-    arrived = relay(msg2, [(2, 1), (3, 0)])
-    msg1, dpre1 = relay_step(1, arrived)
-    arrived = relay(msg1, [(1, 0), (3, 2)])
-    dpre = call(bottom_kernel, "bottom", [VMEM, VMEM, ANY, ANY, ANY], act)(
-        arrived, slope, dpre3, dpre2, dpre1
-    )
-    near_grads = [dpre] + [swap(dpre, 2 * k) for k in range(1, 4)]
+        stack_kernel, [VMEM] * 9, VMEM((448, 1024), bf16), [VMEM((432, 1024), bf16)]
+    )(*near, *far, dpre)
     far_grads = [swap(value, 1) for value in near_grads]
-    grads, head_grad = call(
-        last_kernel,
-        "last",
-        [VMEM, VMEM, ANY, VMEM, ANY, ANY, ANY],
-        (act, sds((12, 128), f32)),
-        [weights[0], VMEM((16, CH), bf16), weights[1]],
-    )(arrived, dpre, w_hbm, head3, msg3, msg2, msg1)
-    part = sds((112, CH), bf16)
+    part = VMEM((112, CH), bf16)
     own, *parts = call(
-        wgrad_kernel, "wgrad", [VMEM] * 9, (sds((112, CH), f32), part, part, part)
+        wgrad_kernel, [VMEM] * 9, (VMEM((112, CH), f32), part, part, part)
     )(stack, *near_grads, *far_grads)
     parts = [swap(parts[k - 1], 8 * k) for k in range(1, 4)]
-    wgrad = call(sum_kernel, "sum", [VMEM] * 4, sds((108, 1, CH), f32))(own, *parts)
+    grads, head_grad = call(
+        last_kernel, [VMEM] * 8, (sds((ROWS, CH), bf16), sds((12, 128), f32))
+    )(arrived, dpre, w, head3, msg3, msg2, msg1, own)
+    wgrad = call(sum_kernel, [VMEM] * 4, sds((108, 1, CH), f32))(own, *parts)
     return (
         grads.reshape(saved.shape),
         wgrad.reshape(1, 12, 3, 3, CH),

time: 92.7 us -> 68 us (0.73)
  Pallas kernels: 24.1 us -> 7.14 us
  local copies, waits for them, and re-layouts: 4.5 us -> 1.3 us
  waiting for transfers between devices: 12.8 us -> 10.3 us
    pallas_call x10 -> x9, Pallas kernels: 24.1 us -> 7.14 us  [with_operands(): run(*[value if space is SMEM else pltpu.with_memory_space_constraint(valu...]
    ppermute x3, starting transfers between devices: 13.2 us -> 9.45 us  [relayed(): return lax.ppermute(value, 'section', both)]
    unnamed x40 -> x4, local copies, waits for them, and re-layouts: 4.5 us -> 1.3 us
    ppermute x17, starting transfers between devices: 19.5 us -> 22.3 us  [swap(): return lax.ppermute(value, 'dp', [(d, d ^ bits) for d in range(ranks)])]
    ppermute x3, waiting for transfers between devices: 7.83 us -> 5.07 us  [relayed(): return lax.ppermute(value, 'section', both)]
  transfers between devices with their start and end apart: 20 -> 20, of which waited for: 9 -> 7; matrix products, arithmetic and copies ran while one was open for 0% -> 0% of each run, Pallas kernels for 9% -> 4%
where the time goes in v2:
time: 68 us; the launch traced here: 67.8 us
  starting transfers between devices  31.8 us (47%)
  blocking collectives  16 us (24%)
  waiting for transfers between devices  10.3 us (15%)
  Pallas kernels  7.14 us (10%)
  between operations  1.37 us (2%)
  local copies, waits for them, and re-layouts  1.3 us (2%)
    ppermute x17, starting transfers between devices, swap(): return lax.ppermute(value, 'dp', [(d, d ^ bits) for d in range(ranks)])  22.3 us
    all_to_all x1, blocking collectives, per_device(): lax.all_to_all(announce.reshape(32, 8, 256), 'dp', 0, 0, tiled=True)  16 us
    ppermute x3, starting transfers between devices, relayed(): return lax.ppermute(value, 'section', both)  9.45 us
    pallas_call x9, Pallas kernels, with_operands(): run(*[value if space is SMEM else pltpu.with_memory_space_constraint(valu...  7.14 us
    ppermute x17, waiting for transfers between devices, swap(): return lax.ppermute(value, 'dp', [(d, d ^ bits) for d in range(ranks)])  5.2 us
    ppermute x3, waiting for transfers between devices, relayed(): return lax.ppermute(value, 'section', both)  5.07 us
  transfers between devices with their start and end apart: 20, of which 7 were waited for; matrix products, arithmetic and copies ran while one was open for 0% of the time, Pallas kernels for 4%

profile of v2, /device:TPU:1, one launch (start us, length us, event | category | flops | bytes accessed | tf_op | source)
XLA Modules:
  0.0 67.8 jit_solution(2873815897752041030)
XLA Ops:
  1.3 0.0 copy-start
  1.3 0.6 copy-done
  1.9 0.0 copy-start.1
  1.9 0.7 copy-done.1
  2.6 3.0 %shard_map.85 = (f32[128,384]{1,0:T(8,128)S(1)}, bf16[256,256]{1,0:T(8,128)(2,1)S(1)}, bf16[128,384]{1,0:T(8,128)(2,1)S(1)}, bf16[3,3,384,384]{3,2,1,0:T(8,128)(2,1)S(1)}, bf16[384,512]{1,0:T(8,128)(2,1)S(1)}) custom-call(bf16[128,384]{1,0:T(8,128)(2,1)} %bitcast.12, bf16[3,3,384,384]{3,2,1,0:T(8,128)(2,1)} %bitcast.10, bf16[384,512]{1,0:T(8,128)(2,1)} %head_hbm.1, ...), custom_call_target="tpu_custom_call" | custom-call | tf_op jit(solution)/shard_map/pallas_call | solution.py:306
  5.6 16.0 %all_to_all.5 = bf16[32,8,256]{2,1,0:T(8,128)(2,1)S(1)} all-to-all(bf16[32,8,256]{2,1,0:T(8,128)(2,1)S(1)} %bitcast.9), channel_id=1, replica_groups=mesh['section'=4,'dp'=32] {'dp'}, dimensions={0} | all-to-all | bytes 262144 | tf_op jit(solution)/shard_map/all_to_all | solution.py:354
  21.5 0.3 shard_map.86
  21.8 1.7 %collective-permute-start = (bf16[144,384]{1,0:T(8,128)(2,1)S(1)}, bf16[144,384]{1,0:T(8,128)(2,1)S(1)}, u32[]{:S(2)}, u32[]{:S(2)}) collective-permute-start(bf16[144,384]{1,0:T(8,128)(2,1)S(1)} %get-tuple-element.34.msg3), channel_id=1, source_target_pairs={{96,64},{32,0},{64,96},{0,32},{97,65},{33,1},{65,97},{1,33},{98,66... | collective-permute-start | bytes 331784 | tf_op jit(solution)/shard_map/ppermute | solution.py:333
  23.5 2.9 %collective-permute-done.arrived = bf16[144,384]{1,0:T(8,128)(2,1)S(1)} collective-permute-done((bf16[144,384]{1,0:T(8,128)(2,1)S(1)}, bf16[144,384]{1,0:T(8,128)(2,1)S(1)}, u32[]{:S(2)}, u32[]{:S(2)}) %collective-permute-start) | collective-permute-done | bytes 110624 | tf_op jit(solution)/shard_map/ppermute | solution.py:333
  26.5 6.1 %collective-permute-start.1 = (bf16[144,384]{1,0:T(8,128)(2,1)S(1)}, bf16[144,384]{1,0:T(8,128)(2,1)S(1)}, u32[]{:S(2)}, u32[]{:S(2)}) collective-permute-start(bf16[144,384]{1,0:T(8,128)(2,1)S(1)} %get-tuple-element.39.msg2), channel_id=1, source_target_pairs={{64,32},{96,0},{32,64},{0,96},{65,33},{97,1},{33,65},{1,97},{66,34... | collective-permute-start | bytes 331784 | tf_op jit(solution)/shard_map/ppermute | solution.py:333
  32.5 2.1 %collective-permute-done.1.arrived = bf16[144,384]{1,0:T(8,128)(2,1)S(1)} collective-permute-done((bf16[144,384]{1,0:T(8,128)(2,1)S(1)}, bf16[144,384]{1,0:T(8,128)(2,1)S(1)}, u32[]{:S(2)}, u32[]{:S(2)}) %collective-permute-start.1) | collective-permute-done | bytes 110624 | tf_op jit(solution)/shard_map/ppermute | solution.py:333
  34.7 1.7 %collective-permute-start.2 = (bf16[144,384]{1,0:T(8,128)(2,1)S(1)}, bf16[144,384]{1,0:T(8,128)(2,1)S(1)}, u32[]{:S(2)}, u32[]{:S(2)}) collective-permute-start(bf16[144,384]{1,0:T(8,128)(2,1)S(1)} %get-tuple-element.40.msg1), channel_id=1, source_target_pairs={{32,0},{96,64},{0,32},{64,96},{33,1},{97,65},{1,33},{65,97},{34,2}... | collective-permute-start | bytes 331784 | tf_op jit(solution)/shard_map/ppermute | solution.py:333
  36.3 0.5 collective-permute-start.4
  36.8 1.7 %collective-permute-start.6 = (bf16[96,128]{1,0:T(8,128)(2,1)S(1)}, bf16[96,128]{1,0:T(8,128)(2,1)S(1)}, u32[]{:S(2)}, u32[]{:S(2)}) collective-permute-start(bf16[96,128]{1,0:T(8,128)(2,1)S(1)} %get-tuple-element.46), channel_id=1, source_target_pairs={{0,4},{1,5},{2,6},{3,7},{4,0},{5,1},{6,2},{7,3},{8,12},{9,13},{10,... | collective-permute-start | bytes 73736 | tf_op jit(solution)/shard_map/ppermute | solution.py:329
  38.5 1.7 %collective-permute-start.8 = (bf16[96,128]{1,0:T(8,128)(2,1)S(1)}, bf16[96,128]{1,0:T(8,128)(2,1)S(1)}, u32[]{:S(2)}, u32[]{:S(2)}) collective-permute-start(bf16[96,128]{1,0:T(8,128)(2,1)S(1)} %get-tuple-element.47), channel_id=1, source_target_pairs={{0,6},{1,7},{2,4},{3,5},{4,2},{5,3},{6,0},{7,1},{8,14},{9,15},{10,... | collective-permute-start | bytes 73736 | tf_op jit(solution)/shard_map/ppermute | solution.py:329
  40.2 2.7 %collective-permute-start.3 = (bf16[96,128]{1,0:T(8,128)(2,1)S(1)}, bf16[96,128]{1,0:T(8,128)(2,1)S(1)}, u32[]{:S(2)}, u32[]{:S(2)}) collective-permute-start(bf16[96,128]{1,0:T(8,128)(2,1)S(1)} %get-tuple-element.44.refs_0_), channel_id=1, source_target_pairs={{0,1},{1,0},{2,3},{3,2},{4,5},{5,4},{6,7},{7,6},{8,9},{9,8},{10,11... | collective-permute-start | bytes 73736 | tf_op jit(solution)/shard_map/ppermute | solution.py:329
  42.9 0.0 collective-permute-done.4.refs_1_
  42.9 0.0 collective-permute-start.5
  42.9 0.0 collective-permute-done.6.refs_2_
  42.9 1.3 %collective-permute-start.7 = (bf16[96,128]{1,0:T(8,128)(2,1)S(1)}, bf16[96,128]{1,0:T(8,128)(2,1)S(1)}, u32[]{:S(2)}, u32[]{:S(2)}) collective-permute-start(bf16[96,128]{1,0:T(8,128)(2,1)S(1)} %collective-permute-done.6.refs_2_), channel_id=1, source_target_pairs={{0,1},{1,0},{2,3},{3,2},{4,5},{5,4},{6,7},{7,6},{8,9},{9,8},{10,11... | collective-permute-start | bytes 73736 | tf_op jit(solution)/shard_map/ppermute | solution.py:329
  44.2 0.0 collective-permute-done.8.refs_3_
  44.2 1.7 %collective-permute-start.9 = (bf16[96,128]{1,0:T(8,128)(2,1)S(1)}, bf16[96,128]{1,0:T(8,128)(2,1)S(1)}, u32[]{:S(2)}, u32[]{:S(2)}) collective-permute-start(bf16[96,128]{1,0:T(8,128)(2,1)S(1)} %collective-permute-done.8.refs_3_), channel_id=1, source_target_pairs={{0,1},{1,0},{2,3},{3,2},{4,5},{5,4},{6,7},{7,6},{8,9},{9,8},{10,11... | collective-permute-start | bytes 73736 | tf_op jit(solution)/shard_map/ppermute | solution.py:329
  46.0 0.0 collective-permute-done.3.refs_0_.refs_4_
  46.0 0.0 collective-permute-done.5.refs_1_.refs_5_
  46.0 0.0 collective-permute-done.7.refs_2_.refs_6_
  46.0 0.8 %collective-permute-done.9.refs_3_.refs_7_ = bf16[96,128]{1,0:T(8,128)(2,1)S(1)} collective-permute-done((bf16[96,128]{1,0:T(8,128)(2,1)S(1)}, bf16[96,128]{1,0:T(8,128)(2,1)S(1)}, u32[]{:S(2)}, u32[]{:S(2)}) %collective-permute-start.9) | collective-permute-done | bytes 24608 | tf_op jit(solution)/shard_map/ppermute | solution.py:329
  46.8 0.0 collective-permute-done.2.arrived
  46.8 1.8 %collective-permute-start.12 = (bf16[128,384]{1,0:T(8,128)(2,1)S(1)}, bf16[128,384]{1,0:T(8,128)(2,1)S(1)}, u32[]{:S(2)}, u32[]{:S(2)}) collective-permute-start(bf16[128,384]{1,0:T(8,128)(2,1)S(1)} %shard_map.89.refs_8_.refs_0_.dpre), channel_id=1, source_target_pairs={{0,6},{1,7},{2,4},{3,5},{4,2},{5,3},{6,0},{7,1},{8,14},{9,15},{10,... | collective-permute-start | bytes 294920 | tf_op jit(solution)/shard_map/ppermute | solution.py:329
  48.6 0.0 collective-permute-start.11
  48.6 1.6 %collective-permute-start.10 = (bf16[128,384]{1,0:T(8,128)(2,1)S(1)}, bf16[128,384]{1,0:T(8,128)(2,1)S(1)}, u32[]{:S(2)}, u32[]{:S(2)}) collective-permute-start(bf16[128,384]{1,0:T(8,128)(2,1)S(1)} %shard_map.89.refs_8_.refs_0_.dpre), channel_id=1, source_target_pairs={{0,2},{1,3},{2,0},{3,1},{4,6},{5,7},{6,4},{7,5},{8,10},{9,11},{10,... | collective-permute-start | bytes 294920 | tf_op jit(solution)/shard_map/ppermute | solution.py:329
  50.2 1.2 %collective-permute-start.13 = (bf16[128,384]{1,0:T(8,128)(2,1)S(1)}, bf16[128,384]{1,0:T(8,128)(2,1)S(1)}, u32[]{:S(2)}, u32[]{:S(2)}) collective-permute-start(bf16[128,384]{1,0:T(8,128)(2,1)S(1)} %shard_map.89.refs_8_.refs_0_.dpre), channel_id=1, source_target_pairs={{0,1},{1,0},{2,3},{3,2},{4,5},{5,4},{6,7},{7,6},{8,9},{9,8},{10,11... | collective-permute-start | bytes 294920 | tf_op jit(solution)/shard_map/ppermute | solution.py:329
  51.4 0.8 %collective-permute-done.12.refs_3_ = bf16[128,384]{1,0:T(8,128)(2,1)S(1)} collective-permute-done((bf16[128,384]{1,0:T(8,128)(2,1)S(1)}, bf16[128,384]{1,0:T(8,128)(2,1)S(1)}, u32[]{:S(2)}, u32[]{:S(2)}) %collective-permute-start.12) | collective-permute-done | bytes 98336 | tf_op jit(solution)/shard_map/ppermute | solution.py:329
  52.1 2.4 %collective-permute-start.16 = (bf16[128,384]{1,0:T(8,128)(2,1)S(1)}, bf16[128,384]{1,0:T(8,128)(2,1)S(1)}, u32[]{:S(2)}, u32[]{:S(2)}) collective-permute-start(bf16[128,384]{1,0:T(8,128)(2,1)S(1)} %collective-permute-done.12.refs_3_), channel_id=1, source_target_pairs={{0,1},{1,0},{2,3},{3,2},{4,5},{5,4},{6,7},{7,6},{8,9},{9,8},{10,11... | collective-permute-start | bytes 294920 | tf_op jit(solution)/shard_map/ppermute | solution.py:329
  54.5 0.0 collective-permute-done.11.refs_2_
  54.5 1.9 %collective-permute-start.15 = (bf16[128,384]{1,0:T(8,128)(2,1)S(1)}, bf16[128,384]{1,0:T(8,128)(2,1)S(1)}, u32[]{:S(2)}, u32[]{:S(2)}) collective-permute-start(bf16[128,384]{1,0:T(8,128)(2,1)S(1)} %collective-permute-done.11.refs_2_), channel_id=1, source_target_pairs={{0,1},{1,0},{2,3},{3,2},{4,5},{5,4},{6,7},{7,6},{8,9},{9,8},{10,11... | collective-permute-start | bytes 294920 | tf_op jit(solution)/shard_map/ppermute | solution.py:329
  56.4 0.0 collective-permute-done.10.refs_1_
  56.4 0.0 collective-permute-start.14
  56.4 0.9 %shard_map.90.stack = bf16[448,1024]{1,0:T(8,128)(2,1)S(1)} custom-call(bf16[96,128]{1,0:T(8,128)(2,1)S(1)} %get-tuple-element.44.refs_0_, bf16[96,128]{1,0:T(8,128)(2,1)S(1)} %collective-permute-done.4.refs_1_, bf16[96,128]{1,0:T(8,128)(2,1)S(1)} %collective-permute-done.6.refs_2_, bf16[96,128]{1,0:T(8,128)(2,1)S(1)} %collective-permute-done.8.refs_3_, ...), custom_call_target="tpu_custom_call" | custom-call | tf_op jit(solution)/shard_map/pallas_call | solution.py:306
  57.3 0.0 collective-permute-done.13.refs_4_
  57.3 0.0 collective-permute-done.16.refs_7_
  57.3 0.0 collective-permute-done.15.refs_6_
  57.4 0.3 collective-permute-done.14.refs_5_
  57.7 0.6 shard_map.91
  58.3 0.4 collective-permute-start.17
  58.8 1.7 %collective-permute-start.18 = (bf16[112,384]{1,0:T(8,128)(2,1)S(1)}, bf16[112,384]{1,0:T(8,128)(2,1)S(1)}, u32[]{:S(2)}, u32[]{:S(2)}) collective-permute-start(bf16[112,384]{1,0:T(8,128)(2,1)S(1)} %get-tuple-element.52), channel_id=1, source_target_pairs={{0,16},{1,17},{2,18},{3,19},{4,20},{5,21},{6,22},{7,23},{8,24},{9,... | collective-permute-start | bytes 258056 | tf_op jit(solution)/shard_map/ppermute | solution.py:329
  60.5 1.8 %collective-permute-start.19 = (bf16[112,384]{1,0:T(8,128)(2,1)S(1)}, bf16[112,384]{1,0:T(8,128)(2,1)S(1)}, u32[]{:S(2)}, u32[]{:S(2)}) collective-permute-start(bf16[112,384]{1,0:T(8,128)(2,1)S(1)} %get-tuple-element.53), channel_id=1, source_target_pairs={{0,24},{1,25},{2,26},{3,27},{4,28},{5,29},{6,30},{7,31},{8,16},{9,... | collective-permute-start | bytes 258056 | tf_op jit(solution)/shard_map/ppermute | solution.py:329
  62.3 1.6 %shard_map.92 = (bf16[128,384]{1,0:T(8,128)(2,1)}, f32[12,128]{1,0:T(8,128)}) custom-call(bf16[144,384]{1,0:T(8,128)(2,1)S(1)} %collective-permute-done.2.arrived, bf16[128,384]{1,0:T(8,128)(2,1)S(1)} %shard_map.89.refs_8_.refs_0_.dpre, bf16[3,3,384,384]{3,2,1,0:T(8,128)(2,1)S(1)} %get-tuple-element.32.w, f32[16,128]{1,0:T(8,128)S(1)} %get-tuple-element.48.head3, ...), custom_call_target="tpu_custom_call" | custom-call | tf_op jit(solution)/shard_map/pallas_call | solution.py:306
  63.9 0.0 collective-permute-done.17.part1
  63.9 1.0 %collective-permute-done.18.part2 = bf16[112,384]{1,0:T(8,128)(2,1)S(1)} collective-permute-done((bf16[112,384]{1,0:T(8,128)(2,1)S(1)}, bf16[112,384]{1,0:T(8,128)(2,1)S(1)}, u32[]{:S(2)}, u32[]{:S(2)}) %collective-permute-start.18) | collective-permute-done | bytes 86048 | tf_op jit(solution)/shard_map/ppermute | solution.py:329
  64.8 2.2 %collective-permute-done.19.part3 = bf16[112,384]{1,0:T(8,128)(2,1)S(1)} collective-permute-done((bf16[112,384]{1,0:T(8,128)(2,1)S(1)}, bf16[112,384]{1,0:T(8,128)(2,1)S(1)}, u32[]{:S(2)}, u32[]{:S(2)}) %collective-permute-start.19) | collective-permute-done | bytes 86048 | tf_op jit(solution)/shard_map/ppermute | solution.py:329
  67.1 0.7 %shard_map.93 = f32[108,1,384]{2,1,0:T(1,128)} custom-call(f32[112,384]{1,0:T(8,128)S(1)} %get-tuple-element.49.own, bf16[112,384]{1,0:T(8,128)(2,1)S(1)} %collective-permute-done.17.part1, bf16[112,384]{1,0:T(8,128)(2,1)S(1)} %collective-permute-done.18.part2, bf16[112,384]{1,0:T(8,128)(2,1)S(1)} %collective-permute-done.19.part3), custom_call_target="tpu_custom_call" | custom-call | tf_op jit(solution)/shard_map/pallas_call | solution.py:306
  (3 shorter events, 0.0 us)
Async XLA Ops:
  1.3 0.7 copy-start
  1.9 0.7 copy-start.1
  21.8 4.6 %collective-permute-start = (bf16[144,384]{1,0:T(8,128)(2,1)S(1)}, bf16[144,384]{1,0:T(8,128)(2,1)S(1)}, u32[]{:S(2)}, u32[]{:S(2)}) collective-permute-start(bf16[144,384]{1,0:T(8,128)(2,1)S(1)} %get-tuple-element.34.msg3), channel_id=1, source_target_pairs={{96,64},{32,0},{64,96},{0,32},{97,65},{33,1},{65,97},{1,33},{98,66... | collective-permute-start | bytes 331784 | tf_op jit(solution)/shard_map/ppermute | solution.py:333
  26.5 8.2 %collective-permute-start.1 = (bf16[144,384]{1,0:T(8,128)(2,1)S(1)}, bf16[144,384]{1,0:T(8,128)(2,1)S(1)}, u32[]{:S(2)}, u32[]{:S(2)}) collective-permute-start(bf16[144,384]{1,0:T(8,128)(2,1)S(1)} %get-tuple-element.39.msg2), channel_id=1, source_target_pairs={{64,32},{96,0},{32,64},{0,96},{65,33},{97,1},{33,65},{1,97},{66,34... | collective-permute-start | bytes 331784 | tf_op jit(solution)/shard_map/ppermute | solution.py:333
  34.7 12.1 %collective-permute-start.2 = (bf16[144,384]{1,0:T(8,128)(2,1)S(1)}, bf16[144,384]{1,0:T(8,128)(2,1)S(1)}, u32[]{:S(2)}, u32[]{:S(2)}) collective-permute-start(bf16[144,384]{1,0:T(8,128)(2,1)S(1)} %get-tuple-element.40.msg1), channel_id=1, source_target_pairs={{32,0},{96,64},{0,32},{64,96},{33,1},{97,65},{1,33},{65,97},{34,2}... | collective-permute-start | bytes 331784 | tf_op jit(solution)/shard_map/ppermute | solution.py:333
  36.3 6.5 %collective-permute-start.4 = (bf16[96,128]{1,0:T(8,128)(2,1)S(1)}, bf16[96,128]{1,0:T(8,128)(2,1)S(1)}, u32[]{:S(2)}, u32[]{:S(2)}) collective-permute-start(bf16[96,128]{1,0:T(8,128)(2,1)S(1)} %get-tuple-element.45), channel_id=1, source_target_pairs={{0,2},{1,3},{2,0},{3,1},{4,6},{5,7},{6,4},{7,5},{8,10},{9,11},{10,... | collective-permute-start | bytes 73736 | tf_op jit(solution)/shard_map/ppermute | solution.py:329
  36.8 6.1 %collective-permute-start.6 = (bf16[96,128]{1,0:T(8,128)(2,1)S(1)}, bf16[96,128]{1,0:T(8,128)(2,1)S(1)}, u32[]{:S(2)}, u32[]{:S(2)}) collective-permute-start(bf16[96,128]{1,0:T(8,128)(2,1)S(1)} %get-tuple-element.46), channel_id=1, source_target_pairs={{0,4},{1,5},{2,6},{3,7},{4,0},{5,1},{6,2},{7,3},{8,12},{9,13},{10,... | collective-permute-start | bytes 73736 | tf_op jit(solution)/shard_map/ppermute | solution.py:329
  38.5 5.7 %collective-permute-start.8 = (bf16[96,128]{1,0:T(8,128)(2,1)S(1)}, bf16[96,128]{1,0:T(8,128)(2,1)S(1)}, u32[]{:S(2)}, u32[]{:S(2)}) collective-permute-start(bf16[96,128]{1,0:T(8,128)(2,1)S(1)} %get-tuple-element.47), channel_id=1, source_target_pairs={{0,6},{1,7},{2,4},{3,5},{4,2},{5,3},{6,0},{7,1},{8,14},{9,15},{10,... | collective-permute-start | bytes 73736 | tf_op jit(solution)/shard_map/ppermute | solution.py:329
  40.2 5.8 %collective-permute-start.3 = (bf16[96,128]{1,0:T(8,128)(2,1)S(1)}, bf16[96,128]{1,0:T(8,128)(2,1)S(1)}, u32[]{:S(2)}, u32[]{:S(2)}) collective-permute-start(bf16[96,128]{1,0:T(8,128)(2,1)S(1)} %get-tuple-element.44.refs_0_), channel_id=1, source_target_pairs={{0,1},{1,0},{2,3},{3,2},{4,5},{5,4},{6,7},{7,6},{8,9},{9,8},{10,11... | collective-permute-start | bytes 73736 | tf_op jit(solution)/shard_map/ppermute | solution.py:329
  42.9 3.1 %collective-permute-start.5 = (bf16[96,128]{1,0:T(8,128)(2,1)S(1)}, bf16[96,128]{1,0:T(8,128)(2,1)S(1)}, u32[]{:S(2)}, u32[]{:S(2)}) collective-permute-start(bf16[96,128]{1,0:T(8,128)(2,1)S(1)} %collective-permute-done.4.refs_1_), channel_id=1, source_target_pairs={{0,1},{1,0},{2,3},{3,2},{4,5},{5,4},{6,7},{7,6},{8,9},{9,8},{10,11... | collective-permute-start | bytes 73736 | tf_op jit(solution)/shard_map/ppermute | solution.py:329
  42.9 3.1 %collective-permute-start.7 = (bf16[96,128]{1,0:T(8,128)(2,1)S(1)}, bf16[96,128]{1,0:T(8,128)(2,1)S(1)}, u32[]{:S(2)}, u32[]{:S(2)}) collective-permute-start(bf16[96,128]{1,0:T(8,128)(2,1)S(1)} %collective-permute-done.6.refs_2_), channel_id=1, source_target_pairs={{0,1},{1,0},{2,3},{3,2},{4,5},{5,4},{6,7},{7,6},{8,9},{9,8},{10,11... | collective-permute-start | bytes 73736 | tf_op jit(solution)/shard_map/ppermute | solution.py:329
  44.2 2.6 %collective-permute-start.9 = (bf16[96,128]{1,0:T(8,128)(2,1)S(1)}, bf16[96,128]{1,0:T(8,128)(2,1)S(1)}, u32[]{:S(2)}, u32[]{:S(2)}) collective-permute-start(bf16[96,128]{1,0:T(8,128)(2,1)S(1)} %collective-permute-done.8.refs_3_), channel_id=1, source_target_pairs={{0,1},{1,0},{2,3},{3,2},{4,5},{5,4},{6,7},{7,6},{8,9},{9,8},{10,11... | collective-permute-start | bytes 73736 | tf_op jit(solution)/shard_map/ppermute | solution.py:329
  46.8 5.3 %collective-permute-start.12 = (bf16[128,384]{1,0:T(8,128)(2,1)S(1)}, bf16[128,384]{1,0:T(8,128)(2,1)S(1)}, u32[]{:S(2)}, u32[]{:S(2)}) collective-permute-start(bf16[128,384]{1,0:T(8,128)(2,1)S(1)} %shard_map.89.refs_8_.refs_0_.dpre), channel_id=1, source_target_pairs={{0,6},{1,7},{2,4},{3,5},{4,2},{5,3},{6,0},{7,1},{8,14},{9,15},{10,... | collective-permute-start | bytes 294920 | tf_op jit(solution)/shard_map/ppermute | solution.py:329
  48.6 5.9 %collective-permute-start.11 = (bf16[128,384]{1,0:T(8,128)(2,1)S(1)}, bf16[128,384]{1,0:T(8,128)(2,1)S(1)}, u32[]{:S(2)}, u32[]{:S(2)}) collective-permute-start(bf16[128,384]{1,0:T(8,128)(2,1)S(1)} %shard_map.89.refs_8_.refs_0_.dpre), channel_id=1, source_target_pairs={{0,4},{1,5},{2,6},{3,7},{4,0},{5,1},{6,2},{7,3},{8,12},{9,13},{10,... | collective-permute-start | bytes 294920 | tf_op jit(solution)/shard_map/ppermute | solution.py:329
  48.6 7.8 %collective-permute-start.10 = (bf16[128,384]{1,0:T(8,128)(2,1)S(1)}, bf16[128,384]{1,0:T(8,128)(2,1)S(1)}, u32[]{:S(2)}, u32[]{:S(2)}) collective-permute-start(bf16[128,384]{1,0:T(8,128)(2,1)S(1)} %shard_map.89.refs_8_.refs_0_.dpre), channel_id=1, source_target_pairs={{0,2},{1,3},{2,0},{3,1},{4,6},{5,7},{6,4},{7,5},{8,10},{9,11},{10,... | collective-permute-start | bytes 294920 | tf_op jit(solution)/shard_map/ppermute | solution.py:329
  50.2 7.2 %collective-permute-start.13 = (bf16[128,384]{1,0:T(8,128)(2,1)S(1)}, bf16[128,384]{1,0:T(8,128)(2,1)S(1)}, u32[]{:S(2)}, u32[]{:S(2)}) collective-permute-start(bf16[128,384]{1,0:T(8,128)(2,1)S(1)} %shard_map.89.refs_8_.refs_0_.dpre), channel_id=1, source_target_pairs={{0,1},{1,0},{2,3},{3,2},{4,5},{5,4},{6,7},{7,6},{8,9},{9,8},{10,11... | collective-permute-start | bytes 294920 | tf_op jit(solution)/shard_map/ppermute | solution.py:329
  52.1 5.2 %collective-permute-start.16 = (bf16[128,384]{1,0:T(8,128)(2,1)S(1)}, bf16[128,384]{1,0:T(8,128)(2,1)S(1)}, u32[]{:S(2)}, u32[]{:S(2)}) collective-permute-start(bf16[128,384]{1,0:T(8,128)(2,1)S(1)} %collective-permute-done.12.refs_3_), channel_id=1, source_target_pairs={{0,1},{1,0},{2,3},{3,2},{4,5},{5,4},{6,7},{7,6},{8,9},{9,8},{10,11... | collective-permute-start | bytes 294920 | tf_op jit(solution)/shard_map/ppermute | solution.py:329
  54.5 2.9 %collective-permute-start.15 = (bf16[128,384]{1,0:T(8,128)(2,1)S(1)}, bf16[128,384]{1,0:T(8,128)(2,1)S(1)}, u32[]{:S(2)}, u32[]{:S(2)}) collective-permute-start(bf16[128,384]{1,0:T(8,128)(2,1)S(1)} %collective-permute-done.11.refs_2_), channel_id=1, source_target_pairs={{0,1},{1,0},{2,3},{3,2},{4,5},{5,4},{6,7},{7,6},{8,9},{9,8},{10,11... | collective-permute-start | bytes 294920 | tf_op jit(solution)/shard_map/ppermute | solution.py:329
  56.4 1.3 %collective-permute-start.14 = (bf16[128,384]{1,0:T(8,128)(2,1)S(1)}, bf16[128,384]{1,0:T(8,128)(2,1)S(1)}, u32[]{:S(2)}, u32[]{:S(2)}) collective-permute-start(bf16[128,384]{1,0:T(8,128)(2,1)S(1)} %collective-permute-done.10.refs_1_), channel_id=1, source_target_pairs={{0,1},{1,0},{2,3},{3,2},{4,5},{5,4},{6,7},{7,6},{8,9},{9,8},{10,11... | collective-permute-start | bytes 294920 | tf_op jit(solution)/shard_map/ppermute | solution.py:329
  58.3 5.5 %collective-permute-start.17 = (bf16[112,384]{1,0:T(8,128)(2,1)S(1)}, bf16[112,384]{1,0:T(8,128)(2,1)S(1)}, u32[]{:S(2)}, u32[]{:S(2)}) collective-permute-start(bf16[112,384]{1,0:T(8,128)(2,1)S(1)} %get-tuple-element.51), channel_id=1, source_target_pairs={{0,8},{1,9},{2,10},{3,11},{4,12},{5,13},{6,14},{7,15},{8,0},{9,1},... | collective-permute-start | bytes 258056 | tf_op jit(solution)/shard_map/ppermute | solution.py:329
  58.8 6.1 %collective-permute-start.18 = (bf16[112,384]{1,0:T(8,128)(2,1)S(1)}, bf16[112,384]{1,0:T(8,128)(2,1)S(1)}, u32[]{:S(2)}, u32[]{:S(2)}) collective-permute-start(bf16[112,384]{1,0:T(8,128)(2,1)S(1)} %get-tuple-element.52), channel_id=1, source_target_pairs={{0,16},{1,17},{2,18},{3,19},{4,20},{5,21},{6,22},{7,23},{8,24},{9,... | collective-permute-start | bytes 258056 | tf_op jit(solution)/shard_map/ppermute | solution.py:329
  60.5 6.6 %collective-permute-start.19 = (bf16[112,384]{1,0:T(8,128)(2,1)S(1)}, bf16[112,384]{1,0:T(8,128)(2,1)S(1)}, u32[]{:S(2)}, u32[]{:S(2)}) collective-permute-start(bf16[112,384]{1,0:T(8,128)(2,1)S(1)} %get-tuple-element.53), channel_id=1, source_target_pairs={{0,24},{1,25},{2,26},{3,27},{4,28},{5,29},{6,30},{7,31},{8,16},{9,... | collective-permute-start | bytes 258056 | tf_op jit(solution)/shard_map/ppermute | solution.py:329

commit v3 on v2

--- a/solution.py
+++ b/solution.py
@@ -71,10 +71,11 @@
 
 
 def forward_kernel(
-    saved_hbm, w_hbm, head_hbm, counts, pairs, valid, slope, message, saved, w, head, sem
+    saved_hbm, w_hbm, head_hbm, counts, pairs_hbm, valid_hbm,
+    slope, message, saved, w, head, pairs, valid, sem,
 ):
-    sources = [saved_hbm, w_hbm.at[0], w_hbm.at[1], w_hbm.at[2], head_hbm]
-    targets = [saved, w.at[0], w.at[1], w.at[2], head]
+    sources = [saved_hbm, w_hbm.at[0], w_hbm.at[1], w_hbm.at[2], pairs_hbm, valid_hbm, head_hbm]
+    targets = [saved, w.at[0], w.at[1], w.at[2], pairs, valid, head]
     copies = [
         pltpu.make_async_copy(source, target, sem.at[n])
         for n, (source, target) in enumerate(zip(sources, targets, strict=True))
@@ -96,7 +97,8 @@
     slope[...] = sigma * (1.0 + pre * (1.0 - sigma))
     feature = (v + pre * sigma).reshape(4, CELLS, CH)
     pooled = jnp.sum(feature, axis=1) / CELLS
-    copies[4].wait()
+    for copy in copies[4:]:
+        copy.wait()
     at = (row_iota((4, 128)), col_iota((4, 128)))
     extra = jnp.zeros((4, 128), f32)
     for slot in range(4):
@@ -159,19 +161,22 @@
     return dpooled[:4].astype(f32), mm(pooled_mine, dproj)
 
 
-def split_saved(saved, outs):
+def split_kernel(saved, order, *outs):
     _, _, y, x, c = position()
     m = row_iota((CH, 1))
     q = (m * 43691) >> 19
     i = m - 12 * q
-    channel = (y ^ (q & 3)) * 96 + (x ^ (q >> 3)) * 24 + (c ^ ((q >> 2) & 1)) * 12 + i
+    j, k = q & 3, q >> 3
+    to_y = y ^ (k >> 1) ^ (3 * (j >> 1))
+    to_x = x ^ (k & 1) ^ (3 * (j & 1))
+    channel = to_y * 96 + to_x * 24 + (c ^ ((q >> 2) & 1)) * 12 + i
     pick = jnp.where(col_iota((CH, CH)) == channel, 1.0, 0.0).astype(bf16)
     turned = mm(pick, saved[...], NT).astype(bf16)
     for k, out in enumerate(outs):
         out[...] = turned[96 * k : 96 * k + 96]
 
 
-def top_kernel(gathered, head, slope, w, saved, message, dpre_out, head_out, *split):
+def top_kernel(gathered, head, slope, w, message, dpre_out, head_out):
     section, rank, _, _, _ = position()
 
     @pl.when(section == 3)
@@ -186,10 +191,6 @@
         below = cot + conv_back(dpre.astype(f32), w)
         message[:128, :] = below.astype(bf16)
 
-    @pl.when(section != 3)
-    def _():
-        split_saved(saved, split)
-
 
 def relay(active, arrived, slope, w, message, dpre_out):
     @pl.when(lax.axis_index("section") == active)
@@ -202,12 +203,8 @@
         message[:128, :] = below.astype(bf16)
 
 
-def relay2_kernel(arrived, slope, w, saved, *refs):
-    relay(2, arrived, slope, w, refs[4], refs[5])
-
-    @pl.when(lax.axis_index("section") == 3)
-    def _():
-        split_saved(saved, refs[6:])
+def relay2_kernel(arrived, slope, w, message, dpre_out):
+    relay(2, arrived, slope, w, message, dpre_out)
 
 
 def relay1_kernel(arrived, slope, w, message, dpre_out):
@@ -324,6 +321,8 @@
     act = VMEM((ROWS, CH), bf16)
     msg = VMEM((MSG, CH), bf16)
     piece = VMEM((96, 128), bf16)
+    gather = (0, 2, 8, 10)
+    reduce = (0, 6, 24, 30)
 
     def swap(value, bits):
         return lax.ppermute(value, "dp", [(d, d ^ bits) for d in range(ranks)])
@@ -334,7 +333,7 @@
 
     slope, announce, rows, w, head = call(
         forward_kernel,
-        [HBM] * 3 + [SMEM] * 3,
+        [HBM] * 3 + [SMEM] + [HBM] * 2,
         (
             VMEM((ROWS, CH), f32),
             VMEM((256, 256), bf16),
@@ -342,7 +341,7 @@
             VMEM((3, 3, CH, CH), bf16),
             VMEM((CH, EMB), bf16),
         ),
-        [pltpu.SemaphoreType.DMA((5,))],
+        [SMEM((4,), jnp.int32), SMEM((4,), jnp.int32), pltpu.SemaphoreType.DMA((7,))],
     )(
         saved.reshape(ROWS, CH),
         jnp.transpose(kernels[0], (1, 2, 0, 3)),
@@ -352,25 +351,21 @@
         valid,
     )
     gathered = lax.all_to_all(announce.reshape(32, 8, 256), "dp", 0, 0, tiled=True)
-    msg3, dpre3, head3, *split = call(
-        top_kernel, [VMEM] * 5, (msg, act, VMEM((16, 128), f32)) + (piece,) * 4
-    )(gathered.reshape(256, 256), head, slope, w, rows)
+    msg3, dpre3, head3 = call(
+        top_kernel, [VMEM] * 4, (msg, act, VMEM((16, 128), f32))
+    )(gathered.reshape(256, 256), head, slope, w)
     arrived = relayed(msg3, [(3, 2), (1, 0)])
-    msg2, dpre2, *split = call(
-        relay2_kernel,
-        [VMEM] * 8,
-        (msg, act) + (piece,) * 4,
-        aliases={4 + k: 2 + k for k in range(4)},
-    )(arrived, slope, w, rows, *split)
+    split = call(split_kernel, [VMEM] * 2, (piece,) * 4)(rows, msg3)
+    near = [split[0]] + [swap(split[k], gather[k]) for k in range(1, 4)]
+    msg2, dpre2 = call(relay2_kernel, [VMEM] * 3, (msg, act))(arrived, slope, w)
     arrived = relayed(msg2, [(2, 1), (3, 0)])
-    near = [split[0]] + [swap(split[k], 2 * k) for k in range(1, 4)]
     msg1, dpre1 = call(relay1_kernel, [VMEM] * 3, (msg, act))(arrived, slope, w)
     arrived = relayed(msg1, [(1, 0), (3, 2)])
     far = [swap(value, 1) for value in near]
     dpre = call(bottom_kernel, [VMEM] * 9, act)(
         arrived, slope, dpre3, dpre2, dpre1, *far
     )
-    near_grads = [dpre] + [swap(dpre, 2 * k) for k in range(1, 4)]
+    near_grads = [dpre] + [swap(dpre, gather[k]) for k in range(1, 4)]
     stack = call(
         stack_kernel, [VMEM] * 9, VMEM((448, 1024), bf16), [VMEM((432, 1024), bf16)]
     )(*near, *far, dpre)
@@ -379,7 +374,7 @@
     own, *parts = call(
         wgrad_kernel, [VMEM] * 9, (VMEM((112, CH), f32), part, part, part)
     )(stack, *near_grads, *far_grads)
-    parts = [swap(parts[k - 1], 8 * k) for k in range(1, 4)]
+    parts = [swap(parts[k - 1], reduce[k]) for k in range(1, 4)]
     grads, head_grad = call(
         last_kernel, [VMEM] * 8, (sds((ROWS, CH), bf16), sds((12, 128), f32))
     )(arrived, dpre, w, head3, msg3, msg2, msg1, own)

time: 68 us -> 63.8 us (0.938)
  starting transfers between devices: 31.8 us -> 28.6 us
  local copies, waits for them, and re-layouts: 1.3 us -> 0 us
    ppermute x17, starting transfers between devices: 22.3 us -> 18.9 us  [swap(): return lax.ppermute(value, 'dp', [(d, d ^ bits) for d in range(ranks)])]
    unnamed x4 -> x0, local copies, waits for them, and re-layouts: 1.3 us -> none
    pallas_call x9 -> x10, Pallas kernels: 7.14 us -> 6.67 us  [with_operands(): run(*[value if space is SMEM else pltpu.with_memory_space_constraint(valu...]
where the time goes in v3:
time: 63.8 us; the launch traced here: 63.1 us
  starting transfers between devices  28.6 us (45%)
  blocking collectives  16 us (25%)
  waiting for transfers between devices  10.5 us (16%)
  Pallas kernels  6.67 us (10%)
  between operations  1.36 us (2%)
    ppermute x17, starting transfers between devices, swap(): return lax.ppermute(value, 'dp', [(d, d ^ bits) for d in range(ranks)])  18.9 us
    all_to_all x1, blocking collectives, per_device(): lax.all_to_all(announce.reshape(32, 8, 256), 'dp', 0, 0, tiled=True)  16 us
    ppermute x3, starting transfers between devices, relayed(): return lax.ppermute(value, 'section', both)  9.73 us
    pallas_call x10, Pallas kernels, with_operands(): run(*[value if space is SMEM else pltpu.with_memory_space_constraint(valu...  6.67 us
    ppermute x17, waiting for transfers between devices, swap(): return lax.ppermute(value, 'dp', [(d, d ^ bits) for d in range(ranks)])  5.43 us
    ppermute x3, waiting for transfers between devices, relayed(): return lax.ppermute(value, 'section', both)  5.06 us
  transfers between devices with their start and end apart: 20, of which 7 were waited for; matrix products, arithmetic and copies ran while one was open for 0% of the time, Pallas kernels for 4%

profile of v3, /device:TPU:1, one launch (start us, length us, event | category | flops | bytes accessed | tf_op | source)
XLA Modules:
  0.0 63.1 jit_solution(12152006940689718581)
XLA Ops:
  1.3 2.5 %shard_map.85 = (f32[128,384]{1,0:T(8,128)S(1)}, bf16[256,256]{1,0:T(8,128)(2,1)S(1)}, bf16[128,384]{1,0:T(8,128)(2,1)S(1)}, bf16[3,3,384,384]{3,2,1,0:T(8,128)(2,1)S(1)}, bf16[384,512]{1,0:T(8,128)(2,1)S(1)}) custom-call(bf16[128,384]{1,0:T(8,128)(2,1)} %bitcast.12, bf16[3,3,384,384]{3,2,1,0:T(8,128)(2,1)} %bitcast.10, bf16[384,512]{1,0:T(8,128)(2,1)} %head_hbm.1, ...), custom_call_target="tpu_custom_call" | custom-call | tf_op jit(solution)/shard_map/pallas_call | solution.py:303
  3.7 16.0 %all_to_all.5 = bf16[32,8,256]{2,1,0:T(8,128)(2,1)S(1)} all-to-all(bf16[32,8,256]{2,1,0:T(8,128)(2,1)S(1)} %bitcast.9), channel_id=1, replica_groups=mesh['section'=4,'dp'=32] {'dp'}, dimensions={0} | all-to-all | bytes 262144 | tf_op jit(solution)/shard_map/all_to_all | solution.py:353
  19.7 1.6 %collective-permute-start = (bf16[144,384]{1,0:T(8,128)(2,1)S(1)}, bf16[144,384]{1,0:T(8,128)(2,1)S(1)}, u32[]{:S(2)}, u32[]{:S(2)}) collective-permute-start(bf16[144,384]{1,0:T(8,128)(2,1)S(1)} %get-tuple-element.29.order.msg3), channel_id=1, source_target_pairs={{96,64},{32,0},{64,96},{0,32},{97,65},{33,1},{65,97},{1,33},{98,66... | collective-permute-start | bytes 331784 | tf_op jit(solution)/shard_map/ppermute | solution.py:332
  21.4 2.9 %collective-permute-done.arrived = bf16[144,384]{1,0:T(8,128)(2,1)S(1)} collective-permute-done((bf16[144,384]{1,0:T(8,128)(2,1)S(1)}, bf16[144,384]{1,0:T(8,128)(2,1)S(1)}, u32[]{:S(2)}, u32[]{:S(2)}) %collective-permute-start) | collective-permute-done | bytes 110624 | tf_op jit(solution)/shard_map/ppermute | solution.py:332
  24.3 6.1 %collective-permute-start.1 = (bf16[144,384]{1,0:T(8,128)(2,1)S(1)}, bf16[144,384]{1,0:T(8,128)(2,1)S(1)}, u32[]{:S(2)}, u32[]{:S(2)}) collective-permute-start(bf16[144,384]{1,0:T(8,128)(2,1)S(1)} %get-tuple-element.30.msg2), channel_id=1, source_target_pairs={{64,32},{96,0},{32,64},{0,96},{65,33},{97,1},{33,65},{1,97},{66,34... | collective-permute-start | bytes 331784 | tf_op jit(solution)/shard_map/ppermute | solution.py:332
  30.3 2.1 %collective-permute-done.1.arrived = bf16[144,384]{1,0:T(8,128)(2,1)S(1)} collective-permute-done((bf16[144,384]{1,0:T(8,128)(2,1)S(1)}, bf16[144,384]{1,0:T(8,128)(2,1)S(1)}, u32[]{:S(2)}, u32[]{:S(2)}) %collective-permute-start.1) | collective-permute-done | bytes 110624 | tf_op jit(solution)/shard_map/ppermute | solution.py:332
  32.5 2.0 %collective-permute-start.2 = (bf16[144,384]{1,0:T(8,128)(2,1)S(1)}, bf16[144,384]{1,0:T(8,128)(2,1)S(1)}, u32[]{:S(2)}, u32[]{:S(2)}) collective-permute-start(bf16[144,384]{1,0:T(8,128)(2,1)S(1)} %get-tuple-element.31.msg1), channel_id=1, source_target_pairs={{32,0},{96,64},{0,32},{64,96},{33,1},{97,65},{1,33},{65,97},{34,2}... | collective-permute-start | bytes 331784 | tf_op jit(solution)/shard_map/ppermute | solution.py:332
  34.5 0.3 shard_map.89
  34.8 0.6 collective-permute-start.4
  35.4 0.4 collective-permute-start.6
  35.7 1.8 %collective-permute-start.8 = (bf16[96,128]{1,0:T(8,128)(2,1)S(1)}, bf16[96,128]{1,0:T(8,128)(2,1)S(1)}, u32[]{:S(2)}, u32[]{:S(2)}) collective-permute-start(bf16[96,128]{1,0:T(8,128)(2,1)S(1)} %get-tuple-element.39), channel_id=1, source_target_pairs={{0,10},{1,11},{2,8},{3,9},{4,14},{5,15},{6,12},{7,13},{8,2},{9,3},... | collective-permute-start | bytes 73736 | tf_op jit(solution)/shard_map/ppermute | solution.py:328
  37.5 2.7 %collective-permute-start.3 = (bf16[96,128]{1,0:T(8,128)(2,1)S(1)}, bf16[96,128]{1,0:T(8,128)(2,1)S(1)}, u32[]{:S(2)}, u32[]{:S(2)}) collective-permute-start(bf16[96,128]{1,0:T(8,128)(2,1)S(1)} %get-tuple-element.36.refs_0_), channel_id=1, source_target_pairs={{0,1},{1,0},{2,3},{3,2},{4,5},{5,4},{6,7},{7,6},{8,9},{9,8},{10,11... | collective-permute-start | bytes 73736 | tf_op jit(solution)/shard_map/ppermute | solution.py:328
  40.2 0.0 collective-permute-done.4.refs_1_
  40.2 0.3 collective-permute-start.5
  40.6 0.0 collective-permute-done.6.refs_2_
  40.6 0.7 %collective-permute-start.7 = (bf16[96,128]{1,0:T(8,128)(2,1)S(1)}, bf16[96,128]{1,0:T(8,128)(2,1)S(1)}, u32[]{:S(2)}, u32[]{:S(2)}) collective-permute-start(bf16[96,128]{1,0:T(8,128)(2,1)S(1)} %collective-permute-done.6.refs_2_), channel_id=1, source_target_pairs={{0,1},{1,0},{2,3},{3,2},{4,5},{5,4},{6,7},{7,6},{8,9},{9,8},{10,11... | collective-permute-start | bytes 73736 | tf_op jit(solution)/shard_map/ppermute | solution.py:328
  41.3 0.0 collective-permute-done.8.refs_3_
  41.3 1.5 %collective-permute-start.9 = (bf16[96,128]{1,0:T(8,128)(2,1)S(1)}, bf16[96,128]{1,0:T(8,128)(2,1)S(1)}, u32[]{:S(2)}, u32[]{:S(2)}) collective-permute-start(bf16[96,128]{1,0:T(8,128)(2,1)S(1)} %collective-permute-done.8.refs_3_), channel_id=1, source_target_pairs={{0,1},{1,0},{2,3},{3,2},{4,5},{5,4},{6,7},{7,6},{8,9},{9,8},{10,11... | collective-permute-start | bytes 73736 | tf_op jit(solution)/shard_map/ppermute | solution.py:328
  42.8 0.0 collective-permute-done.3.refs_0_.refs_4_
  42.8 0.0 collective-permute-done.5.refs_1_.refs_5_
  42.8 0.0 collective-permute-done.7.refs_2_.refs_6_
  42.8 0.8 %collective-permute-done.9.refs_3_.refs_7_ = bf16[96,128]{1,0:T(8,128)(2,1)S(1)} collective-permute-done((bf16[96,128]{1,0:T(8,128)(2,1)S(1)}, bf16[96,128]{1,0:T(8,128)(2,1)S(1)}, u32[]{:S(2)}, u32[]{:S(2)}) %collective-permute-start.9) | collective-permute-done | bytes 24608 | tf_op jit(solution)/shard_map/ppermute | solution.py:328
  43.7 0.0 collective-permute-done.2.arrived
  43.7 1.9 %collective-permute-start.12 = (bf16[128,384]{1,0:T(8,128)(2,1)S(1)}, bf16[128,384]{1,0:T(8,128)(2,1)S(1)}, u32[]{:S(2)}, u32[]{:S(2)}) collective-permute-start(bf16[128,384]{1,0:T(8,128)(2,1)S(1)} %shard_map.90.refs_8_.refs_0_.dpre), channel_id=1, source_target_pairs={{0,10},{1,11},{2,8},{3,9},{4,14},{5,15},{6,12},{7,13},{8,2},{9,3},... | collective-permute-start | bytes 294920 | tf_op jit(solution)/shard_map/ppermute | solution.py:328
  45.6 0.4 collective-permute-start.11
  46.0 0.4 collective-permute-start.10
  46.4 1.2 %collective-permute-start.13 = (bf16[128,384]{1,0:T(8,128)(2,1)S(1)}, bf16[128,384]{1,0:T(8,128)(2,1)S(1)}, u32[]{:S(2)}, u32[]{:S(2)}) collective-permute-start(bf16[128,384]{1,0:T(8,128)(2,1)S(1)} %shard_map.90.refs_8_.refs_0_.dpre), channel_id=1, source_target_pairs={{0,1},{1,0},{2,3},{3,2},{4,5},{5,4},{6,7},{7,6},{8,9},{9,8},{10,11... | collective-permute-start | bytes 294920 | tf_op jit(solution)/shard_map/ppermute | solution.py:328
  47.6 1.1 %collective-permute-done.12.refs_3_ = bf16[128,384]{1,0:T(8,128)(2,1)S(1)} collective-permute-done((bf16[128,384]{1,0:T(8,128)(2,1)S(1)}, bf16[128,384]{1,0:T(8,128)(2,1)S(1)}, u32[]{:S(2)}, u32[]{:S(2)}) %collective-permute-start.12) | collective-permute-done | bytes 98336 | tf_op jit(solution)/shard_map/ppermute | solution.py:328
  48.7 1.3 %collective-permute-start.16 = (bf16[128,384]{1,0:T(8,128)(2,1)S(1)}, bf16[128,384]{1,0:T(8,128)(2,1)S(1)}, u32[]{:S(2)}, u32[]{:S(2)}) collective-permute-start(bf16[128,384]{1,0:T(8,128)(2,1)S(1)} %collective-permute-done.12.refs_3_), channel_id=1, source_target_pairs={{0,1},{1,0},{2,3},{3,2},{4,5},{5,4},{6,7},{7,6},{8,9},{9,8},{10,11... | collective-permute-start | bytes 294920 | tf_op jit(solution)/shard_map/ppermute | solution.py:328
  50.0 1.5 %collective-permute-done.11.refs_2_ = bf16[128,384]{1,0:T(8,128)(2,1)S(1)} collective-permute-done((bf16[128,384]{1,0:T(8,128)(2,1)S(1)}, bf16[128,384]{1,0:T(8,128)(2,1)S(1)}, u32[]{:S(2)}, u32[]{:S(2)}) %collective-permute-start.11) | collective-permute-done | bytes 98336 | tf_op jit(solution)/shard_map/ppermute | solution.py:328
  51.5 0.5 collective-permute-start.15
  52.0 0.0 collective-permute-done.10.refs_1_
  52.0 0.0 collective-permute-start.14
  52.0 0.9 %shard_map.91.stack = bf16[448,1024]{1,0:T(8,128)(2,1)S(1)} custom-call(bf16[96,128]{1,0:T(8,128)(2,1)S(1)} %get-tuple-element.36.refs_0_, bf16[96,128]{1,0:T(8,128)(2,1)S(1)} %collective-permute-done.4.refs_1_, bf16[96,128]{1,0:T(8,128)(2,1)S(1)} %collective-permute-done.6.refs_2_, bf16[96,128]{1,0:T(8,128)(2,1)S(1)} %collective-permute-done.8.refs_3_, ...), custom_call_target="tpu_custom_call" | custom-call | tf_op jit(solution)/shard_map/pallas_call | solution.py:303
  52.9 0.0 collective-permute-done.13.refs_4_
  53.0 0.0 collective-permute-done.16.refs_7_
  53.0 0.0 collective-permute-done.15.refs_6_
  53.0 0.3 collective-permute-done.14.refs_5_
  53.3 0.6 %shard_map.92 = (f32[112,384]{1,0:T(8,128)S(1)}, bf16[112,384]{1,0:T(8,128)(2,1)S(1)}, bf16[112,384]{1,0:T(8,128)(2,1)S(1)}, bf16[112,384]{1,0:T(8,128)(2,1)S(1)}) custom-call(bf16[448,1024]{1,0:T(8,128)(2,1)S(1)} %shard_map.91.stack, bf16[128,384]{1,0:T(8,128)(2,1)S(1)} %shard_map.90.refs_8_.refs_0_.dpre, ...), custom_call_target="tpu_custom_call" | custom-call | tf_op jit(solution)/shard_map/pallas_call | solution.py:303
  53.9 0.7 %collective-permute-start.17 = (bf16[112,384]{1,0:T(8,128)(2,1)S(1)}, bf16[112,384]{1,0:T(8,128)(2,1)S(1)}, u32[]{:S(2)}, u32[]{:S(2)}) collective-permute-start(bf16[112,384]{1,0:T(8,128)(2,1)S(1)} %get-tuple-element.43), channel_id=1, source_target_pairs={{0,6},{1,7},{2,4},{3,5},{4,2},{5,3},{6,0},{7,1},{8,14},{9,15},{10,... | collective-permute-start | bytes 258056 | tf_op jit(solution)/shard_map/ppermute | solution.py:328
  54.7 1.0 %collective-permute-start.18 = (bf16[112,384]{1,0:T(8,128)(2,1)S(1)}, bf16[112,384]{1,0:T(8,128)(2,1)S(1)}, u32[]{:S(2)}, u32[]{:S(2)}) collective-permute-start(bf16[112,384]{1,0:T(8,128)(2,1)S(1)} %get-tuple-element.44), channel_id=1, source_target_pairs={{0,24},{1,25},{2,26},{3,27},{4,28},{5,29},{6,30},{7,31},{8,16},{9,... | collective-permute-start | bytes 258056 | tf_op jit(solution)/shard_map/ppermute | solution.py:328
  55.7 3.4 %collective-permute-start.19 = (bf16[112,384]{1,0:T(8,128)(2,1)S(1)}, bf16[112,384]{1,0:T(8,128)(2,1)S(1)}, u32[]{:S(2)}, u32[]{:S(2)}) collective-permute-start(bf16[112,384]{1,0:T(8,128)(2,1)S(1)} %get-tuple-element.45), channel_id=1, source_target_pairs={{0,30},{1,31},{2,28},{3,29},{4,26},{5,27},{6,24},{7,25},{8,22},{9,... | collective-permute-start | bytes 258056 | tf_op jit(solution)/shard_map/ppermute | solution.py:328
  59.1 1.6 %shard_map.93 = (bf16[128,384]{1,0:T(8,128)(2,1)}, f32[12,128]{1,0:T(8,128)}) custom-call(bf16[144,384]{1,0:T(8,128)(2,1)S(1)} %collective-permute-done.2.arrived, bf16[128,384]{1,0:T(8,128)(2,1)S(1)} %shard_map.90.refs_8_.refs_0_.dpre, bf16[3,3,384,384]{3,2,1,0:T(8,128)(2,1)S(1)} %get-tuple-element.28.w, f32[16,128]{1,0:T(8,128)S(1)} %get-tuple-element.40.head3, ...), custom_call_target="tpu_custom_call" | custom-call | tf_op jit(solution)/shard_map/pallas_call | solution.py:303
  60.7 0.0 collective-permute-done.17.part1
  60.7 0.0 collective-permute-done.18.part2
  60.7 1.7 %collective-permute-done.19.part3 = bf16[112,384]{1,0:T(8,128)(2,1)S(1)} collective-permute-done((bf16[112,384]{1,0:T(8,128)(2,1)S(1)}, bf16[112,384]{1,0:T(8,128)(2,1)S(1)}, u32[]{:S(2)}, u32[]{:S(2)}) %collective-permute-start.19) | collective-permute-done | bytes 86048 | tf_op jit(solution)/shard_map/ppermute | solution.py:328
  62.3 0.7 %shard_map.94 = f32[108,1,384]{2,1,0:T(1,128)} custom-call(f32[112,384]{1,0:T(8,128)S(1)} %get-tuple-element.41.own, bf16[112,384]{1,0:T(8,128)(2,1)S(1)} %collective-permute-done.17.part1, bf16[112,384]{1,0:T(8,128)(2,1)S(1)} %collective-permute-done.18.part2, bf16[112,384]{1,0:T(8,128)(2,1)S(1)} %collective-permute-done.19.part3), custom_call_target="tpu_custom_call" | custom-call | tf_op jit(solution)/shard_map/pallas_call | solution.py:303
  (4 shorter events, 0.0 us)
Async XLA Ops:
  19.7 4.6 %collective-permute-start = (bf16[144,384]{1,0:T(8,128)(2,1)S(1)}, bf16[144,384]{1,0:T(8,128)(2,1)S(1)}, u32[]{:S(2)}, u32[]{:S(2)}) collective-permute-start(bf16[144,384]{1,0:T(8,128)(2,1)S(1)} %get-tuple-element.29.order.msg3), channel_id=1, source_target_pairs={{96,64},{32,0},{64,96},{0,32},{97,65},{33,1},{65,97},{1,33},{98,66... | collective-permute-start | bytes 331784 | tf_op jit(solution)/shard_map/ppermute | solution.py:332
  24.3 8.2 %collective-permute-start.1 = (bf16[144,384]{1,0:T(8,128)(2,1)S(1)}, bf16[144,384]{1,0:T(8,128)(2,1)S(1)}, u32[]{:S(2)}, u32[]{:S(2)}) collective-permute-start(bf16[144,384]{1,0:T(8,128)(2,1)S(1)} %get-tuple-element.30.msg2), channel_id=1, source_target_pairs={{64,32},{96,0},{32,64},{0,96},{65,33},{97,1},{33,65},{1,97},{66,34... | collective-permute-start | bytes 331784 | tf_op jit(solution)/shard_map/ppermute | solution.py:332
  32.5 11.2 %collective-permute-start.2 = (bf16[144,384]{1,0:T(8,128)(2,1)S(1)}, bf16[144,384]{1,0:T(8,128)(2,1)S(1)}, u32[]{:S(2)}, u32[]{:S(2)}) collective-permute-start(bf16[144,384]{1,0:T(8,128)(2,1)S(1)} %get-tuple-element.31.msg1), channel_id=1, source_target_pairs={{32,0},{96,64},{0,32},{64,96},{33,1},{97,65},{1,33},{65,97},{34,2}... | collective-permute-start | bytes 331784 | tf_op jit(solution)/shard_map/ppermute | solution.py:332
  34.8 5.4 %collective-permute-start.4 = (bf16[96,128]{1,0:T(8,128)(2,1)S(1)}, bf16[96,128]{1,0:T(8,128)(2,1)S(1)}, u32[]{:S(2)}, u32[]{:S(2)}) collective-permute-start(bf16[96,128]{1,0:T(8,128)(2,1)S(1)} %get-tuple-element.37), channel_id=1, source_target_pairs={{0,2},{1,3},{2,0},{3,1},{4,6},{5,7},{6,4},{7,5},{8,10},{9,11},{10,... | collective-permute-start | bytes 73736 | tf_op jit(solution)/shard_map/ppermute | solution.py:328
  35.4 5.2 %collective-permute-start.6 = (bf16[96,128]{1,0:T(8,128)(2,1)S(1)}, bf16[96,128]{1,0:T(8,128)(2,1)S(1)}, u32[]{:S(2)}, u32[]{:S(2)}) collective-permute-start(bf16[96,128]{1,0:T(8,128)(2,1)S(1)} %get-tuple-element.38), channel_id=1, source_target_pairs={{0,8},{1,9},{2,10},{3,11},{4,12},{5,13},{6,14},{7,15},{8,0},{9,1},... | collective-permute-start | bytes 73736 | tf_op jit(solution)/shard_map/ppermute | solution.py:328
  35.7 5.5 %collective-permute-start.8 = (bf16[96,128]{1,0:T(8,128)(2,1)S(1)}, bf16[96,128]{1,0:T(8,128)(2,1)S(1)}, u32[]{:S(2)}, u32[]{:S(2)}) collective-permute-start(bf16[96,128]{1,0:T(8,128)(2,1)S(1)} %get-tuple-element.39), channel_id=1, source_target_pairs={{0,10},{1,11},{2,8},{3,9},{4,14},{5,15},{6,12},{7,13},{8,2},{9,3},... | collective-permute-start | bytes 73736 | tf_op jit(solution)/shard_map/ppermute | solution.py:328
  37.5 5.3 %collective-permute-start.3 = (bf16[96,128]{1,0:T(8,128)(2,1)S(1)}, bf16[96,128]{1,0:T(8,128)(2,1)S(1)}, u32[]{:S(2)}, u32[]{:S(2)}) collective-permute-start(bf16[96,128]{1,0:T(8,128)(2,1)S(1)} %get-tuple-element.36.refs_0_), channel_id=1, source_target_pairs={{0,1},{1,0},{2,3},{3,2},{4,5},{5,4},{6,7},{7,6},{8,9},{9,8},{10,11... | collective-permute-start | bytes 73736 | tf_op jit(solution)/shard_map/ppermute | solution.py:328
  40.2 2.6 %collective-permute-start.5 = (bf16[96,128]{1,0:T(8,128)(2,1)S(1)}, bf16[96,128]{1,0:T(8,128)(2,1)S(1)}, u32[]{:S(2)}, u32[]{:S(2)}) collective-permute-start(bf16[96,128]{1,0:T(8,128)(2,1)S(1)} %collective-permute-done.4.refs_1_), channel_id=1, source_target_pairs={{0,1},{1,0},{2,3},{3,2},{4,5},{5,4},{6,7},{7,6},{8,9},{9,8},{10,11... | collective-permute-start | bytes 73736 | tf_op jit(solution)/shard_map/ppermute | solution.py:328
  40.6 2.3 %collective-permute-start.7 = (bf16[96,128]{1,0:T(8,128)(2,1)S(1)}, bf16[96,128]{1,0:T(8,128)(2,1)S(1)}, u32[]{:S(2)}, u32[]{:S(2)}) collective-permute-start(bf16[96,128]{1,0:T(8,128)(2,1)S(1)} %collective-permute-done.6.refs_2_), channel_id=1, source_target_pairs={{0,1},{1,0},{2,3},{3,2},{4,5},{5,4},{6,7},{7,6},{8,9},{9,8},{10,11... | collective-permute-start | bytes 73736 | tf_op jit(solution)/shard_map/ppermute | solution.py:328
  41.3 2.4 %collective-permute-start.9 = (bf16[96,128]{1,0:T(8,128)(2,1)S(1)}, bf16[96,128]{1,0:T(8,128)(2,1)S(1)}, u32[]{:S(2)}, u32[]{:S(2)}) collective-permute-start(bf16[96,128]{1,0:T(8,128)(2,1)S(1)} %collective-permute-done.8.refs_3_), channel_id=1, source_target_pairs={{0,1},{1,0},{2,3},{3,2},{4,5},{5,4},{6,7},{7,6},{8,9},{9,8},{10,11... | collective-permute-start | bytes 73736 | tf_op jit(solution)/shard_map/ppermute | solution.py:328
  43.7 5.0 %collective-permute-start.12 = (bf16[128,384]{1,0:T(8,128)(2,1)S(1)}, bf16[128,384]{1,0:T(8,128)(2,1)S(1)}, u32[]{:S(2)}, u32[]{:S(2)}) collective-permute-start(bf16[128,384]{1,0:T(8,128)(2,1)S(1)} %shard_map.90.refs_8_.refs_0_.dpre), channel_id=1, source_target_pairs={{0,10},{1,11},{2,8},{3,9},{4,14},{5,15},{6,12},{7,13},{8,2},{9,3},... | collective-permute-start | bytes 294920 | tf_op jit(solution)/shard_map/ppermute | solution.py:328
  45.6 5.9 %collective-permute-start.11 = (bf16[128,384]{1,0:T(8,128)(2,1)S(1)}, bf16[128,384]{1,0:T(8,128)(2,1)S(1)}, u32[]{:S(2)}, u32[]{:S(2)}) collective-permute-start(bf16[128,384]{1,0:T(8,128)(2,1)S(1)} %shard_map.90.refs_8_.refs_0_.dpre), channel_id=1, source_target_pairs={{0,8},{1,9},{2,10},{3,11},{4,12},{5,13},{6,14},{7,15},{8,0},{9,1},... | collective-permute-start | bytes 294920 | tf_op jit(solution)/shard_map/ppermute | solution.py:328
  46.0 6.0 %collective-permute-start.10 = (bf16[128,384]{1,0:T(8,128)(2,1)S(1)}, bf16[128,384]{1,0:T(8,128)(2,1)S(1)}, u32[]{:S(2)}, u32[]{:S(2)}) collective-permute-start(bf16[128,384]{1,0:T(8,128)(2,1)S(1)} %shard_map.90.refs_8_.refs_0_.dpre), channel_id=1, source_target_pairs={{0,2},{1,3},{2,0},{3,1},{4,6},{5,7},{6,4},{7,5},{8,10},{9,11},{10,... | collective-permute-start | bytes 294920 | tf_op jit(solution)/shard_map/ppermute | solution.py:328
  46.4 6.5 %collective-permute-start.13 = (bf16[128,384]{1,0:T(8,128)(2,1)S(1)}, bf16[128,384]{1,0:T(8,128)(2,1)S(1)}, u32[]{:S(2)}, u32[]{:S(2)}) collective-permute-start(bf16[128,384]{1,0:T(8,128)(2,1)S(1)} %shard_map.90.refs_8_.refs_0_.dpre), channel_id=1, source_target_pairs={{0,1},{1,0},{2,3},{3,2},{4,5},{5,4},{6,7},{7,6},{8,9},{9,8},{10,11... | collective-permute-start | bytes 294920 | tf_op jit(solution)/shard_map/ppermute | solution.py:328
  48.7 4.3 %collective-permute-start.16 = (bf16[128,384]{1,0:T(8,128)(2,1)S(1)}, bf16[128,384]{1,0:T(8,128)(2,1)S(1)}, u32[]{:S(2)}, u32[]{:S(2)}) collective-permute-start(bf16[128,384]{1,0:T(8,128)(2,1)S(1)} %collective-permute-done.12.refs_3_), channel_id=1, source_target_pairs={{0,1},{1,0},{2,3},{3,2},{4,5},{5,4},{6,7},{7,6},{8,9},{9,8},{10,11... | collective-permute-start | bytes 294920 | tf_op jit(solution)/shard_map/ppermute | solution.py:328
  51.5 1.5 %collective-permute-start.15 = (bf16[128,384]{1,0:T(8,128)(2,1)S(1)}, bf16[128,384]{1,0:T(8,128)(2,1)S(1)}, u32[]{:S(2)}, u32[]{:S(2)}) collective-permute-start(bf16[128,384]{1,0:T(8,128)(2,1)S(1)} %collective-permute-done.11.refs_2_), channel_id=1, source_target_pairs={{0,1},{1,0},{2,3},{3,2},{4,5},{5,4},{6,7},{7,6},{8,9},{9,8},{10,11... | collective-permute-start | bytes 294920 | tf_op jit(solution)/shard_map/ppermute | solution.py:328
  52.0 1.3 %collective-permute-start.14 = (bf16[128,384]{1,0:T(8,128)(2,1)S(1)}, bf16[128,384]{1,0:T(8,128)(2,1)S(1)}, u32[]{:S(2)}, u32[]{:S(2)}) collective-permute-start(bf16[128,384]{1,0:T(8,128)(2,1)S(1)} %collective-permute-done.10.refs_1_), channel_id=1, source_target_pairs={{0,1},{1,0},{2,3},{3,2},{4,5},{5,4},{6,7},{7,6},{8,9},{9,8},{10,11... | collective-permute-start | bytes 294920 | tf_op jit(solution)/shard_map/ppermute | solution.py:328
  53.9 6.7 %collective-permute-start.17 = (bf16[112,384]{1,0:T(8,128)(2,1)S(1)}, bf16[112,384]{1,0:T(8,128)(2,1)S(1)}, u32[]{:S(2)}, u32[]{:S(2)}) collective-permute-start(bf16[112,384]{1,0:T(8,128)(2,1)S(1)} %get-tuple-element.43), channel_id=1, source_target_pairs={{0,6},{1,7},{2,4},{3,5},{4,2},{5,3},{6,0},{7,1},{8,14},{9,15},{10,... | collective-permute-start | bytes 258056 | tf_op jit(solution)/shard_map/ppermute | solution.py:328
  54.7 6.0 %collective-permute-start.18 = (bf16[112,384]{1,0:T(8,128)(2,1)S(1)}, bf16[112,384]{1,0:T(8,128)(2,1)S(1)}, u32[]{:S(2)}, u32[]{:S(2)}) collective-permute-start(bf16[112,384]{1,0:T(8,128)(2,1)S(1)} %get-tuple-element.44), channel_id=1, source_target_pairs={{0,24},{1,25},{2,26},{3,27},{4,28},{5,29},{6,30},{7,31},{8,16},{9,... | collective-permute-start | bytes 258056 | tf_op jit(solution)/shard_map/ppermute | solution.py:328
  55.7 6.7 %collective-permute-start.19 = (bf16[112,384]{1,0:T(8,128)(2,1)S(1)}, bf16[112,384]{1,0:T(8,128)(2,1)S(1)}, u32[]{:S(2)}, u32[]{:S(2)}) collective-permute-start(bf16[112,384]{1,0:T(8,128)(2,1)S(1)} %get-tuple-element.45), channel_id=1, source_target_pairs={{0,30},{1,31},{2,28},{3,29},{4,26},{5,27},{6,24},{7,25},{8,22},{9,... | collective-permute-start | bytes 258056 | tf_op jit(solution)/shard_map/ppermute | solution.py:328

commit v4 on v3

--- a/solution.py
+++ b/solution.py
@@ -167,9 +167,13 @@
     q = (m * 43691) >> 19
     i = m - 12 * q
     j, k = q & 3, q >> 3
-    to_y = y ^ (k >> 1) ^ (3 * (j >> 1))
-    to_x = x ^ (k & 1) ^ (3 * (j & 1))
-    channel = to_y * 96 + to_x * 24 + (c ^ ((q >> 2) & 1)) * 12 + i
+    core = c ^ ((q >> 2) & 1)
+    flip_x = jnp.where((j == 3) | ((j > 0) & (core == 0)), 3, 0)
+    flip_y = jnp.where((j == 3) | ((j > 0) & (core == 1)), 3, 0)
+    to_y = y ^ (k >> 1) ^ flip_y
+    to_x = x ^ (k & 1) ^ flip_x
+    to_core = core ^ jnp.where(j == 2, 1, 0)
+    channel = to_y * 96 + to_x * 24 + to_core * 12 + i
     pick = jnp.where(col_iota((CH, CH)) == channel, 1.0, 0.0).astype(bf16)
     turned = mm(pick, saved[...], NT).astype(bf16)
     for k, out in enumerate(outs):
@@ -275,14 +279,14 @@
     rows = jnp.concatenate([g[...] for g in grads], axis=0)
     total = mm(stack[...], rows)
     outs[0][...] = total[:112]
-    for k in range(1, 4):
-        outs[k][...] = total[112 * k : 112 * k + 112].astype(bf16)
-
-
-def sum_kernel(own, part1, part2, part3, out):
-    total = own[...] + part1[...].astype(f32)
-    total = total + part2[...].astype(f32)
-    total = total + part3[...].astype(f32)
+    outs[1][...] = total[112:336].astype(bf16)
+    outs[2][...] = total[336:].astype(bf16)
+
+
+def sum_kernel(own, pair, crossed, diagonal, out):
+    total = own[...] + pair[:112, :].astype(f32)
+    total = total + crossed[112:, :].astype(f32)
+    total = total + diagonal[...].astype(f32)
     out[...] = total[:108].reshape(108, 1, CH)
 
 
@@ -322,10 +326,10 @@
     msg = VMEM((MSG, CH), bf16)
     piece = VMEM((96, 128), bf16)
     gather = (0, 2, 8, 10)
-    reduce = (0, 6, 24, 30)
-
-    def swap(value, bits):
-        return lax.ppermute(value, "dp", [(d, d ^ bits) for d in range(ranks)])
+
+    def swap(value, bits, odd_bits=None):
+        pairs_of = [(d, d ^ (odd_bits if odd_bits and d & 1 else bits)) for d in range(ranks)]
+        return lax.ppermute(value, "dp", pairs_of)
 
     def relayed(value, pairs_of):
         both = [(a, b) for a, b in pairs_of] + [(b, a) for a, b in pairs_of]
@@ -370,15 +374,18 @@
         stack_kernel, [VMEM] * 9, VMEM((448, 1024), bf16), [VMEM((432, 1024), bf16)]
     )(*near, *far, dpre)
     far_grads = [swap(value, 1) for value in near_grads]
-    part = VMEM((112, CH), bf16)
-    own, *parts = call(
-        wgrad_kernel, [VMEM] * 9, (VMEM((112, CH), f32), part, part, part)
+    own, pair, diagonal = call(
+        wgrad_kernel,
+        [VMEM] * 9,
+        (VMEM((112, CH), f32), VMEM((224, CH), bf16), VMEM((112, CH), bf16)),
     )(stack, *near_grads, *far_grads)
-    parts = [swap(parts[k - 1], reduce[k]) for k in range(1, 4)]
+    pair = swap(pair, 6, 24)
+    diagonal = swap(diagonal, 30)
+    crossed = swap(pair, 1)
     grads, head_grad = call(
         last_kernel, [VMEM] * 8, (sds((ROWS, CH), bf16), sds((12, 128), f32))
     )(arrived, dpre, w, head3, msg3, msg2, msg1, own)
-    wgrad = call(sum_kernel, [VMEM] * 4, sds((108, 1, CH), f32))(own, *parts)
+    wgrad = call(sum_kernel, [VMEM] * 4, sds((108, 1, CH), f32))(own, pair, crossed, diagonal)
     return (
         grads.reshape(saved.shape),
         wgrad.reshape(1, 12, 3, 3, CH),

time: 63.8 us -> 69.2 us (1.085)
  waiting for transfers between devices: 10.5 us -> 18.2 us
  starting transfers between devices: 28.6 us -> 26.8 us
    ppermute x17, waiting for transfers between devices: 5.43 us -> 13.1 us  [swap(): return lax.ppermute(value, 'dp', pairs_of)]
    ppermute x17, starting transfers between devices: 18.9 us -> 17.1 us  [swap(): return lax.ppermute(value, 'dp', pairs_of)]
  transfers between devices with their start and end apart: 20 -> 20, of which waited for: 7 -> 8; matrix products, arithmetic and copies ran while one was open for 0% -> 0% of each run, Pallas kernels for 4% -> 4%
where the time goes in v4:
time: 69.2 us; the launch traced here: 69 us
  starting transfers between devices  26.8 us (39%)
  waiting for transfers between devices  18.2 us (26%)
  blocking collectives  16 us (23%)
  Pallas kernels  6.71 us (10%)
  between operations  1.36 us (2%)
    ppermute x17, starting transfers between devices, swap(): return lax.ppermute(value, 'dp', pairs_of)  17.1 us
    all_to_all x1, blocking collectives, per_device(): lax.all_to_all(announce.reshape(32, 8, 256), 'dp', 0, 0, tiled=True)  16 us
    ppermute x17, waiting for transfers between devices, swap(): return lax.ppermute(value, 'dp', pairs_of)  13.1 us
    ppermute x3, starting transfers between devices, relayed(): return lax.ppermute(value, 'section', both)  9.73 us
    pallas_call x10, Pallas kernels, with_operands(): run(*[value if space is SMEM else pltpu.with_memory_space_constraint(valu...  6.71 us
    ppermute x3, waiting for transfers between devices, relayed(): return lax.ppermute(value, 'section', both)  5.06 us
  transfers between devices with their start and end apart: 20, of which 8 were waited for; matrix products, arithmetic and copies ran while one was open for 0% of the time, Pallas kernels for 4%

profile of v4, /device:TPU:1, one launch (start us, length us, event | category | flops | bytes accessed | tf_op | source)
XLA Modules:
  0.0 69.0 jit_solution(8094598849495238066)
XLA Ops:
  1.3 2.5 %shard_map.85 = (f32[128,384]{1,0:T(8,128)S(1)}, bf16[256,256]{1,0:T(8,128)(2,1)S(1)}, bf16[128,384]{1,0:T(8,128)(2,1)S(1)}, bf16[3,3,384,384]{3,2,1,0:T(8,128)(2,1)S(1)}, bf16[384,512]{1,0:T(8,128)(2,1)S(1)}) custom-call(bf16[128,384]{1,0:T(8,128)(2,1)} %bitcast.12, bf16[3,3,384,384]{3,2,1,0:T(8,128)(2,1)} %bitcast.10, bf16[384,512]{1,0:T(8,128)(2,1)} %head_hbm.1, ...), custom_call_target="tpu_custom_call" | custom-call | tf_op jit(solution)/shard_map/pallas_call | solution.py:307
  3.7 16.0 %all_to_all.5 = bf16[32,8,256]{2,1,0:T(8,128)(2,1)S(1)} all-to-all(bf16[32,8,256]{2,1,0:T(8,128)(2,1)S(1)} %bitcast.9), channel_id=1, replica_groups=mesh['section'=4,'dp'=32] {'dp'}, dimensions={0} | all-to-all | bytes 262144 | tf_op jit(solution)/shard_map/all_to_all | solution.py:357
  19.7 1.6 %collective-permute-start = (bf16[144,384]{1,0:T(8,128)(2,1)S(1)}, bf16[144,384]{1,0:T(8,128)(2,1)S(1)}, u32[]{:S(2)}, u32[]{:S(2)}) collective-permute-start(bf16[144,384]{1,0:T(8,128)(2,1)S(1)} %get-tuple-element.28.order.msg3), channel_id=1, source_target_pairs={{96,64},{32,0},{64,96},{0,32},{97,65},{33,1},{65,97},{1,33},{98,66... | collective-permute-start | bytes 331784 | tf_op jit(solution)/shard_map/ppermute | solution.py:336
  21.4 2.9 %collective-permute-done.arrived = bf16[144,384]{1,0:T(8,128)(2,1)S(1)} collective-permute-done((bf16[144,384]{1,0:T(8,128)(2,1)S(1)}, bf16[144,384]{1,0:T(8,128)(2,1)S(1)}, u32[]{:S(2)}, u32[]{:S(2)}) %collective-permute-start) | collective-permute-done | bytes 110624 | tf_op jit(solution)/shard_map/ppermute | solution.py:336
  24.3 6.1 %collective-permute-start.1 = (bf16[144,384]{1,0:T(8,128)(2,1)S(1)}, bf16[144,384]{1,0:T(8,128)(2,1)S(1)}, u32[]{:S(2)}, u32[]{:S(2)}) collective-permute-start(bf16[144,384]{1,0:T(8,128)(2,1)S(1)} %get-tuple-element.29.msg2), channel_id=1, source_target_pairs={{64,32},{96,0},{32,64},{0,96},{65,33},{97,1},{33,65},{1,97},{66,34... | collective-permute-start | bytes 331784 | tf_op jit(solution)/shard_map/ppermute | solution.py:336
  30.3 2.1 %collective-permute-done.1.arrived = bf16[144,384]{1,0:T(8,128)(2,1)S(1)} collective-permute-done((bf16[144,384]{1,0:T(8,128)(2,1)S(1)}, bf16[144,384]{1,0:T(8,128)(2,1)S(1)}, u32[]{:S(2)}, u32[]{:S(2)}) %collective-permute-start.1) | collective-permute-done | bytes 110624 | tf_op jit(solution)/shard_map/ppermute | solution.py:336
  32.5 2.0 %collective-permute-start.2 = (bf16[144,384]{1,0:T(8,128)(2,1)S(1)}, bf16[144,384]{1,0:T(8,128)(2,1)S(1)}, u32[]{:S(2)}, u32[]{:S(2)}) collective-permute-start(bf16[144,384]{1,0:T(8,128)(2,1)S(1)} %get-tuple-element.30.msg1), channel_id=1, source_target_pairs={{32,0},{96,64},{0,32},{64,96},{33,1},{97,65},{1,33},{65,97},{34,2}... | collective-permute-start | bytes 331784 | tf_op jit(solution)/shard_map/ppermute | solution.py:336
  34.5 0.3 shard_map.89
  34.9 0.6 collective-permute-start.4
  35.4 0.4 collective-permute-start.6
  35.8 1.8 %collective-permute-start.8 = (bf16[96,128]{1,0:T(8,128)(2,1)S(1)}, bf16[96,128]{1,0:T(8,128)(2,1)S(1)}, u32[]{:S(2)}, u32[]{:S(2)}) collective-permute-start(bf16[96,128]{1,0:T(8,128)(2,1)S(1)} %get-tuple-element.38), channel_id=1, source_target_pairs={{0,10},{1,11},{2,8},{3,9},{4,14},{5,15},{6,12},{7,13},{8,2},{9,3},... | collective-permute-start | bytes 73736 | tf_op jit(solution)/shard_map/ppermute | solution.py:332
  37.6 2.7 %collective-permute-start.3 = (bf16[96,128]{1,0:T(8,128)(2,1)S(1)}, bf16[96,128]{1,0:T(8,128)(2,1)S(1)}, u32[]{:S(2)}, u32[]{:S(2)}) collective-permute-start(bf16[96,128]{1,0:T(8,128)(2,1)S(1)} %get-tuple-element.35.refs_0_), channel_id=1, source_target_pairs={{0,1},{1,0},{2,3},{3,2},{4,5},{5,4},{6,7},{7,6},{8,9},{9,8},{10,11... | collective-permute-start | bytes 73736 | tf_op jit(solution)/shard_map/ppermute | solution.py:332
  40.3 0.0 collective-permute-done.4.refs_1_
  40.3 0.3 collective-permute-start.5
  40.6 0.0 collective-permute-done.6.refs_2_
  40.6 0.7 %collective-permute-start.7 = (bf16[96,128]{1,0:T(8,128)(2,1)S(1)}, bf16[96,128]{1,0:T(8,128)(2,1)S(1)}, u32[]{:S(2)}, u32[]{:S(2)}) collective-permute-start(bf16[96,128]{1,0:T(8,128)(2,1)S(1)} %collective-permute-done.6.refs_2_), channel_id=1, source_target_pairs={{0,1},{1,0},{2,3},{3,2},{4,5},{5,4},{6,7},{7,6},{8,9},{9,8},{10,11... | collective-permute-start | bytes 73736 | tf_op jit(solution)/shard_map/ppermute | solution.py:332
  41.3 0.0 collective-permute-done.8.refs_3_
  41.3 1.5 %collective-permute-start.9 = (bf16[96,128]{1,0:T(8,128)(2,1)S(1)}, bf16[96,128]{1,0:T(8,128)(2,1)S(1)}, u32[]{:S(2)}, u32[]{:S(2)}) collective-permute-start(bf16[96,128]{1,0:T(8,128)(2,1)S(1)} %collective-permute-done.8.refs_3_), channel_id=1, source_target_pairs={{0,1},{1,0},{2,3},{3,2},{4,5},{5,4},{6,7},{7,6},{8,9},{9,8},{10,11... | collective-permute-start | bytes 73736 | tf_op jit(solution)/shard_map/ppermute | solution.py:332
  42.8 0.0 collective-permute-done.3.refs_0_.refs_4_
  42.8 0.0 collective-permute-done.5.refs_1_.refs_5_
  42.9 0.0 collective-permute-done.7.refs_2_.refs_6_
  42.9 0.8 %collective-permute-done.9.refs_3_.refs_7_ = bf16[96,128]{1,0:T(8,128)(2,1)S(1)} collective-permute-done((bf16[96,128]{1,0:T(8,128)(2,1)S(1)}, bf16[96,128]{1,0:T(8,128)(2,1)S(1)}, u32[]{:S(2)}, u32[]{:S(2)}) %collective-permute-start.9) | collective-permute-done | bytes 24608 | tf_op jit(solution)/shard_map/ppermute | solution.py:332
  43.7 0.0 collective-permute-done.2.arrived
  43.7 1.9 %collective-permute-start.12 = (bf16[128,384]{1,0:T(8,128)(2,1)S(1)}, bf16[128,384]{1,0:T(8,128)(2,1)S(1)}, u32[]{:S(2)}, u32[]{:S(2)}) collective-permute-start(bf16[128,384]{1,0:T(8,128)(2,1)S(1)} %shard_map.90.refs_8_.refs_0_.dpre), channel_id=1, source_target_pairs={{0,10},{1,11},{2,8},{3,9},{4,14},{5,15},{6,12},{7,13},{8,2},{9,3},... | collective-permute-start | bytes 294920 | tf_op jit(solution)/shard_map/ppermute | solution.py:332
  45.7 0.4 collective-permute-start.11
  46.0 0.4 collective-permute-start.10
  46.5 1.2 %collective-permute-start.13 = (bf16[128,384]{1,0:T(8,128)(2,1)S(1)}, bf16[128,384]{1,0:T(8,128)(2,1)S(1)}, u32[]{:S(2)}, u32[]{:S(2)}) collective-permute-start(bf16[128,384]{1,0:T(8,128)(2,1)S(1)} %shard_map.90.refs_8_.refs_0_.dpre), channel_id=1, source_target_pairs={{0,1},{1,0},{2,3},{3,2},{4,5},{5,4},{6,7},{7,6},{8,9},{9,8},{10,11... | collective-permute-start | bytes 294920 | tf_op jit(solution)/shard_map/ppermute | solution.py:332
  47.6 1.1 %collective-permute-done.12.refs_3_ = bf16[128,384]{1,0:T(8,128)(2,1)S(1)} collective-permute-done((bf16[128,384]{1,0:T(8,128)(2,1)S(1)}, bf16[128,384]{1,0:T(8,128)(2,1)S(1)}, u32[]{:S(2)}, u32[]{:S(2)}) %collective-permute-start.12) | collective-permute-done | bytes 98336 | tf_op jit(solution)/shard_map/ppermute | solution.py:332
  48.7 1.3 %collective-permute-start.16 = (bf16[128,384]{1,0:T(8,128)(2,1)S(1)}, bf16[128,384]{1,0:T(8,128)(2,1)S(1)}, u32[]{:S(2)}, u32[]{:S(2)}) collective-permute-start(bf16[128,384]{1,0:T(8,128)(2,1)S(1)} %collective-permute-done.12.refs_3_), channel_id=1, source_target_pairs={{0,1},{1,0},{2,3},{3,2},{4,5},{5,4},{6,7},{7,6},{8,9},{9,8},{10,11... | collective-permute-start | bytes 294920 | tf_op jit(solution)/shard_map/ppermute | solution.py:332
  50.0 1.5 %collective-permute-done.11.refs_2_ = bf16[128,384]{1,0:T(8,128)(2,1)S(1)} collective-permute-done((bf16[128,384]{1,0:T(8,128)(2,1)S(1)}, bf16[128,384]{1,0:T(8,128)(2,1)S(1)}, u32[]{:S(2)}, u32[]{:S(2)}) %collective-permute-start.11) | collective-permute-done | bytes 98336 | tf_op jit(solution)/shard_map/ppermute | solution.py:332
  51.5 0.5 collective-permute-start.15
  52.0 0.0 collective-permute-done.10.refs_1_
  52.0 0.0 collective-permute-start.14
  52.0 0.9 %shard_map.91.stack = bf16[448,1024]{1,0:T(8,128)(2,1)S(1)} custom-call(bf16[96,128]{1,0:T(8,128)(2,1)S(1)} %get-tuple-element.35.refs_0_, bf16[96,128]{1,0:T(8,128)(2,1)S(1)} %collective-permute-done.4.refs_1_, bf16[96,128]{1,0:T(8,128)(2,1)S(1)} %collective-permute-done.6.refs_2_, bf16[96,128]{1,0:T(8,128)(2,1)S(1)} %collective-permute-done.8.refs_3_, ...), custom_call_target="tpu_custom_call" | custom-call | tf_op jit(solution)/shard_map/pallas_call | solution.py:307
  53.0 0.0 collective-permute-done.13.refs_4_
  53.0 0.0 collective-permute-done.16.refs_7_
  53.0 0.0 collective-permute-done.15.refs_6_
  53.0 0.3 collective-permute-done.14.refs_5_
  53.3 0.6 shard_map.92
  54.0 1.0 %collective-permute-start.17 = (bf16[224,384]{1,0:T(8,128)(2,1)S(1)}, bf16[224,384]{1,0:T(8,128)(2,1)S(1)}, u32[]{:S(2)}, u32[]{:S(2)}) collective-permute-start(bf16[224,384]{1,0:T(8,128)(2,1)S(1)} %get-tuple-element.42), channel_id=1, source_target_pairs={{0,6},{1,25},{2,4},{3,27},{4,2},{5,29},{6,0},{7,31},{8,14},{9,17},... | collective-permute-start | bytes 516104 | tf_op jit(solution)/shard_map/ppermute | solution.py:332
  55.0 4.9 %collective-permute-done.17.pair = bf16[224,384]{1,0:T(8,128)(2,1)S(1)} collective-permute-done((bf16[224,384]{1,0:T(8,128)(2,1)S(1)}, bf16[224,384]{1,0:T(8,128)(2,1)S(1)}, u32[]{:S(2)}, u32[]{:S(2)}) %collective-permute-start.17) | collective-permute-done | bytes 172064 | tf_op jit(solution)/shard_map/ppermute | solution.py:332
  59.8 1.0 %collective-permute-start.18 = (bf16[224,384]{1,0:T(8,128)(2,1)S(1)}, bf16[224,384]{1,0:T(8,128)(2,1)S(1)}, u32[]{:S(2)}, u32[]{:S(2)}) collective-permute-start(bf16[224,384]{1,0:T(8,128)(2,1)S(1)} %collective-permute-done.17.pair), channel_id=1, source_target_pairs={{0,1},{1,0},{2,3},{3,2},{4,5},{5,4},{6,7},{7,6},{8,9},{9,8},{10,11... | collective-permute-start | bytes 516104 | tf_op jit(solution)/shard_map/ppermute | solution.py:332
  60.9 1.4 %collective-permute-start.19 = (bf16[112,384]{1,0:T(8,128)(2,1)S(1)}, bf16[112,384]{1,0:T(8,128)(2,1)S(1)}, u32[]{:S(2)}, u32[]{:S(2)}) collective-permute-start(bf16[112,384]{1,0:T(8,128)(2,1)S(1)} %get-tuple-element.43), channel_id=1, source_target_pairs={{0,30},{1,31},{2,28},{3,29},{4,26},{5,27},{6,24},{7,25},{8,22},{9,... | collective-permute-start | bytes 258056 | tf_op jit(solution)/shard_map/ppermute | solution.py:332
  62.2 1.6 %shard_map.93 = (bf16[128,384]{1,0:T(8,128)(2,1)}, f32[12,128]{1,0:T(8,128)}) custom-call(bf16[144,384]{1,0:T(8,128)(2,1)S(1)} %collective-permute-done.2.arrived, bf16[128,384]{1,0:T(8,128)(2,1)S(1)} %shard_map.90.refs_8_.refs_0_.dpre, bf16[3,3,384,384]{3,2,1,0:T(8,128)(2,1)S(1)} %get-tuple-element.27.w, f32[16,128]{1,0:T(8,128)S(1)} %get-tuple-element.39.head3, ...), custom_call_target="tpu_custom_call" | custom-call | tf_op jit(solution)/shard_map/pallas_call | solution.py:307
  63.8 4.5 %collective-permute-done.19.diagonal = bf16[112,384]{1,0:T(8,128)(2,1)S(1)} collective-permute-done((bf16[112,384]{1,0:T(8,128)(2,1)S(1)}, bf16[112,384]{1,0:T(8,128)(2,1)S(1)}, u32[]{:S(2)}, u32[]{:S(2)}) %collective-permute-start.19) | collective-permute-done | bytes 86048 | tf_op jit(solution)/shard_map/ppermute | solution.py:332
  68.3 0.0 collective-permute-done.18.crossed
  68.3 0.7 %shard_map.94 = f32[108,1,384]{2,1,0:T(1,128)} custom-call(f32[112,384]{1,0:T(8,128)S(1)} %get-tuple-element.40.own, bf16[224,384]{1,0:T(8,128)(2,1)S(1)} %collective-permute-done.17.pair, bf16[224,384]{1,0:T(8,128)(2,1)S(1)} %collective-permute-done.18.crossed, bf16[112,384]{1,0:T(8,128)(2,1)S(1)} %collective-permute-done.19.diagonal), custom_call_target="tpu_custom_call" | custom-call | tf_op jit(solution)/shard_map/pallas_call | solution.py:307
  (4 shorter events, 0.0 us)
Async XLA Ops:
  19.7 4.6 %collective-permute-start = (bf16[144,384]{1,0:T(8,128)(2,1)S(1)}, bf16[144,384]{1,0:T(8,128)(2,1)S(1)}, u32[]{:S(2)}, u32[]{:S(2)}) collective-permute-start(bf16[144,384]{1,0:T(8,128)(2,1)S(1)} %get-tuple-element.28.order.msg3), channel_id=1, source_target_pairs={{96,64},{32,0},{64,96},{0,32},{97,65},{33,1},{65,97},{1,33},{98,66... | collective-permute-start | bytes 331784 | tf_op jit(solution)/shard_map/ppermute | solution.py:336
  24.3 8.2 %collective-permute-start.1 = (bf16[144,384]{1,0:T(8,128)(2,1)S(1)}, bf16[144,384]{1,0:T(8,128)(2,1)S(1)}, u32[]{:S(2)}, u32[]{:S(2)}) collective-permute-start(bf16[144,384]{1,0:T(8,128)(2,1)S(1)} %get-tuple-element.29.msg2), channel_id=1, source_target_pairs={{64,32},{96,0},{32,64},{0,96},{65,33},{97,1},{33,65},{1,97},{66,34... | collective-permute-start | bytes 331784 | tf_op jit(solution)/shard_map/ppermute | solution.py:336
  32.5 11.2 %collective-permute-start.2 = (bf16[144,384]{1,0:T(8,128)(2,1)S(1)}, bf16[144,384]{1,0:T(8,128)(2,1)S(1)}, u32[]{:S(2)}, u32[]{:S(2)}) collective-permute-start(bf16[144,384]{1,0:T(8,128)(2,1)S(1)} %get-tuple-element.30.msg1), channel_id=1, source_target_pairs={{32,0},{96,64},{0,32},{64,96},{33,1},{97,65},{1,33},{65,97},{34,2}... | collective-permute-start | bytes 331784 | tf_op jit(solution)/shard_map/ppermute | solution.py:336
  34.9 5.4 %collective-permute-start.4 = (bf16[96,128]{1,0:T(8,128)(2,1)S(1)}, bf16[96,128]{1,0:T(8,128)(2,1)S(1)}, u32[]{:S(2)}, u32[]{:S(2)}) collective-permute-start(bf16[96,128]{1,0:T(8,128)(2,1)S(1)} %get-tuple-element.36), channel_id=1, source_target_pairs={{0,2},{1,3},{2,0},{3,1},{4,6},{5,7},{6,4},{7,5},{8,10},{9,11},{10,... | collective-permute-start | bytes 73736 | tf_op jit(solution)/shard_map/ppermute | solution.py:332
  35.4 5.2 %collective-permute-start.6 = (bf16[96,128]{1,0:T(8,128)(2,1)S(1)}, bf16[96,128]{1,0:T(8,128)(2,1)S(1)}, u32[]{:S(2)}, u32[]{:S(2)}) collective-permute-start(bf16[96,128]{1,0:T(8,128)(2,1)S(1)} %get-tuple-element.37), channel_id=1, source_target_pairs={{0,8},{1,9},{2,10},{3,11},{4,12},{5,13},{6,14},{7,15},{8,0},{9,1},... | collective-permute-start | bytes 73736 | tf_op jit(solution)/shard_map/ppermute | solution.py:332
  35.8 5.5 %collective-permute-start.8 = (bf16[96,128]{1,0:T(8,128)(2,1)S(1)}, bf16[96,128]{1,0:T(8,128)(2,1)S(1)}, u32[]{:S(2)}, u32[]{:S(2)}) collective-permute-start(bf16[96,128]{1,0:T(8,128)(2,1)S(1)} %get-tuple-element.38), channel_id=1, source_target_pairs={{0,10},{1,11},{2,8},{3,9},{4,14},{5,15},{6,12},{7,13},{8,2},{9,3},... | collective-permute-start | bytes 73736 | tf_op jit(solution)/shard_map/ppermute | solution.py:332
  37.6 5.3 %collective-permute-start.3 = (bf16[96,128]{1,0:T(8,128)(2,1)S(1)}, bf16[96,128]{1,0:T(8,128)(2,1)S(1)}, u32[]{:S(2)}, u32[]{:S(2)}) collective-permute-start(bf16[96,128]{1,0:T(8,128)(2,1)S(1)} %get-tuple-element.35.refs_0_), channel_id=1, source_target_pairs={{0,1},{1,0},{2,3},{3,2},{4,5},{5,4},{6,7},{7,6},{8,9},{9,8},{10,11... | collective-permute-start | bytes 73736 | tf_op jit(solution)/shard_map/ppermute | solution.py:332
  40.3 2.6 %collective-permute-start.5 = (bf16[96,128]{1,0:T(8,128)(2,1)S(1)}, bf16[96,128]{1,0:T(8,128)(2,1)S(1)}, u32[]{:S(2)}, u32[]{:S(2)}) collective-permute-start(bf16[96,128]{1,0:T(8,128)(2,1)S(1)} %collective-permute-done.4.refs_1_), channel_id=1, source_target_pairs={{0,1},{1,0},{2,3},{3,2},{4,5},{5,4},{6,7},{7,6},{8,9},{9,8},{10,11... | collective-permute-start | bytes 73736 | tf_op jit(solution)/shard_map/ppermute | solution.py:332
  40.6 2.3 %collective-permute-start.7 = (bf16[96,128]{1,0:T(8,128)(2,1)S(1)}, bf16[96,128]{1,0:T(8,128)(2,1)S(1)}, u32[]{:S(2)}, u32[]{:S(2)}) collective-permute-start(bf16[96,128]{1,0:T(8,128)(2,1)S(1)} %collective-permute-done.6.refs_2_), channel_id=1, source_target_pairs={{0,1},{1,0},{2,3},{3,2},{4,5},{5,4},{6,7},{7,6},{8,9},{9,8},{10,11... | collective-permute-start | bytes 73736 | tf_op jit(solution)/shard_map/ppermute | solution.py:332
  41.3 2.4 %collective-permute-start.9 = (bf16[96,128]{1,0:T(8,128)(2,1)S(1)}, bf16[96,128]{1,0:T(8,128)(2,1)S(1)}, u32[]{:S(2)}, u32[]{:S(2)}) collective-permute-start(bf16[96,128]{1,0:T(8,128)(2,1)S(1)} %collective-permute-done.8.refs_3_), channel_id=1, source_target_pairs={{0,1},{1,0},{2,3},{3,2},{4,5},{5,4},{6,7},{7,6},{8,9},{9,8},{10,11... | collective-permute-start | bytes 73736 | tf_op jit(solution)/shard_map/ppermute | solution.py:332
  43.7 5.0 %collective-permute-start.12 = (bf16[128,384]{1,0:T(8,128)(2,1)S(1)}, bf16[128,384]{1,0:T(8,128)(2,1)S(1)}, u32[]{:S(2)}, u32[]{:S(2)}) collective-permute-start(bf16[128,384]{1,0:T(8,128)(2,1)S(1)} %shard_map.90.refs_8_.refs_0_.dpre), channel_id=1, source_target_pairs={{0,10},{1,11},{2,8},{3,9},{4,14},{5,15},{6,12},{7,13},{8,2},{9,3},... | collective-permute-start | bytes 294920 | tf_op jit(solution)/shard_map/ppermute | solution.py:332
  45.7 5.9 %collective-permute-start.11 = (bf16[128,384]{1,0:T(8,128)(2,1)S(1)}, bf16[128,384]{1,0:T(8,128)(2,1)S(1)}, u32[]{:S(2)}, u32[]{:S(2)}) collective-permute-start(bf16[128,384]{1,0:T(8,128)(2,1)S(1)} %shard_map.90.refs_8_.refs_0_.dpre), channel_id=1, source_target_pairs={{0,8},{1,9},{2,10},{3,11},{4,12},{5,13},{6,14},{7,15},{8,0},{9,1},... | collective-permute-start | bytes 294920 | tf_op jit(solution)/shard_map/ppermute | solution.py:332
  46.0 6.0 %collective-permute-start.10 = (bf16[128,384]{1,0:T(8,128)(2,1)S(1)}, bf16[128,384]{1,0:T(8,128)(2,1)S(1)}, u32[]{:S(2)}, u32[]{:S(2)}) collective-permute-start(bf16[128,384]{1,0:T(8,128)(2,1)S(1)} %shard_map.90.refs_8_.refs_0_.dpre), channel_id=1, source_target_pairs={{0,2},{1,3},{2,0},{3,1},{4,6},{5,7},{6,4},{7,5},{8,10},{9,11},{10,... | collective-permute-start | bytes 294920 | tf_op jit(solution)/shard_map/ppermute | solution.py:332
  46.5 6.5 %collective-permute-start.13 = (bf16[128,384]{1,0:T(8,128)(2,1)S(1)}, bf16[128,384]{1,0:T(8,128)(2,1)S(1)}, u32[]{:S(2)}, u32[]{:S(2)}) collective-permute-start(bf16[128,384]{1,0:T(8,128)(2,1)S(1)} %shard_map.90.refs_8_.refs_0_.dpre), channel_id=1, source_target_pairs={{0,1},{1,0},{2,3},{3,2},{4,5},{5,4},{6,7},{7,6},{8,9},{9,8},{10,11... | collective-permute-start | bytes 294920 | tf_op jit(solution)/shard_map/ppermute | solution.py:332
  48.7 4.3 %collective-permute-start.16 = (bf16[128,384]{1,0:T(8,128)(2,1)S(1)}, bf16[128,384]{1,0:T(8,128)(2,1)S(1)}, u32[]{:S(2)}, u32[]{:S(2)}) collective-permute-start(bf16[128,384]{1,0:T(8,128)(2,1)S(1)} %collective-permute-done.12.refs_3_), channel_id=1, source_target_pairs={{0,1},{1,0},{2,3},{3,2},{4,5},{5,4},{6,7},{7,6},{8,9},{9,8},{10,11... | collective-permute-start | bytes 294920 | tf_op jit(solution)/shard_map/ppermute | solution.py:332
  51.5 1.5 %collective-permute-start.15 = (bf16[128,384]{1,0:T(8,128)(2,1)S(1)}, bf16[128,384]{1,0:T(8,128)(2,1)S(1)}, u32[]{:S(2)}, u32[]{:S(2)}) collective-permute-start(bf16[128,384]{1,0:T(8,128)(2,1)S(1)} %collective-permute-done.11.refs_2_), channel_id=1, source_target_pairs={{0,1},{1,0},{2,3},{3,2},{4,5},{5,4},{6,7},{7,6},{8,9},{9,8},{10,11... | collective-permute-start | bytes 294920 | tf_op jit(solution)/shard_map/ppermute | solution.py:332
  52.0 1.3 %collective-permute-start.14 = (bf16[128,384]{1,0:T(8,128)(2,1)S(1)}, bf16[128,384]{1,0:T(8,128)(2,1)S(1)}, u32[]{:S(2)}, u32[]{:S(2)}) collective-permute-start(bf16[128,384]{1,0:T(8,128)(2,1)S(1)} %collective-permute-done.10.refs_1_), channel_id=1, source_target_pairs={{0,1},{1,0},{2,3},{3,2},{4,5},{5,4},{6,7},{7,6},{8,9},{9,8},{10,11... | collective-permute-start | bytes 294920 | tf_op jit(solution)/shard_map/ppermute | solution.py:332
  54.0 5.8 %collective-permute-start.17 = (bf16[224,384]{1,0:T(8,128)(2,1)S(1)}, bf16[224,384]{1,0:T(8,128)(2,1)S(1)}, u32[]{:S(2)}, u32[]{:S(2)}) collective-permute-start(bf16[224,384]{1,0:T(8,128)(2,1)S(1)} %get-tuple-element.42), channel_id=1, source_target_pairs={{0,6},{1,25},{2,4},{3,27},{4,2},{5,29},{6,0},{7,31},{8,14},{9,17},... | collective-permute-start | bytes 516104 | tf_op jit(solution)/shard_map/ppermute | solution.py:332
  59.8 8.5 %collective-permute-start.18 = (bf16[224,384]{1,0:T(8,128)(2,1)S(1)}, bf16[224,384]{1,0:T(8,128)(2,1)S(1)}, u32[]{:S(2)}, u32[]{:S(2)}) collective-permute-start(bf16[224,384]{1,0:T(8,128)(2,1)S(1)} %collective-permute-done.17.pair), channel_id=1, source_target_pairs={{0,1},{1,0},{2,3},{3,2},{4,5},{5,4},{6,7},{7,6},{8,9},{9,8},{10,11... | collective-permute-start | bytes 516104 | tf_op jit(solution)/shard_map/ppermute | solution.py:332
  60.9 7.4 %collective-permute-start.19 = (bf16[112,384]{1,0:T(8,128)(2,1)S(1)}, bf16[112,384]{1,0:T(8,128)(2,1)S(1)}, u32[]{:S(2)}, u32[]{:S(2)}) collective-permute-start(bf16[112,384]{1,0:T(8,128)(2,1)S(1)} %get-tuple-element.43), channel_id=1, source_target_pairs={{0,30},{1,31},{2,28},{3,29},{4,26},{5,27},{6,24},{7,25},{8,22},{9,... | collective-permute-start | bytes 258056 | tf_op jit(solution)/shard_map/ppermute | solution.py:332

commit v5 on v4

--- a/solution.py
+++ b/solution.py
@@ -1,3 +1,5 @@
+import functools
+
 import jax
 import jax.numpy as jnp
 from jax import lax
@@ -18,7 +20,7 @@
 NT = (((1,), (1,)), ((), ()))
 
 ROWS, CELLS, CH, EMB = 128, 32, 384, 512
-MSG = 144
+HALF = 64
 
 
 def mm(a, b, dims=NN):
@@ -39,22 +41,24 @@
 
 
 def column_shifts(v):
-    pw = row_iota((ROWS, 1)) & 7
+    rows = v.shape[0]
+    pw = row_iota((rows, 1)) & 7
     left = jnp.where(pw > 0, pltpu.roll(v, 1, 0), 0.0)
-    right = jnp.where(pw < 7, pltpu.roll(v, ROWS - 1, 0), 0.0)
+    right = jnp.where(pw < 7, pltpu.roll(v, rows - 1, 0), 0.0)
     return left, v, right
 
 
 def row_shift(v, dh):
     if dh == 0:
         return v
-    v = v.reshape(4, CELLS, CH)
-    zero = jnp.zeros((4, 8, CH), v.dtype)
+    rows = v.shape[0]
+    v = v.reshape(rows // CELLS, CELLS, CH)
+    zero = jnp.zeros((rows // CELLS, 8, CH), v.dtype)
     if dh > 0:
         v = jnp.concatenate([v[:, 8:], zero], axis=1)
     else:
         v = jnp.concatenate([zero, v[:, :24]], axis=1)
-    return v.reshape(ROWS, CH)
+    return v.reshape(rows, CH)
 
 
 def conv_back(dpre, w):
@@ -180,7 +184,7 @@
         out[...] = turned[96 * k : 96 * k + 96]
 
 
-def top_kernel(gathered, head, slope, w, message, dpre_out, head_out):
+def top_a_kernel(gathered, head, slope, w, message, dpre_out, head_out, top_out):
     section, rank, _, _, _ = position()
 
     @pl.when(section == 3)
@@ -190,65 +194,80 @@
         cot = jnp.broadcast_to(top[:, None, :], (4, CELLS, CH)).reshape(ROWS, CH)
         dpre = (cot * slope[...]).astype(bf16)
         dpre_out[...] = dpre
-        head_out[...] = head_grad[:, 384:]
-        message[128:, :] = head_grad[:, :384].astype(bf16)
-        below = cot + conv_back(dpre.astype(f32), w)
-        message[:128, :] = below.astype(bf16)
-
-
-def relay(active, arrived, slope, w, message, dpre_out):
+        head_out[...] = head_grad
+        top_out[0:4, :] = top
+        below = cot[:HALF] + conv_back(dpre[:HALF].astype(f32), w)
+        message[...] = below.astype(bf16)
+
+
+def top_b_kernel(top, dpre, head_grad, w, message):
+    @pl.when(lax.axis_index("section") == 3)
+    def _():
+        cot = jnp.broadcast_to(top[2:4, :][:, None, :], (2, CELLS, CH)).reshape(HALF, CH)
+        below = cot + conv_back(dpre[HALF:, :].astype(f32), w)
+        message[:HALF, :] = below.astype(bf16)
+        message[HALF:, :] = head_grad[:, :384].astype(bf16)
+
+
+def relay_kernel(active, half, arrived, slope, w, message, dpre_out):
     @pl.when(lax.axis_index("section") == active)
     def _():
-        cot = arrived[:128, :].astype(f32)
-        dpre = (cot * slope[...]).astype(bf16)
+        cot = arrived[:HALF, :].astype(f32)
+        dpre = (cot * slope[HALF * half : HALF * half + HALF, :]).astype(bf16)
         dpre_out[...] = dpre
-        message[128:, :] = arrived[128:, :]
         below = cot + conv_back(dpre.astype(f32), w)
-        message[:128, :] = below.astype(bf16)
-
-
-def relay2_kernel(arrived, slope, w, message, dpre_out):
-    relay(2, arrived, slope, w, message, dpre_out)
-
-
-def relay1_kernel(arrived, slope, w, message, dpre_out):
-    relay(1, arrived, slope, w, message, dpre_out)
-
-
-def bottom_kernel(arrived, slope, dpre3, dpre2, dpre1, *refs):
+        message[:HALF, :] = below.astype(bf16)
+        if half:
+            message[HALF:, :] = arrived[HALF:, :]
+
+
+def bottom_kernel(*refs):
+    arrived, slope, dpre3, held2, held1, dpre_out = (
+        refs[0:2], refs[2], refs[3], refs[4:6], refs[6:8], refs[8]
+    )
     section = lax.axis_index("section")
-    dpre_out = refs[-1]
-    for at, held in ((3, dpre3), (2, dpre2), (1, dpre1)):
+
+    @pl.when(section == 3)
+    def _():
+        dpre_out[...] = dpre3[...]
+
+    for half in range(2):
+        rows = slice(HALF * half, HALF * half + HALF)
+        for at, held in ((2, held2), (1, held1)):
+
+            @pl.when(section == at)
+            def _():
+                dpre_out[rows, :] = held[half][...]
+
+        @pl.when(section == 0)
+        def _():
+            cot = arrived[half][:HALF, :].astype(f32)
+            dpre_out[rows, :] = (cot * slope[rows, :]).astype(bf16)
+
+
+def last_kernel(*refs):
+    arrived, dpre, w, head3, sent, grads, head_out = (
+        refs[0:2], refs[2], refs[3], refs[4], refs[5:11], refs[12], refs[13]
+    )
+    section = lax.axis_index("section")
+    for at in (3, 2, 1):
 
         @pl.when(section == at)
         def _():
-            dpre_out[...] = held[...]
+            first, second = sent[6 - 2 * at], sent[7 - 2 * at]
+            grads[:HALF, :] = first[...]
+            grads[HALF:, :] = second[:HALF, :]
+            if at == 3:
+                head_out[...] = head3[:12, 384:]
+            else:
+                head_out[...] = second[HALF:, at * 128 : at * 128 + 128].astype(f32)[:12]
 
     @pl.when(section == 0)
     def _():
-        dpre_out[...] = (arrived[:128, :].astype(f32) * slope[...]).astype(bf16)
-
-
-def last_kernel(arrived, dpre, w, head3, msg3, msg2, msg1, own, grads, head_out):
-    section = lax.axis_index("section")
-
-    @pl.when(section == 3)
-    def _():
-        grads[...] = msg3[:128, :]
-        head_out[...] = head3[:12, :]
-
-    for at, sent in ((2, msg2), (1, msg1)):
-
-        @pl.when(section == at)
-        def _():
-            grads[...] = sent[:128, :]
-            head_out[...] = sent[128:, at * 128 : at * 128 + 128].astype(f32)[:12]
-
-    @pl.when(section == 0)
-    def _():
-        below = arrived[:128, :].astype(f32) + conv_back(dpre[...].astype(f32), w)
+        cot = jnp.concatenate([arrived[0][...], arrived[1][:HALF, :]], axis=0)
+        below = cot.astype(f32) + conv_back(dpre[...].astype(f32), w)
         grads[...] = below.astype(bf16)
-        head_out[...] = arrived[128:, :128].astype(f32)[:12]
+        head_out[...] = arrived[1][HALF:, :128].astype(f32)[:12]
 
 
 def stack_kernel(*refs):
@@ -323,7 +342,8 @@
 def per_device(saved, kernels, head, counts, pairs, valid):
     ranks = lax.axis_size("dp")
     act = VMEM((ROWS, CH), bf16)
-    msg = VMEM((MSG, CH), bf16)
+    msg_a, msg_b = VMEM((HALF, CH), bf16), VMEM((HALF + 16, CH), bf16)
+    half_act = VMEM((HALF, CH), bf16)
     piece = VMEM((96, 128), bf16)
     gather = (0, 2, 8, 10)
 
@@ -355,20 +375,34 @@
         valid,
     )
     gathered = lax.all_to_all(announce.reshape(32, 8, 256), "dp", 0, 0, tiled=True)
-    msg3, dpre3, head3 = call(
-        top_kernel, [VMEM] * 4, (msg, act, VMEM((16, 128), f32))
+    sent_a, dpre3, head3, top = call(
+        top_a_kernel, [VMEM] * 4, (msg_a, act, VMEM((16, EMB), f32), VMEM((8, CH), f32))
     )(gathered.reshape(256, 256), head, slope, w)
-    arrived = relayed(msg3, [(3, 2), (1, 0)])
-    split = call(split_kernel, [VMEM] * 2, (piece,) * 4)(rows, msg3)
+    arrived_a = relayed(sent_a, [(3, 2), (1, 0)])
+    sent_b = call(top_b_kernel, [VMEM] * 4, msg_b)(top, dpre3, head3, w)
+    arrived_b = relayed(sent_b, [(3, 2), (1, 0)])
+    split = call(split_kernel, [VMEM] * 2, (piece,) * 4)(rows, sent_b)
     near = [split[0]] + [swap(split[k], gather[k]) for k in range(1, 4)]
-    msg2, dpre2 = call(relay2_kernel, [VMEM] * 3, (msg, act))(arrived, slope, w)
-    arrived = relayed(msg2, [(2, 1), (3, 0)])
-    msg1, dpre1 = call(relay1_kernel, [VMEM] * 3, (msg, act))(arrived, slope, w)
-    arrived = relayed(msg1, [(1, 0), (3, 2)])
+    sent, held = [sent_a, sent_b], []
+
+    def relay(active, half, arrived):
+        message, dpre = call(
+            functools.partial(relay_kernel, active, half),
+            [VMEM] * 3,
+            (msg_b if half else msg_a, half_act),
+        )(arrived, slope, w)
+        sent.append(message)
+        held.append(dpre)
+        return message
+
+    for active, pairs_of in ((2, [(2, 1), (3, 0)]), (1, [(1, 0), (3, 2)])):
+        next_a = relayed(relay(active, 0, arrived_a), pairs_of)
+        next_b = relayed(relay(active, 1, arrived_b), pairs_of)
+        arrived_a, arrived_b = next_a, next_b
+    dpre = call(bottom_kernel, [VMEM] * 8, act)(
+        arrived_a, arrived_b, slope, dpre3, *held
+    )
     far = [swap(value, 1) for value in near]
-    dpre = call(bottom_kernel, [VMEM] * 9, act)(
-        arrived, slope, dpre3, dpre2, dpre1, *far
-    )
     near_grads = [dpre] + [swap(dpre, gather[k]) for k in range(1, 4)]
     stack = call(
         stack_kernel, [VMEM] * 9, VMEM((448, 1024), bf16), [VMEM((432, 1024), bf16)]
@@ -383,8 +417,8 @@
     diagonal = swap(diagonal, 30)
     crossed = swap(pair, 1)
     grads, head_grad = call(
-        last_kernel, [VMEM] * 8, (sds((ROWS, CH), bf16), sds((12, 128), f32))
-    )(arrived, dpre, w, head3, msg3, msg2, msg1, own)
+        last_kernel, [VMEM] * 12, (sds((ROWS, CH), bf16), sds((12, 128), f32))
+    )(arrived_a, arrived_b, dpre, w, head3, *sent, own)
     wgrad = call(sum_kernel, [VMEM] * 4, sds((108, 1, CH), f32))(own, pair, crossed, diagonal)
     return (
         grads.reshape(saved.shape),

time: 69.2 us -> 75.6 us (1.092)
  starting transfers between devices: 26.8 us -> 33 us
    ppermute x3 -> x6, starting transfers between devices: 9.73 us -> 12.9 us  [relayed(): return lax.ppermute(value, 'section', both)]
    ppermute x17, starting transfers between devices: 17.1 us -> 20.1 us  [swap(): return lax.ppermute(value, 'dp', pairs_of)]
    ppermute x3 -> x6, waiting for transfers between devices: 5.06 us -> 4.67 us  [relayed(): return lax.ppermute(value, 'section', both)]
    pallas_call x10 -> x13, Pallas kernels: 6.71 us -> 6.71 us  [with_operands(): run(*[value if space is SMEM else pltpu.with_memory_space_constraint(valu...]
  transfers between devices with their start and end apart: 20 -> 23, of which waited for: 8 -> 10; matrix products, arithmetic and copies ran while one was open for 0% -> 0% of each run, Pallas kernels for 4% -> 4%
where the time goes in v5:
time: 75.6 us; the launch traced here: 75.5 us
  starting transfers between devices  33 us (44%)
  waiting for transfers between devices  18.4 us (24%)
  blocking collectives  16 us (21%)
  Pallas kernels  6.71 us (9%)
  between operations  1.37 us (2%)
    ppermute x17, starting transfers between devices, swap(): return lax.ppermute(value, 'dp', pairs_of)  20.1 us
    all_to_all x1, blocking collectives, per_device(): lax.all_to_all(announce.reshape(32, 8, 256), 'dp', 0, 0, tiled=True)  16 us
    ppermute x17, waiting for transfers between devices, swap(): return lax.ppermute(value, 'dp', pairs_of)  13.7 us
    ppermute x6, starting transfers between devices, relayed(): return lax.ppermute(value, 'section', both)  12.9 us
    pallas_call x13, Pallas kernels, with_operands(): run(*[value if space is SMEM else pltpu.with_memory_space_constraint(valu...  6.71 us
    ppermute x6, waiting for transfers between devices, relayed(): return lax.ppermute(value, 'section', both)  4.67 us
  transfers between devices with their start and end apart: 23, of which 10 were waited for; matrix products, arithmetic and copies ran while one was open for 0% of the time, Pallas kernels for 4%

profile of v5, /device:TPU:1, one launch (start us, length us, event | category | flops | bytes accessed | tf_op | source)
XLA Modules:
  0.0 75.5 jit_solution(14395971780963439283)
XLA Ops:
  1.3 2.4 %shard_map.85 = (f32[128,384]{1,0:T(8,128)S(1)}, bf16[256,256]{1,0:T(8,128)(2,1)S(1)}, bf16[128,384]{1,0:T(8,128)(2,1)S(1)}, bf16[3,3,384,384]{3,2,1,0:T(8,128)(2,1)S(1)}, bf16[384,512]{1,0:T(8,128)(2,1)S(1)}) custom-call(bf16[128,384]{1,0:T(8,128)(2,1)} %bitcast.12, bf16[3,3,384,384]{3,2,1,0:T(8,128)(2,1)} %bitcast.10, bf16[384,512]{1,0:T(8,128)(2,1)} %head_hbm.1, ...), custom_call_target="tpu_custom_call" | custom-call | tf_op jit(solution)/shard_map/pallas_call | solution.py:326
  3.7 16.0 %all_to_all.5 = bf16[32,8,256]{2,1,0:T(8,128)(2,1)S(1)} all-to-all(bf16[32,8,256]{2,1,0:T(8,128)(2,1)S(1)} %bitcast.9), channel_id=1, replica_groups=mesh['section'=4,'dp'=32] {'dp'}, dimensions={0} | all-to-all | bytes 262144 | tf_op jit(solution)/shard_map/all_to_all | solution.py:377
  19.7 1.6 %collective-permute-start.3 = (bf16[80,384]{1,0:T(8,128)(2,1)S(1)}, bf16[80,384]{1,0:T(8,128)(2,1)S(1)}, u32[]{:S(2)}, u32[]{:S(2)}) collective-permute-start(bf16[80,384]{1,0:T(8,128)(2,1)S(1)} %shard_map.89.order.refs_6_), channel_id=1, source_target_pairs={{96,64},{32,0},{64,96},{0,32},{97,65},{33,1},{65,97},{1,33},{98,66... | collective-permute-start | bytes 184328 | tf_op jit(solution)/shard_map/ppermute | solution.py:356
  21.4 0.0 collective-permute-start
  21.4 1.6 %collective-permute-done.3.arrived = bf16[80,384]{1,0:T(8,128)(2,1)S(1)} collective-permute-done((bf16[80,384]{1,0:T(8,128)(2,1)S(1)}, bf16[80,384]{1,0:T(8,128)(2,1)S(1)}, u32[]{:S(2)}, u32[]{:S(2)}) %collective-permute-start.3) | collective-permute-done | bytes 61472 | tf_op jit(solution)/shard_map/ppermute | solution.py:356
  23.0 7.2 %collective-permute-start.4 = (bf16[80,384]{1,0:T(8,128)(2,1)S(1)}, bf16[80,384]{1,0:T(8,128)(2,1)S(1)}, u32[]{:S(2)}, u32[]{:S(2)}) collective-permute-start(bf16[80,384]{1,0:T(8,128)(2,1)S(1)} %get-tuple-element.39.refs_8_), channel_id=1, source_target_pairs={{64,32},{96,0},{32,64},{0,96},{65,33},{97,1},{33,65},{1,97},{66,34... | collective-permute-start | bytes 184328 | tf_op jit(solution)/shard_map/ppermute | solution.py:356
  30.2 0.0 collective-permute-done.arrived
  30.2 1.1 %collective-permute-start.1 = (bf16[64,384]{1,0:T(8,128)(2,1)S(1)}, bf16[64,384]{1,0:T(8,128)(2,1)S(1)}, u32[]{:S(2)}, u32[]{:S(2)}) collective-permute-start(bf16[64,384]{1,0:T(8,128)(2,1)S(1)} %get-tuple-element.34.refs_7_), channel_id=1, source_target_pairs={{64,32},{96,0},{32,64},{0,96},{65,33},{97,1},{33,65},{1,97},{66,34... | collective-permute-start | bytes 147464 | tf_op jit(solution)/shard_map/ppermute | solution.py:356
  31.4 0.5 collective-permute-done.4.arrived
  31.8 1.8 %collective-permute-start.5 = (bf16[80,384]{1,0:T(8,128)(2,1)S(1)}, bf16[80,384]{1,0:T(8,128)(2,1)S(1)}, u32[]{:S(2)}, u32[]{:S(2)}) collective-permute-start(bf16[80,384]{1,0:T(8,128)(2,1)S(1)} %get-tuple-element.40.refs_10_), channel_id=1, source_target_pairs={{32,0},{96,64},{0,32},{64,96},{33,1},{97,65},{1,33},{65,97},{34,2}... | collective-permute-start | bytes 184328 | tf_op jit(solution)/shard_map/ppermute | solution.py:356
  33.7 0.7 collective-permute-done.1.arrived
  34.4 1.1 %collective-permute-start.2 = (bf16[64,384]{1,0:T(8,128)(2,1)S(1)}, bf16[64,384]{1,0:T(8,128)(2,1)S(1)}, u32[]{:S(2)}, u32[]{:S(2)}) collective-permute-start(bf16[64,384]{1,0:T(8,128)(2,1)S(1)} %get-tuple-element.35.refs_9_), channel_id=1, source_target_pairs={{32,0},{96,64},{0,32},{64,96},{33,1},{97,65},{1,33},{65,97},{34,2}... | collective-permute-start | bytes 147464 | tf_op jit(solution)/shard_map/ppermute | solution.py:356
  35.4 1.9 %collective-permute-done.2.refs_0_ = bf16[64,384]{1,0:T(8,128)(2,1)S(1)} collective-permute-done((bf16[64,384]{1,0:T(8,128)(2,1)S(1)}, bf16[64,384]{1,0:T(8,128)(2,1)S(1)}, u32[]{:S(2)}, u32[]{:S(2)}) %collective-permute-start.2) | collective-permute-done | bytes 49184 | tf_op jit(solution)/shard_map/ppermute | solution.py:356
  37.3 0.0 collective-permute-done.5.refs_1_
  37.4 0.5 collective-permute-start.15
  37.9 1.1 %collective-permute-start.14 = (bf16[128,384]{1,0:T(8,128)(2,1)S(1)}, bf16[128,384]{1,0:T(8,128)(2,1)S(1)}, u32[]{:S(2)}, u32[]{:S(2)}) collective-permute-start(bf16[128,384]{1,0:T(8,128)(2,1)S(1)} %shard_map.92.refs_8_.refs_0_.refs_2_), channel_id=1, source_target_pairs={{0,8},{1,9},{2,10},{3,11},{4,12},{5,13},{6,14},{7,15},{8,0},{9,1},... | collective-permute-start | bytes 294920 | tf_op jit(solution)/shard_map/ppermute | solution.py:352
  39.0 1.1 %collective-permute-start.13 = (bf16[128,384]{1,0:T(8,128)(2,1)S(1)}, bf16[128,384]{1,0:T(8,128)(2,1)S(1)}, u32[]{:S(2)}, u32[]{:S(2)}) collective-permute-start(bf16[128,384]{1,0:T(8,128)(2,1)S(1)} %shard_map.92.refs_8_.refs_0_.refs_2_), channel_id=1, source_target_pairs={{0,2},{1,3},{2,0},{3,1},{4,6},{5,7},{6,4},{7,5},{8,10},{9,11},{10,... | collective-permute-start | bytes 294920 | tf_op jit(solution)/shard_map/ppermute | solution.py:352
  40.1 0.3 shard_map.93
  40.5 0.5 collective-permute-start.6
  40.9 0.3 collective-permute-start.7
  41.2 2.0 %collective-permute-done.6.refs_1_ = bf16[96,128]{1,0:T(8,128)(2,1)S(1)} collective-permute-done((bf16[96,128]{1,0:T(8,128)(2,1)S(1)}, bf16[96,128]{1,0:T(8,128)(2,1)S(1)}, u32[]{:S(2)}, u32[]{:S(2)}) %collective-permute-start.6) | collective-permute-done | bytes 24608 | tf_op jit(solution)/shard_map/ppermute | solution.py:352
  43.2 0.7 collective-permute-start.8
  43.9 0.0 collective-permute-done.7.refs_2_
  43.9 6.4 %collective-permute-start.9 = (bf16[96,128]{1,0:T(8,128)(2,1)S(1)}, bf16[96,128]{1,0:T(8,128)(2,1)S(1)}, u32[]{:S(2)}, u32[]{:S(2)}) collective-permute-start(bf16[96,128]{1,0:T(8,128)(2,1)S(1)} %get-tuple-element.46.refs_0_), channel_id=1, source_target_pairs={{0,1},{1,0},{2,3},{3,2},{4,5},{5,4},{6,7},{7,6},{8,9},{9,8},{10,11... | collective-permute-start | bytes 73736 | tf_op jit(solution)/shard_map/ppermute | solution.py:352
  50.3 0.0 collective-permute-done.8.refs_3_
  50.3 4.0 %collective-permute-start.16 = (bf16[128,384]{1,0:T(8,128)(2,1)S(1)}, bf16[128,384]{1,0:T(8,128)(2,1)S(1)}, u32[]{:S(2)}, u32[]{:S(2)}) collective-permute-start(bf16[128,384]{1,0:T(8,128)(2,1)S(1)} %shard_map.92.refs_8_.refs_0_.refs_2_), channel_id=1, source_target_pairs={{0,1},{1,0},{2,3},{3,2},{4,5},{5,4},{6,7},{7,6},{8,9},{9,8},{10,11... | collective-permute-start | bytes 294920 | tf_op jit(solution)/shard_map/ppermute | solution.py:352
  54.3 0.0 collective-permute-done.15.refs_3_
  54.4 0.0 collective-permute-start.19
  54.4 0.0 collective-permute-done.14.refs_2_
  54.4 0.5 collective-permute-start.18
  54.9 0.0 collective-permute-done.13.refs_1_
  54.9 0.1 collective-permute-start.17
  55.0 0.0 collective-permute-done.9.refs_4_
  55.0 0.4 collective-permute-start.10
  55.4 0.8 %collective-permute-done.10.refs_5_ = bf16[96,128]{1,0:T(8,128)(2,1)S(1)} collective-permute-done((bf16[96,128]{1,0:T(8,128)(2,1)S(1)}, bf16[96,128]{1,0:T(8,128)(2,1)S(1)}, u32[]{:S(2)}, u32[]{:S(2)}) %collective-permute-start.10) | collective-permute-done | bytes 24608 | tf_op jit(solution)/shard_map/ppermute | solution.py:352
  56.2 0.3 collective-permute-start.11
  56.6 0.8 %collective-permute-done.11.refs_6_ = bf16[96,128]{1,0:T(8,128)(2,1)S(1)} collective-permute-done((bf16[96,128]{1,0:T(8,128)(2,1)S(1)}, bf16[96,128]{1,0:T(8,128)(2,1)S(1)}, u32[]{:S(2)}, u32[]{:S(2)}) %collective-permute-start.11) | collective-permute-done | bytes 24608 | tf_op jit(solution)/shard_map/ppermute | solution.py:352
  57.4 0.3 collective-permute-start.12
  57.8 0.8 %collective-permute-done.12.refs_7_ = bf16[96,128]{1,0:T(8,128)(2,1)S(1)} collective-permute-done((bf16[96,128]{1,0:T(8,128)(2,1)S(1)}, bf16[96,128]{1,0:T(8,128)(2,1)S(1)}, u32[]{:S(2)}, u32[]{:S(2)}) %collective-permute-start.12) | collective-permute-done | bytes 24608 | tf_op jit(solution)/shard_map/ppermute | solution.py:352
  58.6 0.9 %shard_map.94.stack = bf16[448,1024]{1,0:T(8,128)(2,1)S(1)} custom-call(bf16[96,128]{1,0:T(8,128)(2,1)S(1)} %get-tuple-element.46.refs_0_, bf16[96,128]{1,0:T(8,128)(2,1)S(1)} %collective-permute-done.6.refs_1_, bf16[96,128]{1,0:T(8,128)(2,1)S(1)} %collective-permute-done.7.refs_2_, bf16[96,128]{1,0:T(8,128)(2,1)S(1)} %collective-permute-done.8.refs_3_, ...), custom_call_target="tpu_custom_call" | custom-call | tf_op jit(solution)/shard_map/pallas_call | solution.py:326
  59.6 0.0 collective-permute-done.16.refs_4_
  59.6 0.0 collective-permute-done.19.refs_7_
  59.6 0.0 collective-permute-done.18.refs_6_
  59.6 0.0 collective-permute-done.17.refs_5_
  59.6 0.6 shard_map.95
  60.3 0.9 %collective-permute-start.20 = (bf16[224,384]{1,0:T(8,128)(2,1)S(1)}, bf16[224,384]{1,0:T(8,128)(2,1)S(1)}, u32[]{:S(2)}, u32[]{:S(2)}) collective-permute-start(bf16[224,384]{1,0:T(8,128)(2,1)S(1)} %get-tuple-element.52), channel_id=1, source_target_pairs={{0,6},{1,25},{2,4},{3,27},{4,2},{5,29},{6,0},{7,31},{8,14},{9,17},... | collective-permute-start | bytes 516104 | tf_op jit(solution)/shard_map/ppermute | solution.py:352
  61.2 4.9 %collective-permute-done.20.pair = bf16[224,384]{1,0:T(8,128)(2,1)S(1)} collective-permute-done((bf16[224,384]{1,0:T(8,128)(2,1)S(1)}, bf16[224,384]{1,0:T(8,128)(2,1)S(1)}, u32[]{:S(2)}, u32[]{:S(2)}) %collective-permute-start.20) | collective-permute-done | bytes 172064 | tf_op jit(solution)/shard_map/ppermute | solution.py:352
  66.1 1.2 %collective-permute-start.21 = (bf16[224,384]{1,0:T(8,128)(2,1)S(1)}, bf16[224,384]{1,0:T(8,128)(2,1)S(1)}, u32[]{:S(2)}, u32[]{:S(2)}) collective-permute-start(bf16[224,384]{1,0:T(8,128)(2,1)S(1)} %collective-permute-done.20.pair), channel_id=1, source_target_pairs={{0,1},{1,0},{2,3},{3,2},{4,5},{5,4},{6,7},{7,6},{8,9},{9,8},{10,11... | collective-permute-start | bytes 516104 | tf_op jit(solution)/shard_map/ppermute | solution.py:352
  67.3 1.6 %collective-permute-start.22 = (bf16[112,384]{1,0:T(8,128)(2,1)S(1)}, bf16[112,384]{1,0:T(8,128)(2,1)S(1)}, u32[]{:S(2)}, u32[]{:S(2)}) collective-permute-start(bf16[112,384]{1,0:T(8,128)(2,1)S(1)} %get-tuple-element.53), channel_id=1, source_target_pairs={{0,30},{1,31},{2,28},{3,29},{4,26},{5,27},{6,24},{7,25},{8,22},{9,... | collective-permute-start | bytes 258056 | tf_op jit(solution)/shard_map/ppermute | solution.py:352
  68.9 1.6 %shard_map.96 = (bf16[128,384]{1,0:T(8,128)(2,1)}, f32[12,128]{1,0:T(8,128)}) custom-call(bf16[64,384]{1,0:T(8,128)(2,1)S(1)} %collective-permute-done.2.refs_0_, bf16[80,384]{1,0:T(8,128)(2,1)S(1)} %collective-permute-done.5.refs_1_, bf16[128,384]{1,0:T(8,128)(2,1)S(1)} %shard_map.92.refs_8_.refs_0_.refs_2_, ...), custom_call_target="tpu_custom_call" | custom-call | tf_op jit(solution)/shard_map/pallas_call | solution.py:326
  70.5 4.2 %collective-permute-done.22.diagonal = bf16[112,384]{1,0:T(8,128)(2,1)S(1)} collective-permute-done((bf16[112,384]{1,0:T(8,128)(2,1)S(1)}, bf16[112,384]{1,0:T(8,128)(2,1)S(1)}, u32[]{:S(2)}, u32[]{:S(2)}) %collective-permute-start.22) | collective-permute-done | bytes 86048 | tf_op jit(solution)/shard_map/ppermute | solution.py:352
  74.7 0.0 collective-permute-done.21.crossed
  74.7 0.7 shard_map.97
  (7 shorter events, 0.0 us)
Async XLA Ops:
  19.7 3.2 %collective-permute-start.3 = (bf16[80,384]{1,0:T(8,128)(2,1)S(1)}, bf16[80,384]{1,0:T(8,128)(2,1)S(1)}, u32[]{:S(2)}, u32[]{:S(2)}) collective-permute-start(bf16[80,384]{1,0:T(8,128)(2,1)S(1)} %shard_map.89.order.refs_6_), channel_id=1, source_target_pairs={{96,64},{32,0},{64,96},{0,32},{97,65},{33,1},{65,97},{1,33},{98,66... | collective-permute-start | bytes 184328 | tf_op jit(solution)/shard_map/ppermute | solution.py:356
  21.4 8.9 %collective-permute-start = (bf16[64,384]{1,0:T(8,128)(2,1)S(1)}, bf16[64,384]{1,0:T(8,128)(2,1)S(1)}, u32[]{:S(2)}, u32[]{:S(2)}) collective-permute-start(bf16[64,384]{1,0:T(8,128)(2,1)S(1)} %get-tuple-element.33.refs_5_), channel_id=1, source_target_pairs={{96,64},{32,0},{64,96},{0,32},{97,65},{33,1},{65,97},{1,33},{98,66... | collective-permute-start | bytes 147464 | tf_op jit(solution)/shard_map/ppermute | solution.py:356
  23.0 8.9 %collective-permute-start.4 = (bf16[80,384]{1,0:T(8,128)(2,1)S(1)}, bf16[80,384]{1,0:T(8,128)(2,1)S(1)}, u32[]{:S(2)}, u32[]{:S(2)}) collective-permute-start(bf16[80,384]{1,0:T(8,128)(2,1)S(1)} %get-tuple-element.39.refs_8_), channel_id=1, source_target_pairs={{64,32},{96,0},{32,64},{0,96},{65,33},{97,1},{33,65},{1,97},{66,34... | collective-permute-start | bytes 184328 | tf_op jit(solution)/shard_map/ppermute | solution.py:356
  30.2 4.2 %collective-permute-start.1 = (bf16[64,384]{1,0:T(8,128)(2,1)S(1)}, bf16[64,384]{1,0:T(8,128)(2,1)S(1)}, u32[]{:S(2)}, u32[]{:S(2)}) collective-permute-start(bf16[64,384]{1,0:T(8,128)(2,1)S(1)} %get-tuple-element.34.refs_7_), channel_id=1, source_target_pairs={{64,32},{96,0},{32,64},{0,96},{65,33},{97,1},{33,65},{1,97},{66,34... | collective-permute-start | bytes 147464 | tf_op jit(solution)/shard_map/ppermute | solution.py:356
  31.8 5.5 %collective-permute-start.5 = (bf16[80,384]{1,0:T(8,128)(2,1)S(1)}, bf16[80,384]{1,0:T(8,128)(2,1)S(1)}, u32[]{:S(2)}, u32[]{:S(2)}) collective-permute-start(bf16[80,384]{1,0:T(8,128)(2,1)S(1)} %get-tuple-element.40.refs_10_), channel_id=1, source_target_pairs={{32,0},{96,64},{0,32},{64,96},{33,1},{97,65},{1,33},{65,97},{34,2}... | collective-permute-start | bytes 184328 | tf_op jit(solution)/shard_map/ppermute | solution.py:356
  34.4 2.9 %collective-permute-start.2 = (bf16[64,384]{1,0:T(8,128)(2,1)S(1)}, bf16[64,384]{1,0:T(8,128)(2,1)S(1)}, u32[]{:S(2)}, u32[]{:S(2)}) collective-permute-start(bf16[64,384]{1,0:T(8,128)(2,1)S(1)} %get-tuple-element.35.refs_9_), channel_id=1, source_target_pairs={{32,0},{96,64},{0,32},{64,96},{33,1},{97,65},{1,33},{65,97},{34,2}... | collective-permute-start | bytes 147464 | tf_op jit(solution)/shard_map/ppermute | solution.py:356
  37.4 17.0 %collective-permute-start.15 = (bf16[128,384]{1,0:T(8,128)(2,1)S(1)}, bf16[128,384]{1,0:T(8,128)(2,1)S(1)}, u32[]{:S(2)}, u32[]{:S(2)}) collective-permute-start(bf16[128,384]{1,0:T(8,128)(2,1)S(1)} %shard_map.92.refs_8_.refs_0_.refs_2_), channel_id=1, source_target_pairs={{0,10},{1,11},{2,8},{3,9},{4,14},{5,15},{6,12},{7,13},{8,2},{9,3},... | collective-permute-start | bytes 294920 | tf_op jit(solution)/shard_map/ppermute | solution.py:352
  37.9 16.5 %collective-permute-start.14 = (bf16[128,384]{1,0:T(8,128)(2,1)S(1)}, bf16[128,384]{1,0:T(8,128)(2,1)S(1)}, u32[]{:S(2)}, u32[]{:S(2)}) collective-permute-start(bf16[128,384]{1,0:T(8,128)(2,1)S(1)} %shard_map.92.refs_8_.refs_0_.refs_2_), channel_id=1, source_target_pairs={{0,8},{1,9},{2,10},{3,11},{4,12},{5,13},{6,14},{7,15},{8,0},{9,1},... | collective-permute-start | bytes 294920 | tf_op jit(solution)/shard_map/ppermute | solution.py:352
  39.0 15.8 %collective-permute-start.13 = (bf16[128,384]{1,0:T(8,128)(2,1)S(1)}, bf16[128,384]{1,0:T(8,128)(2,1)S(1)}, u32[]{:S(2)}, u32[]{:S(2)}) collective-permute-start(bf16[128,384]{1,0:T(8,128)(2,1)S(1)} %shard_map.92.refs_8_.refs_0_.refs_2_), channel_id=1, source_target_pairs={{0,2},{1,3},{2,0},{3,1},{4,6},{5,7},{6,4},{7,5},{8,10},{9,11},{10,... | collective-permute-start | bytes 294920 | tf_op jit(solution)/shard_map/ppermute | solution.py:352
  40.5 2.8 %collective-permute-start.6 = (bf16[96,128]{1,0:T(8,128)(2,1)S(1)}, bf16[96,128]{1,0:T(8,128)(2,1)S(1)}, u32[]{:S(2)}, u32[]{:S(2)}) collective-permute-start(bf16[96,128]{1,0:T(8,128)(2,1)S(1)} %get-tuple-element.47), channel_id=1, source_target_pairs={{0,2},{1,3},{2,0},{3,1},{4,6},{5,7},{6,4},{7,5},{8,10},{9,11},{10,... | collective-permute-start | bytes 73736 | tf_op jit(solution)/shard_map/ppermute | solution.py:352
  40.9 3.0 %collective-permute-start.7 = (bf16[96,128]{1,0:T(8,128)(2,1)S(1)}, bf16[96,128]{1,0:T(8,128)(2,1)S(1)}, u32[]{:S(2)}, u32[]{:S(2)}) collective-permute-start(bf16[96,128]{1,0:T(8,128)(2,1)S(1)} %get-tuple-element.48), channel_id=1, source_target_pairs={{0,8},{1,9},{2,10},{3,11},{4,12},{5,13},{6,14},{7,15},{8,0},{9,1},... | collective-permute-start | bytes 73736 | tf_op jit(solution)/shard_map/ppermute | solution.py:352
  43.2 7.1 %collective-permute-start.8 = (bf16[96,128]{1,0:T(8,128)(2,1)S(1)}, bf16[96,128]{1,0:T(8,128)(2,1)S(1)}, u32[]{:S(2)}, u32[]{:S(2)}) collective-permute-start(bf16[96,128]{1,0:T(8,128)(2,1)S(1)} %get-tuple-element.49), channel_id=1, source_target_pairs={{0,10},{1,11},{2,8},{3,9},{4,14},{5,15},{6,12},{7,13},{8,2},{9,3},... | collective-permute-start | bytes 73736 | tf_op jit(solution)/shard_map/ppermute | solution.py:352
  43.9 11.1 %collective-permute-start.9 = (bf16[96,128]{1,0:T(8,128)(2,1)S(1)}, bf16[96,128]{1,0:T(8,128)(2,1)S(1)}, u32[]{:S(2)}, u32[]{:S(2)}) collective-permute-start(bf16[96,128]{1,0:T(8,128)(2,1)S(1)} %get-tuple-element.46.refs_0_), channel_id=1, source_target_pairs={{0,1},{1,0},{2,3},{3,2},{4,5},{5,4},{6,7},{7,6},{8,9},{9,8},{10,11... | collective-permute-start | bytes 73736 | tf_op jit(solution)/shard_map/ppermute | solution.py:352
  50.3 9.2 %collective-permute-start.16 = (bf16[128,384]{1,0:T(8,128)(2,1)S(1)}, bf16[128,384]{1,0:T(8,128)(2,1)S(1)}, u32[]{:S(2)}, u32[]{:S(2)}) collective-permute-start(bf16[128,384]{1,0:T(8,128)(2,1)S(1)} %shard_map.92.refs_8_.refs_0_.refs_2_), channel_id=1, source_target_pairs={{0,1},{1,0},{2,3},{3,2},{4,5},{5,4},{6,7},{7,6},{8,9},{9,8},{10,11... | collective-permute-start | bytes 294920 | tf_op jit(solution)/shard_map/ppermute | solution.py:352
  54.4 5.2 %collective-permute-start.19 = (bf16[128,384]{1,0:T(8,128)(2,1)S(1)}, bf16[128,384]{1,0:T(8,128)(2,1)S(1)}, u32[]{:S(2)}, u32[]{:S(2)}) collective-permute-start(bf16[128,384]{1,0:T(8,128)(2,1)S(1)} %collective-permute-done.15.refs_3_), channel_id=1, source_target_pairs={{0,1},{1,0},{2,3},{3,2},{4,5},{5,4},{6,7},{7,6},{8,9},{9,8},{10,11... | collective-permute-start | bytes 294920 | tf_op jit(solution)/shard_map/ppermute | solution.py:352
  54.4 5.2 %collective-permute-start.18 = (bf16[128,384]{1,0:T(8,128)(2,1)S(1)}, bf16[128,384]{1,0:T(8,128)(2,1)S(1)}, u32[]{:S(2)}, u32[]{:S(2)}) collective-permute-start(bf16[128,384]{1,0:T(8,128)(2,1)S(1)} %collective-permute-done.14.refs_2_), channel_id=1, source_target_pairs={{0,1},{1,0},{2,3},{3,2},{4,5},{5,4},{6,7},{7,6},{8,9},{9,8},{10,11... | collective-permute-start | bytes 294920 | tf_op jit(solution)/shard_map/ppermute | solution.py:352
  54.9 4.7 %collective-permute-start.17 = (bf16[128,384]{1,0:T(8,128)(2,1)S(1)}, bf16[128,384]{1,0:T(8,128)(2,1)S(1)}, u32[]{:S(2)}, u32[]{:S(2)}) collective-permute-start(bf16[128,384]{1,0:T(8,128)(2,1)S(1)} %collective-permute-done.13.refs_1_), channel_id=1, source_target_pairs={{0,1},{1,0},{2,3},{3,2},{4,5},{5,4},{6,7},{7,6},{8,9},{9,8},{10,11... | collective-permute-start | bytes 294920 | tf_op jit(solution)/shard_map/ppermute | solution.py:352
  55.0 1.3 %collective-permute-start.10 = (bf16[96,128]{1,0:T(8,128)(2,1)S(1)}, bf16[96,128]{1,0:T(8,128)(2,1)S(1)}, u32[]{:S(2)}, u32[]{:S(2)}) collective-permute-start(bf16[96,128]{1,0:T(8,128)(2,1)S(1)} %collective-permute-done.6.refs_1_), channel_id=1, source_target_pairs={{0,1},{1,0},{2,3},{3,2},{4,5},{5,4},{6,7},{7,6},{8,9},{9,8},{10,11... | collective-permute-start | bytes 73736 | tf_op jit(solution)/shard_map/ppermute | solution.py:352
  56.2 1.2 %collective-permute-start.11 = (bf16[96,128]{1,0:T(8,128)(2,1)S(1)}, bf16[96,128]{1,0:T(8,128)(2,1)S(1)}, u32[]{:S(2)}, u32[]{:S(2)}) collective-permute-start(bf16[96,128]{1,0:T(8,128)(2,1)S(1)} %collective-permute-done.7.refs_2_), channel_id=1, source_target_pairs={{0,1},{1,0},{2,3},{3,2},{4,5},{5,4},{6,7},{7,6},{8,9},{9,8},{10,11... | collective-permute-start | bytes 73736 | tf_op jit(solution)/shard_map/ppermute | solution.py:352
  57.4 1.2 %collective-permute-start.12 = (bf16[96,128]{1,0:T(8,128)(2,1)S(1)}, bf16[96,128]{1,0:T(8,128)(2,1)S(1)}, u32[]{:S(2)}, u32[]{:S(2)}) collective-permute-start(bf16[96,128]{1,0:T(8,128)(2,1)S(1)} %collective-permute-done.8.refs_3_), channel_id=1, source_target_pairs={{0,1},{1,0},{2,3},{3,2},{4,5},{5,4},{6,7},{7,6},{8,9},{9,8},{10,11... | collective-permute-start | bytes 73736 | tf_op jit(solution)/shard_map/ppermute | solution.py:352
  60.3 5.8 %collective-permute-start.20 = (bf16[224,384]{1,0:T(8,128)(2,1)S(1)}, bf16[224,384]{1,0:T(8,128)(2,1)S(1)}, u32[]{:S(2)}, u32[]{:S(2)}) collective-permute-start(bf16[224,384]{1,0:T(8,128)(2,1)S(1)} %get-tuple-element.52), channel_id=1, source_target_pairs={{0,6},{1,25},{2,4},{3,27},{4,2},{5,29},{6,0},{7,31},{8,14},{9,17},... | collective-permute-start | bytes 516104 | tf_op jit(solution)/shard_map/ppermute | solution.py:352
  66.1 8.6 %collective-permute-start.21 = (bf16[224,384]{1,0:T(8,128)(2,1)S(1)}, bf16[224,384]{1,0:T(8,128)(2,1)S(1)}, u32[]{:S(2)}, u32[]{:S(2)}) collective-permute-start(bf16[224,384]{1,0:T(8,128)(2,1)S(1)} %collective-permute-done.20.pair), channel_id=1, source_target_pairs={{0,1},{1,0},{2,3},{3,2},{4,5},{5,4},{6,7},{7,6},{8,9},{9,8},{10,11... | collective-permute-start | bytes 516104 | tf_op jit(solution)/shard_map/ppermute | solution.py:352
  67.3 7.4 %collective-permute-start.22 = (bf16[112,384]{1,0:T(8,128)(2,1)S(1)}, bf16[112,384]{1,0:T(8,128)(2,1)S(1)}, u32[]{:S(2)}, u32[]{:S(2)}) collective-permute-start(bf16[112,384]{1,0:T(8,128)(2,1)S(1)} %get-tuple-element.53), channel_id=1, source_target_pairs={{0,30},{1,31},{2,28},{3,29},{4,26},{5,27},{6,24},{7,25},{8,22},{9,... | collective-permute-start | bytes 258056 | tf_op jit(solution)/shard_map/ppermute | solution.py:352

commit v6 on v4

--- a/solution.py
+++ b/solution.py
@@ -18,7 +18,6 @@
 NT = (((1,), (1,)), ((), ()))
 
 ROWS, CELLS, CH, EMB = 128, 32, 384, 512
-MSG = 144
 
 
 def mm(a, b, dims=NN):
@@ -59,23 +58,19 @@
 
 def conv_back(dpre, w):
     cols = column_shifts(dpre)
-    total = None
-    for kh in range(3):
-        lhs = jnp.concatenate(
-            [row_shift(cols[2 - kw], 1 - kh).astype(bf16) for kw in range(3)], axis=1
-        )
-        rhs = jnp.concatenate([w[kh, kw] for kw in range(3)], axis=1)
-        part = mm(lhs, rhs, NT)
-        total = part if total is None else total + part
-    return total
+    lhs = [row_shift(cols[2 - tap % 3], 1 - tap // 3).astype(bf16) for tap in range(9)]
+    rhs = [w[tap] for tap in range(9)]
+    return mm(jnp.concatenate(lhs, axis=1), jnp.concatenate(rhs, axis=1), NT)
 
 
 def forward_kernel(
     saved_hbm, w_hbm, head_hbm, counts, pairs_hbm, valid_hbm,
     slope, message, saved, w, head, pairs, valid, sem,
 ):
-    sources = [saved_hbm, w_hbm.at[0], w_hbm.at[1], w_hbm.at[2], pairs_hbm, valid_hbm, head_hbm]
-    targets = [saved, w.at[0], w.at[1], w.at[2], pairs, valid, head]
+    sources = [saved_hbm] + [w_hbm.at[tap] for tap in range(9)]
+    targets = [saved] + [w.at[tap] for tap in range(9)]
+    sources += [pairs_hbm, valid_hbm, head_hbm]
+    targets += [pairs, valid, head]
     copies = [
         pltpu.make_async_copy(source, target, sem.at[n])
         for n, (source, target) in enumerate(zip(sources, targets, strict=True))
@@ -86,18 +81,18 @@
     v = saved[...].astype(f32)
     cols = column_shifts(v)
     pre = None
-    for kh in range(3):
-        lhs = jnp.concatenate(
-            [row_shift(cols[kw], kh - 1).astype(bf16) for kw in range(3)], axis=1
-        )
-        copies[1 + kh].wait()
-        part = mm(lhs, w[kh].reshape(3 * CH, CH))
+    for taps in ((0, 1), (2, 3), (4, 5), (6, 7), (8,)):
+        lhs = [row_shift(cols[tap % 3], tap // 3 - 1).astype(bf16) for tap in taps]
+        for tap in taps:
+            copies[1 + tap].wait()
+        rhs = [w[tap] for tap in taps]
+        part = mm(jnp.concatenate(lhs, axis=1), jnp.concatenate(rhs, axis=0))
         pre = part if pre is None else pre + part
     sigma = jax.nn.sigmoid(pre)
     slope[...] = sigma * (1.0 + pre * (1.0 - sigma))
     feature = (v + pre * sigma).reshape(4, CELLS, CH)
     pooled = jnp.sum(feature, axis=1) / CELLS
-    for copy in copies[4:]:
+    for copy in copies[10:]:
         copy.wait()
     at = (row_iota((4, 128)), col_iota((4, 128)))
     extra = jnp.zeros((4, 128), f32)
@@ -180,7 +175,7 @@
         out[...] = turned[96 * k : 96 * k + 96]
 
 
-def top_kernel(gathered, head, slope, w, message, dpre_out, head_out):
+def top_kernel(gathered, head, slope, w, message, dpre_out, head_out, head_sent):
     section, rank, _, _, _ = position()
 
     @pl.when(section == 3)
@@ -191,20 +186,19 @@
         dpre = (cot * slope[...]).astype(bf16)
         dpre_out[...] = dpre
         head_out[...] = head_grad[:, 384:]
-        message[128:, :] = head_grad[:, :384].astype(bf16)
+        head_sent[...] = head_grad[:, :384].astype(bf16)
         below = cot + conv_back(dpre.astype(f32), w)
-        message[:128, :] = below.astype(bf16)
+        message[...] = below.astype(bf16)
 
 
 def relay(active, arrived, slope, w, message, dpre_out):
     @pl.when(lax.axis_index("section") == active)
     def _():
-        cot = arrived[:128, :].astype(f32)
+        cot = arrived[...].astype(f32)
         dpre = (cot * slope[...]).astype(bf16)
         dpre_out[...] = dpre
-        message[128:, :] = arrived[128:, :]
         below = cot + conv_back(dpre.astype(f32), w)
-        message[:128, :] = below.astype(bf16)
+        message[...] = below.astype(bf16)
 
 
 def relay2_kernel(arrived, slope, w, message, dpre_out):
@@ -226,29 +220,31 @@
 
     @pl.when(section == 0)
     def _():
-        dpre_out[...] = (arrived[:128, :].astype(f32) * slope[...]).astype(bf16)
-
-
-def last_kernel(arrived, dpre, w, head3, msg3, msg2, msg1, own, grads, head_out):
+        dpre_out[...] = (arrived[...].astype(f32) * slope[...]).astype(bf16)
+
+
+def last_kernel(
+    arrived, dpre, w, head3, head2, head1, head0, msg3, msg2, msg1, own, grads, head_out
+):
     section = lax.axis_index("section")
 
     @pl.when(section == 3)
     def _():
-        grads[...] = msg3[:128, :]
+        grads[...] = msg3[...]
         head_out[...] = head3[:12, :]
 
-    for at, sent in ((2, msg2), (1, msg1)):
+    for at, sent, head in ((2, msg2, head2), (1, msg1, head1)):
 
         @pl.when(section == at)
         def _():
-            grads[...] = sent[:128, :]
-            head_out[...] = sent[128:, at * 128 : at * 128 + 128].astype(f32)[:12]
+            grads[...] = sent[...]
+            head_out[...] = head[:, at * 128 : at * 128 + 128].astype(f32)[:12]
 
     @pl.when(section == 0)
     def _():
-        below = arrived[:128, :].astype(f32) + conv_back(dpre[...].astype(f32), w)
+        below = arrived[...].astype(f32) + conv_back(dpre[...].astype(f32), w)
         grads[...] = below.astype(bf16)
-        head_out[...] = arrived[128:, :128].astype(f32)[:12]
+        head_out[...] = head0[:, :128].astype(f32)[:12]
 
 
 def stack_kernel(*refs):
@@ -256,7 +252,7 @@
     r = col_iota((48, 128))
     ph, pw = (r >> 3) & 3, r & 7
     for g in range(8):
-        held = near[g][0:48, :] if g < 4 else far[g - 4][48:96, :]
+        held = far[g // 2][48:96, :] if g % 2 else near[g // 2][0:48, :]
         v = held.astype(f32)
         for tap in range(9):
             dh, dw = tap // 3 - 1, tap % 3 - 1
@@ -274,13 +270,17 @@
     out[...] = mm(pick, scratch[...]).astype(bf16)
 
 
-def wgrad_kernel(stack, *refs):
-    grads, outs = refs[:8], refs[8:]
-    rows = jnp.concatenate([g[...] for g in grads], axis=0)
-    total = mm(stack[...], rows)
-    outs[0][...] = total[:112]
-    outs[1][...] = total[112:336].astype(bf16)
-    outs[2][...] = total[336:].astype(bf16)
+def wgrad_a_kernel(stack, *refs):
+    rows = jnp.concatenate([grad[...] for grad in refs[:6]], axis=0)
+    refs[7][...] = mm(stack[:, :768], rows)
+
+
+def wgrad_b_kernel(stack, part, near, far, own, pair, diagonal):
+    rows = jnp.concatenate([near[...], far[...]], axis=0)
+    total = part[...] + mm(stack[:, 768:], rows)
+    own[...] = total[:112]
+    pair[...] = total[112:336].astype(bf16)
+    diagonal[...] = total[336:].astype(bf16)
 
 
 def sum_kernel(own, pair, crossed, diagonal, out):
@@ -323,7 +323,6 @@
 def per_device(saved, kernels, head, counts, pairs, valid):
     ranks = lax.axis_size("dp")
     act = VMEM((ROWS, CH), bf16)
-    msg = VMEM((MSG, CH), bf16)
     piece = VMEM((96, 128), bf16)
     gather = (0, 2, 8, 10)
 
@@ -342,29 +341,32 @@
             VMEM((ROWS, CH), f32),
             VMEM((256, 256), bf16),
             act,
-            VMEM((3, 3, CH, CH), bf16),
+            VMEM((9, CH, CH), bf16),
             VMEM((CH, EMB), bf16),
         ),
-        [SMEM((4,), jnp.int32), SMEM((4,), jnp.int32), pltpu.SemaphoreType.DMA((7,))],
+        [SMEM((4,), jnp.int32), SMEM((4,), jnp.int32), pltpu.SemaphoreType.DMA((13,))],
     )(
         saved.reshape(ROWS, CH),
-        jnp.transpose(kernels[0], (1, 2, 0, 3)),
+        jnp.transpose(kernels[0], (1, 2, 0, 3)).reshape(9, CH, CH),
         head,
         counts,
         pairs,
         valid,
     )
     gathered = lax.all_to_all(announce.reshape(32, 8, 256), "dp", 0, 0, tiled=True)
-    msg3, dpre3, head3 = call(
-        top_kernel, [VMEM] * 4, (msg, act, VMEM((16, 128), f32))
+    msg3, dpre3, head3, head_sent = call(
+        top_kernel, [VMEM] * 4, (act, act, VMEM((16, 128), f32), VMEM((16, CH), bf16))
     )(gathered.reshape(256, 256), head, slope, w)
     arrived = relayed(msg3, [(3, 2), (1, 0)])
+    head2 = relayed(head_sent, [(3, 2), (1, 0)])
     split = call(split_kernel, [VMEM] * 2, (piece,) * 4)(rows, msg3)
     near = [split[0]] + [swap(split[k], gather[k]) for k in range(1, 4)]
-    msg2, dpre2 = call(relay2_kernel, [VMEM] * 3, (msg, act))(arrived, slope, w)
+    msg2, dpre2 = call(relay2_kernel, [VMEM] * 3, (act, act))(arrived, slope, w)
     arrived = relayed(msg2, [(2, 1), (3, 0)])
-    msg1, dpre1 = call(relay1_kernel, [VMEM] * 3, (msg, act))(arrived, slope, w)
+    head1 = relayed(head2, [(2, 1), (3, 0)])
+    msg1, dpre1 = call(relay1_kernel, [VMEM] * 3, (act, act))(arrived, slope, w)
     arrived = relayed(msg1, [(1, 0), (3, 2)])
+    head0 = relayed(head1, [(1, 0), (3, 2)])
     far = [swap(value, 1) for value in near]
     dpre = call(bottom_kernel, [VMEM] * 9, act)(
         arrived, slope, dpre3, dpre2, dpre1, *far
@@ -374,17 +376,21 @@
         stack_kernel, [VMEM] * 9, VMEM((448, 1024), bf16), [VMEM((432, 1024), bf16)]
     )(*near, *far, dpre)
     far_grads = [swap(value, 1) for value in near_grads]
+    by_member = [value for both in zip(near_grads, far_grads) for value in both]
+    part = call(wgrad_a_kernel, [VMEM] * 8, VMEM((448, CH), f32))(
+        stack, *by_member[:6], near_grads[3]
+    )
     own, pair, diagonal = call(
-        wgrad_kernel,
-        [VMEM] * 9,
+        wgrad_b_kernel,
+        [VMEM] * 4,
         (VMEM((112, CH), f32), VMEM((224, CH), bf16), VMEM((112, CH), bf16)),
-    )(stack, *near_grads, *far_grads)
+    )(stack, part, *by_member[6:])
     pair = swap(pair, 6, 24)
     diagonal = swap(diagonal, 30)
     crossed = swap(pair, 1)
     grads, head_grad = call(
-        last_kernel, [VMEM] * 8, (sds((ROWS, CH), bf16), sds((12, 128), f32))
-    )(arrived, dpre, w, head3, msg3, msg2, msg1, own)
+        last_kernel, [VMEM] * 11, (sds((ROWS, CH), bf16), sds((12, 128), f32))
+    )(arrived, dpre, w, head3, head2, head1, head0, msg3, msg2, msg1, own)
     wgrad = call(sum_kernel, [VMEM] * 4, sds((108, 1, CH), f32))(own, pair, crossed, diagonal)
     return (
         grads.reshape(saved.shape),

time: 69.2 us -> 75.8 us (1.095)
  the two profiles are of different devices: /device:TPU:1 before, /device:TPU:0 now
where the time goes in v6:
time: 75.8 us; the launch traced here: 75.7 us
  waiting for transfers between devices  29.6 us (39%)
  starting transfers between devices  22.7 us (30%)
  blocking collectives  15 us (20%)
  Pallas kernels  6.98 us (9%)
  between operations  1.38 us (2%)
    ppermute x6, waiting for transfers between devices, relayed(): return lax.ppermute(value, 'section', both)  16 us
    all_to_all x1, blocking collectives, per_device(): lax.all_to_all(announce.reshape(32, 8, 256), 'dp', 0, 0, tiled=True)  15 us
    ppermute x17, waiting for transfers between devices, swap(): return lax.ppermute(value, 'dp', pairs_of)  13.6 us
    ppermute x6, starting transfers between devices, relayed(): return lax.ppermute(value, 'section', both)  12.1 us
    ppermute x17, starting transfers between devices, swap(): return lax.ppermute(value, 'dp', pairs_of)  10.6 us
    pallas_call x11, Pallas kernels, with_operands(): run(*[value if space is SMEM else pltpu.with_memory_space_constraint(valu...  6.98 us
  transfers between devices with their start and end apart: 23, of which 13 were waited for; matrix products, arithmetic and copies ran while one was open for 0% of the time, Pallas kernels for 4%

profile of v6, /device:TPU:0, one launch (start us, length us, event | category | flops | bytes accessed | tf_op | source)
XLA Modules:
  0.0 75.7 jit_solution(3948361990789147906)
XLA Ops:
  1.3 2.6 %shard_map.85 = (f32[128,384]{1,0:T(8,128)S(1)}, bf16[256,256]{1,0:T(8,128)(2,1)S(1)}, bf16[128,384]{1,0:T(8,128)(2,1)S(1)}, bf16[9,384,384]{2,1,0:T(8,128)(2,1)S(1)}, bf16[384,512]{1,0:T(8,128)(2,1)S(1)}) custom-call(bf16[128,384]{1,0:T(8,128)(2,1)} %bitcast.14, bf16[9,384,384]{2,1,0:T(8,128)(2,1)} %bitcast.12, bf16[384,512]{1,0:T(8,128)(2,1)} %head_hbm.1, ...), custom_call_target="tpu_custom_call" | custom-call | tf_op jit(solution)/shard_map/pallas_call | solution.py:307
  3.9 15.0 %all_to_all.5 = bf16[32,8,256]{2,1,0:T(8,128)(2,1)S(1)} all-to-all(bf16[32,8,256]{2,1,0:T(8,128)(2,1)S(1)} %bitcast.11), channel_id=1, replica_groups=mesh['section'=4,'dp'=32] {'dp'}, dimensions={0} | all-to-all | bytes 262144 | tf_op jit(solution)/shard_map/all_to_all | solution.py:356
  18.9 1.9 %collective-permute-start = (bf16[128,384]{1,0:T(8,128)(2,1)S(1)}, bf16[128,384]{1,0:T(8,128)(2,1)S(1)}, u32[]{:S(2)}, u32[]{:S(2)}) collective-permute-start(bf16[128,384]{1,0:T(8,128)(2,1)S(1)} %get-tuple-element.29.order.msg3), channel_id=1, source_target_pairs={{96,64},{32,0},{64,96},{0,32},{97,65},{33,1},{65,97},{1,33},{98,66... | collective-permute-start | bytes 294920 | tf_op jit(solution)/shard_map/ppermute | solution.py:335
  20.8 3.1 %collective-permute-done.arrived = bf16[128,384]{1,0:T(8,128)(2,1)S(1)} collective-permute-done((bf16[128,384]{1,0:T(8,128)(2,1)S(1)}, bf16[128,384]{1,0:T(8,128)(2,1)S(1)}, u32[]{:S(2)}, u32[]{:S(2)}) %collective-permute-start) | collective-permute-done | bytes 98336 | tf_op jit(solution)/shard_map/ppermute | solution.py:335
  23.9 6.5 %collective-permute-start.1 = (bf16[128,384]{1,0:T(8,128)(2,1)S(1)}, bf16[128,384]{1,0:T(8,128)(2,1)S(1)}, u32[]{:S(2)}, u32[]{:S(2)}) collective-permute-start(bf16[128,384]{1,0:T(8,128)(2,1)S(1)} %get-tuple-element.30.msg2), channel_id=1, source_target_pairs={{64,32},{96,0},{32,64},{0,96},{65,33},{97,1},{33,65},{1,97},{66,34... | collective-permute-start | bytes 294920 | tf_op jit(solution)/shard_map/ppermute | solution.py:335
  30.4 2.6 %collective-permute-done.1.arrived = bf16[128,384]{1,0:T(8,128)(2,1)S(1)} collective-permute-done((bf16[128,384]{1,0:T(8,128)(2,1)S(1)}, bf16[128,384]{1,0:T(8,128)(2,1)S(1)}, u32[]{:S(2)}, u32[]{:S(2)}) %collective-permute-start.1) | collective-permute-done | bytes 98336 | tf_op jit(solution)/shard_map/ppermute | solution.py:335
  33.0 1.7 %collective-permute-start.2 = (bf16[128,384]{1,0:T(8,128)(2,1)S(1)}, bf16[128,384]{1,0:T(8,128)(2,1)S(1)}, u32[]{:S(2)}, u32[]{:S(2)}) collective-permute-start(bf16[128,384]{1,0:T(8,128)(2,1)S(1)} %get-tuple-element.31.msg1), channel_id=1, source_target_pairs={{32,0},{96,64},{0,32},{64,96},{33,1},{97,65},{1,33},{65,97},{34,2}... | collective-permute-start | bytes 294920 | tf_op jit(solution)/shard_map/ppermute | solution.py:335
  34.6 0.3 shard_map.89
  35.0 0.8 collective-permute-start.4
  35.7 0.6 collective-permute-start.6
  36.4 2.2 %collective-permute-start.8 = (bf16[96,128]{1,0:T(8,128)(2,1)S(1)}, bf16[96,128]{1,0:T(8,128)(2,1)S(1)}, u32[]{:S(2)}, u32[]{:S(2)}) collective-permute-start(bf16[96,128]{1,0:T(8,128)(2,1)S(1)} %get-tuple-element.39), channel_id=1, source_target_pairs={{0,10},{1,11},{2,8},{3,9},{4,14},{5,15},{6,12},{7,13},{8,2},{9,3},... | collective-permute-start | bytes 73736 | tf_op jit(solution)/shard_map/ppermute | solution.py:331
  38.6 0.0 collective-permute-start.3
  38.6 0.3 collective-permute-done.4.refs_1_
  38.9 0.2 collective-permute-start.5
  39.1 0.5 collective-permute-done.6.refs_2_
  39.6 0.0 collective-permute-start.7
  39.6 1.5 %collective-permute-done.8.refs_3_ = bf16[96,128]{1,0:T(8,128)(2,1)S(1)} collective-permute-done((bf16[96,128]{1,0:T(8,128)(2,1)S(1)}, bf16[96,128]{1,0:T(8,128)(2,1)S(1)}, u32[]{:S(2)}, u32[]{:S(2)}) %collective-permute-start.8) | collective-permute-done | bytes 24608 | tf_op jit(solution)/shard_map/ppermute | solution.py:331
  41.1 0.0 collective-permute-start.9
  41.1 0.0 collective-permute-done.3.refs_0_.refs_4_
  41.1 0.0 collective-permute-done.5.refs_1_.refs_5_
  41.1 0.0 collective-permute-done.7.refs_2_.refs_6_
  41.1 1.2 %collective-permute-done.9.refs_3_.refs_7_ = bf16[96,128]{1,0:T(8,128)(2,1)S(1)} collective-permute-done((bf16[96,128]{1,0:T(8,128)(2,1)S(1)}, bf16[96,128]{1,0:T(8,128)(2,1)S(1)}, u32[]{:S(2)}, u32[]{:S(2)}) %collective-permute-start.9) | collective-permute-done | bytes 24608 | tf_op jit(solution)/shard_map/ppermute | solution.py:331
  42.3 0.0 collective-permute-done.2.arrived
  42.3 1.4 %collective-permute-start.14 = (bf16[128,384]{1,0:T(8,128)(2,1)S(1)}, bf16[128,384]{1,0:T(8,128)(2,1)S(1)}, u32[]{:S(2)}, u32[]{:S(2)}) collective-permute-start(bf16[128,384]{1,0:T(8,128)(2,1)S(1)} %shard_map.90.refs_8_.refs_0_.dpre), channel_id=1, source_target_pairs={{0,2},{1,3},{2,0},{3,1},{4,6},{5,7},{6,4},{7,5},{8,10},{9,11},{10,... | collective-permute-start | bytes 294920 | tf_op jit(solution)/shard_map/ppermute | solution.py:331
  43.8 1.4 %collective-permute-start.16 = (bf16[128,384]{1,0:T(8,128)(2,1)S(1)}, bf16[128,384]{1,0:T(8,128)(2,1)S(1)}, u32[]{:S(2)}, u32[]{:S(2)}) collective-permute-start(bf16[128,384]{1,0:T(8,128)(2,1)S(1)} %shard_map.90.refs_8_.refs_0_.dpre), channel_id=1, source_target_pairs={{0,8},{1,9},{2,10},{3,11},{4,12},{5,13},{6,14},{7,15},{8,0},{9,1},... | collective-permute-start | bytes 294920 | tf_op jit(solution)/shard_map/ppermute | solution.py:331
  45.2 0.7 collective-permute-start.18
  45.9 0.0 collective-permute-start.13
  45.9 1.4 %collective-permute-done.14.refs_2_ = bf16[128,384]{1,0:T(8,128)(2,1)S(1)} collective-permute-done((bf16[128,384]{1,0:T(8,128)(2,1)S(1)}, bf16[128,384]{1,0:T(8,128)(2,1)S(1)}, u32[]{:S(2)}, u32[]{:S(2)}) %collective-permute-start.14) | collective-permute-done | bytes 98336 | tf_op jit(solution)/shard_map/ppermute | solution.py:331
  47.3 0.0 collective-permute-start.15
  47.3 2.2 %collective-permute-done.16.refs_4_ = bf16[128,384]{1,0:T(8,128)(2,1)S(1)} collective-permute-done((bf16[128,384]{1,0:T(8,128)(2,1)S(1)}, bf16[128,384]{1,0:T(8,128)(2,1)S(1)}, u32[]{:S(2)}, u32[]{:S(2)}) %collective-permute-start.16) | collective-permute-done | bytes 98336 | tf_op jit(solution)/shard_map/ppermute | solution.py:331
  49.4 0.0 collective-permute-start.17
  49.4 1.2 %collective-permute-done.18.refs_6_.near = bf16[128,384]{1,0:T(8,128)(2,1)S(1)} collective-permute-done((bf16[128,384]{1,0:T(8,128)(2,1)S(1)}, bf16[128,384]{1,0:T(8,128)(2,1)S(1)}, u32[]{:S(2)}, u32[]{:S(2)}) %collective-permute-start.18) | collective-permute-done | bytes 98336 | tf_op jit(solution)/shard_map/ppermute | solution.py:331
  50.7 0.0 collective-permute-start.19
  50.7 0.9 %shard_map.91.stack = bf16[448,1024]{1,0:T(8,128)(2,1)S(1)} custom-call(bf16[96,128]{1,0:T(8,128)(2,1)S(1)} %get-tuple-element.36.refs_0_, bf16[96,128]{1,0:T(8,128)(2,1)S(1)} %collective-permute-done.4.refs_1_, bf16[96,128]{1,0:T(8,128)(2,1)S(1)} %collective-permute-done.6.refs_2_, bf16[96,128]{1,0:T(8,128)(2,1)S(1)} %collective-permute-done.8.refs_3_, ...), custom_call_target="tpu_custom_call" | custom-call | tf_op jit(solution)/shard_map/pallas_call | solution.py:307
  51.6 0.0 collective-permute-done.13.refs_1_
  51.6 0.0 collective-permute-done.15.refs_3_
  51.6 0.0 collective-permute-done.17.refs_5_
  51.6 0.5 shard_map.92.part
  52.2 0.0 collective-permute-done.19.far
  52.2 0.3 shard_map.93
  52.5 1.4 %collective-permute-start.20 = (bf16[224,384]{1,0:T(8,128)(2,1)S(1)}, bf16[224,384]{1,0:T(8,128)(2,1)S(1)}, u32[]{:S(2)}, u32[]{:S(2)}) collective-permute-start(bf16[224,384]{1,0:T(8,128)(2,1)S(1)} %get-tuple-element.44), channel_id=1, source_target_pairs={{0,6},{1,25},{2,4},{3,27},{4,2},{5,29},{6,0},{7,31},{8,14},{9,17},... | collective-permute-start | bytes 516104 | tf_op jit(solution)/shard_map/ppermute | solution.py:331
  53.8 5.3 %collective-permute-done.20.pair = bf16[224,384]{1,0:T(8,128)(2,1)S(1)} collective-permute-done((bf16[224,384]{1,0:T(8,128)(2,1)S(1)}, bf16[224,384]{1,0:T(8,128)(2,1)S(1)}, u32[]{:S(2)}, u32[]{:S(2)}) %collective-permute-start.20) | collective-permute-done | bytes 172064 | tf_op jit(solution)/shard_map/ppermute | solution.py:331
  59.1 0.0 collective-permute-start.21
  59.2 1.9 %collective-permute-start.22 = (bf16[112,384]{1,0:T(8,128)(2,1)S(1)}, bf16[112,384]{1,0:T(8,128)(2,1)S(1)}, u32[]{:S(2)}, u32[]{:S(2)}) collective-permute-start(bf16[112,384]{1,0:T(8,128)(2,1)S(1)} %get-tuple-element.45), channel_id=1, source_target_pairs={{0,30},{1,31},{2,28},{3,29},{4,26},{5,27},{6,24},{7,25},{8,22},{9,... | collective-permute-start | bytes 258056 | tf_op jit(solution)/shard_map/ppermute | solution.py:331
  61.0 0.3 collective-permute-start.10
  61.4 3.4 %collective-permute-done.10.head2 = bf16[16,384]{1,0:T(8,128)(2,1)S(1)} collective-permute-done((bf16[16,384]{1,0:T(8,128)(2,1)S(1)}, bf16[16,384]{1,0:T(8,128)(2,1)S(1)}, u32[]{:S(2)}, u32[]{:S(2)}) %collective-permute-start.10) | collective-permute-done | bytes 12320 | tf_op jit(solution)/shard_map/ppermute | solution.py:335
  64.7 1.6 %collective-permute-start.11 = (bf16[16,384]{1,0:T(8,128)(2,1)S(1)}, bf16[16,384]{1,0:T(8,128)(2,1)S(1)}, u32[]{:S(2)}, u32[]{:S(2)}) collective-permute-start(bf16[16,384]{1,0:T(8,128)(2,1)S(1)} %collective-permute-done.10.head2), channel_id=1, source_target_pairs={{64,32},{96,0},{32,64},{0,96},{65,33},{97,1},{33,65},{1,97},{66,34... | collective-permute-start | bytes 36872 | tf_op jit(solution)/shard_map/ppermute | solution.py:335
  66.4 3.3 %collective-permute-done.11.head1 = bf16[16,384]{1,0:T(8,128)(2,1)S(1)} collective-permute-done((bf16[16,384]{1,0:T(8,128)(2,1)S(1)}, bf16[16,384]{1,0:T(8,128)(2,1)S(1)}, u32[]{:S(2)}, u32[]{:S(2)}) %collective-permute-start.11) | collective-permute-done | bytes 12320 | tf_op jit(solution)/shard_map/ppermute | solution.py:335
  69.6 0.0 collective-permute-start.12
  69.6 3.7 %collective-permute-done.12.head0 = bf16[16,384]{1,0:T(8,128)(2,1)S(1)} collective-permute-done((bf16[16,384]{1,0:T(8,128)(2,1)S(1)}, bf16[16,384]{1,0:T(8,128)(2,1)S(1)}, u32[]{:S(2)}, u32[]{:S(2)}) %collective-permute-start.12) | collective-permute-done | bytes 12320 | tf_op jit(solution)/shard_map/ppermute | solution.py:335
  73.3 1.6 %shard_map.94 = (bf16[128,384]{1,0:T(8,128)(2,1)}, f32[12,128]{1,0:T(8,128)}) custom-call(bf16[128,384]{1,0:T(8,128)(2,1)S(1)} %collective-permute-done.2.arrived, bf16[128,384]{1,0:T(8,128)(2,1)S(1)} %shard_map.90.refs_8_.refs_0_.dpre, bf16[9,384,384]{2,1,0:T(8,128)(2,1)S(1)} %get-tuple-element.28.w, f32[16,128]{1,0:T(8,128)S(1)} %get-tuple-element.40.head3, ...), custom_call_target="tpu_custom_call" | custom-call | tf_op jit(solution)/shard_map/pallas_call | solution.py:307
  74.9 0.0 collective-permute-done.22.diagonal
  74.9 0.0 collective-permute-done.21.crossed
  74.9 0.7 shard_map.95
  (4 shorter events, 0.0 us)
Async XLA Ops:
  18.9 5.0 %collective-permute-start = (bf16[128,384]{1,0:T(8,128)(2,1)S(1)}, bf16[128,384]{1,0:T(8,128)(2,1)S(1)}, u32[]{:S(2)}, u32[]{:S(2)}) collective-permute-start(bf16[128,384]{1,0:T(8,128)(2,1)S(1)} %get-tuple-element.29.order.msg3), channel_id=1, source_target_pairs={{96,64},{32,0},{64,96},{0,32},{97,65},{33,1},{65,97},{1,33},{98,66... | collective-permute-start | bytes 294920 | tf_op jit(solution)/shard_map/ppermute | solution.py:335
  23.9 9.1 %collective-permute-start.1 = (bf16[128,384]{1,0:T(8,128)(2,1)S(1)}, bf16[128,384]{1,0:T(8,128)(2,1)S(1)}, u32[]{:S(2)}, u32[]{:S(2)}) collective-permute-start(bf16[128,384]{1,0:T(8,128)(2,1)S(1)} %get-tuple-element.30.msg2), channel_id=1, source_target_pairs={{64,32},{96,0},{32,64},{0,96},{65,33},{97,1},{33,65},{1,97},{66,34... | collective-permute-start | bytes 294920 | tf_op jit(solution)/shard_map/ppermute | solution.py:335
  33.0 9.3 %collective-permute-start.2 = (bf16[128,384]{1,0:T(8,128)(2,1)S(1)}, bf16[128,384]{1,0:T(8,128)(2,1)S(1)}, u32[]{:S(2)}, u32[]{:S(2)}) collective-permute-start(bf16[128,384]{1,0:T(8,128)(2,1)S(1)} %get-tuple-element.31.msg1), channel_id=1, source_target_pairs={{32,0},{96,64},{0,32},{64,96},{33,1},{97,65},{1,33},{65,97},{34,2}... | collective-permute-start | bytes 294920 | tf_op jit(solution)/shard_map/ppermute | solution.py:335
  35.0 3.9 %collective-permute-start.4 = (bf16[96,128]{1,0:T(8,128)(2,1)S(1)}, bf16[96,128]{1,0:T(8,128)(2,1)S(1)}, u32[]{:S(2)}, u32[]{:S(2)}) collective-permute-start(bf16[96,128]{1,0:T(8,128)(2,1)S(1)} %get-tuple-element.37), channel_id=1, source_target_pairs={{0,2},{1,3},{2,0},{3,1},{4,6},{5,7},{6,4},{7,5},{8,10},{9,11},{10,... | collective-permute-start | bytes 73736 | tf_op jit(solution)/shard_map/ppermute | solution.py:331
  35.7 3.8 %collective-permute-start.6 = (bf16[96,128]{1,0:T(8,128)(2,1)S(1)}, bf16[96,128]{1,0:T(8,128)(2,1)S(1)}, u32[]{:S(2)}, u32[]{:S(2)}) collective-permute-start(bf16[96,128]{1,0:T(8,128)(2,1)S(1)} %get-tuple-element.38), channel_id=1, source_target_pairs={{0,8},{1,9},{2,10},{3,11},{4,12},{5,13},{6,14},{7,15},{8,0},{9,1},... | collective-permute-start | bytes 73736 | tf_op jit(solution)/shard_map/ppermute | solution.py:331
  36.4 4.7 %collective-permute-start.8 = (bf16[96,128]{1,0:T(8,128)(2,1)S(1)}, bf16[96,128]{1,0:T(8,128)(2,1)S(1)}, u32[]{:S(2)}, u32[]{:S(2)}) collective-permute-start(bf16[96,128]{1,0:T(8,128)(2,1)S(1)} %get-tuple-element.39), channel_id=1, source_target_pairs={{0,10},{1,11},{2,8},{3,9},{4,14},{5,15},{6,12},{7,13},{8,2},{9,3},... | collective-permute-start | bytes 73736 | tf_op jit(solution)/shard_map/ppermute | solution.py:331
  38.6 2.5 %collective-permute-start.3 = (bf16[96,128]{1,0:T(8,128)(2,1)S(1)}, bf16[96,128]{1,0:T(8,128)(2,1)S(1)}, u32[]{:S(2)}, u32[]{:S(2)}) collective-permute-start(bf16[96,128]{1,0:T(8,128)(2,1)S(1)} %get-tuple-element.36.refs_0_), channel_id=1, source_target_pairs={{0,1},{1,0},{2,3},{3,2},{4,5},{5,4},{6,7},{7,6},{8,9},{9,8},{10,11... | collective-permute-start | bytes 73736 | tf_op jit(solution)/shard_map/ppermute | solution.py:331
  38.9 2.2 %collective-permute-start.5 = (bf16[96,128]{1,0:T(8,128)(2,1)S(1)}, bf16[96,128]{1,0:T(8,128)(2,1)S(1)}, u32[]{:S(2)}, u32[]{:S(2)}) collective-permute-start(bf16[96,128]{1,0:T(8,128)(2,1)S(1)} %collective-permute-done.4.refs_1_), channel_id=1, source_target_pairs={{0,1},{1,0},{2,3},{3,2},{4,5},{5,4},{6,7},{7,6},{8,9},{9,8},{10,11... | collective-permute-start | bytes 73736 | tf_op jit(solution)/shard_map/ppermute | solution.py:331
  39.6 1.5 %collective-permute-start.7 = (bf16[96,128]{1,0:T(8,128)(2,1)S(1)}, bf16[96,128]{1,0:T(8,128)(2,1)S(1)}, u32[]{:S(2)}, u32[]{:S(2)}) collective-permute-start(bf16[96,128]{1,0:T(8,128)(2,1)S(1)} %collective-permute-done.6.refs_2_), channel_id=1, source_target_pairs={{0,1},{1,0},{2,3},{3,2},{4,5},{5,4},{6,7},{7,6},{8,9},{9,8},{10,11... | collective-permute-start | bytes 73736 | tf_op jit(solution)/shard_map/ppermute | solution.py:331
  41.1 1.2 %collective-permute-start.9 = (bf16[96,128]{1,0:T(8,128)(2,1)S(1)}, bf16[96,128]{1,0:T(8,128)(2,1)S(1)}, u32[]{:S(2)}, u32[]{:S(2)}) collective-permute-start(bf16[96,128]{1,0:T(8,128)(2,1)S(1)} %collective-permute-done.8.refs_3_), channel_id=1, source_target_pairs={{0,1},{1,0},{2,3},{3,2},{4,5},{5,4},{6,7},{7,6},{8,9},{9,8},{10,11... | collective-permute-start | bytes 73736 | tf_op jit(solution)/shard_map/ppermute | solution.py:331
  42.3 4.9 %collective-permute-start.14 = (bf16[128,384]{1,0:T(8,128)(2,1)S(1)}, bf16[128,384]{1,0:T(8,128)(2,1)S(1)}, u32[]{:S(2)}, u32[]{:S(2)}) collective-permute-start(bf16[128,384]{1,0:T(8,128)(2,1)S(1)} %shard_map.90.refs_8_.refs_0_.dpre), channel_id=1, source_target_pairs={{0,2},{1,3},{2,0},{3,1},{4,6},{5,7},{6,4},{7,5},{8,10},{9,11},{10,... | collective-permute-start | bytes 294920 | tf_op jit(solution)/shard_map/ppermute | solution.py:331
  43.8 5.7 %collective-permute-start.16 = (bf16[128,384]{1,0:T(8,128)(2,1)S(1)}, bf16[128,384]{1,0:T(8,128)(2,1)S(1)}, u32[]{:S(2)}, u32[]{:S(2)}) collective-permute-start(bf16[128,384]{1,0:T(8,128)(2,1)S(1)} %shard_map.90.refs_8_.refs_0_.dpre), channel_id=1, source_target_pairs={{0,8},{1,9},{2,10},{3,11},{4,12},{5,13},{6,14},{7,15},{8,0},{9,1},... | collective-permute-start | bytes 294920 | tf_op jit(solution)/shard_map/ppermute | solution.py:331
  45.2 5.5 %collective-permute-start.18 = (bf16[128,384]{1,0:T(8,128)(2,1)S(1)}, bf16[128,384]{1,0:T(8,128)(2,1)S(1)}, u32[]{:S(2)}, u32[]{:S(2)}) collective-permute-start(bf16[128,384]{1,0:T(8,128)(2,1)S(1)} %shard_map.90.refs_8_.refs_0_.dpre), channel_id=1, source_target_pairs={{0,10},{1,11},{2,8},{3,9},{4,14},{5,15},{6,12},{7,13},{8,2},{9,3},... | collective-permute-start | bytes 294920 | tf_op jit(solution)/shard_map/ppermute | solution.py:331
  45.9 5.7 %collective-permute-start.13 = (bf16[128,384]{1,0:T(8,128)(2,1)S(1)}, bf16[128,384]{1,0:T(8,128)(2,1)S(1)}, u32[]{:S(2)}, u32[]{:S(2)}) collective-permute-start(bf16[128,384]{1,0:T(8,128)(2,1)S(1)} %shard_map.90.refs_8_.refs_0_.dpre), channel_id=1, source_target_pairs={{0,1},{1,0},{2,3},{3,2},{4,5},{5,4},{6,7},{7,6},{8,9},{9,8},{10,11... | collective-permute-start | bytes 294920 | tf_op jit(solution)/shard_map/ppermute | solution.py:331
  47.3 4.4 %collective-permute-start.15 = (bf16[128,384]{1,0:T(8,128)(2,1)S(1)}, bf16[128,384]{1,0:T(8,128)(2,1)S(1)}, u32[]{:S(2)}, u32[]{:S(2)}) collective-permute-start(bf16[128,384]{1,0:T(8,128)(2,1)S(1)} %collective-permute-done.14.refs_2_), channel_id=1, source_target_pairs={{0,1},{1,0},{2,3},{3,2},{4,5},{5,4},{6,7},{7,6},{8,9},{9,8},{10,11... | collective-permute-start | bytes 294920 | tf_op jit(solution)/shard_map/ppermute | solution.py:331
  49.4 2.2 %collective-permute-start.17 = (bf16[128,384]{1,0:T(8,128)(2,1)S(1)}, bf16[128,384]{1,0:T(8,128)(2,1)S(1)}, u32[]{:S(2)}, u32[]{:S(2)}) collective-permute-start(bf16[128,384]{1,0:T(8,128)(2,1)S(1)} %collective-permute-done.16.refs_4_), channel_id=1, source_target_pairs={{0,1},{1,0},{2,3},{3,2},{4,5},{5,4},{6,7},{7,6},{8,9},{9,8},{10,11... | collective-permute-start | bytes 294920 | tf_op jit(solution)/shard_map/ppermute | solution.py:331
  50.7 1.5 %collective-permute-start.19 = (bf16[128,384]{1,0:T(8,128)(2,1)S(1)}, bf16[128,384]{1,0:T(8,128)(2,1)S(1)}, u32[]{:S(2)}, u32[]{:S(2)}) collective-permute-start(bf16[128,384]{1,0:T(8,128)(2,1)S(1)} %collective-permute-done.18.refs_6_.near), channel_id=1, source_target_pairs={{0,1},{1,0},{2,3},{3,2},{4,5},{5,4},{6,7},{7,6},{8,9},{9,8},{10,11... | collective-permute-start | bytes 294920 | tf_op jit(solution)/shard_map/ppermute | solution.py:331
  52.5 6.7 %collective-permute-start.20 = (bf16[224,384]{1,0:T(8,128)(2,1)S(1)}, bf16[224,384]{1,0:T(8,128)(2,1)S(1)}, u32[]{:S(2)}, u32[]{:S(2)}) collective-permute-start(bf16[224,384]{1,0:T(8,128)(2,1)S(1)} %get-tuple-element.44), channel_id=1, source_target_pairs={{0,6},{1,25},{2,4},{3,27},{4,2},{5,29},{6,0},{7,31},{8,14},{9,17},... | collective-permute-start | bytes 516104 | tf_op jit(solution)/shard_map/ppermute | solution.py:331
  59.1 15.8 %collective-permute-start.21 = (bf16[224,384]{1,0:T(8,128)(2,1)S(1)}, bf16[224,384]{1,0:T(8,128)(2,1)S(1)}, u32[]{:S(2)}, u32[]{:S(2)}) collective-permute-start(bf16[224,384]{1,0:T(8,128)(2,1)S(1)} %collective-permute-done.20.pair), channel_id=1, source_target_pairs={{0,1},{1,0},{2,3},{3,2},{4,5},{5,4},{6,7},{7,6},{8,9},{9,8},{10,11... | collective-permute-start | bytes 516104 | tf_op jit(solution)/shard_map/ppermute | solution.py:331
  59.2 15.8 %collective-permute-start.22 = (bf16[112,384]{1,0:T(8,128)(2,1)S(1)}, bf16[112,384]{1,0:T(8,128)(2,1)S(1)}, u32[]{:S(2)}, u32[]{:S(2)}) collective-permute-start(bf16[112,384]{1,0:T(8,128)(2,1)S(1)} %get-tuple-element.45), channel_id=1, source_target_pairs={{0,30},{1,31},{2,28},{3,29},{4,26},{5,27},{6,24},{7,25},{8,22},{9,... | collective-permute-start | bytes 258056 | tf_op jit(solution)/shard_map/ppermute | solution.py:331
  61.0 3.7 %collective-permute-start.10 = (bf16[16,384]{1,0:T(8,128)(2,1)S(1)}, bf16[16,384]{1,0:T(8,128)(2,1)S(1)}, u32[]{:S(2)}, u32[]{:S(2)}) collective-permute-start(bf16[16,384]{1,0:T(8,128)(2,1)S(1)} %get-tuple-element.41), channel_id=1, source_target_pairs={{96,64},{32,0},{64,96},{0,32},{97,65},{33,1},{65,97},{1,33},{98,66... | collective-permute-start | bytes 36872 | tf_op jit(solution)/shard_map/ppermute | solution.py:335
  64.7 4.9 %collective-permute-start.11 = (bf16[16,384]{1,0:T(8,128)(2,1)S(1)}, bf16[16,384]{1,0:T(8,128)(2,1)S(1)}, u32[]{:S(2)}, u32[]{:S(2)}) collective-permute-start(bf16[16,384]{1,0:T(8,128)(2,1)S(1)} %collective-permute-done.10.head2), channel_id=1, source_target_pairs={{64,32},{96,0},{32,64},{0,96},{65,33},{97,1},{33,65},{1,97},{66,34... | collective-permute-start | bytes 36872 | tf_op jit(solution)/shard_map/ppermute | solution.py:335
  69.6 3.7 %collective-permute-start.12 = (bf16[16,384]{1,0:T(8,128)(2,1)S(1)}, bf16[16,384]{1,0:T(8,128)(2,1)S(1)}, u32[]{:S(2)}, u32[]{:S(2)}) collective-permute-start(bf16[16,384]{1,0:T(8,128)(2,1)S(1)} %collective-permute-done.11.head1), channel_id=1, source_target_pairs={{32,0},{96,64},{0,32},{64,96},{33,1},{97,65},{1,33},{65,97},{34,2}... | collective-permute-start | bytes 36872 | tf_op jit(solution)/shard_map/ppermute | solution.py:335

commit v7 on v4

--- a/solution.py
+++ b/solution.py
@@ -18,7 +18,6 @@
 NT = (((1,), (1,)), ((), ()))
 
 ROWS, CELLS, CH, EMB = 128, 32, 384, 512
-MSG = 144
 
 
 def mm(a, b, dims=NN):
@@ -118,47 +117,69 @@
         message[at_row : at_row + 16, :] = pair
 
 
-def contrast(gathered, head, rank):
-    slot = row_iota((128, 256))
-    lane = col_iota((128, 256))
-    home = ((slot >> 2) << 3) + (slot & 3)
+def scores_of(unit_b, others, ids, lanes):
+    return jnp.where(ids == lanes, 0.0, jnp.exp(mm(unit_b, others, NT) / tau_value))
+
+
+def normalized(pooled, head):
+    proj = mm(pooled, head)
+    inv = lax.rsqrt(jnp.sum(proj * proj, axis=1, keepdims=True) + norm_eps)
+    return proj * inv, inv
+
+
+def projected_grad(mixing, unit_b, unit, inv):
+    dunit = mm(mixing, unit_b) * (loss_scale / tau_value)
+    along = jnp.sum(unit * dunit, axis=1, keepdims=True)
+    return ((dunit - unit * along) * inv).astype(bf16)
+
+
+def slot_rows(gathered, home):
+    lane = col_iota((home.shape[0], 256))
     first = mm(jnp.where(lane == home, 1.0, 0.0).astype(bf16), gathered)
     second = mm(jnp.where(lane == home + 4, 1.0, 0.0).astype(bf16), gathered)
     pooled = jnp.concatenate([first, second[:, :128]], axis=1).astype(bf16)
-    live = second[:, 128:129]
-    pairs = second[:, 129:130]
-    proj = mm(pooled, head)
-    inv = lax.rsqrt(jnp.sum(proj * proj, axis=1, keepdims=True) + norm_eps)
-    unit = proj * inv
+    return pooled, second[:, 128:129], second[:, 129:130]
+
+
+def contrast(gathered, head, rank):
+    slot = row_iota((128, 1))
+    pooled, live, pairs = slot_rows(gathered, ((slot >> 2) << 3) + (slot & 3))
+    own_slot = row_iota((16, 1))
+    own_pooled, own_live, own_pairs = slot_rows(
+        gathered, jnp.where(own_slot < 4, 8 * rank + own_slot, -8)
+    )
+    unit, inv = normalized(pooled, head)
+    own_unit, own_inv = normalized(own_pooled, head)
     unit_b = unit.astype(bf16)
-    i = row_iota((128, 128))
     j = col_iota((128, 128))
-    same = i == j
+    same = slot == j
 
     def across(column):
         return jnp.sum(jnp.where(same, column, 0.0), axis=0, keepdims=True)
 
-    expo = jnp.where(same, 0.0, jnp.exp(mm(unit_b, unit_b, NT) / tau_value))
-    mate = pairs == j.astype(f32)
     live_row = across(live)
-    total = jnp.sum(expo * live_row, axis=1, keepdims=True)
-    share = live * jnp.sum(jnp.where(mate, live_row, 0.0), axis=1, keepdims=True)
-    coef = (share / total).astype(bf16).astype(f32)
+
+    def weights(expo, live, pairs):
+        mate = pairs == col_iota(expo.shape).astype(f32)
+        total = jnp.sum(expo * live_row, axis=1, keepdims=True)
+        share = live * jnp.sum(jnp.where(mate, live_row, 0.0), axis=1, keepdims=True)
+        coef = (share / total).astype(bf16).astype(f32)
+        return coef, 2.0 * jnp.where(mate, share, 0.0)
+
+    expo = scores_of(unit_b, unit_b, slot, j)
+    own_expo = scores_of(own_unit.astype(bf16), unit_b, own_slot + 4 * rank, col_iota((16, 128)))
+    coef, drawn = weights(expo, live, pairs)
+    own_coef, own_drawn = weights(own_expo, own_live, own_pairs)
     coef_row = across(coef)
-    mixing = expo * (coef * live_row + coef_row * live) - 2.0 * jnp.where(mate, share, 0.0)
-    dunit = mm(mixing.astype(bf16), unit_b) * (loss_scale / tau_value)
-    along = jnp.sum(unit * dunit, axis=1, keepdims=True)
-    dproj = ((dunit - unit * along) * inv).astype(bf16)
-    own = jnp.where(
-        col_iota((16, 128)) == row_iota((16, 128)) + 4 * rank, 1.0, 0.0
-    ).astype(bf16)
-    dproj_own = mm(own, dproj).astype(bf16)
-    dpooled = mm(dproj_own, head, NT).astype(bf16)
+    mixing = expo * (coef * live_row + coef_row * live) - drawn
+    own_mixing = own_expo * (own_coef * live_row + coef_row * own_live) - own_drawn
+    dproj = projected_grad(own_mixing.astype(bf16), unit_b, own_unit, own_inv)
+    dpooled = mm(dproj, head, NT).astype(bf16)
     mine = jnp.where(
         col_iota((16, CH)) == row_iota((16, CH)) + 12 * rank, 1.0, 0.0
     ).astype(bf16)
     pooled_mine = mm(mine, pooled, NT).astype(bf16)
-    return dpooled[:4].astype(f32), mm(pooled_mine, dproj)
+    return dpooled[:4].astype(f32), (mixing.astype(bf16), unit, inv, pooled_mine)
 
 
 def split_kernel(saved, order, *outs):
@@ -180,39 +201,59 @@
         out[...] = turned[96 * k : 96 * k + 96]
 
 
-def top_kernel(gathered, head, slope, w, message, dpre_out, head_out):
+def top_kernel(
+    gathered, head, slope, w, message, dpre_out, mixing_out, unit_out, inv_out, mine_out
+):
     section, rank, _, _, _ = position()
 
     @pl.when(section == 3)
     def _():
-        dpooled, head_grad = contrast(gathered[...], head[...], rank)
+        dpooled, (mixing, unit, inv, mine) = contrast(gathered[...], head[...], rank)
+        mixing_out[...] = mixing
+        unit_out[...] = unit
+        inv_out[...] = jnp.broadcast_to(inv, (128, 128))
+        mine_out[...] = mine
         top = (dpooled / CELLS).astype(bf16).astype(f32)
         cot = jnp.broadcast_to(top[:, None, :], (4, CELLS, CH)).reshape(ROWS, CH)
         dpre = (cot * slope[...]).astype(bf16)
         dpre_out[...] = dpre
-        head_out[...] = head_grad[:, 384:]
-        message[128:, :] = head_grad[:, :384].astype(bf16)
         below = cot + conv_back(dpre.astype(f32), w)
-        message[:128, :] = below.astype(bf16)
+        message[...] = below.astype(bf16)
 
 
 def relay(active, arrived, slope, w, message, dpre_out):
     @pl.when(lax.axis_index("section") == active)
     def _():
-        cot = arrived[:128, :].astype(f32)
+        cot = arrived[...].astype(f32)
         dpre = (cot * slope[...]).astype(bf16)
         dpre_out[...] = dpre
-        message[128:, :] = arrived[128:, :]
         below = cot + conv_back(dpre.astype(f32), w)
-        message[:128, :] = below.astype(bf16)
-
-
-def relay2_kernel(arrived, slope, w, message, dpre_out):
+        message[...] = below.astype(bf16)
+
+
+def relay2_kernel(arrived, slope, w, mixing, unit, inv, mine, message, dpre_out, head_out):
     relay(2, arrived, slope, w, message, dpre_out)
 
-
-def relay1_kernel(arrived, slope, w, message, dpre_out):
+    @pl.when(lax.axis_index("section") == 3)
+    def _():
+        units = unit[...]
+        dproj = projected_grad(mixing[...], units.astype(bf16), units, inv[:, :1])
+        head_grad = mm(mine[...], dproj)
+        head_out[...] = head_grad
+        message[:16, :] = head_grad[:, :384].astype(bf16)
+
+
+def relay1_kernel(arrived, slope, w, head_grad, message, dpre_out):
     relay(1, arrived, slope, w, message, dpre_out)
+    section = lax.axis_index("section")
+
+    @pl.when(section == 3)
+    def _():
+        message[:16, :] = head_grad[:, :384].astype(bf16)
+
+    @pl.when(section == 0)
+    def _():
+        message[:16, :] = arrived[:16, :]
 
 
 def bottom_kernel(arrived, slope, dpre3, dpre2, dpre1, *refs):
@@ -226,29 +267,29 @@
 
     @pl.when(section == 0)
     def _():
-        dpre_out[...] = (arrived[:128, :].astype(f32) * slope[...]).astype(bf16)
-
-
-def last_kernel(arrived, dpre, w, head3, msg3, msg2, msg1, own, grads, head_out):
+        dpre_out[...] = (arrived[...].astype(f32) * slope[...]).astype(bf16)
+
+
+def last_kernel(arrived, earlier, dpre, w, head_grad, msg3, msg2, msg1, own, grads, head_out):
     section = lax.axis_index("section")
 
     @pl.when(section == 3)
     def _():
-        grads[...] = msg3[:128, :]
-        head_out[...] = head3[:12, :]
+        grads[...] = msg3[...]
+        head_out[...] = head_grad[:12, 384:]
 
     for at, sent in ((2, msg2), (1, msg1)):
 
         @pl.when(section == at)
         def _():
-            grads[...] = sent[:128, :]
-            head_out[...] = sent[128:, at * 128 : at * 128 + 128].astype(f32)[:12]
+            grads[...] = sent[...]
+            head_out[...] = arrived[:16, at * 128 : at * 128 + 128].astype(f32)[:12]
 
     @pl.when(section == 0)
     def _():
-        below = arrived[:128, :].astype(f32) + conv_back(dpre[...].astype(f32), w)
+        below = arrived[...].astype(f32) + conv_back(dpre[...].astype(f32), w)
         grads[...] = below.astype(bf16)
-        head_out[...] = arrived[128:, :128].astype(f32)[:12]
+        head_out[...] = earlier[:16, :128].astype(f32)[:12]
 
 
 def stack_kernel(*refs):
@@ -323,7 +364,6 @@
 def per_device(saved, kernels, head, counts, pairs, valid):
     ranks = lax.axis_size("dp")
     act = VMEM((ROWS, CH), bf16)
-    msg = VMEM((MSG, CH), bf16)
     piece = VMEM((96, 128), bf16)
     gather = (0, 2, 8, 10)
 
@@ -355,15 +395,20 @@
         valid,
     )
     gathered = lax.all_to_all(announce.reshape(32, 8, 256), "dp", 0, 0, tiled=True)
-    msg3, dpre3, head3 = call(
-        top_kernel, [VMEM] * 4, (msg, act, VMEM((16, 128), f32))
+    msg3, dpre3, *for_head = call(
+        top_kernel,
+        [VMEM] * 4,
+        (act, act, VMEM((128, 128), bf16), VMEM((128, EMB), f32), VMEM((128, 128), f32))
+        + (VMEM((16, 128), bf16),),
     )(gathered.reshape(256, 256), head, slope, w)
     arrived = relayed(msg3, [(3, 2), (1, 0)])
     split = call(split_kernel, [VMEM] * 2, (piece,) * 4)(rows, msg3)
     near = [split[0]] + [swap(split[k], gather[k]) for k in range(1, 4)]
-    msg2, dpre2 = call(relay2_kernel, [VMEM] * 3, (msg, act))(arrived, slope, w)
-    arrived = relayed(msg2, [(2, 1), (3, 0)])
-    msg1, dpre1 = call(relay1_kernel, [VMEM] * 3, (msg, act))(arrived, slope, w)
+    msg2, dpre2, head_grad = call(
+        relay2_kernel, [VMEM] * 7, (act, act, VMEM((16, EMB), f32))
+    )(arrived, slope, w, *for_head)
+    arrived = earlier = relayed(msg2, [(2, 1), (3, 0)])
+    msg1, dpre1 = call(relay1_kernel, [VMEM] * 4, (act, act))(arrived, slope, w, head_grad)
     arrived = relayed(msg1, [(1, 0), (3, 2)])
     far = [swap(value, 1) for value in near]
     dpre = call(bottom_kernel, [VMEM] * 9, act)(
@@ -383,8 +428,8 @@
     diagonal = swap(diagonal, 30)
     crossed = swap(pair, 1)
     grads, head_grad = call(
-        last_kernel, [VMEM] * 8, (sds((ROWS, CH), bf16), sds((12, 128), f32))
-    )(arrived, dpre, w, head3, msg3, msg2, msg1, own)
+        last_kernel, [VMEM] * 9, (sds((ROWS, CH), bf16), sds((12, 128), f32))
+    )(arrived, earlier, dpre, w, head_grad, msg3, msg2, msg1, own)
     wgrad = call(sum_kernel, [VMEM] * 4, sds((108, 1, CH), f32))(own, pair, crossed, diagonal)
     return (
         grads.reshape(saved.shape),

time: 69.2 us -> 68.4 us (0.988)
  no operation moved by 1% of the time
where the time goes in v7:
time: 68.4 us; the launch traced here: 68.3 us
  starting transfers between devices  26.5 us (39%)
  waiting for transfers between devices  17.7 us (26%)
  blocking collectives  16 us (23%)
  Pallas kernels  6.71 us (10%)
  between operations  1.36 us (2%)
    ppermute x17, starting transfers between devices, swap(): return lax.ppermute(value, 'dp', pairs_of)  17.4 us
    all_to_all x1, blocking collectives, per_device(): lax.all_to_all(announce.reshape(32, 8, 256), 'dp', 0, 0, tiled=True)  16 us
    ppermute x17, waiting for transfers between devices, swap(): return lax.ppermute(value, 'dp', pairs_of)  13.1 us
    ppermute x3, starting transfers between devices, relayed(): return lax.ppermute(value, 'section', both)  9.15 us
    pallas_call x10, Pallas kernels, with_operands(): run(*[value if space is SMEM else pltpu.with_memory_space_constraint(valu...  6.71 us
    ppermute x3, waiting for transfers between devices, relayed(): return lax.ppermute(value, 'section', both)  4.66 us
  transfers between devices with their start and end apart: 20, of which 8 were waited for; matrix products, arithmetic and copies ran while one was open for 0% of the time, Pallas kernels for 4%

profile of v7, /device:TPU:1, one launch (start us, length us, event | category | flops | bytes accessed | tf_op | source)
XLA Modules:
  0.0 68.3 jit_solution(17939457866848340450)
XLA Ops:
  1.3 2.5 %shard_map.85 = (f32[128,384]{1,0:T(8,128)S(1)}, bf16[256,256]{1,0:T(8,128)(2,1)S(1)}, bf16[128,384]{1,0:T(8,128)(2,1)S(1)}, bf16[3,3,384,384]{3,2,1,0:T(8,128)(2,1)S(1)}, bf16[384,512]{1,0:T(8,128)(2,1)S(1)}) custom-call(bf16[128,384]{1,0:T(8,128)(2,1)} %bitcast.12, bf16[3,3,384,384]{3,2,1,0:T(8,128)(2,1)} %bitcast.10, bf16[384,512]{1,0:T(8,128)(2,1)} %head_hbm.1, ...), custom_call_target="tpu_custom_call" | custom-call | tf_op jit(solution)/shard_map/pallas_call | solution.py:348
  3.7 16.0 %all_to_all.5 = bf16[32,8,256]{2,1,0:T(8,128)(2,1)S(1)} all-to-all(bf16[32,8,256]{2,1,0:T(8,128)(2,1)S(1)} %bitcast.9), channel_id=1, replica_groups=mesh['section'=4,'dp'=32] {'dp'}, dimensions={0} | all-to-all | bytes 262144 | tf_op jit(solution)/shard_map/all_to_all | solution.py:397
  19.7 1.6 %collective-permute-start = (bf16[128,384]{1,0:T(8,128)(2,1)S(1)}, bf16[128,384]{1,0:T(8,128)(2,1)S(1)}, u32[]{:S(2)}, u32[]{:S(2)}) collective-permute-start(bf16[128,384]{1,0:T(8,128)(2,1)S(1)} %get-tuple-element.32.order.msg3), channel_id=1, source_target_pairs={{96,64},{32,0},{64,96},{0,32},{97,65},{33,1},{65,97},{1,33},{98,66... | collective-permute-start | bytes 294920 | tf_op jit(solution)/shard_map/ppermute | solution.py:376
  21.4 2.7 %collective-permute-done.arrived = bf16[128,384]{1,0:T(8,128)(2,1)S(1)} collective-permute-done((bf16[128,384]{1,0:T(8,128)(2,1)S(1)}, bf16[128,384]{1,0:T(8,128)(2,1)S(1)}, u32[]{:S(2)}, u32[]{:S(2)}) %collective-permute-start) | collective-permute-done | bytes 98336 | tf_op jit(solution)/shard_map/ppermute | solution.py:376
  24.0 6.2 %collective-permute-start.1 = (bf16[128,384]{1,0:T(8,128)(2,1)S(1)}, bf16[128,384]{1,0:T(8,128)(2,1)S(1)}, u32[]{:S(2)}, u32[]{:S(2)}) collective-permute-start(bf16[128,384]{1,0:T(8,128)(2,1)S(1)} %get-tuple-element.37.msg2), channel_id=1, source_target_pairs={{64,32},{96,0},{32,64},{0,96},{65,33},{97,1},{33,65},{1,97},{66,34... | collective-permute-start | bytes 294920 | tf_op jit(solution)/shard_map/ppermute | solution.py:376
  30.2 2.0 %collective-permute-done.1.arrived.earlier = bf16[128,384]{1,0:T(8,128)(2,1)S(1)} collective-permute-done((bf16[128,384]{1,0:T(8,128)(2,1)S(1)}, bf16[128,384]{1,0:T(8,128)(2,1)S(1)}, u32[]{:S(2)}, u32[]{:S(2)}) %collective-permute-start.1) | collective-permute-done | bytes 98336 | tf_op jit(solution)/shard_map/ppermute | solution.py:376
  32.2 1.3 %collective-permute-start.2 = (bf16[128,384]{1,0:T(8,128)(2,1)S(1)}, bf16[128,384]{1,0:T(8,128)(2,1)S(1)}, u32[]{:S(2)}, u32[]{:S(2)}) collective-permute-start(bf16[128,384]{1,0:T(8,128)(2,1)S(1)} %get-tuple-element.39.msg1), channel_id=1, source_target_pairs={{32,0},{96,64},{0,32},{64,96},{33,1},{97,65},{1,33},{65,97},{34,2}... | collective-permute-start | bytes 294920 | tf_op jit(solution)/shard_map/ppermute | solution.py:376
  33.5 0.3 shard_map.89
  33.9 0.5 collective-permute-start.4
  34.4 0.4 collective-permute-start.6
  34.7 1.9 %collective-permute-start.8 = (bf16[96,128]{1,0:T(8,128)(2,1)S(1)}, bf16[96,128]{1,0:T(8,128)(2,1)S(1)}, u32[]{:S(2)}, u32[]{:S(2)}) collective-permute-start(bf16[96,128]{1,0:T(8,128)(2,1)S(1)} %get-tuple-element.47), channel_id=1, source_target_pairs={{0,10},{1,11},{2,8},{3,9},{4,14},{5,15},{6,12},{7,13},{8,2},{9,3},... | collective-permute-start | bytes 73736 | tf_op jit(solution)/shard_map/ppermute | solution.py:372
  36.6 3.0 %collective-permute-start.3 = (bf16[96,128]{1,0:T(8,128)(2,1)S(1)}, bf16[96,128]{1,0:T(8,128)(2,1)S(1)}, u32[]{:S(2)}, u32[]{:S(2)}) collective-permute-start(bf16[96,128]{1,0:T(8,128)(2,1)S(1)} %get-tuple-element.44.refs_0_), channel_id=1, source_target_pairs={{0,1},{1,0},{2,3},{3,2},{4,5},{5,4},{6,7},{7,6},{8,9},{9,8},{10,11... | collective-permute-start | bytes 73736 | tf_op jit(solution)/shard_map/ppermute | solution.py:372
  39.6 0.0 collective-permute-done.4.refs_1_
  39.6 0.3 collective-permute-start.5
  39.9 0.0 collective-permute-done.6.refs_2_
  39.9 0.7 collective-permute-start.7
  40.6 0.0 collective-permute-done.8.refs_3_
  40.6 1.5 %collective-permute-start.9 = (bf16[96,128]{1,0:T(8,128)(2,1)S(1)}, bf16[96,128]{1,0:T(8,128)(2,1)S(1)}, u32[]{:S(2)}, u32[]{:S(2)}) collective-permute-start(bf16[96,128]{1,0:T(8,128)(2,1)S(1)} %collective-permute-done.8.refs_3_), channel_id=1, source_target_pairs={{0,1},{1,0},{2,3},{3,2},{4,5},{5,4},{6,7},{7,6},{8,9},{9,8},{10,11... | collective-permute-start | bytes 73736 | tf_op jit(solution)/shard_map/ppermute | solution.py:372
  42.1 0.0 collective-permute-done.3.refs_0_.refs_4_
  42.1 0.0 collective-permute-done.5.refs_1_.refs_5_
  42.1 0.0 collective-permute-done.7.refs_2_.refs_6_
  42.1 0.8 %collective-permute-done.9.refs_3_.refs_7_ = bf16[96,128]{1,0:T(8,128)(2,1)S(1)} collective-permute-done((bf16[96,128]{1,0:T(8,128)(2,1)S(1)}, bf16[96,128]{1,0:T(8,128)(2,1)S(1)}, u32[]{:S(2)}, u32[]{:S(2)}) %collective-permute-start.9) | collective-permute-done | bytes 24608 | tf_op jit(solution)/shard_map/ppermute | solution.py:372
  42.9 0.0 collective-permute-done.2.arrived
  43.0 2.0 %collective-permute-start.12 = (bf16[128,384]{1,0:T(8,128)(2,1)S(1)}, bf16[128,384]{1,0:T(8,128)(2,1)S(1)}, u32[]{:S(2)}, u32[]{:S(2)}) collective-permute-start(bf16[128,384]{1,0:T(8,128)(2,1)S(1)} %shard_map.90.refs_8_.refs_0_.dpre), channel_id=1, source_target_pairs={{0,10},{1,11},{2,8},{3,9},{4,14},{5,15},{6,12},{7,13},{8,2},{9,3},... | collective-permute-start | bytes 294920 | tf_op jit(solution)/shard_map/ppermute | solution.py:372
  45.0 0.3 collective-permute-start.11
  45.3 0.4 collective-permute-start.10
  45.7 1.2 %collective-permute-start.13 = (bf16[128,384]{1,0:T(8,128)(2,1)S(1)}, bf16[128,384]{1,0:T(8,128)(2,1)S(1)}, u32[]{:S(2)}, u32[]{:S(2)}) collective-permute-start(bf16[128,384]{1,0:T(8,128)(2,1)S(1)} %shard_map.90.refs_8_.refs_0_.dpre), channel_id=1, source_target_pairs={{0,1},{1,0},{2,3},{3,2},{4,5},{5,4},{6,7},{7,6},{8,9},{9,8},{10,11... | collective-permute-start | bytes 294920 | tf_op jit(solution)/shard_map/ppermute | solution.py:372
  46.9 1.1 %collective-permute-done.12.refs_3_ = bf16[128,384]{1,0:T(8,128)(2,1)S(1)} collective-permute-done((bf16[128,384]{1,0:T(8,128)(2,1)S(1)}, bf16[128,384]{1,0:T(8,128)(2,1)S(1)}, u32[]{:S(2)}, u32[]{:S(2)}) %collective-permute-start.12) | collective-permute-done | bytes 98336 | tf_op jit(solution)/shard_map/ppermute | solution.py:372
  48.0 1.3 %collective-permute-start.16 = (bf16[128,384]{1,0:T(8,128)(2,1)S(1)}, bf16[128,384]{1,0:T(8,128)(2,1)S(1)}, u32[]{:S(2)}, u32[]{:S(2)}) collective-permute-start(bf16[128,384]{1,0:T(8,128)(2,1)S(1)} %collective-permute-done.12.refs_3_), channel_id=1, source_target_pairs={{0,1},{1,0},{2,3},{3,2},{4,5},{5,4},{6,7},{7,6},{8,9},{9,8},{10,11... | collective-permute-start | bytes 294920 | tf_op jit(solution)/shard_map/ppermute | solution.py:372
  49.3 1.5 %collective-permute-done.11.refs_2_ = bf16[128,384]{1,0:T(8,128)(2,1)S(1)} collective-permute-done((bf16[128,384]{1,0:T(8,128)(2,1)S(1)}, bf16[128,384]{1,0:T(8,128)(2,1)S(1)}, u32[]{:S(2)}, u32[]{:S(2)}) %collective-permute-start.11) | collective-permute-done | bytes 98336 | tf_op jit(solution)/shard_map/ppermute | solution.py:372
  50.8 0.5 collective-permute-start.15
  51.3 0.0 collective-permute-done.10.refs_1_
  51.3 0.0 collective-permute-start.14
  51.3 0.9 %shard_map.91.stack = bf16[448,1024]{1,0:T(8,128)(2,1)S(1)} custom-call(bf16[96,128]{1,0:T(8,128)(2,1)S(1)} %get-tuple-element.44.refs_0_, bf16[96,128]{1,0:T(8,128)(2,1)S(1)} %collective-permute-done.4.refs_1_, bf16[96,128]{1,0:T(8,128)(2,1)S(1)} %collective-permute-done.6.refs_2_, bf16[96,128]{1,0:T(8,128)(2,1)S(1)} %collective-permute-done.8.refs_3_, ...), custom_call_target="tpu_custom_call" | custom-call | tf_op jit(solution)/shard_map/pallas_call | solution.py:348
  52.2 0.0 collective-permute-done.13.refs_4_
  52.2 0.0 collective-permute-done.16.refs_7_
  52.2 0.0 collective-permute-done.15.refs_6_
  52.3 0.3 collective-permute-done.14.refs_5_
  52.6 0.6 shard_map.92
  53.2 1.0 %collective-permute-start.17 = (bf16[224,384]{1,0:T(8,128)(2,1)S(1)}, bf16[224,384]{1,0:T(8,128)(2,1)S(1)}, u32[]{:S(2)}, u32[]{:S(2)}) collective-permute-start(bf16[224,384]{1,0:T(8,128)(2,1)S(1)} %get-tuple-element.50), channel_id=1, source_target_pairs={{0,6},{1,25},{2,4},{3,27},{4,2},{5,29},{6,0},{7,31},{8,14},{9,17},... | collective-permute-start | bytes 516104 | tf_op jit(solution)/shard_map/ppermute | solution.py:372
  54.2 4.8 %collective-permute-done.17.pair = bf16[224,384]{1,0:T(8,128)(2,1)S(1)} collective-permute-done((bf16[224,384]{1,0:T(8,128)(2,1)S(1)}, bf16[224,384]{1,0:T(8,128)(2,1)S(1)}, u32[]{:S(2)}, u32[]{:S(2)}) %collective-permute-start.17) | collective-permute-done | bytes 172064 | tf_op jit(solution)/shard_map/ppermute | solution.py:372
  59.1 1.0 %collective-permute-start.18 = (bf16[224,384]{1,0:T(8,128)(2,1)S(1)}, bf16[224,384]{1,0:T(8,128)(2,1)S(1)}, u32[]{:S(2)}, u32[]{:S(2)}) collective-permute-start(bf16[224,384]{1,0:T(8,128)(2,1)S(1)} %collective-permute-done.17.pair), channel_id=1, source_target_pairs={{0,1},{1,0},{2,3},{3,2},{4,5},{5,4},{6,7},{7,6},{8,9},{9,8},{10,11... | collective-permute-start | bytes 516104 | tf_op jit(solution)/shard_map/ppermute | solution.py:372
  60.1 1.4 %collective-permute-start.19 = (bf16[112,384]{1,0:T(8,128)(2,1)S(1)}, bf16[112,384]{1,0:T(8,128)(2,1)S(1)}, u32[]{:S(2)}, u32[]{:S(2)}) collective-permute-start(bf16[112,384]{1,0:T(8,128)(2,1)S(1)} %get-tuple-element.51), channel_id=1, source_target_pairs={{0,30},{1,31},{2,28},{3,29},{4,26},{5,27},{6,24},{7,25},{8,22},{9,... | collective-permute-start | bytes 258056 | tf_op jit(solution)/shard_map/ppermute | solution.py:372
  61.5 1.6 %shard_map.93 = (bf16[128,384]{1,0:T(8,128)(2,1)}, f32[12,128]{1,0:T(8,128)}) custom-call(bf16[128,384]{1,0:T(8,128)(2,1)S(1)} %collective-permute-done.2.arrived, bf16[128,384]{1,0:T(8,128)(2,1)S(1)} %collective-permute-done.1.arrived.earlier, bf16[128,384]{1,0:T(8,128)(2,1)S(1)} %shard_map.90.refs_8_.refs_0_.dpre, ...), custom_call_target="tpu_custom_call" | custom-call | tf_op jit(solution)/shard_map/pallas_call | solution.py:348
  63.1 4.5 %collective-permute-done.19.diagonal = bf16[112,384]{1,0:T(8,128)(2,1)S(1)} collective-permute-done((bf16[112,384]{1,0:T(8,128)(2,1)S(1)}, bf16[112,384]{1,0:T(8,128)(2,1)S(1)}, u32[]{:S(2)}, u32[]{:S(2)}) %collective-permute-start.19) | collective-permute-done | bytes 86048 | tf_op jit(solution)/shard_map/ppermute | solution.py:372
  67.5 0.0 collective-permute-done.18.crossed
  67.5 0.7 %shard_map.94 = f32[108,1,384]{2,1,0:T(1,128)} custom-call(f32[112,384]{1,0:T(8,128)S(1)} %get-tuple-element.48.own, bf16[224,384]{1,0:T(8,128)(2,1)S(1)} %collective-permute-done.17.pair, bf16[224,384]{1,0:T(8,128)(2,1)S(1)} %collective-permute-done.18.crossed, bf16[112,384]{1,0:T(8,128)(2,1)S(1)} %collective-permute-done.19.diagonal), custom_call_target="tpu_custom_call" | custom-call | tf_op jit(solution)/shard_map/pallas_call | solution.py:348
  (4 shorter events, 0.0 us)
Async XLA Ops:
  19.7 4.3 %collective-permute-start = (bf16[128,384]{1,0:T(8,128)(2,1)S(1)}, bf16[128,384]{1,0:T(8,128)(2,1)S(1)}, u32[]{:S(2)}, u32[]{:S(2)}) collective-permute-start(bf16[128,384]{1,0:T(8,128)(2,1)S(1)} %get-tuple-element.32.order.msg3), channel_id=1, source_target_pairs={{96,64},{32,0},{64,96},{0,32},{97,65},{33,1},{65,97},{1,33},{98,66... | collective-permute-start | bytes 294920 | tf_op jit(solution)/shard_map/ppermute | solution.py:376
  24.0 8.2 %collective-permute-start.1 = (bf16[128,384]{1,0:T(8,128)(2,1)S(1)}, bf16[128,384]{1,0:T(8,128)(2,1)S(1)}, u32[]{:S(2)}, u32[]{:S(2)}) collective-permute-start(bf16[128,384]{1,0:T(8,128)(2,1)S(1)} %get-tuple-element.37.msg2), channel_id=1, source_target_pairs={{64,32},{96,0},{32,64},{0,96},{65,33},{97,1},{33,65},{1,97},{66,34... | collective-permute-start | bytes 294920 | tf_op jit(solution)/shard_map/ppermute | solution.py:376
  32.2 10.8 %collective-permute-start.2 = (bf16[128,384]{1,0:T(8,128)(2,1)S(1)}, bf16[128,384]{1,0:T(8,128)(2,1)S(1)}, u32[]{:S(2)}, u32[]{:S(2)}) collective-permute-start(bf16[128,384]{1,0:T(8,128)(2,1)S(1)} %get-tuple-element.39.msg1), channel_id=1, source_target_pairs={{32,0},{96,64},{0,32},{64,96},{33,1},{97,65},{1,33},{65,97},{34,2}... | collective-permute-start | bytes 294920 | tf_op jit(solution)/shard_map/ppermute | solution.py:376
  33.9 5.7 %collective-permute-start.4 = (bf16[96,128]{1,0:T(8,128)(2,1)S(1)}, bf16[96,128]{1,0:T(8,128)(2,1)S(1)}, u32[]{:S(2)}, u32[]{:S(2)}) collective-permute-start(bf16[96,128]{1,0:T(8,128)(2,1)S(1)} %get-tuple-element.45), channel_id=1, source_target_pairs={{0,2},{1,3},{2,0},{3,1},{4,6},{5,7},{6,4},{7,5},{8,10},{9,11},{10,... | collective-permute-start | bytes 73736 | tf_op jit(solution)/shard_map/ppermute | solution.py:372
  34.4 5.5 %collective-permute-start.6 = (bf16[96,128]{1,0:T(8,128)(2,1)S(1)}, bf16[96,128]{1,0:T(8,128)(2,1)S(1)}, u32[]{:S(2)}, u32[]{:S(2)}) collective-permute-start(bf16[96,128]{1,0:T(8,128)(2,1)S(1)} %get-tuple-element.46), channel_id=1, source_target_pairs={{0,8},{1,9},{2,10},{3,11},{4,12},{5,13},{6,14},{7,15},{8,0},{9,1},... | collective-permute-start | bytes 73736 | tf_op jit(solution)/shard_map/ppermute | solution.py:372
  34.7 5.8 %collective-permute-start.8 = (bf16[96,128]{1,0:T(8,128)(2,1)S(1)}, bf16[96,128]{1,0:T(8,128)(2,1)S(1)}, u32[]{:S(2)}, u32[]{:S(2)}) collective-permute-start(bf16[96,128]{1,0:T(8,128)(2,1)S(1)} %get-tuple-element.47), channel_id=1, source_target_pairs={{0,10},{1,11},{2,8},{3,9},{4,14},{5,15},{6,12},{7,13},{8,2},{9,3},... | collective-permute-start | bytes 73736 | tf_op jit(solution)/shard_map/ppermute | solution.py:372
  36.6 5.5 %collective-permute-start.3 = (bf16[96,128]{1,0:T(8,128)(2,1)S(1)}, bf16[96,128]{1,0:T(8,128)(2,1)S(1)}, u32[]{:S(2)}, u32[]{:S(2)}) collective-permute-start(bf16[96,128]{1,0:T(8,128)(2,1)S(1)} %get-tuple-element.44.refs_0_), channel_id=1, source_target_pairs={{0,1},{1,0},{2,3},{3,2},{4,5},{5,4},{6,7},{7,6},{8,9},{9,8},{10,11... | collective-permute-start | bytes 73736 | tf_op jit(solution)/shard_map/ppermute | solution.py:372
  39.6 2.5 %collective-permute-start.5 = (bf16[96,128]{1,0:T(8,128)(2,1)S(1)}, bf16[96,128]{1,0:T(8,128)(2,1)S(1)}, u32[]{:S(2)}, u32[]{:S(2)}) collective-permute-start(bf16[96,128]{1,0:T(8,128)(2,1)S(1)} %collective-permute-done.4.refs_1_), channel_id=1, source_target_pairs={{0,1},{1,0},{2,3},{3,2},{4,5},{5,4},{6,7},{7,6},{8,9},{9,8},{10,11... | collective-permute-start | bytes 73736 | tf_op jit(solution)/shard_map/ppermute | solution.py:372
  39.9 2.2 %collective-permute-start.7 = (bf16[96,128]{1,0:T(8,128)(2,1)S(1)}, bf16[96,128]{1,0:T(8,128)(2,1)S(1)}, u32[]{:S(2)}, u32[]{:S(2)}) collective-permute-start(bf16[96,128]{1,0:T(8,128)(2,1)S(1)} %collective-permute-done.6.refs_2_), channel_id=1, source_target_pairs={{0,1},{1,0},{2,3},{3,2},{4,5},{5,4},{6,7},{7,6},{8,9},{9,8},{10,11... | collective-permute-start | bytes 73736 | tf_op jit(solution)/shard_map/ppermute | solution.py:372
  40.6 2.4 %collective-permute-start.9 = (bf16[96,128]{1,0:T(8,128)(2,1)S(1)}, bf16[96,128]{1,0:T(8,128)(2,1)S(1)}, u32[]{:S(2)}, u32[]{:S(2)}) collective-permute-start(bf16[96,128]{1,0:T(8,128)(2,1)S(1)} %collective-permute-done.8.refs_3_), channel_id=1, source_target_pairs={{0,1},{1,0},{2,3},{3,2},{4,5},{5,4},{6,7},{7,6},{8,9},{9,8},{10,11... | collective-permute-start | bytes 73736 | tf_op jit(solution)/shard_map/ppermute | solution.py:372
  43.0 5.0 %collective-permute-start.12 = (bf16[128,384]{1,0:T(8,128)(2,1)S(1)}, bf16[128,384]{1,0:T(8,128)(2,1)S(1)}, u32[]{:S(2)}, u32[]{:S(2)}) collective-permute-start(bf16[128,384]{1,0:T(8,128)(2,1)S(1)} %shard_map.90.refs_8_.refs_0_.dpre), channel_id=1, source_target_pairs={{0,10},{1,11},{2,8},{3,9},{4,14},{5,15},{6,12},{7,13},{8,2},{9,3},... | collective-permute-start | bytes 294920 | tf_op jit(solution)/shard_map/ppermute | solution.py:372
  45.0 5.8 %collective-permute-start.11 = (bf16[128,384]{1,0:T(8,128)(2,1)S(1)}, bf16[128,384]{1,0:T(8,128)(2,1)S(1)}, u32[]{:S(2)}, u32[]{:S(2)}) collective-permute-start(bf16[128,384]{1,0:T(8,128)(2,1)S(1)} %shard_map.90.refs_8_.refs_0_.dpre), channel_id=1, source_target_pairs={{0,8},{1,9},{2,10},{3,11},{4,12},{5,13},{6,14},{7,15},{8,0},{9,1},... | collective-permute-start | bytes 294920 | tf_op jit(solution)/shard_map/ppermute | solution.py:372
  45.3 6.0 %collective-permute-start.10 = (bf16[128,384]{1,0:T(8,128)(2,1)S(1)}, bf16[128,384]{1,0:T(8,128)(2,1)S(1)}, u32[]{:S(2)}, u32[]{:S(2)}) collective-permute-start(bf16[128,384]{1,0:T(8,128)(2,1)S(1)} %shard_map.90.refs_8_.refs_0_.dpre), channel_id=1, source_target_pairs={{0,2},{1,3},{2,0},{3,1},{4,6},{5,7},{6,4},{7,5},{8,10},{9,11},{10,... | collective-permute-start | bytes 294920 | tf_op jit(solution)/shard_map/ppermute | solution.py:372
  45.7 6.5 %collective-permute-start.13 = (bf16[128,384]{1,0:T(8,128)(2,1)S(1)}, bf16[128,384]{1,0:T(8,128)(2,1)S(1)}, u32[]{:S(2)}, u32[]{:S(2)}) collective-permute-start(bf16[128,384]{1,0:T(8,128)(2,1)S(1)} %shard_map.90.refs_8_.refs_0_.dpre), channel_id=1, source_target_pairs={{0,1},{1,0},{2,3},{3,2},{4,5},{5,4},{6,7},{7,6},{8,9},{9,8},{10,11... | collective-permute-start | bytes 294920 | tf_op jit(solution)/shard_map/ppermute | solution.py:372
  48.0 4.3 %collective-permute-start.16 = (bf16[128,384]{1,0:T(8,128)(2,1)S(1)}, bf16[128,384]{1,0:T(8,128)(2,1)S(1)}, u32[]{:S(2)}, u32[]{:S(2)}) collective-permute-start(bf16[128,384]{1,0:T(8,128)(2,1)S(1)} %collective-permute-done.12.refs_3_), channel_id=1, source_target_pairs={{0,1},{1,0},{2,3},{3,2},{4,5},{5,4},{6,7},{7,6},{8,9},{9,8},{10,11... | collective-permute-start | bytes 294920 | tf_op jit(solution)/shard_map/ppermute | solution.py:372
  50.8 1.5 %collective-permute-start.15 = (bf16[128,384]{1,0:T(8,128)(2,1)S(1)}, bf16[128,384]{1,0:T(8,128)(2,1)S(1)}, u32[]{:S(2)}, u32[]{:S(2)}) collective-permute-start(bf16[128,384]{1,0:T(8,128)(2,1)S(1)} %collective-permute-done.11.refs_2_), channel_id=1, source_target_pairs={{0,1},{1,0},{2,3},{3,2},{4,5},{5,4},{6,7},{7,6},{8,9},{9,8},{10,11... | collective-permute-start | bytes 294920 | tf_op jit(solution)/shard_map/ppermute | solution.py:372
  51.3 1.3 %collective-permute-start.14 = (bf16[128,384]{1,0:T(8,128)(2,1)S(1)}, bf16[128,384]{1,0:T(8,128)(2,1)S(1)}, u32[]{:S(2)}, u32[]{:S(2)}) collective-permute-start(bf16[128,384]{1,0:T(8,128)(2,1)S(1)} %collective-permute-done.10.refs_1_), channel_id=1, source_target_pairs={{0,1},{1,0},{2,3},{3,2},{4,5},{5,4},{6,7},{7,6},{8,9},{9,8},{10,11... | collective-permute-start | bytes 294920 | tf_op jit(solution)/shard_map/ppermute | solution.py:372
  53.2 5.8 %collective-permute-start.17 = (bf16[224,384]{1,0:T(8,128)(2,1)S(1)}, bf16[224,384]{1,0:T(8,128)(2,1)S(1)}, u32[]{:S(2)}, u32[]{:S(2)}) collective-permute-start(bf16[224,384]{1,0:T(8,128)(2,1)S(1)} %get-tuple-element.50), channel_id=1, source_target_pairs={{0,6},{1,25},{2,4},{3,27},{4,2},{5,29},{6,0},{7,31},{8,14},{9,17},... | collective-permute-start | bytes 516104 | tf_op jit(solution)/shard_map/ppermute | solution.py:372
  59.1 8.5 %collective-permute-start.18 = (bf16[224,384]{1,0:T(8,128)(2,1)S(1)}, bf16[224,384]{1,0:T(8,128)(2,1)S(1)}, u32[]{:S(2)}, u32[]{:S(2)}) collective-permute-start(bf16[224,384]{1,0:T(8,128)(2,1)S(1)} %collective-permute-done.17.pair), channel_id=1, source_target_pairs={{0,1},{1,0},{2,3},{3,2},{4,5},{5,4},{6,7},{7,6},{8,9},{9,8},{10,11... | collective-permute-start | bytes 516104 | tf_op jit(solution)/shard_map/ppermute | solution.py:372
  60.1 7.4 %collective-permute-start.19 = (bf16[112,384]{1,0:T(8,128)(2,1)S(1)}, bf16[112,384]{1,0:T(8,128)(2,1)S(1)}, u32[]{:S(2)}, u32[]{:S(2)}) collective-permute-start(bf16[112,384]{1,0:T(8,128)(2,1)S(1)} %get-tuple-element.51), channel_id=1, source_target_pairs={{0,30},{1,31},{2,28},{3,29},{4,26},{5,27},{6,24},{7,25},{8,22},{9,... | collective-permute-start | bytes 258056 | tf_op jit(solution)/shard_map/ppermute | solution.py:372

commit v8 on v7

--- a/solution.py
+++ b/solution.py
@@ -231,7 +231,9 @@
         message[...] = below.astype(bf16)
 
 
-def relay2_kernel(arrived, slope, w, mixing, unit, inv, mine, message, dpre_out, head_out):
+def relay2_kernel(
+    arrived, slope, w, mixing, unit, inv, mine, message, dpre_out, head_out, head_sent
+):
     relay(2, arrived, slope, w, message, dpre_out)
 
     @pl.when(lax.axis_index("section") == 3)
@@ -239,19 +241,15 @@
         units = unit[...]
         dproj = projected_grad(mixing[...], units.astype(bf16), units, inv[:, :1])
         head_grad = mm(mine[...], dproj)
-        head_out[...] = head_grad
+        head_out[...] = head_grad[:, 384:]
+        head_sent[...] = head_grad[:, :128].astype(bf16)
         message[:16, :] = head_grad[:, :384].astype(bf16)
 
 
-def relay1_kernel(arrived, slope, w, head_grad, message, dpre_out):
+def relay1_kernel(arrived, slope, w, message, dpre_out):
     relay(1, arrived, slope, w, message, dpre_out)
-    section = lax.axis_index("section")
-
-    @pl.when(section == 3)
-    def _():
-        message[:16, :] = head_grad[:, :384].astype(bf16)
-
-    @pl.when(section == 0)
+
+    @pl.when(lax.axis_index("section") == 2)
     def _():
         message[:16, :] = arrived[:16, :]
 
@@ -270,26 +268,28 @@
         dpre_out[...] = (arrived[...].astype(f32) * slope[...]).astype(bf16)
 
 
-def last_kernel(arrived, earlier, dpre, w, head_grad, msg3, msg2, msg1, own, grads, head_out):
+def last_kernel(
+    arrived, earlier, head_up, dpre, w, head_grad, msg3, msg2, msg1, own, grads, head_out
+):
     section = lax.axis_index("section")
 
     @pl.when(section == 3)
     def _():
         grads[...] = msg3[...]
-        head_out[...] = head_grad[:12, 384:]
-
-    for at, sent in ((2, msg2), (1, msg1)):
+        head_out[...] = head_grad[:12, :]
+
+    for at, sent, head in ((2, msg2, earlier), (1, msg1, arrived)):
 
         @pl.when(section == at)
         def _():
             grads[...] = sent[...]
-            head_out[...] = arrived[:16, at * 128 : at * 128 + 128].astype(f32)[:12]
+            head_out[...] = head[:16, at * 128 : at * 128 + 128].astype(f32)[:12]
 
     @pl.when(section == 0)
     def _():
         below = arrived[...].astype(f32) + conv_back(dpre[...].astype(f32), w)
         grads[...] = below.astype(bf16)
-        head_out[...] = earlier[:16, :128].astype(f32)[:12]
+        head_out[...] = head_up[...].astype(f32)[:12]
 
 
 def stack_kernel(*refs):
@@ -363,6 +363,7 @@
 
 def per_device(saved, kernels, head, counts, pairs, valid):
     ranks = lax.axis_size("dp")
+    sections = lax.axis_size("section")
     act = VMEM((ROWS, CH), bf16)
     piece = VMEM((96, 128), bf16)
     gather = (0, 2, 8, 10)
@@ -371,9 +372,9 @@
         pairs_of = [(d, d ^ (odd_bits if odd_bits and d & 1 else bits)) for d in range(ranks)]
         return lax.ppermute(value, "dp", pairs_of)
 
-    def relayed(value, pairs_of):
-        both = [(a, b) for a, b in pairs_of] + [(b, a) for a, b in pairs_of]
-        return lax.ppermute(value, "section", both)
+    def relayed(value, step=-1):
+        around = [(at, (at + step) % sections) for at in range(sections)]
+        return lax.ppermute(value, "section", around)
 
     slope, announce, rows, w, head = call(
         forward_kernel,
@@ -401,15 +402,16 @@
         (act, act, VMEM((128, 128), bf16), VMEM((128, EMB), f32), VMEM((128, 128), f32))
         + (VMEM((16, 128), bf16),),
     )(gathered.reshape(256, 256), head, slope, w)
-    arrived = relayed(msg3, [(3, 2), (1, 0)])
+    arrived = relayed(msg3)
     split = call(split_kernel, [VMEM] * 2, (piece,) * 4)(rows, msg3)
     near = [split[0]] + [swap(split[k], gather[k]) for k in range(1, 4)]
-    msg2, dpre2, head_grad = call(
-        relay2_kernel, [VMEM] * 7, (act, act, VMEM((16, EMB), f32))
+    msg2, dpre2, head_grad, head_sent = call(
+        relay2_kernel, [VMEM] * 7, (act, act, VMEM((16, 128), f32), VMEM((16, 128), bf16))
     )(arrived, slope, w, *for_head)
-    arrived = earlier = relayed(msg2, [(2, 1), (3, 0)])
-    msg1, dpre1 = call(relay1_kernel, [VMEM] * 4, (act, act))(arrived, slope, w, head_grad)
-    arrived = relayed(msg1, [(1, 0), (3, 2)])
+    arrived = earlier = relayed(msg2)
+    head_up = relayed(head_sent, 1)
+    msg1, dpre1 = call(relay1_kernel, [VMEM] * 3, (act, act))(arrived, slope, w)
+    arrived = relayed(msg1)
     far = [swap(value, 1) for value in near]
     dpre = call(bottom_kernel, [VMEM] * 9, act)(
         arrived, slope, dpre3, dpre2, dpre1, *far
@@ -428,8 +430,8 @@
     diagonal = swap(diagonal, 30)
     crossed = swap(pair, 1)
     grads, head_grad = call(
-        last_kernel, [VMEM] * 9, (sds((ROWS, CH), bf16), sds((12, 128), f32))
-    )(arrived, earlier, dpre, w, head_grad, msg3, msg2, msg1, own)
+        last_kernel, [VMEM] * 10, (sds((ROWS, CH), bf16), sds((12, 128), f32))
+    )(arrived, earlier, head_up, dpre, w, head_grad, msg3, msg2, msg1, own)
     wgrad = call(sum_kernel, [VMEM] * 4, sds((108, 1, CH), f32))(own, pair, crossed, diagonal)
     return (
         grads.reshape(saved.shape),

time: 68.4 us -> 71.5 us (1.045)
  starting transfers between devices: 26.5 us -> 31 us
  waiting for transfers between devices: 17.7 us -> 16.4 us
    ppermute x3 -> x4, starting transfers between devices: 9.15 us -> 13.1 us  [relayed(): return lax.ppermute(value, 'section', around)]
    ppermute x17, waiting for transfers between devices: 13.1 us -> 9.4 us  [swap(): return lax.ppermute(value, 'dp', pairs_of)]
    ppermute x3 -> x4, waiting for transfers between devices: 4.66 us -> 6.95 us  [relayed(): return lax.ppermute(value, 'section', around)]
  transfers between devices with their start and end apart: 20 -> 21, of which waited for: 8 -> 9; matrix products, arithmetic and copies ran while one was open for 0% -> 0% of each run, Pallas kernels for 4% -> 4%
where the time goes in v8:
time: 71.5 us; the launch traced here: 71.4 us
  starting transfers between devices  31 us (43%)
  waiting for transfers between devices  16.4 us (23%)
  blocking collectives  16 us (22%)
  Pallas kernels  6.71 us (9%)
  between operations  1.36 us (2%)
    ppermute x17, starting transfers between devices, swap(): return lax.ppermute(value, 'dp', pairs_of)  17.9 us
    all_to_all x1, blocking collectives, per_device(): lax.all_to_all(announce.reshape(32, 8, 256), 'dp', 0, 0, tiled=True)  16 us
    ppermute x4, starting transfers between devices, relayed(): return lax.ppermute(value, 'section', around)  13.1 us
    ppermute x17, waiting for transfers between devices, swap(): return lax.ppermute(value, 'dp', pairs_of)  9.4 us
    ppermute x4, waiting for transfers between devices, relayed(): return lax.ppermute(value, 'section', around)  6.95 us
    pallas_call x10, Pallas kernels, with_operands(): run(*[value if space is SMEM else pltpu.with_memory_space_constraint(valu...  6.71 us
  transfers between devices with their start and end apart: 21, of which 9 were waited for; matrix products, arithmetic and copies ran while one was open for 0% of the time, Pallas kernels for 4%

profile of v8, /device:TPU:1, one launch (start us, length us, event | category | flops | bytes accessed | tf_op | source)
XLA Modules:
  0.0 71.4 jit_solution(17053056842089216789)
XLA Ops:
  1.3 2.5 %shard_map.85 = (f32[128,384]{1,0:T(8,128)S(1)}, bf16[256,256]{1,0:T(8,128)(2,1)S(1)}, bf16[128,384]{1,0:T(8,128)(2,1)S(1)}, bf16[3,3,384,384]{3,2,1,0:T(8,128)(2,1)S(1)}, bf16[384,512]{1,0:T(8,128)(2,1)S(1)}) custom-call(bf16[128,384]{1,0:T(8,128)(2,1)} %bitcast.12, bf16[3,3,384,384]{3,2,1,0:T(8,128)(2,1)} %bitcast.10, bf16[384,512]{1,0:T(8,128)(2,1)} %head_hbm.1, ...), custom_call_target="tpu_custom_call" | custom-call | tf_op jit(solution)/shard_map/pallas_call | solution.py:348
  3.7 16.0 %all_to_all.5 = bf16[32,8,256]{2,1,0:T(8,128)(2,1)S(1)} all-to-all(bf16[32,8,256]{2,1,0:T(8,128)(2,1)S(1)} %bitcast.9), channel_id=1, replica_groups=mesh['section'=4,'dp'=32] {'dp'}, dimensions={0} | all-to-all | bytes 262144 | tf_op jit(solution)/shard_map/all_to_all | solution.py:398
  19.7 6.1 %collective-permute-start = (bf16[128,384]{1,0:T(8,128)(2,1)S(1)}, bf16[128,384]{1,0:T(8,128)(2,1)S(1)}, u32[]{:S(2)}, u32[]{:S(2)}) collective-permute-start(bf16[128,384]{1,0:T(8,128)(2,1)S(1)} %get-tuple-element.33.order.msg3), channel_id=1, source_target_pairs={{0,96},{32,0},{64,32},{96,64},{1,97},{33,1},{65,33},{97,65},{2,98}... | collective-permute-start | bytes 294920 | tf_op jit(solution)/shard_map/ppermute | solution.py:377
  25.8 1.6 %collective-permute-done.arrived = bf16[128,384]{1,0:T(8,128)(2,1)S(1)} collective-permute-done((bf16[128,384]{1,0:T(8,128)(2,1)S(1)}, bf16[128,384]{1,0:T(8,128)(2,1)S(1)}, u32[]{:S(2)}, u32[]{:S(2)}) %collective-permute-start) | collective-permute-done | bytes 98336 | tf_op jit(solution)/shard_map/ppermute | solution.py:377
  27.5 3.9 %collective-permute-start.1 = (bf16[128,384]{1,0:T(8,128)(2,1)S(1)}, bf16[128,384]{1,0:T(8,128)(2,1)S(1)}, u32[]{:S(2)}, u32[]{:S(2)}) collective-permute-start(bf16[128,384]{1,0:T(8,128)(2,1)S(1)} %get-tuple-element.38.msg2), channel_id=1, source_target_pairs={{0,96},{32,0},{64,32},{96,64},{1,97},{33,1},{65,33},{97,65},{2,98}... | collective-permute-start | bytes 294920 | tf_op jit(solution)/shard_map/ppermute | solution.py:377
  31.4 1.6 %collective-permute-done.1.arrived.earlier = bf16[128,384]{1,0:T(8,128)(2,1)S(1)} collective-permute-done((bf16[128,384]{1,0:T(8,128)(2,1)S(1)}, bf16[128,384]{1,0:T(8,128)(2,1)S(1)}, u32[]{:S(2)}, u32[]{:S(2)}) %collective-permute-start.1) | collective-permute-done | bytes 98336 | tf_op jit(solution)/shard_map/ppermute | solution.py:377
  33.0 3.0 %collective-permute-start.2 = (bf16[128,384]{1,0:T(8,128)(2,1)S(1)}, bf16[128,384]{1,0:T(8,128)(2,1)S(1)}, u32[]{:S(2)}, u32[]{:S(2)}) collective-permute-start(bf16[128,384]{1,0:T(8,128)(2,1)S(1)} %get-tuple-element.39.msg1), channel_id=1, source_target_pairs={{0,96},{32,0},{64,32},{96,64},{1,97},{33,1},{65,33},{97,65},{2,98}... | collective-permute-start | bytes 294920 | tf_op jit(solution)/shard_map/ppermute | solution.py:377
  36.1 0.3 shard_map.89
  36.4 0.5 collective-permute-start.5
  36.9 0.4 collective-permute-start.7
  37.3 1.9 %collective-permute-start.9 = (bf16[96,128]{1,0:T(8,128)(2,1)S(1)}, bf16[96,128]{1,0:T(8,128)(2,1)S(1)}, u32[]{:S(2)}, u32[]{:S(2)}) collective-permute-start(bf16[96,128]{1,0:T(8,128)(2,1)S(1)} %get-tuple-element.48), channel_id=1, source_target_pairs={{0,10},{1,11},{2,8},{3,9},{4,14},{5,15},{6,12},{7,13},{8,2},{9,3},... | collective-permute-start | bytes 73736 | tf_op jit(solution)/shard_map/ppermute | solution.py:373
  39.1 3.5 %collective-permute-start.4 = (bf16[96,128]{1,0:T(8,128)(2,1)S(1)}, bf16[96,128]{1,0:T(8,128)(2,1)S(1)}, u32[]{:S(2)}, u32[]{:S(2)}) collective-permute-start(bf16[96,128]{1,0:T(8,128)(2,1)S(1)} %get-tuple-element.45.refs_0_), channel_id=1, source_target_pairs={{0,1},{1,0},{2,3},{3,2},{4,5},{5,4},{6,7},{7,6},{8,9},{9,8},{10,11... | collective-permute-start | bytes 73736 | tf_op jit(solution)/shard_map/ppermute | solution.py:373
  42.7 0.0 collective-permute-done.5.refs_1_
  42.7 0.3 collective-permute-start.6
  43.0 0.0 collective-permute-done.7.refs_2_
  43.0 0.7 collective-permute-start.8
  43.7 0.0 collective-permute-done.9.refs_3_
  43.7 1.5 %collective-permute-start.10 = (bf16[96,128]{1,0:T(8,128)(2,1)S(1)}, bf16[96,128]{1,0:T(8,128)(2,1)S(1)}, u32[]{:S(2)}, u32[]{:S(2)}) collective-permute-start(bf16[96,128]{1,0:T(8,128)(2,1)S(1)} %collective-permute-done.9.refs_3_), channel_id=1, source_target_pairs={{0,1},{1,0},{2,3},{3,2},{4,5},{5,4},{6,7},{7,6},{8,9},{9,8},{10,11... | collective-permute-start | bytes 73736 | tf_op jit(solution)/shard_map/ppermute | solution.py:373
  45.2 0.0 collective-permute-done.4.refs_0_.refs_4_
  45.2 0.0 collective-permute-done.6.refs_1_.refs_5_
  45.2 0.0 collective-permute-done.8.refs_2_.refs_6_
  45.2 0.8 %collective-permute-done.10.refs_3_.refs_7_ = bf16[96,128]{1,0:T(8,128)(2,1)S(1)} collective-permute-done((bf16[96,128]{1,0:T(8,128)(2,1)S(1)}, bf16[96,128]{1,0:T(8,128)(2,1)S(1)}, u32[]{:S(2)}, u32[]{:S(2)}) %collective-permute-start.10) | collective-permute-done | bytes 24608 | tf_op jit(solution)/shard_map/ppermute | solution.py:373
  46.1 0.0 collective-permute-done.2.arrived
  46.1 2.0 %collective-permute-start.13 = (bf16[128,384]{1,0:T(8,128)(2,1)S(1)}, bf16[128,384]{1,0:T(8,128)(2,1)S(1)}, u32[]{:S(2)}, u32[]{:S(2)}) collective-permute-start(bf16[128,384]{1,0:T(8,128)(2,1)S(1)} %shard_map.90.refs_8_.refs_0_.dpre), channel_id=1, source_target_pairs={{0,10},{1,11},{2,8},{3,9},{4,14},{5,15},{6,12},{7,13},{8,2},{9,3},... | collective-permute-start | bytes 294920 | tf_op jit(solution)/shard_map/ppermute | solution.py:373
  48.1 0.3 collective-permute-start.12
  48.4 0.4 collective-permute-start.11
  48.8 1.2 %collective-permute-start.14 = (bf16[128,384]{1,0:T(8,128)(2,1)S(1)}, bf16[128,384]{1,0:T(8,128)(2,1)S(1)}, u32[]{:S(2)}, u32[]{:S(2)}) collective-permute-start(bf16[128,384]{1,0:T(8,128)(2,1)S(1)} %shard_map.90.refs_8_.refs_0_.dpre), channel_id=1, source_target_pairs={{0,1},{1,0},{2,3},{3,2},{4,5},{5,4},{6,7},{7,6},{8,9},{9,8},{10,11... | collective-permute-start | bytes 294920 | tf_op jit(solution)/shard_map/ppermute | solution.py:373
  50.0 1.1 %collective-permute-done.13.refs_3_ = bf16[128,384]{1,0:T(8,128)(2,1)S(1)} collective-permute-done((bf16[128,384]{1,0:T(8,128)(2,1)S(1)}, bf16[128,384]{1,0:T(8,128)(2,1)S(1)}, u32[]{:S(2)}, u32[]{:S(2)}) %collective-permute-start.13) | collective-permute-done | bytes 98336 | tf_op jit(solution)/shard_map/ppermute | solution.py:373
  51.1 1.3 %collective-permute-start.17 = (bf16[128,384]{1,0:T(8,128)(2,1)S(1)}, bf16[128,384]{1,0:T(8,128)(2,1)S(1)}, u32[]{:S(2)}, u32[]{:S(2)}) collective-permute-start(bf16[128,384]{1,0:T(8,128)(2,1)S(1)} %collective-permute-done.13.refs_3_), channel_id=1, source_target_pairs={{0,1},{1,0},{2,3},{3,2},{4,5},{5,4},{6,7},{7,6},{8,9},{9,8},{10,11... | collective-permute-start | bytes 294920 | tf_op jit(solution)/shard_map/ppermute | solution.py:373
  52.4 1.5 %collective-permute-done.12.refs_2_ = bf16[128,384]{1,0:T(8,128)(2,1)S(1)} collective-permute-done((bf16[128,384]{1,0:T(8,128)(2,1)S(1)}, bf16[128,384]{1,0:T(8,128)(2,1)S(1)}, u32[]{:S(2)}, u32[]{:S(2)}) %collective-permute-start.12) | collective-permute-done | bytes 98336 | tf_op jit(solution)/shard_map/ppermute | solution.py:373
  53.9 0.5 collective-permute-start.16
  54.4 0.0 collective-permute-done.11.refs_1_
  54.4 0.0 collective-permute-start.15
  54.4 0.9 %shard_map.91.stack = bf16[448,1024]{1,0:T(8,128)(2,1)S(1)} custom-call(bf16[96,128]{1,0:T(8,128)(2,1)S(1)} %get-tuple-element.45.refs_0_, bf16[96,128]{1,0:T(8,128)(2,1)S(1)} %collective-permute-done.5.refs_1_, bf16[96,128]{1,0:T(8,128)(2,1)S(1)} %collective-permute-done.7.refs_2_, bf16[96,128]{1,0:T(8,128)(2,1)S(1)} %collective-permute-done.9.refs_3_, ...), custom_call_target="tpu_custom_call" | custom-call | tf_op jit(solution)/shard_map/pallas_call | solution.py:348
  55.3 0.0 collective-permute-done.14.refs_4_
  55.3 0.0 collective-permute-done.17.refs_7_
  55.4 0.0 collective-permute-done.16.refs_6_
  55.4 0.3 collective-permute-done.15.refs_5_
  55.7 0.6 shard_map.92
  56.3 1.0 %collective-permute-start.18 = (bf16[224,384]{1,0:T(8,128)(2,1)S(1)}, bf16[224,384]{1,0:T(8,128)(2,1)S(1)}, u32[]{:S(2)}, u32[]{:S(2)}) collective-permute-start(bf16[224,384]{1,0:T(8,128)(2,1)S(1)} %get-tuple-element.52), channel_id=1, source_target_pairs={{0,6},{1,25},{2,4},{3,27},{4,2},{5,29},{6,0},{7,31},{8,14},{9,17},... | collective-permute-start | bytes 516104 | tf_op jit(solution)/shard_map/ppermute | solution.py:373
  57.4 4.8 %collective-permute-done.18.pair = bf16[224,384]{1,0:T(8,128)(2,1)S(1)} collective-permute-done((bf16[224,384]{1,0:T(8,128)(2,1)S(1)}, bf16[224,384]{1,0:T(8,128)(2,1)S(1)}, u32[]{:S(2)}, u32[]{:S(2)}) %collective-permute-start.18) | collective-permute-done | bytes 172064 | tf_op jit(solution)/shard_map/ppermute | solution.py:373
  62.2 1.0 %collective-permute-start.19 = (bf16[224,384]{1,0:T(8,128)(2,1)S(1)}, bf16[224,384]{1,0:T(8,128)(2,1)S(1)}, u32[]{:S(2)}, u32[]{:S(2)}) collective-permute-start(bf16[224,384]{1,0:T(8,128)(2,1)S(1)} %collective-permute-done.18.pair), channel_id=1, source_target_pairs={{0,1},{1,0},{2,3},{3,2},{4,5},{5,4},{6,7},{7,6},{8,9},{9,8},{10,11... | collective-permute-start | bytes 516104 | tf_op jit(solution)/shard_map/ppermute | solution.py:373
  63.2 1.4 %collective-permute-start.20 = (bf16[112,384]{1,0:T(8,128)(2,1)S(1)}, bf16[112,384]{1,0:T(8,128)(2,1)S(1)}, u32[]{:S(2)}, u32[]{:S(2)}) collective-permute-start(bf16[112,384]{1,0:T(8,128)(2,1)S(1)} %get-tuple-element.53), channel_id=1, source_target_pairs={{0,30},{1,31},{2,28},{3,29},{4,26},{5,27},{6,24},{7,25},{8,22},{9,... | collective-permute-start | bytes 258056 | tf_op jit(solution)/shard_map/ppermute | solution.py:373
  64.6 0.0 collective-permute-start.3
  64.6 3.7 %collective-permute-done.3.head_up = bf16[16,128]{1,0:T(8,128)(2,1)S(1)} collective-permute-done((bf16[16,128]{1,0:T(8,128)(2,1)S(1)}, bf16[16,128]{1,0:T(8,128)(2,1)S(1)}, u32[]{:S(2)}, u32[]{:S(2)}) %collective-permute-start.3) | collective-permute-done | bytes 4128 | tf_op jit(solution)/shard_map/ppermute | solution.py:377
  68.3 1.6 %shard_map.93 = (bf16[128,384]{1,0:T(8,128)(2,1)}, f32[12,128]{1,0:T(8,128)}) custom-call(bf16[128,384]{1,0:T(8,128)(2,1)S(1)} %collective-permute-done.2.arrived, bf16[128,384]{1,0:T(8,128)(2,1)S(1)} %collective-permute-done.1.arrived.earlier, bf16[16,128]{1,0:T(8,128)(2,1)S(1)} %collective-permute-done.3.head_up, ...), custom_call_target="tpu_custom_call" | custom-call | tf_op jit(solution)/shard_map/pallas_call | solution.py:348
  69.8 0.8 %collective-permute-done.20.diagonal = bf16[112,384]{1,0:T(8,128)(2,1)S(1)} collective-permute-done((bf16[112,384]{1,0:T(8,128)(2,1)S(1)}, bf16[112,384]{1,0:T(8,128)(2,1)S(1)}, u32[]{:S(2)}, u32[]{:S(2)}) %collective-permute-start.20) | collective-permute-done | bytes 86048 | tf_op jit(solution)/shard_map/ppermute | solution.py:373
  70.6 0.0 collective-permute-done.19.crossed
  70.6 0.7 %shard_map.94 = f32[108,1,384]{2,1,0:T(1,128)} custom-call(f32[112,384]{1,0:T(8,128)S(1)} %get-tuple-element.50.own, bf16[224,384]{1,0:T(8,128)(2,1)S(1)} %collective-permute-done.18.pair, bf16[224,384]{1,0:T(8,128)(2,1)S(1)} %collective-permute-done.19.crossed, bf16[112,384]{1,0:T(8,128)(2,1)S(1)} %collective-permute-done.20.diagonal), custom_call_target="tpu_custom_call" | custom-call | tf_op jit(solution)/shard_map/pallas_call | solution.py:348
  (4 shorter events, 0.0 us)
Async XLA Ops:
  19.7 7.8 %collective-permute-start = (bf16[128,384]{1,0:T(8,128)(2,1)S(1)}, bf16[128,384]{1,0:T(8,128)(2,1)S(1)}, u32[]{:S(2)}, u32[]{:S(2)}) collective-permute-start(bf16[128,384]{1,0:T(8,128)(2,1)S(1)} %get-tuple-element.33.order.msg3), channel_id=1, source_target_pairs={{0,96},{32,0},{64,32},{96,64},{1,97},{33,1},{65,33},{97,65},{2,98}... | collective-permute-start | bytes 294920 | tf_op jit(solution)/shard_map/ppermute | solution.py:377
  27.5 5.6 %collective-permute-start.1 = (bf16[128,384]{1,0:T(8,128)(2,1)S(1)}, bf16[128,384]{1,0:T(8,128)(2,1)S(1)}, u32[]{:S(2)}, u32[]{:S(2)}) collective-permute-start(bf16[128,384]{1,0:T(8,128)(2,1)S(1)} %get-tuple-element.38.msg2), channel_id=1, source_target_pairs={{0,96},{32,0},{64,32},{96,64},{1,97},{33,1},{65,33},{97,65},{2,98}... | collective-permute-start | bytes 294920 | tf_op jit(solution)/shard_map/ppermute | solution.py:377
  33.0 13.0 %collective-permute-start.2 = (bf16[128,384]{1,0:T(8,128)(2,1)S(1)}, bf16[128,384]{1,0:T(8,128)(2,1)S(1)}, u32[]{:S(2)}, u32[]{:S(2)}) collective-permute-start(bf16[128,384]{1,0:T(8,128)(2,1)S(1)} %get-tuple-element.39.msg1), channel_id=1, source_target_pairs={{0,96},{32,0},{64,32},{96,64},{1,97},{33,1},{65,33},{97,65},{2,98}... | collective-permute-start | bytes 294920 | tf_op jit(solution)/shard_map/ppermute | solution.py:377
  36.4 6.3 %collective-permute-start.5 = (bf16[96,128]{1,0:T(8,128)(2,1)S(1)}, bf16[96,128]{1,0:T(8,128)(2,1)S(1)}, u32[]{:S(2)}, u32[]{:S(2)}) collective-permute-start(bf16[96,128]{1,0:T(8,128)(2,1)S(1)} %get-tuple-element.46), channel_id=1, source_target_pairs={{0,2},{1,3},{2,0},{3,1},{4,6},{5,7},{6,4},{7,5},{8,10},{9,11},{10,... | collective-permute-start | bytes 73736 | tf_op jit(solution)/shard_map/ppermute | solution.py:373
  36.9 6.1 %collective-permute-start.7 = (bf16[96,128]{1,0:T(8,128)(2,1)S(1)}, bf16[96,128]{1,0:T(8,128)(2,1)S(1)}, u32[]{:S(2)}, u32[]{:S(2)}) collective-permute-start(bf16[96,128]{1,0:T(8,128)(2,1)S(1)} %get-tuple-element.47), channel_id=1, source_target_pairs={{0,8},{1,9},{2,10},{3,11},{4,12},{5,13},{6,14},{7,15},{8,0},{9,1},... | collective-permute-start | bytes 73736 | tf_op jit(solution)/shard_map/ppermute | solution.py:373
  37.3 6.4 %collective-permute-start.9 = (bf16[96,128]{1,0:T(8,128)(2,1)S(1)}, bf16[96,128]{1,0:T(8,128)(2,1)S(1)}, u32[]{:S(2)}, u32[]{:S(2)}) collective-permute-start(bf16[96,128]{1,0:T(8,128)(2,1)S(1)} %get-tuple-element.48), channel_id=1, source_target_pairs={{0,10},{1,11},{2,8},{3,9},{4,14},{5,15},{6,12},{7,13},{8,2},{9,3},... | collective-permute-start | bytes 73736 | tf_op jit(solution)/shard_map/ppermute | solution.py:373
  39.1 6.1 %collective-permute-start.4 = (bf16[96,128]{1,0:T(8,128)(2,1)S(1)}, bf16[96,128]{1,0:T(8,128)(2,1)S(1)}, u32[]{:S(2)}, u32[]{:S(2)}) collective-permute-start(bf16[96,128]{1,0:T(8,128)(2,1)S(1)} %get-tuple-element.45.refs_0_), channel_id=1, source_target_pairs={{0,1},{1,0},{2,3},{3,2},{4,5},{5,4},{6,7},{7,6},{8,9},{9,8},{10,11... | collective-permute-start | bytes 73736 | tf_op jit(solution)/shard_map/ppermute | solution.py:373
  42.7 2.5 %collective-permute-start.6 = (bf16[96,128]{1,0:T(8,128)(2,1)S(1)}, bf16[96,128]{1,0:T(8,128)(2,1)S(1)}, u32[]{:S(2)}, u32[]{:S(2)}) collective-permute-start(bf16[96,128]{1,0:T(8,128)(2,1)S(1)} %collective-permute-done.5.refs_1_), channel_id=1, source_target_pairs={{0,1},{1,0},{2,3},{3,2},{4,5},{5,4},{6,7},{7,6},{8,9},{9,8},{10,11... | collective-permute-start | bytes 73736 | tf_op jit(solution)/shard_map/ppermute | solution.py:373
  43.0 2.2 %collective-permute-start.8 = (bf16[96,128]{1,0:T(8,128)(2,1)S(1)}, bf16[96,128]{1,0:T(8,128)(2,1)S(1)}, u32[]{:S(2)}, u32[]{:S(2)}) collective-permute-start(bf16[96,128]{1,0:T(8,128)(2,1)S(1)} %collective-permute-done.7.refs_2_), channel_id=1, source_target_pairs={{0,1},{1,0},{2,3},{3,2},{4,5},{5,4},{6,7},{7,6},{8,9},{9,8},{10,11... | collective-permute-start | bytes 73736 | tf_op jit(solution)/shard_map/ppermute | solution.py:373
  43.7 2.4 %collective-permute-start.10 = (bf16[96,128]{1,0:T(8,128)(2,1)S(1)}, bf16[96,128]{1,0:T(8,128)(2,1)S(1)}, u32[]{:S(2)}, u32[]{:S(2)}) collective-permute-start(bf16[96,128]{1,0:T(8,128)(2,1)S(1)} %collective-permute-done.9.refs_3_), channel_id=1, source_target_pairs={{0,1},{1,0},{2,3},{3,2},{4,5},{5,4},{6,7},{7,6},{8,9},{9,8},{10,11... | collective-permute-start | bytes 73736 | tf_op jit(solution)/shard_map/ppermute | solution.py:373
  46.1 5.0 %collective-permute-start.13 = (bf16[128,384]{1,0:T(8,128)(2,1)S(1)}, bf16[128,384]{1,0:T(8,128)(2,1)S(1)}, u32[]{:S(2)}, u32[]{:S(2)}) collective-permute-start(bf16[128,384]{1,0:T(8,128)(2,1)S(1)} %shard_map.90.refs_8_.refs_0_.dpre), channel_id=1, source_target_pairs={{0,10},{1,11},{2,8},{3,9},{4,14},{5,15},{6,12},{7,13},{8,2},{9,3},... | collective-permute-start | bytes 294920 | tf_op jit(solution)/shard_map/ppermute | solution.py:373
  48.1 5.8 %collective-permute-start.12 = (bf16[128,384]{1,0:T(8,128)(2,1)S(1)}, bf16[128,384]{1,0:T(8,128)(2,1)S(1)}, u32[]{:S(2)}, u32[]{:S(2)}) collective-permute-start(bf16[128,384]{1,0:T(8,128)(2,1)S(1)} %shard_map.90.refs_8_.refs_0_.dpre), channel_id=1, source_target_pairs={{0,8},{1,9},{2,10},{3,11},{4,12},{5,13},{6,14},{7,15},{8,0},{9,1},... | collective-permute-start | bytes 294920 | tf_op jit(solution)/shard_map/ppermute | solution.py:373
  48.4 6.0 %collective-permute-start.11 = (bf16[128,384]{1,0:T(8,128)(2,1)S(1)}, bf16[128,384]{1,0:T(8,128)(2,1)S(1)}, u32[]{:S(2)}, u32[]{:S(2)}) collective-permute-start(bf16[128,384]{1,0:T(8,128)(2,1)S(1)} %shard_map.90.refs_8_.refs_0_.dpre), channel_id=1, source_target_pairs={{0,2},{1,3},{2,0},{3,1},{4,6},{5,7},{6,4},{7,5},{8,10},{9,11},{10,... | collective-permute-start | bytes 294920 | tf_op jit(solution)/shard_map/ppermute | solution.py:373
  48.8 6.5 %collective-permute-start.14 = (bf16[128,384]{1,0:T(8,128)(2,1)S(1)}, bf16[128,384]{1,0:T(8,128)(2,1)S(1)}, u32[]{:S(2)}, u32[]{:S(2)}) collective-permute-start(bf16[128,384]{1,0:T(8,128)(2,1)S(1)} %shard_map.90.refs_8_.refs_0_.dpre), channel_id=1, source_target_pairs={{0,1},{1,0},{2,3},{3,2},{4,5},{5,4},{6,7},{7,6},{8,9},{9,8},{10,11... | collective-permute-start | bytes 294920 | tf_op jit(solution)/shard_map/ppermute | solution.py:373
  51.1 4.3 %collective-permute-start.17 = (bf16[128,384]{1,0:T(8,128)(2,1)S(1)}, bf16[128,384]{1,0:T(8,128)(2,1)S(1)}, u32[]{:S(2)}, u32[]{:S(2)}) collective-permute-start(bf16[128,384]{1,0:T(8,128)(2,1)S(1)} %collective-permute-done.13.refs_3_), channel_id=1, source_target_pairs={{0,1},{1,0},{2,3},{3,2},{4,5},{5,4},{6,7},{7,6},{8,9},{9,8},{10,11... | collective-permute-start | bytes 294920 | tf_op jit(solution)/shard_map/ppermute | solution.py:373
  53.9 1.5 %collective-permute-start.16 = (bf16[128,384]{1,0:T(8,128)(2,1)S(1)}, bf16[128,384]{1,0:T(8,128)(2,1)S(1)}, u32[]{:S(2)}, u32[]{:S(2)}) collective-permute-start(bf16[128,384]{1,0:T(8,128)(2,1)S(1)} %collective-permute-done.12.refs_2_), channel_id=1, source_target_pairs={{0,1},{1,0},{2,3},{3,2},{4,5},{5,4},{6,7},{7,6},{8,9},{9,8},{10,11... | collective-permute-start | bytes 294920 | tf_op jit(solution)/shard_map/ppermute | solution.py:373
  54.4 1.3 %collective-permute-start.15 = (bf16[128,384]{1,0:T(8,128)(2,1)S(1)}, bf16[128,384]{1,0:T(8,128)(2,1)S(1)}, u32[]{:S(2)}, u32[]{:S(2)}) collective-permute-start(bf16[128,384]{1,0:T(8,128)(2,1)S(1)} %collective-permute-done.11.refs_1_), channel_id=1, source_target_pairs={{0,1},{1,0},{2,3},{3,2},{4,5},{5,4},{6,7},{7,6},{8,9},{9,8},{10,11... | collective-permute-start | bytes 294920 | tf_op jit(solution)/shard_map/ppermute | solution.py:373
  56.3 5.8 %collective-permute-start.18 = (bf16[224,384]{1,0:T(8,128)(2,1)S(1)}, bf16[224,384]{1,0:T(8,128)(2,1)S(1)}, u32[]{:S(2)}, u32[]{:S(2)}) collective-permute-start(bf16[224,384]{1,0:T(8,128)(2,1)S(1)} %get-tuple-element.52), channel_id=1, source_target_pairs={{0,6},{1,25},{2,4},{3,27},{4,2},{5,29},{6,0},{7,31},{8,14},{9,17},... | collective-permute-start | bytes 516104 | tf_op jit(solution)/shard_map/ppermute | solution.py:373
  62.2 8.5 %collective-permute-start.19 = (bf16[224,384]{1,0:T(8,128)(2,1)S(1)}, bf16[224,384]{1,0:T(8,128)(2,1)S(1)}, u32[]{:S(2)}, u32[]{:S(2)}) collective-permute-start(bf16[224,384]{1,0:T(8,128)(2,1)S(1)} %collective-permute-done.18.pair), channel_id=1, source_target_pairs={{0,1},{1,0},{2,3},{3,2},{4,5},{5,4},{6,7},{7,6},{8,9},{9,8},{10,11... | collective-permute-start | bytes 516104 | tf_op jit(solution)/shard_map/ppermute | solution.py:373
  63.2 7.4 %collective-permute-start.20 = (bf16[112,384]{1,0:T(8,128)(2,1)S(1)}, bf16[112,384]{1,0:T(8,128)(2,1)S(1)}, u32[]{:S(2)}, u32[]{:S(2)}) collective-permute-start(bf16[112,384]{1,0:T(8,128)(2,1)S(1)} %get-tuple-element.53), channel_id=1, source_target_pairs={{0,30},{1,31},{2,28},{3,29},{4,26},{5,27},{6,24},{7,25},{8,22},{9,... | collective-permute-start | bytes 258056 | tf_op jit(solution)/shard_map/ppermute | solution.py:373
  64.6 3.7 %collective-permute-start.3 = (bf16[16,128]{1,0:T(8,128)(2,1)S(1)}, bf16[16,128]{1,0:T(8,128)(2,1)S(1)}, u32[]{:S(2)}, u32[]{:S(2)}) collective-permute-start(bf16[16,128]{1,0:T(8,128)(2,1)S(1)} %get-tuple-element.40), channel_id=1, source_target_pairs={{0,32},{32,64},{64,96},{96,0},{1,33},{33,65},{65,97},{97,1},{2,34}... | collective-permute-start | bytes 12296 | tf_op jit(solution)/shard_map/ppermute | solution.py:377

commit v9 on v7

--- a/solution.py
+++ b/solution.py
@@ -243,17 +243,17 @@
         message[:16, :] = head_grad[:, :384].astype(bf16)
 
 
-def relay1_kernel(arrived, slope, w, head_grad, message, dpre_out):
+def relay1_kernel(arrived, slope, w, head_grad, message, dpre_out, head_sent):
     relay(1, arrived, slope, w, message, dpre_out)
     section = lax.axis_index("section")
 
     @pl.when(section == 3)
     def _():
-        message[:16, :] = head_grad[:, :384].astype(bf16)
-
-    @pl.when(section == 0)
-    def _():
-        message[:16, :] = arrived[:16, :]
+        head_sent[...] = head_grad[:, :384].astype(bf16)
+
+    @pl.when(section == 2)
+    def _():
+        head_sent[...] = arrived[:16, :]
 
 
 def bottom_kernel(arrived, slope, dpre3, dpre2, dpre1, *refs):
@@ -270,7 +270,9 @@
         dpre_out[...] = (arrived[...].astype(f32) * slope[...]).astype(bf16)
 
 
-def last_kernel(arrived, earlier, dpre, w, head_grad, msg3, msg2, msg1, own, grads, head_out):
+def last_kernel(
+    arrived, earlier, head_down, dpre, w, head_grad, msg3, msg2, msg1, own, grads, head_out
+):
     section = lax.axis_index("section")
 
     @pl.when(section == 3)
@@ -278,18 +280,18 @@
         grads[...] = msg3[...]
         head_out[...] = head_grad[:12, 384:]
 
-    for at, sent in ((2, msg2), (1, msg1)):
+    for at, sent, head in ((2, msg2, earlier), (1, msg1, head_down)):
 
         @pl.when(section == at)
         def _():
             grads[...] = sent[...]
-            head_out[...] = arrived[:16, at * 128 : at * 128 + 128].astype(f32)[:12]
+            head_out[...] = head[:16, at * 128 : at * 128 + 128].astype(f32)[:12]
 
     @pl.when(section == 0)
     def _():
         below = arrived[...].astype(f32) + conv_back(dpre[...].astype(f32), w)
         grads[...] = below.astype(bf16)
-        head_out[...] = earlier[:16, :128].astype(f32)[:12]
+        head_out[...] = head_down[:, :128].astype(f32)[:12]
 
 
 def stack_kernel(*refs):
@@ -371,9 +373,11 @@
         pairs_of = [(d, d ^ (odd_bits if odd_bits and d & 1 else bits)) for d in range(ranks)]
         return lax.ppermute(value, "dp", pairs_of)
 
-    def relayed(value, pairs_of):
-        both = [(a, b) for a, b in pairs_of] + [(b, a) for a, b in pairs_of]
-        return lax.ppermute(value, "section", both)
+    def relayed(value, routes):
+        return lax.ppermute(value, "section", routes)
+
+    def swaps(*pairs_of):
+        return [(a, b) for a, b in pairs_of] + [(b, a) for a, b in pairs_of]
 
     slope, announce, rows, w, head = call(
         forward_kernel,
@@ -401,15 +405,18 @@
         (act, act, VMEM((128, 128), bf16), VMEM((128, EMB), f32), VMEM((128, 128), f32))
         + (VMEM((16, 128), bf16),),
     )(gathered.reshape(256, 256), head, slope, w)
-    arrived = relayed(msg3, [(3, 2), (1, 0)])
+    arrived = relayed(msg3, swaps((3, 2), (1, 0)))
     split = call(split_kernel, [VMEM] * 2, (piece,) * 4)(rows, msg3)
     near = [split[0]] + [swap(split[k], gather[k]) for k in range(1, 4)]
     msg2, dpre2, head_grad = call(
         relay2_kernel, [VMEM] * 7, (act, act, VMEM((16, EMB), f32))
     )(arrived, slope, w, *for_head)
-    arrived = earlier = relayed(msg2, [(2, 1), (3, 0)])
-    msg1, dpre1 = call(relay1_kernel, [VMEM] * 4, (act, act))(arrived, slope, w, head_grad)
-    arrived = relayed(msg1, [(1, 0), (3, 2)])
+    arrived = earlier = relayed(msg2, [(3, 2), (2, 1), (1, 0), (0, 3)])
+    msg1, dpre1, head_sent = call(
+        relay1_kernel, [VMEM] * 4, (act, act, VMEM((16, CH), bf16))
+    )(arrived, slope, w, head_grad)
+    arrived = relayed(msg1, swaps((1, 0), (3, 2)))
+    head_down = relayed(head_sent, swaps((3, 0), (2, 1)))
     far = [swap(value, 1) for value in near]
     dpre = call(bottom_kernel, [VMEM] * 9, act)(
         arrived, slope, dpre3, dpre2, dpre1, *far
@@ -428,8 +435,8 @@
     diagonal = swap(diagonal, 30)
     crossed = swap(pair, 1)
     grads, head_grad = call(
-        last_kernel, [VMEM] * 9, (sds((ROWS, CH), bf16), sds((12, 128), f32))
-    )(arrived, earlier, dpre, w, head_grad, msg3, msg2, msg1, own)
+        last_kernel, [VMEM] * 10, (sds((ROWS, CH), bf16), sds((12, 128), f32))
+    )(arrived, earlier, head_down, dpre, w, head_grad, msg3, msg2, msg1, own)
     wgrad = call(sum_kernel, [VMEM] * 4, sds((108, 1, CH), f32))(own, pair, crossed, diagonal)
     return (
         grads.reshape(saved.shape),

time: 68.4 us -> 68.4 us (level)
  starting transfers between devices: 26.5 us -> 28.5 us
  waiting for transfers between devices: 17.7 us -> 15.7 us
    ppermute x17, waiting for transfers between devices: 13.1 us -> 9.32 us  [swap(): return lax.ppermute(value, 'dp', pairs_of)]
    ppermute x3 -> x4, starting transfers between devices: 9.15 us -> 11.1 us  [relayed(): return lax.ppermute(value, 'section', routes)]
    ppermute x3 -> x4, waiting for transfers between devices: 4.66 us -> 6.42 us  [relayed(): return lax.ppermute(value, 'section', routes)]
  transfers between devices with their start and end apart: 20 -> 21, of which waited for: 8 -> 9; matrix products, arithmetic and copies ran while one was open for 0% -> 0% of each run, Pallas kernels for 4% -> 4%
where the time goes in v9:
time: 68.4 us; the launch traced here: 68.3 us
  starting transfers between devices  28.5 us (42%)
  blocking collectives  16 us (23%)
  waiting for transfers between devices  15.7 us (23%)
  Pallas kernels  6.71 us (10%)
  between operations  1.36 us (2%)
    ppermute x17, starting transfers between devices, swap(): return lax.ppermute(value, 'dp', pairs_of)  17.3 us
    all_to_all x1, blocking collectives, per_device(): lax.all_to_all(announce.reshape(32, 8, 256), 'dp', 0, 0, tiled=True)  16 us
    ppermute x4, starting transfers between devices, relayed(): return lax.ppermute(value, 'section', routes)  11.1 us
    ppermute x17, waiting for transfers between devices, swap(): return lax.ppermute(value, 'dp', pairs_of)  9.32 us
    pallas_call x10, Pallas kernels, with_operands(): run(*[value if space is SMEM else pltpu.with_memory_space_constraint(valu...  6.71 us
    ppermute x4, waiting for transfers between devices, relayed(): return lax.ppermute(value, 'section', routes)  6.42 us
  transfers between devices with their start and end apart: 21, of which 9 were waited for; matrix products, arithmetic and copies ran while one was open for 0% of the time, Pallas kernels for 4%

profile of v9, /device:TPU:1, one launch (start us, length us, event | category | flops | bytes accessed | tf_op | source)
XLA Modules:
  0.0 68.3 jit_solution(6323242652770779178)
XLA Ops:
  1.3 2.5 %shard_map.85 = (f32[128,384]{1,0:T(8,128)S(1)}, bf16[256,256]{1,0:T(8,128)(2,1)S(1)}, bf16[128,384]{1,0:T(8,128)(2,1)S(1)}, bf16[3,3,384,384]{3,2,1,0:T(8,128)(2,1)S(1)}, bf16[384,512]{1,0:T(8,128)(2,1)S(1)}) custom-call(bf16[128,384]{1,0:T(8,128)(2,1)} %bitcast.12, bf16[3,3,384,384]{3,2,1,0:T(8,128)(2,1)} %bitcast.10, bf16[384,512]{1,0:T(8,128)(2,1)} %head_hbm.1, ...), custom_call_target="tpu_custom_call" | custom-call | tf_op jit(solution)/shard_map/pallas_call | solution.py:350
  3.7 16.0 %all_to_all.5 = bf16[32,8,256]{2,1,0:T(8,128)(2,1)S(1)} all-to-all(bf16[32,8,256]{2,1,0:T(8,128)(2,1)S(1)} %bitcast.9), channel_id=1, replica_groups=mesh['section'=4,'dp'=32] {'dp'}, dimensions={0} | all-to-all | bytes 262144 | tf_op jit(solution)/shard_map/all_to_all | solution.py:401
  19.7 1.6 %collective-permute-start = (bf16[128,384]{1,0:T(8,128)(2,1)S(1)}, bf16[128,384]{1,0:T(8,128)(2,1)S(1)}, u32[]{:S(2)}, u32[]{:S(2)}) collective-permute-start(bf16[128,384]{1,0:T(8,128)(2,1)S(1)} %get-tuple-element.33.order.msg3), channel_id=1, source_target_pairs={{96,64},{32,0},{64,96},{0,32},{97,65},{33,1},{65,97},{1,33},{98,66... | collective-permute-start | bytes 294920 | tf_op jit(solution)/shard_map/ppermute | solution.py:377
  21.4 2.7 %collective-permute-done.arrived = bf16[128,384]{1,0:T(8,128)(2,1)S(1)} collective-permute-done((bf16[128,384]{1,0:T(8,128)(2,1)S(1)}, bf16[128,384]{1,0:T(8,128)(2,1)S(1)}, u32[]{:S(2)}, u32[]{:S(2)}) %collective-permute-start) | collective-permute-done | bytes 98336 | tf_op jit(solution)/shard_map/ppermute | solution.py:377
  24.0 6.2 %collective-permute-start.1 = (bf16[128,384]{1,0:T(8,128)(2,1)S(1)}, bf16[128,384]{1,0:T(8,128)(2,1)S(1)}, u32[]{:S(2)}, u32[]{:S(2)}) collective-permute-start(bf16[128,384]{1,0:T(8,128)(2,1)S(1)} %get-tuple-element.38.msg2), channel_id=1, source_target_pairs={{96,64},{64,32},{32,0},{0,96},{97,65},{65,33},{33,1},{1,97},{98,66... | collective-permute-start | bytes 294920 | tf_op jit(solution)/shard_map/ppermute | solution.py:377
  30.2 1.6 %collective-permute-done.1.arrived.earlier = bf16[128,384]{1,0:T(8,128)(2,1)S(1)} collective-permute-done((bf16[128,384]{1,0:T(8,128)(2,1)S(1)}, bf16[128,384]{1,0:T(8,128)(2,1)S(1)}, u32[]{:S(2)}, u32[]{:S(2)}) %collective-permute-start.1) | collective-permute-done | bytes 98336 | tf_op jit(solution)/shard_map/ppermute | solution.py:377
  31.8 1.7 %collective-permute-start.2 = (bf16[128,384]{1,0:T(8,128)(2,1)S(1)}, bf16[128,384]{1,0:T(8,128)(2,1)S(1)}, u32[]{:S(2)}, u32[]{:S(2)}) collective-permute-start(bf16[128,384]{1,0:T(8,128)(2,1)S(1)} %get-tuple-element.40.msg1), channel_id=1, source_target_pairs={{32,0},{96,64},{0,32},{64,96},{33,1},{97,65},{1,33},{65,97},{34,2}... | collective-permute-start | bytes 294920 | tf_op jit(solution)/shard_map/ppermute | solution.py:377
  33.5 0.3 shard_map.89
  33.9 0.5 collective-permute-start.5
  34.4 0.4 collective-permute-start.7
  34.7 1.9 %collective-permute-start.9 = (bf16[96,128]{1,0:T(8,128)(2,1)S(1)}, bf16[96,128]{1,0:T(8,128)(2,1)S(1)}, u32[]{:S(2)}, u32[]{:S(2)}) collective-permute-start(bf16[96,128]{1,0:T(8,128)(2,1)S(1)} %get-tuple-element.49), channel_id=1, source_target_pairs={{0,10},{1,11},{2,8},{3,9},{4,14},{5,15},{6,12},{7,13},{8,2},{9,3},... | collective-permute-start | bytes 73736 | tf_op jit(solution)/shard_map/ppermute | solution.py:374
  36.6 3.0 %collective-permute-start.4 = (bf16[96,128]{1,0:T(8,128)(2,1)S(1)}, bf16[96,128]{1,0:T(8,128)(2,1)S(1)}, u32[]{:S(2)}, u32[]{:S(2)}) collective-permute-start(bf16[96,128]{1,0:T(8,128)(2,1)S(1)} %get-tuple-element.46.refs_0_), channel_id=1, source_target_pairs={{0,1},{1,0},{2,3},{3,2},{4,5},{5,4},{6,7},{7,6},{8,9},{9,8},{10,11... | collective-permute-start | bytes 73736 | tf_op jit(solution)/shard_map/ppermute | solution.py:374
  39.6 0.0 collective-permute-done.5.refs_1_
  39.6 0.3 collective-permute-start.6
  39.9 0.0 collective-permute-done.7.refs_2_
  39.9 0.7 collective-permute-start.8
  40.6 0.0 collective-permute-done.9.refs_3_
  40.6 1.5 %collective-permute-start.10 = (bf16[96,128]{1,0:T(8,128)(2,1)S(1)}, bf16[96,128]{1,0:T(8,128)(2,1)S(1)}, u32[]{:S(2)}, u32[]{:S(2)}) collective-permute-start(bf16[96,128]{1,0:T(8,128)(2,1)S(1)} %collective-permute-done.9.refs_3_), channel_id=1, source_target_pairs={{0,1},{1,0},{2,3},{3,2},{4,5},{5,4},{6,7},{7,6},{8,9},{9,8},{10,11... | collective-permute-start | bytes 73736 | tf_op jit(solution)/shard_map/ppermute | solution.py:374
  42.1 0.0 collective-permute-done.4.refs_0_.refs_4_
  42.1 0.0 collective-permute-done.6.refs_1_.refs_5_
  42.1 0.0 collective-permute-done.8.refs_2_.refs_6_
  42.1 0.8 %collective-permute-done.10.refs_3_.refs_7_ = bf16[96,128]{1,0:T(8,128)(2,1)S(1)} collective-permute-done((bf16[96,128]{1,0:T(8,128)(2,1)S(1)}, bf16[96,128]{1,0:T(8,128)(2,1)S(1)}, u32[]{:S(2)}, u32[]{:S(2)}) %collective-permute-start.10) | collective-permute-done | bytes 24608 | tf_op jit(solution)/shard_map/ppermute | solution.py:374
  42.9 0.0 collective-permute-done.2.arrived
  43.0 2.0 %collective-permute-start.13 = (bf16[128,384]{1,0:T(8,128)(2,1)S(1)}, bf16[128,384]{1,0:T(8,128)(2,1)S(1)}, u32[]{:S(2)}, u32[]{:S(2)}) collective-permute-start(bf16[128,384]{1,0:T(8,128)(2,1)S(1)} %shard_map.90.refs_8_.refs_0_.dpre), channel_id=1, source_target_pairs={{0,10},{1,11},{2,8},{3,9},{4,14},{5,15},{6,12},{7,13},{8,2},{9,3},... | collective-permute-start | bytes 294920 | tf_op jit(solution)/shard_map/ppermute | solution.py:374
  45.0 0.3 collective-permute-start.12
  45.3 0.4 collective-permute-start.11
  45.7 1.2 %collective-permute-start.14 = (bf16[128,384]{1,0:T(8,128)(2,1)S(1)}, bf16[128,384]{1,0:T(8,128)(2,1)S(1)}, u32[]{:S(2)}, u32[]{:S(2)}) collective-permute-start(bf16[128,384]{1,0:T(8,128)(2,1)S(1)} %shard_map.90.refs_8_.refs_0_.dpre), channel_id=1, source_target_pairs={{0,1},{1,0},{2,3},{3,2},{4,5},{5,4},{6,7},{7,6},{8,9},{9,8},{10,11... | collective-permute-start | bytes 294920 | tf_op jit(solution)/shard_map/ppermute | solution.py:374
  46.9 1.1 %collective-permute-done.13.refs_3_ = bf16[128,384]{1,0:T(8,128)(2,1)S(1)} collective-permute-done((bf16[128,384]{1,0:T(8,128)(2,1)S(1)}, bf16[128,384]{1,0:T(8,128)(2,1)S(1)}, u32[]{:S(2)}, u32[]{:S(2)}) %collective-permute-start.13) | collective-permute-done | bytes 98336 | tf_op jit(solution)/shard_map/ppermute | solution.py:374
  48.0 1.3 %collective-permute-start.17 = (bf16[128,384]{1,0:T(8,128)(2,1)S(1)}, bf16[128,384]{1,0:T(8,128)(2,1)S(1)}, u32[]{:S(2)}, u32[]{:S(2)}) collective-permute-start(bf16[128,384]{1,0:T(8,128)(2,1)S(1)} %collective-permute-done.13.refs_3_), channel_id=1, source_target_pairs={{0,1},{1,0},{2,3},{3,2},{4,5},{5,4},{6,7},{7,6},{8,9},{9,8},{10,11... | collective-permute-start | bytes 294920 | tf_op jit(solution)/shard_map/ppermute | solution.py:374
  49.3 1.5 %collective-permute-done.12.refs_2_ = bf16[128,384]{1,0:T(8,128)(2,1)S(1)} collective-permute-done((bf16[128,384]{1,0:T(8,128)(2,1)S(1)}, bf16[128,384]{1,0:T(8,128)(2,1)S(1)}, u32[]{:S(2)}, u32[]{:S(2)}) %collective-permute-start.12) | collective-permute-done | bytes 98336 | tf_op jit(solution)/shard_map/ppermute | solution.py:374
  50.8 0.5 collective-permute-start.16
  51.3 0.0 collective-permute-done.11.refs_1_
  51.3 0.0 collective-permute-start.15
  51.3 0.9 %shard_map.91.stack = bf16[448,1024]{1,0:T(8,128)(2,1)S(1)} custom-call(bf16[96,128]{1,0:T(8,128)(2,1)S(1)} %get-tuple-element.46.refs_0_, bf16[96,128]{1,0:T(8,128)(2,1)S(1)} %collective-permute-done.5.refs_1_, bf16[96,128]{1,0:T(8,128)(2,1)S(1)} %collective-permute-done.7.refs_2_, bf16[96,128]{1,0:T(8,128)(2,1)S(1)} %collective-permute-done.9.refs_3_, ...), custom_call_target="tpu_custom_call" | custom-call | tf_op jit(solution)/shard_map/pallas_call | solution.py:350
  52.2 0.0 collective-permute-done.14.refs_4_
  52.2 0.0 collective-permute-done.17.refs_7_
  52.2 0.0 collective-permute-done.16.refs_6_
  52.3 0.3 collective-permute-done.15.refs_5_
  52.6 0.6 shard_map.92
  53.2 1.0 %collective-permute-start.18 = (bf16[224,384]{1,0:T(8,128)(2,1)S(1)}, bf16[224,384]{1,0:T(8,128)(2,1)S(1)}, u32[]{:S(2)}, u32[]{:S(2)}) collective-permute-start(bf16[224,384]{1,0:T(8,128)(2,1)S(1)} %get-tuple-element.52), channel_id=1, source_target_pairs={{0,6},{1,25},{2,4},{3,27},{4,2},{5,29},{6,0},{7,31},{8,14},{9,17},... | collective-permute-start | bytes 516104 | tf_op jit(solution)/shard_map/ppermute | solution.py:374
  54.2 4.8 %collective-permute-done.18.pair = bf16[224,384]{1,0:T(8,128)(2,1)S(1)} collective-permute-done((bf16[224,384]{1,0:T(8,128)(2,1)S(1)}, bf16[224,384]{1,0:T(8,128)(2,1)S(1)}, u32[]{:S(2)}, u32[]{:S(2)}) %collective-permute-start.18) | collective-permute-done | bytes 172064 | tf_op jit(solution)/shard_map/ppermute | solution.py:374
  59.1 1.0 %collective-permute-start.19 = (bf16[224,384]{1,0:T(8,128)(2,1)S(1)}, bf16[224,384]{1,0:T(8,128)(2,1)S(1)}, u32[]{:S(2)}, u32[]{:S(2)}) collective-permute-start(bf16[224,384]{1,0:T(8,128)(2,1)S(1)} %collective-permute-done.18.pair), channel_id=1, source_target_pairs={{0,1},{1,0},{2,3},{3,2},{4,5},{5,4},{6,7},{7,6},{8,9},{9,8},{10,11... | collective-permute-start | bytes 516104 | tf_op jit(solution)/shard_map/ppermute | solution.py:374
  60.1 1.4 %collective-permute-start.20 = (bf16[112,384]{1,0:T(8,128)(2,1)S(1)}, bf16[112,384]{1,0:T(8,128)(2,1)S(1)}, u32[]{:S(2)}, u32[]{:S(2)}) collective-permute-start(bf16[112,384]{1,0:T(8,128)(2,1)S(1)} %get-tuple-element.53), channel_id=1, source_target_pairs={{0,30},{1,31},{2,28},{3,29},{4,26},{5,27},{6,24},{7,25},{8,22},{9,... | collective-permute-start | bytes 258056 | tf_op jit(solution)/shard_map/ppermute | solution.py:374
  61.5 1.6 %collective-permute-start.3 = (bf16[16,384]{1,0:T(8,128)(2,1)S(1)}, bf16[16,384]{1,0:T(8,128)(2,1)S(1)}, u32[]{:S(2)}, u32[]{:S(2)}) collective-permute-start(bf16[16,384]{1,0:T(8,128)(2,1)S(1)} %get-tuple-element.41), channel_id=1, source_target_pairs={{96,0},{64,32},{0,96},{32,64},{97,1},{65,33},{1,97},{33,65},{98,2}... | collective-permute-start | bytes 36872 | tf_op jit(solution)/shard_map/ppermute | solution.py:377
  63.1 2.1 %collective-permute-done.3.head_down = bf16[16,384]{1,0:T(8,128)(2,1)S(1)} collective-permute-done((bf16[16,384]{1,0:T(8,128)(2,1)S(1)}, bf16[16,384]{1,0:T(8,128)(2,1)S(1)}, u32[]{:S(2)}, u32[]{:S(2)}) %collective-permute-start.3) | collective-permute-done | bytes 12320 | tf_op jit(solution)/shard_map/ppermute | solution.py:377
  65.2 1.6 %shard_map.93 = (bf16[128,384]{1,0:T(8,128)(2,1)}, f32[12,128]{1,0:T(8,128)}) custom-call(bf16[128,384]{1,0:T(8,128)(2,1)S(1)} %collective-permute-done.2.arrived, bf16[128,384]{1,0:T(8,128)(2,1)S(1)} %collective-permute-done.1.arrived.earlier, bf16[16,384]{1,0:T(8,128)(2,1)S(1)} %collective-permute-done.3.head_down, ...), custom_call_target="tpu_custom_call" | custom-call | tf_op jit(solution)/shard_map/pallas_call | solution.py:350
  66.8 0.7 %collective-permute-done.20.diagonal = bf16[112,384]{1,0:T(8,128)(2,1)S(1)} collective-permute-done((bf16[112,384]{1,0:T(8,128)(2,1)S(1)}, bf16[112,384]{1,0:T(8,128)(2,1)S(1)}, u32[]{:S(2)}, u32[]{:S(2)}) %collective-permute-start.20) | collective-permute-done | bytes 86048 | tf_op jit(solution)/shard_map/ppermute | solution.py:374
  67.5 0.0 collective-permute-done.19.crossed
  67.5 0.7 %shard_map.94 = f32[108,1,384]{2,1,0:T(1,128)} custom-call(f32[112,384]{1,0:T(8,128)S(1)} %get-tuple-element.50.own, bf16[224,384]{1,0:T(8,128)(2,1)S(1)} %collective-permute-done.18.pair, bf16[224,384]{1,0:T(8,128)(2,1)S(1)} %collective-permute-done.19.crossed, bf16[112,384]{1,0:T(8,128)(2,1)S(1)} %collective-permute-done.20.diagonal), custom_call_target="tpu_custom_call" | custom-call | tf_op jit(solution)/shard_map/pallas_call | solution.py:350
  (4 shorter events, 0.0 us)
Async XLA Ops:
  19.7 4.3 %collective-permute-start = (bf16[128,384]{1,0:T(8,128)(2,1)S(1)}, bf16[128,384]{1,0:T(8,128)(2,1)S(1)}, u32[]{:S(2)}, u32[]{:S(2)}) collective-permute-start(bf16[128,384]{1,0:T(8,128)(2,1)S(1)} %get-tuple-element.33.order.msg3), channel_id=1, source_target_pairs={{96,64},{32,0},{64,96},{0,32},{97,65},{33,1},{65,97},{1,33},{98,66... | collective-permute-start | bytes 294920 | tf_op jit(solution)/shard_map/ppermute | solution.py:377
  24.0 7.8 %collective-permute-start.1 = (bf16[128,384]{1,0:T(8,128)(2,1)S(1)}, bf16[128,384]{1,0:T(8,128)(2,1)S(1)}, u32[]{:S(2)}, u32[]{:S(2)}) collective-permute-start(bf16[128,384]{1,0:T(8,128)(2,1)S(1)} %get-tuple-element.38.msg2), channel_id=1, source_target_pairs={{96,64},{64,32},{32,0},{0,96},{97,65},{65,33},{33,1},{1,97},{98,66... | collective-permute-start | bytes 294920 | tf_op jit(solution)/shard_map/ppermute | solution.py:377
  31.8 11.1 %collective-permute-start.2 = (bf16[128,384]{1,0:T(8,128)(2,1)S(1)}, bf16[128,384]{1,0:T(8,128)(2,1)S(1)}, u32[]{:S(2)}, u32[]{:S(2)}) collective-permute-start(bf16[128,384]{1,0:T(8,128)(2,1)S(1)} %get-tuple-element.40.msg1), channel_id=1, source_target_pairs={{32,0},{96,64},{0,32},{64,96},{33,1},{97,65},{1,33},{65,97},{34,2}... | collective-permute-start | bytes 294920 | tf_op jit(solution)/shard_map/ppermute | solution.py:377
  33.9 5.7 %collective-permute-start.5 = (bf16[96,128]{1,0:T(8,128)(2,1)S(1)}, bf16[96,128]{1,0:T(8,128)(2,1)S(1)}, u32[]{:S(2)}, u32[]{:S(2)}) collective-permute-start(bf16[96,128]{1,0:T(8,128)(2,1)S(1)} %get-tuple-element.47), channel_id=1, source_target_pairs={{0,2},{1,3},{2,0},{3,1},{4,6},{5,7},{6,4},{7,5},{8,10},{9,11},{10,... | collective-permute-start | bytes 73736 | tf_op jit(solution)/shard_map/ppermute | solution.py:374
  34.4 5.5 %collective-permute-start.7 = (bf16[96,128]{1,0:T(8,128)(2,1)S(1)}, bf16[96,128]{1,0:T(8,128)(2,1)S(1)}, u32[]{:S(2)}, u32[]{:S(2)}) collective-permute-start(bf16[96,128]{1,0:T(8,128)(2,1)S(1)} %get-tuple-element.48), channel_id=1, source_target_pairs={{0,8},{1,9},{2,10},{3,11},{4,12},{5,13},{6,14},{7,15},{8,0},{9,1},... | collective-permute-start | bytes 73736 | tf_op jit(solution)/shard_map/ppermute | solution.py:374
  34.7 5.8 %collective-permute-start.9 = (bf16[96,128]{1,0:T(8,128)(2,1)S(1)}, bf16[96,128]{1,0:T(8,128)(2,1)S(1)}, u32[]{:S(2)}, u32[]{:S(2)}) collective-permute-start(bf16[96,128]{1,0:T(8,128)(2,1)S(1)} %get-tuple-element.49), channel_id=1, source_target_pairs={{0,10},{1,11},{2,8},{3,9},{4,14},{5,15},{6,12},{7,13},{8,2},{9,3},... | collective-permute-start | bytes 73736 | tf_op jit(solution)/shard_map/ppermute | solution.py:374
  36.6 5.5 %collective-permute-start.4 = (bf16[96,128]{1,0:T(8,128)(2,1)S(1)}, bf16[96,128]{1,0:T(8,128)(2,1)S(1)}, u32[]{:S(2)}, u32[]{:S(2)}) collective-permute-start(bf16[96,128]{1,0:T(8,128)(2,1)S(1)} %get-tuple-element.46.refs_0_), channel_id=1, source_target_pairs={{0,1},{1,0},{2,3},{3,2},{4,5},{5,4},{6,7},{7,6},{8,9},{9,8},{10,11... | collective-permute-start | bytes 73736 | tf_op jit(solution)/shard_map/ppermute | solution.py:374
  39.6 2.5 %collective-permute-start.6 = (bf16[96,128]{1,0:T(8,128)(2,1)S(1)}, bf16[96,128]{1,0:T(8,128)(2,1)S(1)}, u32[]{:S(2)}, u32[]{:S(2)}) collective-permute-start(bf16[96,128]{1,0:T(8,128)(2,1)S(1)} %collective-permute-done.5.refs_1_), channel_id=1, source_target_pairs={{0,1},{1,0},{2,3},{3,2},{4,5},{5,4},{6,7},{7,6},{8,9},{9,8},{10,11... | collective-permute-start | bytes 73736 | tf_op jit(solution)/shard_map/ppermute | solution.py:374
  39.9 2.2 %collective-permute-start.8 = (bf16[96,128]{1,0:T(8,128)(2,1)S(1)}, bf16[96,128]{1,0:T(8,128)(2,1)S(1)}, u32[]{:S(2)}, u32[]{:S(2)}) collective-permute-start(bf16[96,128]{1,0:T(8,128)(2,1)S(1)} %collective-permute-done.7.refs_2_), channel_id=1, source_target_pairs={{0,1},{1,0},{2,3},{3,2},{4,5},{5,4},{6,7},{7,6},{8,9},{9,8},{10,11... | collective-permute-start | bytes 73736 | tf_op jit(solution)/shard_map/ppermute | solution.py:374
  40.6 2.4 %collective-permute-start.10 = (bf16[96,128]{1,0:T(8,128)(2,1)S(1)}, bf16[96,128]{1,0:T(8,128)(2,1)S(1)}, u32[]{:S(2)}, u32[]{:S(2)}) collective-permute-start(bf16[96,128]{1,0:T(8,128)(2,1)S(1)} %collective-permute-done.9.refs_3_), channel_id=1, source_target_pairs={{0,1},{1,0},{2,3},{3,2},{4,5},{5,4},{6,7},{7,6},{8,9},{9,8},{10,11... | collective-permute-start | bytes 73736 | tf_op jit(solution)/shard_map/ppermute | solution.py:374
  43.0 5.0 %collective-permute-start.13 = (bf16[128,384]{1,0:T(8,128)(2,1)S(1)}, bf16[128,384]{1,0:T(8,128)(2,1)S(1)}, u32[]{:S(2)}, u32[]{:S(2)}) collective-permute-start(bf16[128,384]{1,0:T(8,128)(2,1)S(1)} %shard_map.90.refs_8_.refs_0_.dpre), channel_id=1, source_target_pairs={{0,10},{1,11},{2,8},{3,9},{4,14},{5,15},{6,12},{7,13},{8,2},{9,3},... | collective-permute-start | bytes 294920 | tf_op jit(solution)/shard_map/ppermute | solution.py:374
  45.0 5.8 %collective-permute-start.12 = (bf16[128,384]{1,0:T(8,128)(2,1)S(1)}, bf16[128,384]{1,0:T(8,128)(2,1)S(1)}, u32[]{:S(2)}, u32[]{:S(2)}) collective-permute-start(bf16[128,384]{1,0:T(8,128)(2,1)S(1)} %shard_map.90.refs_8_.refs_0_.dpre), channel_id=1, source_target_pairs={{0,8},{1,9},{2,10},{3,11},{4,12},{5,13},{6,14},{7,15},{8,0},{9,1},... | collective-permute-start | bytes 294920 | tf_op jit(solution)/shard_map/ppermute | solution.py:374
  45.3 6.0 %collective-permute-start.11 = (bf16[128,384]{1,0:T(8,128)(2,1)S(1)}, bf16[128,384]{1,0:T(8,128)(2,1)S(1)}, u32[]{:S(2)}, u32[]{:S(2)}) collective-permute-start(bf16[128,384]{1,0:T(8,128)(2,1)S(1)} %shard_map.90.refs_8_.refs_0_.dpre), channel_id=1, source_target_pairs={{0,2},{1,3},{2,0},{3,1},{4,6},{5,7},{6,4},{7,5},{8,10},{9,11},{10,... | collective-permute-start | bytes 294920 | tf_op jit(solution)/shard_map/ppermute | solution.py:374
  45.7 6.5 %collective-permute-start.14 = (bf16[128,384]{1,0:T(8,128)(2,1)S(1)}, bf16[128,384]{1,0:T(8,128)(2,1)S(1)}, u32[]{:S(2)}, u32[]{:S(2)}) collective-permute-start(bf16[128,384]{1,0:T(8,128)(2,1)S(1)} %shard_map.90.refs_8_.refs_0_.dpre), channel_id=1, source_target_pairs={{0,1},{1,0},{2,3},{3,2},{4,5},{5,4},{6,7},{7,6},{8,9},{9,8},{10,11... | collective-permute-start | bytes 294920 | tf_op jit(solution)/shard_map/ppermute | solution.py:374
  48.0 4.3 %collective-permute-start.17 = (bf16[128,384]{1,0:T(8,128)(2,1)S(1)}, bf16[128,384]{1,0:T(8,128)(2,1)S(1)}, u32[]{:S(2)}, u32[]{:S(2)}) collective-permute-start(bf16[128,384]{1,0:T(8,128)(2,1)S(1)} %collective-permute-done.13.refs_3_), channel_id=1, source_target_pairs={{0,1},{1,0},{2,3},{3,2},{4,5},{5,4},{6,7},{7,6},{8,9},{9,8},{10,11... | collective-permute-start | bytes 294920 | tf_op jit(solution)/shard_map/ppermute | solution.py:374
  50.8 1.5 %collective-permute-start.16 = (bf16[128,384]{1,0:T(8,128)(2,1)S(1)}, bf16[128,384]{1,0:T(8,128)(2,1)S(1)}, u32[]{:S(2)}, u32[]{:S(2)}) collective-permute-start(bf16[128,384]{1,0:T(8,128)(2,1)S(1)} %collective-permute-done.12.refs_2_), channel_id=1, source_target_pairs={{0,1},{1,0},{2,3},{3,2},{4,5},{5,4},{6,7},{7,6},{8,9},{9,8},{10,11... | collective-permute-start | bytes 294920 | tf_op jit(solution)/shard_map/ppermute | solution.py:374
  51.3 1.3 %collective-permute-start.15 = (bf16[128,384]{1,0:T(8,128)(2,1)S(1)}, bf16[128,384]{1,0:T(8,128)(2,1)S(1)}, u32[]{:S(2)}, u32[]{:S(2)}) collective-permute-start(bf16[128,384]{1,0:T(8,128)(2,1)S(1)} %collective-permute-done.11.refs_1_), channel_id=1, source_target_pairs={{0,1},{1,0},{2,3},{3,2},{4,5},{5,4},{6,7},{7,6},{8,9},{9,8},{10,11... | collective-permute-start | bytes 294920 | tf_op jit(solution)/shard_map/ppermute | solution.py:374
  53.2 5.8 %collective-permute-start.18 = (bf16[224,384]{1,0:T(8,128)(2,1)S(1)}, bf16[224,384]{1,0:T(8,128)(2,1)S(1)}, u32[]{:S(2)}, u32[]{:S(2)}) collective-permute-start(bf16[224,384]{1,0:T(8,128)(2,1)S(1)} %get-tuple-element.52), channel_id=1, source_target_pairs={{0,6},{1,25},{2,4},{3,27},{4,2},{5,29},{6,0},{7,31},{8,14},{9,17},... | collective-permute-start | bytes 516104 | tf_op jit(solution)/shard_map/ppermute | solution.py:374
  59.1 8.5 %collective-permute-start.19 = (bf16[224,384]{1,0:T(8,128)(2,1)S(1)}, bf16[224,384]{1,0:T(8,128)(2,1)S(1)}, u32[]{:S(2)}, u32[]{:S(2)}) collective-permute-start(bf16[224,384]{1,0:T(8,128)(2,1)S(1)} %collective-permute-done.18.pair), channel_id=1, source_target_pairs={{0,1},{1,0},{2,3},{3,2},{4,5},{5,4},{6,7},{7,6},{8,9},{9,8},{10,11... | collective-permute-start | bytes 516104 | tf_op jit(solution)/shard_map/ppermute | solution.py:374
  60.1 7.4 %collective-permute-start.20 = (bf16[112,384]{1,0:T(8,128)(2,1)S(1)}, bf16[112,384]{1,0:T(8,128)(2,1)S(1)}, u32[]{:S(2)}, u32[]{:S(2)}) collective-permute-start(bf16[112,384]{1,0:T(8,128)(2,1)S(1)} %get-tuple-element.53), channel_id=1, source_target_pairs={{0,30},{1,31},{2,28},{3,29},{4,26},{5,27},{6,24},{7,25},{8,22},{9,... | collective-permute-start | bytes 258056 | tf_op jit(solution)/shard_map/ppermute | solution.py:374
  61.5 3.8 %collective-permute-start.3 = (bf16[16,384]{1,0:T(8,128)(2,1)S(1)}, bf16[16,384]{1,0:T(8,128)(2,1)S(1)}, u32[]{:S(2)}, u32[]{:S(2)}) collective-permute-start(bf16[16,384]{1,0:T(8,128)(2,1)S(1)} %get-tuple-element.41), channel_id=1, source_target_pairs={{96,0},{64,32},{0,96},{32,64},{97,1},{65,33},{1,97},{33,65},{98,2}... | collective-permute-start | bytes 36872 | tf_op jit(solution)/shard_map/ppermute | solution.py:377

commit v10 on v7

--- a/solution.py
+++ b/solution.py
@@ -182,7 +182,7 @@
     return dpooled[:4].astype(f32), (mixing.astype(bf16), unit, inv, pooled_mine)
 
 
-def split_kernel(saved, order, *outs):
+def split_kernel(saved, order, mixing, unit, inv, mine, head_out, *outs):
     _, _, y, x, c = position()
     m = row_iota((CH, 1))
     q = (m * 43691) >> 19
@@ -200,6 +200,12 @@
     for k, out in enumerate(outs):
         out[...] = turned[96 * k : 96 * k + 96]
 
+    @pl.when(lax.axis_index("section") == 3)
+    def _():
+        units = unit[...]
+        dproj = projected_grad(mixing[...], units.astype(bf16), units, inv[:, :1])
+        head_out[...] = mm(mine[...], dproj)
+
 
 def top_kernel(
     gathered, head, slope, w, message, dpre_out, mixing_out, unit_out, inv_out, mine_out
@@ -231,15 +237,11 @@
         message[...] = below.astype(bf16)
 
 
-def relay2_kernel(arrived, slope, w, mixing, unit, inv, mine, message, dpre_out, head_out):
+def relay2_kernel(arrived, slope, w, head_grad, message, dpre_out):
     relay(2, arrived, slope, w, message, dpre_out)
 
     @pl.when(lax.axis_index("section") == 3)
     def _():
-        units = unit[...]
-        dproj = projected_grad(mixing[...], units.astype(bf16), units, inv[:, :1])
-        head_grad = mm(mine[...], dproj)
-        head_out[...] = head_grad
         message[:16, :] = head_grad[:, :384].astype(bf16)
 
 
@@ -402,11 +404,11 @@
         + (VMEM((16, 128), bf16),),
     )(gathered.reshape(256, 256), head, slope, w)
     arrived = relayed(msg3, [(3, 2), (1, 0)])
-    split = call(split_kernel, [VMEM] * 2, (piece,) * 4)(rows, msg3)
+    head_grad, *split = call(
+        split_kernel, [VMEM] * 6, (VMEM((16, EMB), f32),) + (piece,) * 4
+    )(rows, msg3, *for_head)
     near = [split[0]] + [swap(split[k], gather[k]) for k in range(1, 4)]
-    msg2, dpre2, head_grad = call(
-        relay2_kernel, [VMEM] * 7, (act, act, VMEM((16, EMB), f32))
-    )(arrived, slope, w, *for_head)
+    msg2, dpre2 = call(relay2_kernel, [VMEM] * 4, (act, act))(arrived, slope, w, head_grad)
     arrived = earlier = relayed(msg2, [(2, 1), (3, 0)])
     msg1, dpre1 = call(relay1_kernel, [VMEM] * 4, (act, act))(arrived, slope, w, head_grad)
     arrived = relayed(msg1, [(1, 0), (3, 2)])

time: 68.4 us -> 68 us (level)
  no operation moved by 1% of the time
where the time goes in v10:
time: 68 us; the launch traced here: 67.8 us
  starting transfers between devices  26.4 us (39%)
  waiting for transfers between devices  17.4 us (26%)
  blocking collectives  16 us (24%)
  Pallas kernels  6.71 us (10%)
  between operations  1.36 us (2%)
    ppermute x17, starting transfers between devices, swap(): return lax.ppermute(value, 'dp', pairs_of)  17.3 us
    all_to_all x1, blocking collectives, per_device(): lax.all_to_all(announce.reshape(32, 8, 256), 'dp', 0, 0, tiled=True)  16 us
    ppermute x17, waiting for transfers between devices, swap(): return lax.ppermute(value, 'dp', pairs_of)  13.1 us
    ppermute x3, starting transfers between devices, relayed(): return lax.ppermute(value, 'section', both)  9.15 us
    pallas_call x10, Pallas kernels, with_operands(): run(*[value if space is SMEM else pltpu.with_memory_space_constraint(valu...  6.71 us
    ppermute x3, waiting for transfers between devices, relayed(): return lax.ppermute(value, 'section', both)  4.31 us
  transfers between devices with their start and end apart: 20, of which 8 were waited for; matrix products, arithmetic and copies ran while one was open for 0% of the time, Pallas kernels for 4%

profile of v10, /device:TPU:1, one launch (start us, length us, event | category | flops | bytes accessed | tf_op | source)
XLA Modules:
  0.0 67.8 jit_solution(4908359212330573791)
XLA Ops:
  1.3 2.5 %shard_map.85 = (f32[128,384]{1,0:T(8,128)S(1)}, bf16[256,256]{1,0:T(8,128)(2,1)S(1)}, bf16[128,384]{1,0:T(8,128)(2,1)S(1)}, bf16[3,3,384,384]{3,2,1,0:T(8,128)(2,1)S(1)}, bf16[384,512]{1,0:T(8,128)(2,1)S(1)}) custom-call(bf16[128,384]{1,0:T(8,128)(2,1)} %bitcast.12, bf16[3,3,384,384]{3,2,1,0:T(8,128)(2,1)} %bitcast.10, bf16[384,512]{1,0:T(8,128)(2,1)} %head_hbm.1, ...), custom_call_target="tpu_custom_call" | custom-call | tf_op jit(solution)/shard_map/pallas_call | solution.py:350
  3.7 16.0 %all_to_all.5 = bf16[32,8,256]{2,1,0:T(8,128)(2,1)S(1)} all-to-all(bf16[32,8,256]{2,1,0:T(8,128)(2,1)S(1)} %bitcast.9), channel_id=1, replica_groups=mesh['section'=4,'dp'=32] {'dp'}, dimensions={0} | all-to-all | bytes 262144 | tf_op jit(solution)/shard_map/all_to_all | solution.py:399
  19.7 1.6 %collective-permute-start = (bf16[128,384]{1,0:T(8,128)(2,1)S(1)}, bf16[128,384]{1,0:T(8,128)(2,1)S(1)}, u32[]{:S(2)}, u32[]{:S(2)}) collective-permute-start(bf16[128,384]{1,0:T(8,128)(2,1)S(1)} %get-tuple-element.32.order.msg3), channel_id=1, source_target_pairs={{96,64},{32,0},{64,96},{0,32},{97,65},{33,1},{65,97},{1,33},{98,66... | collective-permute-start | bytes 294920 | tf_op jit(solution)/shard_map/ppermute | solution.py:378
  21.4 0.3 shard_map.87
  21.7 2.3 %collective-permute-done.arrived = bf16[128,384]{1,0:T(8,128)(2,1)S(1)} collective-permute-done((bf16[128,384]{1,0:T(8,128)(2,1)S(1)}, bf16[128,384]{1,0:T(8,128)(2,1)S(1)}, u32[]{:S(2)}, u32[]{:S(2)}) %collective-permute-start) | collective-permute-done | bytes 98336 | tf_op jit(solution)/shard_map/ppermute | solution.py:378
  24.0 5.8 %collective-permute-start.1 = (bf16[128,384]{1,0:T(8,128)(2,1)S(1)}, bf16[128,384]{1,0:T(8,128)(2,1)S(1)}, u32[]{:S(2)}, u32[]{:S(2)}) collective-permute-start(bf16[128,384]{1,0:T(8,128)(2,1)S(1)} %get-tuple-element.39.msg2), channel_id=1, source_target_pairs={{64,32},{96,0},{32,64},{0,96},{65,33},{97,1},{33,65},{1,97},{66,34... | collective-permute-start | bytes 294920 | tf_op jit(solution)/shard_map/ppermute | solution.py:378
  29.8 2.0 %collective-permute-done.1.arrived.earlier = bf16[128,384]{1,0:T(8,128)(2,1)S(1)} collective-permute-done((bf16[128,384]{1,0:T(8,128)(2,1)S(1)}, bf16[128,384]{1,0:T(8,128)(2,1)S(1)}, u32[]{:S(2)}, u32[]{:S(2)}) %collective-permute-start.1) | collective-permute-done | bytes 98336 | tf_op jit(solution)/shard_map/ppermute | solution.py:378
  31.8 1.7 %collective-permute-start.2 = (bf16[128,384]{1,0:T(8,128)(2,1)S(1)}, bf16[128,384]{1,0:T(8,128)(2,1)S(1)}, u32[]{:S(2)}, u32[]{:S(2)}) collective-permute-start(bf16[128,384]{1,0:T(8,128)(2,1)S(1)} %get-tuple-element.40.msg1), channel_id=1, source_target_pairs={{32,0},{96,64},{0,32},{64,96},{33,1},{97,65},{1,33},{65,97},{34,2}... | collective-permute-start | bytes 294920 | tf_op jit(solution)/shard_map/ppermute | solution.py:378
  33.5 0.4 collective-permute-start.4
  34.0 0.4 collective-permute-start.6
  34.3 1.9 %collective-permute-start.8 = (bf16[96,128]{1,0:T(8,128)(2,1)S(1)}, bf16[96,128]{1,0:T(8,128)(2,1)S(1)}, u32[]{:S(2)}, u32[]{:S(2)}) collective-permute-start(bf16[96,128]{1,0:T(8,128)(2,1)S(1)} %get-tuple-element.47), channel_id=1, source_target_pairs={{0,10},{1,11},{2,8},{3,9},{4,14},{5,15},{6,12},{7,13},{8,2},{9,3},... | collective-permute-start | bytes 73736 | tf_op jit(solution)/shard_map/ppermute | solution.py:374
  36.2 3.0 %collective-permute-start.3 = (bf16[96,128]{1,0:T(8,128)(2,1)S(1)}, bf16[96,128]{1,0:T(8,128)(2,1)S(1)}, u32[]{:S(2)}, u32[]{:S(2)}) collective-permute-start(bf16[96,128]{1,0:T(8,128)(2,1)S(1)} %get-tuple-element.44.refs_0_), channel_id=1, source_target_pairs={{0,1},{1,0},{2,3},{3,2},{4,5},{5,4},{6,7},{7,6},{8,9},{9,8},{10,11... | collective-permute-start | bytes 73736 | tf_op jit(solution)/shard_map/ppermute | solution.py:374
  39.1 0.0 collective-permute-done.4.refs_1_
  39.2 0.3 collective-permute-start.5
  39.5 0.0 collective-permute-done.6.refs_2_
  39.5 0.7 collective-permute-start.7
  40.2 0.0 collective-permute-done.8.refs_3_
  40.2 1.5 %collective-permute-start.9 = (bf16[96,128]{1,0:T(8,128)(2,1)S(1)}, bf16[96,128]{1,0:T(8,128)(2,1)S(1)}, u32[]{:S(2)}, u32[]{:S(2)}) collective-permute-start(bf16[96,128]{1,0:T(8,128)(2,1)S(1)} %collective-permute-done.8.refs_3_), channel_id=1, source_target_pairs={{0,1},{1,0},{2,3},{3,2},{4,5},{5,4},{6,7},{7,6},{8,9},{9,8},{10,11... | collective-permute-start | bytes 73736 | tf_op jit(solution)/shard_map/ppermute | solution.py:374
  41.7 0.0 collective-permute-done.3.refs_0_.refs_4_
  41.7 0.0 collective-permute-done.5.refs_1_.refs_5_
  41.7 0.0 collective-permute-done.7.refs_2_.refs_6_
  41.7 0.8 %collective-permute-done.9.refs_3_.refs_7_ = bf16[96,128]{1,0:T(8,128)(2,1)S(1)} collective-permute-done((bf16[96,128]{1,0:T(8,128)(2,1)S(1)}, bf16[96,128]{1,0:T(8,128)(2,1)S(1)}, u32[]{:S(2)}, u32[]{:S(2)}) %collective-permute-start.9) | collective-permute-done | bytes 24608 | tf_op jit(solution)/shard_map/ppermute | solution.py:374
  42.5 0.0 collective-permute-done.2.arrived
  42.5 2.0 %collective-permute-start.12 = (bf16[128,384]{1,0:T(8,128)(2,1)S(1)}, bf16[128,384]{1,0:T(8,128)(2,1)S(1)}, u32[]{:S(2)}, u32[]{:S(2)}) collective-permute-start(bf16[128,384]{1,0:T(8,128)(2,1)S(1)} %shard_map.90.refs_8_.refs_0_.dpre), channel_id=1, source_target_pairs={{0,10},{1,11},{2,8},{3,9},{4,14},{5,15},{6,12},{7,13},{8,2},{9,3},... | collective-permute-start | bytes 294920 | tf_op jit(solution)/shard_map/ppermute | solution.py:374
  44.6 0.3 collective-permute-start.11
  44.9 0.4 collective-permute-start.10
  45.3 1.2 %collective-permute-start.13 = (bf16[128,384]{1,0:T(8,128)(2,1)S(1)}, bf16[128,384]{1,0:T(8,128)(2,1)S(1)}, u32[]{:S(2)}, u32[]{:S(2)}) collective-permute-start(bf16[128,384]{1,0:T(8,128)(2,1)S(1)} %shard_map.90.refs_8_.refs_0_.dpre), channel_id=1, source_target_pairs={{0,1},{1,0},{2,3},{3,2},{4,5},{5,4},{6,7},{7,6},{8,9},{9,8},{10,11... | collective-permute-start | bytes 294920 | tf_op jit(solution)/shard_map/ppermute | solution.py:374
  46.5 1.1 %collective-permute-done.12.refs_3_ = bf16[128,384]{1,0:T(8,128)(2,1)S(1)} collective-permute-done((bf16[128,384]{1,0:T(8,128)(2,1)S(1)}, bf16[128,384]{1,0:T(8,128)(2,1)S(1)}, u32[]{:S(2)}, u32[]{:S(2)}) %collective-permute-start.12) | collective-permute-done | bytes 98336 | tf_op jit(solution)/shard_map/ppermute | solution.py:374
  47.5 1.3 %collective-permute-start.16 = (bf16[128,384]{1,0:T(8,128)(2,1)S(1)}, bf16[128,384]{1,0:T(8,128)(2,1)S(1)}, u32[]{:S(2)}, u32[]{:S(2)}) collective-permute-start(bf16[128,384]{1,0:T(8,128)(2,1)S(1)} %collective-permute-done.12.refs_3_), channel_id=1, source_target_pairs={{0,1},{1,0},{2,3},{3,2},{4,5},{5,4},{6,7},{7,6},{8,9},{9,8},{10,11... | collective-permute-start | bytes 294920 | tf_op jit(solution)/shard_map/ppermute | solution.py:374
  48.8 1.5 %collective-permute-done.11.refs_2_ = bf16[128,384]{1,0:T(8,128)(2,1)S(1)} collective-permute-done((bf16[128,384]{1,0:T(8,128)(2,1)S(1)}, bf16[128,384]{1,0:T(8,128)(2,1)S(1)}, u32[]{:S(2)}, u32[]{:S(2)}) %collective-permute-start.11) | collective-permute-done | bytes 98336 | tf_op jit(solution)/shard_map/ppermute | solution.py:374
  50.4 0.5 collective-permute-start.15
  50.8 0.0 collective-permute-done.10.refs_1_
  50.8 0.0 collective-permute-start.14
  50.9 0.9 %shard_map.91.stack = bf16[448,1024]{1,0:T(8,128)(2,1)S(1)} custom-call(bf16[96,128]{1,0:T(8,128)(2,1)S(1)} %get-tuple-element.44.refs_0_, bf16[96,128]{1,0:T(8,128)(2,1)S(1)} %collective-permute-done.4.refs_1_, bf16[96,128]{1,0:T(8,128)(2,1)S(1)} %collective-permute-done.6.refs_2_, bf16[96,128]{1,0:T(8,128)(2,1)S(1)} %collective-permute-done.8.refs_3_, ...), custom_call_target="tpu_custom_call" | custom-call | tf_op jit(solution)/shard_map/pallas_call | solution.py:350
  51.8 0.0 collective-permute-done.13.refs_4_
  51.8 0.0 collective-permute-done.16.refs_7_
  51.8 0.0 collective-permute-done.15.refs_6_
  51.8 0.3 collective-permute-done.14.refs_5_
  52.1 0.6 shard_map.92
  52.8 1.0 %collective-permute-start.17 = (bf16[224,384]{1,0:T(8,128)(2,1)S(1)}, bf16[224,384]{1,0:T(8,128)(2,1)S(1)}, u32[]{:S(2)}, u32[]{:S(2)}) collective-permute-start(bf16[224,384]{1,0:T(8,128)(2,1)S(1)} %get-tuple-element.50), channel_id=1, source_target_pairs={{0,6},{1,25},{2,4},{3,27},{4,2},{5,29},{6,0},{7,31},{8,14},{9,17},... | collective-permute-start | bytes 516104 | tf_op jit(solution)/shard_map/ppermute | solution.py:374
  53.8 4.8 %collective-permute-done.17.pair = bf16[224,384]{1,0:T(8,128)(2,1)S(1)} collective-permute-done((bf16[224,384]{1,0:T(8,128)(2,1)S(1)}, bf16[224,384]{1,0:T(8,128)(2,1)S(1)}, u32[]{:S(2)}, u32[]{:S(2)}) %collective-permute-start.17) | collective-permute-done | bytes 172064 | tf_op jit(solution)/shard_map/ppermute | solution.py:374
  58.6 1.0 %collective-permute-start.18 = (bf16[224,384]{1,0:T(8,128)(2,1)S(1)}, bf16[224,384]{1,0:T(8,128)(2,1)S(1)}, u32[]{:S(2)}, u32[]{:S(2)}) collective-permute-start(bf16[224,384]{1,0:T(8,128)(2,1)S(1)} %collective-permute-done.17.pair), channel_id=1, source_target_pairs={{0,1},{1,0},{2,3},{3,2},{4,5},{5,4},{6,7},{7,6},{8,9},{9,8},{10,11... | collective-permute-start | bytes 516104 | tf_op jit(solution)/shard_map/ppermute | solution.py:374
  59.7 1.4 %collective-permute-start.19 = (bf16[112,384]{1,0:T(8,128)(2,1)S(1)}, bf16[112,384]{1,0:T(8,128)(2,1)S(1)}, u32[]{:S(2)}, u32[]{:S(2)}) collective-permute-start(bf16[112,384]{1,0:T(8,128)(2,1)S(1)} %get-tuple-element.51), channel_id=1, source_target_pairs={{0,30},{1,31},{2,28},{3,29},{4,26},{5,27},{6,24},{7,25},{8,22},{9,... | collective-permute-start | bytes 258056 | tf_op jit(solution)/shard_map/ppermute | solution.py:374
  61.0 1.6 %shard_map.93 = (bf16[128,384]{1,0:T(8,128)(2,1)}, f32[12,128]{1,0:T(8,128)}) custom-call(bf16[128,384]{1,0:T(8,128)(2,1)S(1)} %collective-permute-done.2.arrived, bf16[128,384]{1,0:T(8,128)(2,1)S(1)} %collective-permute-done.1.arrived.earlier, bf16[128,384]{1,0:T(8,128)(2,1)S(1)} %shard_map.90.refs_8_.refs_0_.dpre, ...), custom_call_target="tpu_custom_call" | custom-call | tf_op jit(solution)/shard_map/pallas_call | solution.py:350
  62.6 4.5 %collective-permute-done.19.diagonal = bf16[112,384]{1,0:T(8,128)(2,1)S(1)} collective-permute-done((bf16[112,384]{1,0:T(8,128)(2,1)S(1)}, bf16[112,384]{1,0:T(8,128)(2,1)S(1)}, u32[]{:S(2)}, u32[]{:S(2)}) %collective-permute-start.19) | collective-permute-done | bytes 86048 | tf_op jit(solution)/shard_map/ppermute | solution.py:374
  67.1 0.0 collective-permute-done.18.crossed
  67.1 0.7 %shard_map.94 = f32[108,1,384]{2,1,0:T(1,128)} custom-call(f32[112,384]{1,0:T(8,128)S(1)} %get-tuple-element.48.own, bf16[224,384]{1,0:T(8,128)(2,1)S(1)} %collective-permute-done.17.pair, bf16[224,384]{1,0:T(8,128)(2,1)S(1)} %collective-permute-done.18.crossed, bf16[112,384]{1,0:T(8,128)(2,1)S(1)} %collective-permute-done.19.diagonal), custom_call_target="tpu_custom_call" | custom-call | tf_op jit(solution)/shard_map/pallas_call | solution.py:350
  (4 shorter events, 0.0 us)
Async XLA Ops:
  19.7 4.3 %collective-permute-start = (bf16[128,384]{1,0:T(8,128)(2,1)S(1)}, bf16[128,384]{1,0:T(8,128)(2,1)S(1)}, u32[]{:S(2)}, u32[]{:S(2)}) collective-permute-start(bf16[128,384]{1,0:T(8,128)(2,1)S(1)} %get-tuple-element.32.order.msg3), channel_id=1, source_target_pairs={{96,64},{32,0},{64,96},{0,32},{97,65},{33,1},{65,97},{1,33},{98,66... | collective-permute-start | bytes 294920 | tf_op jit(solution)/shard_map/ppermute | solution.py:378
  24.0 7.8 %collective-permute-start.1 = (bf16[128,384]{1,0:T(8,128)(2,1)S(1)}, bf16[128,384]{1,0:T(8,128)(2,1)S(1)}, u32[]{:S(2)}, u32[]{:S(2)}) collective-permute-start(bf16[128,384]{1,0:T(8,128)(2,1)S(1)} %get-tuple-element.39.msg2), channel_id=1, source_target_pairs={{64,32},{96,0},{32,64},{0,96},{65,33},{97,1},{33,65},{1,97},{66,34... | collective-permute-start | bytes 294920 | tf_op jit(solution)/shard_map/ppermute | solution.py:378
  31.8 10.7 %collective-permute-start.2 = (bf16[128,384]{1,0:T(8,128)(2,1)S(1)}, bf16[128,384]{1,0:T(8,128)(2,1)S(1)}, u32[]{:S(2)}, u32[]{:S(2)}) collective-permute-start(bf16[128,384]{1,0:T(8,128)(2,1)S(1)} %get-tuple-element.40.msg1), channel_id=1, source_target_pairs={{32,0},{96,64},{0,32},{64,96},{33,1},{97,65},{1,33},{65,97},{34,2}... | collective-permute-start | bytes 294920 | tf_op jit(solution)/shard_map/ppermute | solution.py:378
  33.5 5.6 %collective-permute-start.4 = (bf16[96,128]{1,0:T(8,128)(2,1)S(1)}, bf16[96,128]{1,0:T(8,128)(2,1)S(1)}, u32[]{:S(2)}, u32[]{:S(2)}) collective-permute-start(bf16[96,128]{1,0:T(8,128)(2,1)S(1)} %get-tuple-element.45), channel_id=1, source_target_pairs={{0,2},{1,3},{2,0},{3,1},{4,6},{5,7},{6,4},{7,5},{8,10},{9,11},{10,... | collective-permute-start | bytes 73736 | tf_op jit(solution)/shard_map/ppermute | solution.py:374
  34.0 5.5 %collective-permute-start.6 = (bf16[96,128]{1,0:T(8,128)(2,1)S(1)}, bf16[96,128]{1,0:T(8,128)(2,1)S(1)}, u32[]{:S(2)}, u32[]{:S(2)}) collective-permute-start(bf16[96,128]{1,0:T(8,128)(2,1)S(1)} %get-tuple-element.46), channel_id=1, source_target_pairs={{0,8},{1,9},{2,10},{3,11},{4,12},{5,13},{6,14},{7,15},{8,0},{9,1},... | collective-permute-start | bytes 73736 | tf_op jit(solution)/shard_map/ppermute | solution.py:374
  34.3 5.8 %collective-permute-start.8 = (bf16[96,128]{1,0:T(8,128)(2,1)S(1)}, bf16[96,128]{1,0:T(8,128)(2,1)S(1)}, u32[]{:S(2)}, u32[]{:S(2)}) collective-permute-start(bf16[96,128]{1,0:T(8,128)(2,1)S(1)} %get-tuple-element.47), channel_id=1, source_target_pairs={{0,10},{1,11},{2,8},{3,9},{4,14},{5,15},{6,12},{7,13},{8,2},{9,3},... | collective-permute-start | bytes 73736 | tf_op jit(solution)/shard_map/ppermute | solution.py:374
  36.2 5.5 %collective-permute-start.3 = (bf16[96,128]{1,0:T(8,128)(2,1)S(1)}, bf16[96,128]{1,0:T(8,128)(2,1)S(1)}, u32[]{:S(2)}, u32[]{:S(2)}) collective-permute-start(bf16[96,128]{1,0:T(8,128)(2,1)S(1)} %get-tuple-element.44.refs_0_), channel_id=1, source_target_pairs={{0,1},{1,0},{2,3},{3,2},{4,5},{5,4},{6,7},{7,6},{8,9},{9,8},{10,11... | collective-permute-start | bytes 73736 | tf_op jit(solution)/shard_map/ppermute | solution.py:374
  39.2 2.5 %collective-permute-start.5 = (bf16[96,128]{1,0:T(8,128)(2,1)S(1)}, bf16[96,128]{1,0:T(8,128)(2,1)S(1)}, u32[]{:S(2)}, u32[]{:S(2)}) collective-permute-start(bf16[96,128]{1,0:T(8,128)(2,1)S(1)} %collective-permute-done.4.refs_1_), channel_id=1, source_target_pairs={{0,1},{1,0},{2,3},{3,2},{4,5},{5,4},{6,7},{7,6},{8,9},{9,8},{10,11... | collective-permute-start | bytes 73736 | tf_op jit(solution)/shard_map/ppermute | solution.py:374
  39.5 2.2 %collective-permute-start.7 = (bf16[96,128]{1,0:T(8,128)(2,1)S(1)}, bf16[96,128]{1,0:T(8,128)(2,1)S(1)}, u32[]{:S(2)}, u32[]{:S(2)}) collective-permute-start(bf16[96,128]{1,0:T(8,128)(2,1)S(1)} %collective-permute-done.6.refs_2_), channel_id=1, source_target_pairs={{0,1},{1,0},{2,3},{3,2},{4,5},{5,4},{6,7},{7,6},{8,9},{9,8},{10,11... | collective-permute-start | bytes 73736 | tf_op jit(solution)/shard_map/ppermute | solution.py:374
  40.2 2.4 %collective-permute-start.9 = (bf16[96,128]{1,0:T(8,128)(2,1)S(1)}, bf16[96,128]{1,0:T(8,128)(2,1)S(1)}, u32[]{:S(2)}, u32[]{:S(2)}) collective-permute-start(bf16[96,128]{1,0:T(8,128)(2,1)S(1)} %collective-permute-done.8.refs_3_), channel_id=1, source_target_pairs={{0,1},{1,0},{2,3},{3,2},{4,5},{5,4},{6,7},{7,6},{8,9},{9,8},{10,11... | collective-permute-start | bytes 73736 | tf_op jit(solution)/shard_map/ppermute | solution.py:374
  42.5 5.0 %collective-permute-start.12 = (bf16[128,384]{1,0:T(8,128)(2,1)S(1)}, bf16[128,384]{1,0:T(8,128)(2,1)S(1)}, u32[]{:S(2)}, u32[]{:S(2)}) collective-permute-start(bf16[128,384]{1,0:T(8,128)(2,1)S(1)} %shard_map.90.refs_8_.refs_0_.dpre), channel_id=1, source_target_pairs={{0,10},{1,11},{2,8},{3,9},{4,14},{5,15},{6,12},{7,13},{8,2},{9,3},... | collective-permute-start | bytes 294920 | tf_op jit(solution)/shard_map/ppermute | solution.py:374
  44.6 5.8 %collective-permute-start.11 = (bf16[128,384]{1,0:T(8,128)(2,1)S(1)}, bf16[128,384]{1,0:T(8,128)(2,1)S(1)}, u32[]{:S(2)}, u32[]{:S(2)}) collective-permute-start(bf16[128,384]{1,0:T(8,128)(2,1)S(1)} %shard_map.90.refs_8_.refs_0_.dpre), channel_id=1, source_target_pairs={{0,8},{1,9},{2,10},{3,11},{4,12},{5,13},{6,14},{7,15},{8,0},{9,1},... | collective-permute-start | bytes 294920 | tf_op jit(solution)/shard_map/ppermute | solution.py:374
  44.9 6.0 %collective-permute-start.10 = (bf16[128,384]{1,0:T(8,128)(2,1)S(1)}, bf16[128,384]{1,0:T(8,128)(2,1)S(1)}, u32[]{:S(2)}, u32[]{:S(2)}) collective-permute-start(bf16[128,384]{1,0:T(8,128)(2,1)S(1)} %shard_map.90.refs_8_.refs_0_.dpre), channel_id=1, source_target_pairs={{0,2},{1,3},{2,0},{3,1},{4,6},{5,7},{6,4},{7,5},{8,10},{9,11},{10,... | collective-permute-start | bytes 294920 | tf_op jit(solution)/shard_map/ppermute | solution.py:374
  45.3 6.5 %collective-permute-start.13 = (bf16[128,384]{1,0:T(8,128)(2,1)S(1)}, bf16[128,384]{1,0:T(8,128)(2,1)S(1)}, u32[]{:S(2)}, u32[]{:S(2)}) collective-permute-start(bf16[128,384]{1,0:T(8,128)(2,1)S(1)} %shard_map.90.refs_8_.refs_0_.dpre), channel_id=1, source_target_pairs={{0,1},{1,0},{2,3},{3,2},{4,5},{5,4},{6,7},{7,6},{8,9},{9,8},{10,11... | collective-permute-start | bytes 294920 | tf_op jit(solution)/shard_map/ppermute | solution.py:374
  47.5 4.3 %collective-permute-start.16 = (bf16[128,384]{1,0:T(8,128)(2,1)S(1)}, bf16[128,384]{1,0:T(8,128)(2,1)S(1)}, u32[]{:S(2)}, u32[]{:S(2)}) collective-permute-start(bf16[128,384]{1,0:T(8,128)(2,1)S(1)} %collective-permute-done.12.refs_3_), channel_id=1, source_target_pairs={{0,1},{1,0},{2,3},{3,2},{4,5},{5,4},{6,7},{7,6},{8,9},{9,8},{10,11... | collective-permute-start | bytes 294920 | tf_op jit(solution)/shard_map/ppermute | solution.py:374
  50.4 1.5 %collective-permute-start.15 = (bf16[128,384]{1,0:T(8,128)(2,1)S(1)}, bf16[128,384]{1,0:T(8,128)(2,1)S(1)}, u32[]{:S(2)}, u32[]{:S(2)}) collective-permute-start(bf16[128,384]{1,0:T(8,128)(2,1)S(1)} %collective-permute-done.11.refs_2_), channel_id=1, source_target_pairs={{0,1},{1,0},{2,3},{3,2},{4,5},{5,4},{6,7},{7,6},{8,9},{9,8},{10,11... | collective-permute-start | bytes 294920 | tf_op jit(solution)/shard_map/ppermute | solution.py:374
  50.8 1.3 %collective-permute-start.14 = (bf16[128,384]{1,0:T(8,128)(2,1)S(1)}, bf16[128,384]{1,0:T(8,128)(2,1)S(1)}, u32[]{:S(2)}, u32[]{:S(2)}) collective-permute-start(bf16[128,384]{1,0:T(8,128)(2,1)S(1)} %collective-permute-done.10.refs_1_), channel_id=1, source_target_pairs={{0,1},{1,0},{2,3},{3,2},{4,5},{5,4},{6,7},{7,6},{8,9},{9,8},{10,11... | collective-permute-start | bytes 294920 | tf_op jit(solution)/shard_map/ppermute | solution.py:374
  52.8 5.8 %collective-permute-start.17 = (bf16[224,384]{1,0:T(8,128)(2,1)S(1)}, bf16[224,384]{1,0:T(8,128)(2,1)S(1)}, u32[]{:S(2)}, u32[]{:S(2)}) collective-permute-start(bf16[224,384]{1,0:T(8,128)(2,1)S(1)} %get-tuple-element.50), channel_id=1, source_target_pairs={{0,6},{1,25},{2,4},{3,27},{4,2},{5,29},{6,0},{7,31},{8,14},{9,17},... | collective-permute-start | bytes 516104 | tf_op jit(solution)/shard_map/ppermute | solution.py:374
  58.6 8.5 %collective-permute-start.18 = (bf16[224,384]{1,0:T(8,128)(2,1)S(1)}, bf16[224,384]{1,0:T(8,128)(2,1)S(1)}, u32[]{:S(2)}, u32[]{:S(2)}) collective-permute-start(bf16[224,384]{1,0:T(8,128)(2,1)S(1)} %collective-permute-done.17.pair), channel_id=1, source_target_pairs={{0,1},{1,0},{2,3},{3,2},{4,5},{5,4},{6,7},{7,6},{8,9},{9,8},{10,11... | collective-permute-start | bytes 516104 | tf_op jit(solution)/shard_map/ppermute | solution.py:374
  59.7 7.4 %collective-permute-start.19 = (bf16[112,384]{1,0:T(8,128)(2,1)S(1)}, bf16[112,384]{1,0:T(8,128)(2,1)S(1)}, u32[]{:S(2)}, u32[]{:S(2)}) collective-permute-start(bf16[112,384]{1,0:T(8,128)(2,1)S(1)} %get-tuple-element.51), channel_id=1, source_target_pairs={{0,30},{1,31},{2,28},{3,29},{4,26},{5,27},{6,24},{7,25},{8,22},{9,... | collective-permute-start | bytes 258056 | tf_op jit(solution)/shard_map/ppermute | solution.py:374

commit v11 on v10

--- a/solution.py
+++ b/solution.py
@@ -58,15 +58,10 @@
 
 def conv_back(dpre, w):
     cols = column_shifts(dpre)
-    total = None
-    for kh in range(3):
-        lhs = jnp.concatenate(
-            [row_shift(cols[2 - kw], 1 - kh).astype(bf16) for kw in range(3)], axis=1
-        )
-        rhs = jnp.concatenate([w[kh, kw] for kw in range(3)], axis=1)
-        part = mm(lhs, rhs, NT)
-        total = part if total is None else total + part
-    return total
+    taps = [(kh, kw) for kh in range(3) for kw in range(3)]
+    lhs = [row_shift(cols[2 - kw], 1 - kh).astype(bf16) for kh, kw in taps]
+    rhs = [w[kh, kw] for kh, kw in taps]
+    return mm(jnp.concatenate(lhs, axis=1), jnp.concatenate(rhs, axis=1), NT)
 
 
 def forward_kernel(

time: 68 us -> 67.9 us (level)
  no operation moved by 1% of the time
where the time goes in v11:
time: 67.9 us; the launch traced here: 67.8 us
  starting transfers between devices  26.4 us (39%)
  waiting for transfers between devices  17.4 us (26%)
  blocking collectives  16 us (24%)
  Pallas kernels  6.7 us (10%)
  between operations  1.36 us (2%)
    ppermute x17, starting transfers between devices, swap(): return lax.ppermute(value, 'dp', pairs_of)  17.3 us
    all_to_all x1, blocking collectives, per_device(): lax.all_to_all(announce.reshape(32, 8, 256), 'dp', 0, 0, tiled=True)  16 us
    ppermute x17, waiting for transfers between devices, swap(): return lax.ppermute(value, 'dp', pairs_of)  13.1 us
    ppermute x3, starting transfers between devices, relayed(): return lax.ppermute(value, 'section', both)  9.08 us
    pallas_call x10, Pallas kernels, with_operands(): run(*[value if space is SMEM else pltpu.with_memory_space_constraint(valu...  6.7 us
    ppermute x3, waiting for transfers between devices, relayed(): return lax.ppermute(value, 'section', both)  4.31 us
  transfers between devices with their start and end apart: 20, of which 8 were waited for; matrix products, arithmetic and copies ran while one was open for 0% of the time, Pallas kernels for 4%

profile of v11, /device:TPU:1, one launch (start us, length us, event | category | flops | bytes accessed | tf_op | source)
XLA Modules:
  0.0 67.8 jit_solution(6414359599959995909)
XLA Ops:
  1.3 2.5 %shard_map.85 = (f32[128,384]{1,0:T(8,128)S(1)}, bf16[256,256]{1,0:T(8,128)(2,1)S(1)}, bf16[128,384]{1,0:T(8,128)(2,1)S(1)}, bf16[3,3,384,384]{3,2,1,0:T(8,128)(2,1)S(1)}, bf16[384,512]{1,0:T(8,128)(2,1)S(1)}) custom-call(bf16[128,384]{1,0:T(8,128)(2,1)} %bitcast.12, bf16[3,3,384,384]{3,2,1,0:T(8,128)(2,1)} %bitcast.10, bf16[384,512]{1,0:T(8,128)(2,1)} %head_hbm.1, ...), custom_call_target="tpu_custom_call" | custom-call | tf_op jit(solution)/shard_map/pallas_call | solution.py:345
  3.7 16.0 %all_to_all.5 = bf16[32,8,256]{2,1,0:T(8,128)(2,1)S(1)} all-to-all(bf16[32,8,256]{2,1,0:T(8,128)(2,1)S(1)} %bitcast.9), channel_id=1, replica_groups=mesh['section'=4,'dp'=32] {'dp'}, dimensions={0} | all-to-all | bytes 262144 | tf_op jit(solution)/shard_map/all_to_all | solution.py:394
  19.7 1.6 %collective-permute-start = (bf16[128,384]{1,0:T(8,128)(2,1)S(1)}, bf16[128,384]{1,0:T(8,128)(2,1)S(1)}, u32[]{:S(2)}, u32[]{:S(2)}) collective-permute-start(bf16[128,384]{1,0:T(8,128)(2,1)S(1)} %get-tuple-element.32.order.msg3), channel_id=1, source_target_pairs={{96,64},{32,0},{64,96},{0,32},{97,65},{33,1},{65,97},{1,33},{98,66... | collective-permute-start | bytes 294920 | tf_op jit(solution)/shard_map/ppermute | solution.py:373
  21.4 0.3 shard_map.87
  21.7 2.3 %collective-permute-done.arrived = bf16[128,384]{1,0:T(8,128)(2,1)S(1)} collective-permute-done((bf16[128,384]{1,0:T(8,128)(2,1)S(1)}, bf16[128,384]{1,0:T(8,128)(2,1)S(1)}, u32[]{:S(2)}, u32[]{:S(2)}) %collective-permute-start) | collective-permute-done | bytes 98336 | tf_op jit(solution)/shard_map/ppermute | solution.py:373
  24.0 5.8 %collective-permute-start.1 = (bf16[128,384]{1,0:T(8,128)(2,1)S(1)}, bf16[128,384]{1,0:T(8,128)(2,1)S(1)}, u32[]{:S(2)}, u32[]{:S(2)}) collective-permute-start(bf16[128,384]{1,0:T(8,128)(2,1)S(1)} %get-tuple-element.39.msg2), channel_id=1, source_target_pairs={{64,32},{96,0},{32,64},{0,96},{65,33},{97,1},{33,65},{1,97},{66,34... | collective-permute-start | bytes 294920 | tf_op jit(solution)/shard_map/ppermute | solution.py:373
  29.8 2.0 %collective-permute-done.1.arrived.earlier = bf16[128,384]{1,0:T(8,128)(2,1)S(1)} collective-permute-done((bf16[128,384]{1,0:T(8,128)(2,1)S(1)}, bf16[128,384]{1,0:T(8,128)(2,1)S(1)}, u32[]{:S(2)}, u32[]{:S(2)}) %collective-permute-start.1) | collective-permute-done | bytes 98336 | tf_op jit(solution)/shard_map/ppermute | solution.py:373
  31.8 1.7 %collective-permute-start.2 = (bf16[128,384]{1,0:T(8,128)(2,1)S(1)}, bf16[128,384]{1,0:T(8,128)(2,1)S(1)}, u32[]{:S(2)}, u32[]{:S(2)}) collective-permute-start(bf16[128,384]{1,0:T(8,128)(2,1)S(1)} %get-tuple-element.40.msg1), channel_id=1, source_target_pairs={{32,0},{96,64},{0,32},{64,96},{33,1},{97,65},{1,33},{65,97},{34,2}... | collective-permute-start | bytes 294920 | tf_op jit(solution)/shard_map/ppermute | solution.py:373
  33.5 0.4 collective-permute-start.4
  33.9 0.4 collective-permute-start.6
  34.3 1.9 %collective-permute-start.8 = (bf16[96,128]{1,0:T(8,128)(2,1)S(1)}, bf16[96,128]{1,0:T(8,128)(2,1)S(1)}, u32[]{:S(2)}, u32[]{:S(2)}) collective-permute-start(bf16[96,128]{1,0:T(8,128)(2,1)S(1)} %get-tuple-element.47), channel_id=1, source_target_pairs={{0,10},{1,11},{2,8},{3,9},{4,14},{5,15},{6,12},{7,13},{8,2},{9,3},... | collective-permute-start | bytes 73736 | tf_op jit(solution)/shard_map/ppermute | solution.py:369
  36.1 3.0 %collective-permute-start.3 = (bf16[96,128]{1,0:T(8,128)(2,1)S(1)}, bf16[96,128]{1,0:T(8,128)(2,1)S(1)}, u32[]{:S(2)}, u32[]{:S(2)}) collective-permute-start(bf16[96,128]{1,0:T(8,128)(2,1)S(1)} %get-tuple-element.44.refs_0_), channel_id=1, source_target_pairs={{0,1},{1,0},{2,3},{3,2},{4,5},{5,4},{6,7},{7,6},{8,9},{9,8},{10,11... | collective-permute-start | bytes 73736 | tf_op jit(solution)/shard_map/ppermute | solution.py:369
  39.1 0.0 collective-permute-done.4.refs_1_
  39.1 0.3 collective-permute-start.5
  39.4 0.0 collective-permute-done.6.refs_2_
  39.4 0.7 collective-permute-start.7
  40.1 0.0 collective-permute-done.8.refs_3_
  40.1 1.5 %collective-permute-start.9 = (bf16[96,128]{1,0:T(8,128)(2,1)S(1)}, bf16[96,128]{1,0:T(8,128)(2,1)S(1)}, u32[]{:S(2)}, u32[]{:S(2)}) collective-permute-start(bf16[96,128]{1,0:T(8,128)(2,1)S(1)} %collective-permute-done.8.refs_3_), channel_id=1, source_target_pairs={{0,1},{1,0},{2,3},{3,2},{4,5},{5,4},{6,7},{7,6},{8,9},{9,8},{10,11... | collective-permute-start | bytes 73736 | tf_op jit(solution)/shard_map/ppermute | solution.py:369
  41.6 0.0 collective-permute-done.3.refs_0_.refs_4_
  41.6 0.0 collective-permute-done.5.refs_1_.refs_5_
  41.6 0.0 collective-permute-done.7.refs_2_.refs_6_
  41.6 0.8 %collective-permute-done.9.refs_3_.refs_7_ = bf16[96,128]{1,0:T(8,128)(2,1)S(1)} collective-permute-done((bf16[96,128]{1,0:T(8,128)(2,1)S(1)}, bf16[96,128]{1,0:T(8,128)(2,1)S(1)}, u32[]{:S(2)}, u32[]{:S(2)}) %collective-permute-start.9) | collective-permute-done | bytes 24608 | tf_op jit(solution)/shard_map/ppermute | solution.py:369
  42.5 0.0 collective-permute-done.2.arrived
  42.5 2.0 %collective-permute-start.12 = (bf16[128,384]{1,0:T(8,128)(2,1)S(1)}, bf16[128,384]{1,0:T(8,128)(2,1)S(1)}, u32[]{:S(2)}, u32[]{:S(2)}) collective-permute-start(bf16[128,384]{1,0:T(8,128)(2,1)S(1)} %shard_map.90.refs_8_.refs_0_.dpre), channel_id=1, source_target_pairs={{0,10},{1,11},{2,8},{3,9},{4,14},{5,15},{6,12},{7,13},{8,2},{9,3},... | collective-permute-start | bytes 294920 | tf_op jit(solution)/shard_map/ppermute | solution.py:369
  44.5 0.3 collective-permute-start.11
  44.8 0.4 collective-permute-start.10
  45.2 1.2 %collective-permute-start.13 = (bf16[128,384]{1,0:T(8,128)(2,1)S(1)}, bf16[128,384]{1,0:T(8,128)(2,1)S(1)}, u32[]{:S(2)}, u32[]{:S(2)}) collective-permute-start(bf16[128,384]{1,0:T(8,128)(2,1)S(1)} %shard_map.90.refs_8_.refs_0_.dpre), channel_id=1, source_target_pairs={{0,1},{1,0},{2,3},{3,2},{4,5},{5,4},{6,7},{7,6},{8,9},{9,8},{10,11... | collective-permute-start | bytes 294920 | tf_op jit(solution)/shard_map/ppermute | solution.py:369
  46.4 1.1 %collective-permute-done.12.refs_3_ = bf16[128,384]{1,0:T(8,128)(2,1)S(1)} collective-permute-done((bf16[128,384]{1,0:T(8,128)(2,1)S(1)}, bf16[128,384]{1,0:T(8,128)(2,1)S(1)}, u32[]{:S(2)}, u32[]{:S(2)}) %collective-permute-start.12) | collective-permute-done | bytes 98336 | tf_op jit(solution)/shard_map/ppermute | solution.py:369
  47.5 1.3 %collective-permute-start.16 = (bf16[128,384]{1,0:T(8,128)(2,1)S(1)}, bf16[128,384]{1,0:T(8,128)(2,1)S(1)}, u32[]{:S(2)}, u32[]{:S(2)}) collective-permute-start(bf16[128,384]{1,0:T(8,128)(2,1)S(1)} %collective-permute-done.12.refs_3_), channel_id=1, source_target_pairs={{0,1},{1,0},{2,3},{3,2},{4,5},{5,4},{6,7},{7,6},{8,9},{9,8},{10,11... | collective-permute-start | bytes 294920 | tf_op jit(solution)/shard_map/ppermute | solution.py:369
  48.8 1.5 %collective-permute-done.11.refs_2_ = bf16[128,384]{1,0:T(8,128)(2,1)S(1)} collective-permute-done((bf16[128,384]{1,0:T(8,128)(2,1)S(1)}, bf16[128,384]{1,0:T(8,128)(2,1)S(1)}, u32[]{:S(2)}, u32[]{:S(2)}) %collective-permute-start.11) | collective-permute-done | bytes 98336 | tf_op jit(solution)/shard_map/ppermute | solution.py:369
  50.3 0.5 collective-permute-start.15
  50.8 0.0 collective-permute-done.10.refs_1_
  50.8 0.0 collective-permute-start.14
  50.8 0.9 %shard_map.91.stack = bf16[448,1024]{1,0:T(8,128)(2,1)S(1)} custom-call(bf16[96,128]{1,0:T(8,128)(2,1)S(1)} %get-tuple-element.44.refs_0_, bf16[96,128]{1,0:T(8,128)(2,1)S(1)} %collective-permute-done.4.refs_1_, bf16[96,128]{1,0:T(8,128)(2,1)S(1)} %collective-permute-done.6.refs_2_, bf16[96,128]{1,0:T(8,128)(2,1)S(1)} %collective-permute-done.8.refs_3_, ...), custom_call_target="tpu_custom_call" | custom-call | tf_op jit(solution)/shard_map/pallas_call | solution.py:345
  51.7 0.0 collective-permute-done.13.refs_4_
  51.7 0.0 collective-permute-done.16.refs_7_
  51.8 0.0 collective-permute-done.15.refs_6_
  51.8 0.3 collective-permute-done.14.refs_5_
  52.1 0.6 shard_map.92
  52.7 1.0 %collective-permute-start.17 = (bf16[224,384]{1,0:T(8,128)(2,1)S(1)}, bf16[224,384]{1,0:T(8,128)(2,1)S(1)}, u32[]{:S(2)}, u32[]{:S(2)}) collective-permute-start(bf16[224,384]{1,0:T(8,128)(2,1)S(1)} %get-tuple-element.50), channel_id=1, source_target_pairs={{0,6},{1,25},{2,4},{3,27},{4,2},{5,29},{6,0},{7,31},{8,14},{9,17},... | collective-permute-start | bytes 516104 | tf_op jit(solution)/shard_map/ppermute | solution.py:369
  53.8 4.8 %collective-permute-done.17.pair = bf16[224,384]{1,0:T(8,128)(2,1)S(1)} collective-permute-done((bf16[224,384]{1,0:T(8,128)(2,1)S(1)}, bf16[224,384]{1,0:T(8,128)(2,1)S(1)}, u32[]{:S(2)}, u32[]{:S(2)}) %collective-permute-start.17) | collective-permute-done | bytes 172064 | tf_op jit(solution)/shard_map/ppermute | solution.py:369
  58.6 1.0 %collective-permute-start.18 = (bf16[224,384]{1,0:T(8,128)(2,1)S(1)}, bf16[224,384]{1,0:T(8,128)(2,1)S(1)}, u32[]{:S(2)}, u32[]{:S(2)}) collective-permute-start(bf16[224,384]{1,0:T(8,128)(2,1)S(1)} %collective-permute-done.17.pair), channel_id=1, source_target_pairs={{0,1},{1,0},{2,3},{3,2},{4,5},{5,4},{6,7},{7,6},{8,9},{9,8},{10,11... | collective-permute-start | bytes 516104 | tf_op jit(solution)/shard_map/ppermute | solution.py:369
  59.6 1.4 %collective-permute-start.19 = (bf16[112,384]{1,0:T(8,128)(2,1)S(1)}, bf16[112,384]{1,0:T(8,128)(2,1)S(1)}, u32[]{:S(2)}, u32[]{:S(2)}) collective-permute-start(bf16[112,384]{1,0:T(8,128)(2,1)S(1)} %get-tuple-element.51), channel_id=1, source_target_pairs={{0,30},{1,31},{2,28},{3,29},{4,26},{5,27},{6,24},{7,25},{8,22},{9,... | collective-permute-start | bytes 258056 | tf_op jit(solution)/shard_map/ppermute | solution.py:369
  61.0 1.6 %shard_map.93 = (bf16[128,384]{1,0:T(8,128)(2,1)}, f32[12,128]{1,0:T(8,128)}) custom-call(bf16[128,384]{1,0:T(8,128)(2,1)S(1)} %collective-permute-done.2.arrived, bf16[128,384]{1,0:T(8,128)(2,1)S(1)} %collective-permute-done.1.arrived.earlier, bf16[128,384]{1,0:T(8,128)(2,1)S(1)} %shard_map.90.refs_8_.refs_0_.dpre, ...), custom_call_target="tpu_custom_call" | custom-call | tf_op jit(solution)/shard_map/pallas_call | solution.py:345
  62.6 4.5 %collective-permute-done.19.diagonal = bf16[112,384]{1,0:T(8,128)(2,1)S(1)} collective-permute-done((bf16[112,384]{1,0:T(8,128)(2,1)S(1)}, bf16[112,384]{1,0:T(8,128)(2,1)S(1)}, u32[]{:S(2)}, u32[]{:S(2)}) %collective-permute-start.19) | collective-permute-done | bytes 86048 | tf_op jit(solution)/shard_map/ppermute | solution.py:369
  67.0 0.0 collective-permute-done.18.crossed
  67.0 0.7 %shard_map.94 = f32[108,1,384]{2,1,0:T(1,128)} custom-call(f32[112,384]{1,0:T(8,128)S(1)} %get-tuple-element.48.own, bf16[224,384]{1,0:T(8,128)(2,1)S(1)} %collective-permute-done.17.pair, bf16[224,384]{1,0:T(8,128)(2,1)S(1)} %collective-permute-done.18.crossed, bf16[112,384]{1,0:T(8,128)(2,1)S(1)} %collective-permute-done.19.diagonal), custom_call_target="tpu_custom_call" | custom-call | tf_op jit(solution)/shard_map/pallas_call | solution.py:345
  (4 shorter events, 0.0 us)
Async XLA Ops:
  19.7 4.3 %collective-permute-start = (bf16[128,384]{1,0:T(8,128)(2,1)S(1)}, bf16[128,384]{1,0:T(8,128)(2,1)S(1)}, u32[]{:S(2)}, u32[]{:S(2)}) collective-permute-start(bf16[128,384]{1,0:T(8,128)(2,1)S(1)} %get-tuple-element.32.order.msg3), channel_id=1, source_target_pairs={{96,64},{32,0},{64,96},{0,32},{97,65},{33,1},{65,97},{1,33},{98,66... | collective-permute-start | bytes 294920 | tf_op jit(solution)/shard_map/ppermute | solution.py:373
  24.0 7.8 %collective-permute-start.1 = (bf16[128,384]{1,0:T(8,128)(2,1)S(1)}, bf16[128,384]{1,0:T(8,128)(2,1)S(1)}, u32[]{:S(2)}, u32[]{:S(2)}) collective-permute-start(bf16[128,384]{1,0:T(8,128)(2,1)S(1)} %get-tuple-element.39.msg2), channel_id=1, source_target_pairs={{64,32},{96,0},{32,64},{0,96},{65,33},{97,1},{33,65},{1,97},{66,34... | collective-permute-start | bytes 294920 | tf_op jit(solution)/shard_map/ppermute | solution.py:373
  31.8 10.7 %collective-permute-start.2 = (bf16[128,384]{1,0:T(8,128)(2,1)S(1)}, bf16[128,384]{1,0:T(8,128)(2,1)S(1)}, u32[]{:S(2)}, u32[]{:S(2)}) collective-permute-start(bf16[128,384]{1,0:T(8,128)(2,1)S(1)} %get-tuple-element.40.msg1), channel_id=1, source_target_pairs={{32,0},{96,64},{0,32},{64,96},{33,1},{97,65},{1,33},{65,97},{34,2}... | collective-permute-start | bytes 294920 | tf_op jit(solution)/shard_map/ppermute | solution.py:373
  33.5 5.6 %collective-permute-start.4 = (bf16[96,128]{1,0:T(8,128)(2,1)S(1)}, bf16[96,128]{1,0:T(8,128)(2,1)S(1)}, u32[]{:S(2)}, u32[]{:S(2)}) collective-permute-start(bf16[96,128]{1,0:T(8,128)(2,1)S(1)} %get-tuple-element.45), channel_id=1, source_target_pairs={{0,2},{1,3},{2,0},{3,1},{4,6},{5,7},{6,4},{7,5},{8,10},{9,11},{10,... | collective-permute-start | bytes 73736 | tf_op jit(solution)/shard_map/ppermute | solution.py:369
  33.9 5.5 %collective-permute-start.6 = (bf16[96,128]{1,0:T(8,128)(2,1)S(1)}, bf16[96,128]{1,0:T(8,128)(2,1)S(1)}, u32[]{:S(2)}, u32[]{:S(2)}) collective-permute-start(bf16[96,128]{1,0:T(8,128)(2,1)S(1)} %get-tuple-element.46), channel_id=1, source_target_pairs={{0,8},{1,9},{2,10},{3,11},{4,12},{5,13},{6,14},{7,15},{8,0},{9,1},... | collective-permute-start | bytes 73736 | tf_op jit(solution)/shard_map/ppermute | solution.py:369
  34.3 5.8 %collective-permute-start.8 = (bf16[96,128]{1,0:T(8,128)(2,1)S(1)}, bf16[96,128]{1,0:T(8,128)(2,1)S(1)}, u32[]{:S(2)}, u32[]{:S(2)}) collective-permute-start(bf16[96,128]{1,0:T(8,128)(2,1)S(1)} %get-tuple-element.47), channel_id=1, source_target_pairs={{0,10},{1,11},{2,8},{3,9},{4,14},{5,15},{6,12},{7,13},{8,2},{9,3},... | collective-permute-start | bytes 73736 | tf_op jit(solution)/shard_map/ppermute | solution.py:369
  36.1 5.5 %collective-permute-start.3 = (bf16[96,128]{1,0:T(8,128)(2,1)S(1)}, bf16[96,128]{1,0:T(8,128)(2,1)S(1)}, u32[]{:S(2)}, u32[]{:S(2)}) collective-permute-start(bf16[96,128]{1,0:T(8,128)(2,1)S(1)} %get-tuple-element.44.refs_0_), channel_id=1, source_target_pairs={{0,1},{1,0},{2,3},{3,2},{4,5},{5,4},{6,7},{7,6},{8,9},{9,8},{10,11... | collective-permute-start | bytes 73736 | tf_op jit(solution)/shard_map/ppermute | solution.py:369
  39.1 2.5 %collective-permute-start.5 = (bf16[96,128]{1,0:T(8,128)(2,1)S(1)}, bf16[96,128]{1,0:T(8,128)(2,1)S(1)}, u32[]{:S(2)}, u32[]{:S(2)}) collective-permute-start(bf16[96,128]{1,0:T(8,128)(2,1)S(1)} %collective-permute-done.4.refs_1_), channel_id=1, source_target_pairs={{0,1},{1,0},{2,3},{3,2},{4,5},{5,4},{6,7},{7,6},{8,9},{9,8},{10,11... | collective-permute-start | bytes 73736 | tf_op jit(solution)/shard_map/ppermute | solution.py:369
  39.4 2.2 %collective-permute-start.7 = (bf16[96,128]{1,0:T(8,128)(2,1)S(1)}, bf16[96,128]{1,0:T(8,128)(2,1)S(1)}, u32[]{:S(2)}, u32[]{:S(2)}) collective-permute-start(bf16[96,128]{1,0:T(8,128)(2,1)S(1)} %collective-permute-done.6.refs_2_), channel_id=1, source_target_pairs={{0,1},{1,0},{2,3},{3,2},{4,5},{5,4},{6,7},{7,6},{8,9},{9,8},{10,11... | collective-permute-start | bytes 73736 | tf_op jit(solution)/shard_map/ppermute | solution.py:369
  40.1 2.4 %collective-permute-start.9 = (bf16[96,128]{1,0:T(8,128)(2,1)S(1)}, bf16[96,128]{1,0:T(8,128)(2,1)S(1)}, u32[]{:S(2)}, u32[]{:S(2)}) collective-permute-start(bf16[96,128]{1,0:T(8,128)(2,1)S(1)} %collective-permute-done.8.refs_3_), channel_id=1, source_target_pairs={{0,1},{1,0},{2,3},{3,2},{4,5},{5,4},{6,7},{7,6},{8,9},{9,8},{10,11... | collective-permute-start | bytes 73736 | tf_op jit(solution)/shard_map/ppermute | solution.py:369
  42.5 5.0 %collective-permute-start.12 = (bf16[128,384]{1,0:T(8,128)(2,1)S(1)}, bf16[128,384]{1,0:T(8,128)(2,1)S(1)}, u32[]{:S(2)}, u32[]{:S(2)}) collective-permute-start(bf16[128,384]{1,0:T(8,128)(2,1)S(1)} %shard_map.90.refs_8_.refs_0_.dpre), channel_id=1, source_target_pairs={{0,10},{1,11},{2,8},{3,9},{4,14},{5,15},{6,12},{7,13},{8,2},{9,3},... | collective-permute-start | bytes 294920 | tf_op jit(solution)/shard_map/ppermute | solution.py:369
  44.5 5.8 %collective-permute-start.11 = (bf16[128,384]{1,0:T(8,128)(2,1)S(1)}, bf16[128,384]{1,0:T(8,128)(2,1)S(1)}, u32[]{:S(2)}, u32[]{:S(2)}) collective-permute-start(bf16[128,384]{1,0:T(8,128)(2,1)S(1)} %shard_map.90.refs_8_.refs_0_.dpre), channel_id=1, source_target_pairs={{0,8},{1,9},{2,10},{3,11},{4,12},{5,13},{6,14},{7,15},{8,0},{9,1},... | collective-permute-start | bytes 294920 | tf_op jit(solution)/shard_map/ppermute | solution.py:369
  44.8 6.0 %collective-permute-start.10 = (bf16[128,384]{1,0:T(8,128)(2,1)S(1)}, bf16[128,384]{1,0:T(8,128)(2,1)S(1)}, u32[]{:S(2)}, u32[]{:S(2)}) collective-permute-start(bf16[128,384]{1,0:T(8,128)(2,1)S(1)} %shard_map.90.refs_8_.refs_0_.dpre), channel_id=1, source_target_pairs={{0,2},{1,3},{2,0},{3,1},{4,6},{5,7},{6,4},{7,5},{8,10},{9,11},{10,... | collective-permute-start | bytes 294920 | tf_op jit(solution)/shard_map/ppermute | solution.py:369
  45.2 6.5 %collective-permute-start.13 = (bf16[128,384]{1,0:T(8,128)(2,1)S(1)}, bf16[128,384]{1,0:T(8,128)(2,1)S(1)}, u32[]{:S(2)}, u32[]{:S(2)}) collective-permute-start(bf16[128,384]{1,0:T(8,128)(2,1)S(1)} %shard_map.90.refs_8_.refs_0_.dpre), channel_id=1, source_target_pairs={{0,1},{1,0},{2,3},{3,2},{4,5},{5,4},{6,7},{7,6},{8,9},{9,8},{10,11... | collective-permute-start | bytes 294920 | tf_op jit(solution)/shard_map/ppermute | solution.py:369
  47.5 4.3 %collective-permute-start.16 = (bf16[128,384]{1,0:T(8,128)(2,1)S(1)}, bf16[128,384]{1,0:T(8,128)(2,1)S(1)}, u32[]{:S(2)}, u32[]{:S(2)}) collective-permute-start(bf16[128,384]{1,0:T(8,128)(2,1)S(1)} %collective-permute-done.12.refs_3_), channel_id=1, source_target_pairs={{0,1},{1,0},{2,3},{3,2},{4,5},{5,4},{6,7},{7,6},{8,9},{9,8},{10,11... | collective-permute-start | bytes 294920 | tf_op jit(solution)/shard_map/ppermute | solution.py:369
  50.3 1.5 %collective-permute-start.15 = (bf16[128,384]{1,0:T(8,128)(2,1)S(1)}, bf16[128,384]{1,0:T(8,128)(2,1)S(1)}, u32[]{:S(2)}, u32[]{:S(2)}) collective-permute-start(bf16[128,384]{1,0:T(8,128)(2,1)S(1)} %collective-permute-done.11.refs_2_), channel_id=1, source_target_pairs={{0,1},{1,0},{2,3},{3,2},{4,5},{5,4},{6,7},{7,6},{8,9},{9,8},{10,11... | collective-permute-start | bytes 294920 | tf_op jit(solution)/shard_map/ppermute | solution.py:369
  50.8 1.3 %collective-permute-start.14 = (bf16[128,384]{1,0:T(8,128)(2,1)S(1)}, bf16[128,384]{1,0:T(8,128)(2,1)S(1)}, u32[]{:S(2)}, u32[]{:S(2)}) collective-permute-start(bf16[128,384]{1,0:T(8,128)(2,1)S(1)} %collective-permute-done.10.refs_1_), channel_id=1, source_target_pairs={{0,1},{1,0},{2,3},{3,2},{4,5},{5,4},{6,7},{7,6},{8,9},{9,8},{10,11... | collective-permute-start | bytes 294920 | tf_op jit(solution)/shard_map/ppermute | solution.py:369
  52.7 5.8 %collective-permute-start.17 = (bf16[224,384]{1,0:T(8,128)(2,1)S(1)}, bf16[224,384]{1,0:T(8,128)(2,1)S(1)}, u32[]{:S(2)}, u32[]{:S(2)}) collective-permute-start(bf16[224,384]{1,0:T(8,128)(2,1)S(1)} %get-tuple-element.50), channel_id=1, source_target_pairs={{0,6},{1,25},{2,4},{3,27},{4,2},{5,29},{6,0},{7,31},{8,14},{9,17},... | collective-permute-start | bytes 516104 | tf_op jit(solution)/shard_map/ppermute | solution.py:369
  58.6 8.5 %collective-permute-start.18 = (bf16[224,384]{1,0:T(8,128)(2,1)S(1)}, bf16[224,384]{1,0:T(8,128)(2,1)S(1)}, u32[]{:S(2)}, u32[]{:S(2)}) collective-permute-start(bf16[224,384]{1,0:T(8,128)(2,1)S(1)} %collective-permute-done.17.pair), channel_id=1, source_target_pairs={{0,1},{1,0},{2,3},{3,2},{4,5},{5,4},{6,7},{7,6},{8,9},{9,8},{10,11... | collective-permute-start | bytes 516104 | tf_op jit(solution)/shard_map/ppermute | solution.py:369
  59.6 7.4 %collective-permute-start.19 = (bf16[112,384]{1,0:T(8,128)(2,1)S(1)}, bf16[112,384]{1,0:T(8,128)(2,1)S(1)}, u32[]{:S(2)}, u32[]{:S(2)}) collective-permute-start(bf16[112,384]{1,0:T(8,128)(2,1)S(1)} %get-tuple-element.51), channel_id=1, source_target_pairs={{0,30},{1,31},{2,28},{3,29},{4,26},{5,27},{6,24},{7,25},{8,22},{9,... | collective-permute-start | bytes 258056 | tf_op jit(solution)/shard_map/ppermute | solution.py:369
